TPU v7x, 32 devices: a whole 2x2x4 slice. The times are simulated.
32 devices in a mesh: groups: 2 (over y), seq: 4 (over z), rep: 2 (over x), fsdp: 2 (over core).
Axes of the slice: x: 2, y: 2, z: 4, core: 2. Of those that a mesh axis runs over, the one named last changes fastest.
Arguments:
- activations: bfloat16 [8, 512, 2048], P(('groups', 'rep', 'fsdp'), 'seq'), parts along dimension 0, may hold values from -6 to 6
- queries: bfloat16 [8, 512, 2048], P(('groups', 'rep', 'fsdp'), 'seq'), parts along dimension 0, may hold values from -102 to 102
- key_weight: bfloat16 [2048, 512], P(('seq', 'fsdp')), may hold values from -0.125 to 0.125
- value_weight: bfloat16 [2048, 512], P(('seq', 'fsdp')), may hold values from -0.125 to 0.125
- segment_ids: int32 [8, 512], P(('groups', 'rep', 'fsdp'), 'seq'), parts along dimension 0, may hold values from 0 to 3, never falling along the last dimension, each value on 1 to 384 neighbouring positions
- out_grad: bfloat16 [8, 512, 2048], P(('groups', 'rep', 'fsdp'), 'seq'), parts along dimension 0, may hold values from -6 to 6
Outputs:
- context: bfloat16 [8, 512, 2048], P(('groups', 'rep', 'fsdp'), 'seq'), parts along dimension 0
- query_grad: bfloat16 [8, 512, 2048], P(('groups', 'rep', 'fsdp'), 'seq'), parts along dimension 0
- input_grad: bfloat16 [8, 512, 2048], P(('groups', 'rep', 'fsdp'), 'seq'), parts along dimension 0
- key_weight_grad: bfloat16 [4096, 512], P(('groups', 'seq', 'fsdp')), parts along dimension 0
- value_weight_grad: bfloat16 [4096, 512], P(('groups', 'seq', 'fsdp')), parts along dimension 0
There are 2 independent parts, one for each index of `groups`. A program takes and returns all parts, laid end to end along the dimension named above; an argument that names none is the same for every part. Nothing has to cross between parts.
Inputs may be any that keep to these rules, and one draw needn't show every extreme that they name: `segment_ids`: document numbers never fall along a sequence; a document covers at most 384 positions.
All inputs are finite; a program needn't handle non-finite values.
Results may differ from a plain program's by a relative error of at most 0.025.
The roundings to bfloat16 on the way count: a program that leaves them out, or rounds other values in their place, can miss the bound.
Values may be sent and summed in bfloat16 or wider, within the bound.
No kernel may reach another device: no remote copies, remote signals or barrier semaphores. Data moves between devices by JAX's collectives and lax.ppermute only.
A program may use at most 64 MiB of HBM per device.

v0:
```python
import math

import jax
import jax.numpy as jnp
from jax import lax
from jax.sharding import PartitionSpec as P

HEADS = 16
KV_HEADS = 4
HEAD_DIM = 128


masked_low = -1e30


def block_mask(seg_all, row_start, col_start, block_width):
    row_pos = row_start + lax.iota(jnp.int32, block_width)
    col_pos = col_start + lax.iota(jnp.int32, block_width)
    seg_rows = lax.dynamic_slice_in_dim(seg_all, row_start, block_width)
    seg_cols = lax.dynamic_slice_in_dim(seg_all, col_start, block_width)
    return (col_pos[None, :] <= row_pos[:, None]) & (seg_cols[None, :] == seg_rows[:, None])


def block_scores(query_block, key_block, inv_root):
    return (
        jnp.einsum("qhd,khd->hqk", query_block, key_block, preferred_element_type=jnp.float32)
        * inv_root
    )


def take_block(source, index, block_width):
    return lax.dynamic_slice_in_dim(source, index * block_width, block_width, 0)


def attend(query_part, key_part, value_part, seg_all):
    length, heads_here, head_size = query_part.shape
    block_width = min(512, length)
    block_count = length // block_width
    inv_root = 1.0 / math.sqrt(head_size)

    def stats_row(i, log_totals):
        query_block = take_block(query_part, i, block_width)

        def stats_inner(j, state_now):
            running_max, running_sum = state_now
            scores = block_scores(query_block, take_block(key_part, j, block_width), inv_root)
            allowed = block_mask(seg_all, i * block_width, j * block_width, block_width)[None]
            scores = jnp.where(allowed, scores, masked_low)
            new_max = jnp.maximum(running_max, jnp.max(scores, axis=-1))
            weights = jnp.where(allowed, jnp.exp(scores - new_max[..., None]), 0.0)
            running_sum = running_sum * jnp.exp(running_max - new_max) + jnp.sum(weights, axis=-1)
            return (new_max, running_sum)

        start_state = (
            jnp.full((heads_here, block_width), masked_low, jnp.float32),
            jnp.zeros((heads_here, block_width), jnp.float32),
        )
        running_max, running_sum = lax.fori_loop(0, i + 1, stats_inner, start_state)
        return lax.dynamic_update_slice_in_dim(
            log_totals, running_max + jnp.log(running_sum), i * block_width, 1
        )

    log_totals = lax.fori_loop(
        0, block_count, stats_row, jnp.zeros((heads_here, length), jnp.float32)
    )

    def out_row(i, out_all):
        query_block = take_block(query_part, i, block_width)
        log_block = lax.dynamic_slice_in_dim(log_totals, i * block_width, block_width, 1)

        def out_inner(j, accum_out):
            scores = block_scores(query_block, take_block(key_part, j, block_width), inv_root)
            allowed = block_mask(seg_all, i * block_width, j * block_width, block_width)[None]
            probs_low = jnp.where(allowed, jnp.exp(scores - log_block[..., None]), 0.0).astype(
                jnp.bfloat16
            )
            return accum_out + jnp.einsum(
                "hqk,khd->qhd",
                probs_low,
                take_block(value_part, j, block_width),
                preferred_element_type=jnp.float32,
            )

        accum_out = lax.fori_loop(
            0, i + 1, out_inner, jnp.zeros((block_width, heads_here, head_size), jnp.float32)
        )
        return lax.dynamic_update_slice_in_dim(
            out_all, accum_out.astype(jnp.bfloat16), i * block_width, 0
        )

    out_all = lax.fori_loop(
        0, block_count, out_row, jnp.zeros((length, heads_here, head_size), jnp.bfloat16)
    )
    return (out_all, log_totals)


def attend_grads(query_part, key_part, value_part, seg_all, out_part, log_totals, grad_part):
    length, heads_here, head_size = query_part.shape
    block_width = min(512, length)
    block_count = length // block_width
    inv_root = 1.0 / math.sqrt(head_size)
    row_dots = jnp.einsum("qhd,qhd->hq", grad_part, out_part, preferred_element_type=jnp.float32)

    def grad_row(i, state_now):
        query_all, key_all, value_all = state_now
        query_block = take_block(query_part, i, block_width)
        grad_block = take_block(grad_part, i, block_width)
        log_block = lax.dynamic_slice_in_dim(log_totals, i * block_width, block_width, 1)
        dots_block = lax.dynamic_slice_in_dim(row_dots, i * block_width, block_width, 1)

        def grad_inner(j, inner_state):
            query_accum, key_accum, value_accum = inner_state
            key_block = take_block(key_part, j, block_width)
            value_block = take_block(value_part, j, block_width)
            scores = block_scores(query_block, key_block, inv_root)
            allowed = block_mask(seg_all, i * block_width, j * block_width, block_width)[None]
            probs = jnp.where(allowed, jnp.exp(scores - log_block[..., None]), 0.0)
            probs_low = probs.astype(jnp.bfloat16)
            value_new = take_block(value_accum, j, block_width) + jnp.einsum(
                "hqk,qhd->khd", probs_low, grad_block, preferred_element_type=jnp.float32
            )
            value_accum = lax.dynamic_update_slice_in_dim(
                value_accum, value_new, j * block_width, 0
            )
            prob_grad = jnp.einsum(
                "qhd,khd->hqk", grad_block, value_block, preferred_element_type=jnp.float32
            )
            score_grad = (probs * (prob_grad - dots_block[..., None])).astype(jnp.bfloat16)
            query_accum = query_accum + jnp.einsum(
                "hqk,khd->qhd", score_grad, key_block, preferred_element_type=jnp.float32
            )
            key_new = take_block(key_accum, j, block_width) + jnp.einsum(
                "hqk,qhd->khd", score_grad, query_block, preferred_element_type=jnp.float32
            )
            key_accum = lax.dynamic_update_slice_in_dim(key_accum, key_new, j * block_width, 0)
            return (query_accum, key_accum, value_accum)

        start_state = (
            jnp.zeros((block_width, heads_here, head_size), jnp.float32),
            key_all,
            value_all,
        )
        query_accum, key_all, value_all = lax.fori_loop(0, i + 1, grad_inner, start_state)
        query_all = lax.dynamic_update_slice_in_dim(
            query_all, (query_accum * inv_root).astype(jnp.bfloat16), i * block_width, 0
        )
        return (query_all, key_all, value_all)

    zero_grads = jnp.zeros((length, heads_here, head_size), jnp.float32)
    start_all = (jnp.zeros((length, heads_here, head_size), jnp.bfloat16), zero_grads, zero_grads)
    query_all, key_all, value_all = lax.fori_loop(0, block_count, grad_row, start_all)
    return (query_all, (key_all * inv_root).astype(jnp.bfloat16), value_all.astype(jnp.bfloat16))


def body(activations, queries, key_weight, value_weight, segment_ids, out_grad):
    rows_here = activations.shape[1]
    inputs = activations[0]
    kv_width = key_weight.shape[1]
    seq_devices = lax.axis_size("seq")
    heads_here = HEADS // seq_devices
    kv_group = HEADS // KV_HEADS
    stacked = jnp.concatenate([key_weight, value_weight], axis=1)
    columns = inputs
    projected = jnp.dot(
        columns,
        lax.all_gather(stacked, ("seq", "fsdp"), axis=0, tiled=True),
        preferred_element_type=jnp.float32,
    )
    projected = projected.astype(jnp.bfloat16)
    key_rows = projected[:, :kv_width].reshape(rows_here, KV_HEADS, HEAD_DIM)
    value_rows = projected[:, kv_width:].reshape(rows_here, KV_HEADS, HEAD_DIM)
    kv_copies = max(kv_group // heads_here, 1)
    query_heads = queries[0].reshape(rows_here, HEADS, HEAD_DIM)
    sent = (
        query_heads,
        jnp.repeat(key_rows, kv_copies, axis=1),
        jnp.repeat(value_rows, kv_copies, axis=1),
    )
    query_part, key_part, value_part = (
        lax.all_to_all(sent[0], "seq", split_axis=1, concat_axis=0, tiled=True),
        lax.all_to_all(sent[1], "seq", split_axis=1, concat_axis=0, tiled=True),
        lax.all_to_all(sent[2], "seq", split_axis=1, concat_axis=0, tiled=True),
    )
    widen_by = heads_here // key_part.shape[1]
    key_part = jnp.repeat(key_part, widen_by, axis=1)
    value_part = jnp.repeat(value_part, widen_by, axis=1)
    seg_all = lax.all_gather(segment_ids[0], "seq", axis=0, tiled=True)
    out_part, log_totals = attend(query_part, key_part, value_part, seg_all)
    context = lax.all_to_all(out_part, "seq", split_axis=0, concat_axis=1, tiled=True).reshape(
        1, rows_here, HEADS * HEAD_DIM
    )
    grad_part = lax.all_to_all(
        out_grad[0].reshape(rows_here, HEADS, HEAD_DIM),
        "seq",
        split_axis=1,
        concat_axis=0,
        tiled=True,
    )
    query_back, key_back, value_back = attend_grads(
        query_part, key_part, value_part, seg_all, out_part, log_totals, grad_part
    )
    query_tok, key_tok, value_tok = (
        lax.all_to_all(query_back, "seq", split_axis=0, concat_axis=1, tiled=True),
        lax.all_to_all(key_back, "seq", split_axis=0, concat_axis=1, tiled=True),
        lax.all_to_all(value_back, "seq", split_axis=0, concat_axis=1, tiled=True),
    )
    key_sum = (
        key_tok.reshape(rows_here, KV_HEADS, kv_group, HEAD_DIM).astype(jnp.float32).sum(axis=2)
    )
    value_sum = (
        value_tok.reshape(rows_here, KV_HEADS, kv_group, HEAD_DIM).astype(jnp.float32).sum(axis=2)
    )
    grad_kv = jnp.concatenate(
        [
            key_sum.astype(jnp.bfloat16).reshape(rows_here, kv_width),
            value_sum.astype(jnp.bfloat16).reshape(rows_here, kv_width),
        ],
        axis=1,
    )
    input_grad = lax.dot_general(
        grad_kv,
        lax.all_gather(stacked, ("seq", "fsdp"), axis=0, tiled=True),
        (((1,), (1,)), ((), ())),
        preferred_element_type=jnp.float32,
    )
    input_grad = input_grad.astype(jnp.bfloat16).reshape(1, rows_here, inputs.shape[1])
    columns = inputs
    grad_shard = lax.psum_scatter(
        lax.dot_general(
            columns, grad_kv, (((0,), (0,)), ((), ())), preferred_element_type=jnp.float32
        ).astype(jnp.bfloat16),
        ("seq", "fsdp"),
        scatter_dimension=0,
        tiled=True,
    ).astype(jnp.float32)
    grad_total = lax.psum(grad_shard, "rep").astype(jnp.bfloat16)
    query_grad = query_tok.reshape(1, rows_here, HEADS * HEAD_DIM)
    return (context, query_grad, input_grad, grad_total[:, :kv_width], grad_total[:, kv_width:])


def solution(mesh):
    return jax.shard_map(
        body,
        mesh=mesh,
        in_specs=(
            P(("groups", "rep", "fsdp"), "seq", None),
            P(("groups", "rep", "fsdp"), "seq", None),
            P(("seq", "fsdp"), None),
            P(("seq", "fsdp"), None),
            P(("groups", "rep", "fsdp"), "seq"),
            P(("groups", "rep", "fsdp"), "seq", None),
        ),
        out_specs=(
            P(("groups", "rep", "fsdp"), "seq", None),
            P(("groups", "rep", "fsdp"), "seq", None),
            P(("groups", "rep", "fsdp"), "seq", None),
            P(("groups", "seq", "fsdp"), None),
            P(("groups", "seq", "fsdp"), None),
        ),
        check_vma=False,
    )
```

profile of v0, /device:TPU:0, one launch (start us, length us, event | category | flops | bytes accessed | tf_op | source)
XLA Modules:
  0.0 248.5 jit_solution(1533762481953320926)
XLA Ops:
  7.2 0.0 copy-start
  7.2 0.0 copy-start.3
  7.2 0.0 all-gather.3.cloned.1.call-start
  7.2 1.9 pad_maximum_fusion
  9.2 0.0 all-gather.3.cloned.1.call-update
  9.2 2.0 copy.45
  11.2 6.3 %all-to-all-start.1 = ((bf16[128,16,128]{0,2,1:T(8,128)(2,1)}), bf16[128,16,128]{0,2,1:T(8,128)(2,1)S(1)}, u32[]{:S(2)}, u32[]{:S(2)}) async-start(bf16[128,16,128]{0,2,1:T(8,128)(2,1)} %bitcast.9), calls=%async_computation.1 | async-start | bytes 1048576 | tf_op jit(solution)/shard_map/all_to_all | solution.py:180
  17.5 2.0 copy.52
  19.6 24.7 %all-to-all-done.1 = bf16[128,16,128]{0,2,1:T(8,128)(2,1)S(1)} async-done(((bf16[128,16,128]{0,2,1:T(8,128)(2,1)}), bf16[128,16,128]{0,2,1:T(8,128)(2,1)S(1)}, u32[]{:S(2)}, u32[]{:S(2)}) %all-to-all-start.1) | async-done | bytes 524320 | tf_op jit(solution)/shard_map/all_to_all | solution.py:180
  44.2 3.6 %all-to-all-start.4 = ((bf16[128,16,128]{0,2,1:T(8,128)(2,1)}), bf16[128,16,128]{0,2,1:T(8,128)(2,1)S(1)}, u32[]{:S(2)}, u32[]{:S(2)}) async-start(bf16[128,16,128]{0,2,1:T(8,128)(2,1)} %bitcast.22), calls=%async_computation.4 | async-start | bytes 1048576 | tf_op jit(solution)/shard_map/all_to_all | solution.py:192
  47.9 0.0 copy-done.3
  47.9 21.7 %all-gather = s32[1,512]{1,0:T(1,128)S(1)} all-gather(s32[1,128]{1,0:T(1,128)S(1)} %copy-done.3), channel_id=2, replica_groups=mesh['groups'=2,'seq'=4,'rep'=2,'fsdp'=2] {'seq'}, dimensions={1}, use_global_device_ids=true | all-gather | bytes 2560 | tf_op jit(solution)/shard_map/all_gather | solution.py:187
  69.5 9.1 %all-gather.3.cloned.1.call-done = bf16[2048,1024]{1,0:T(8,128)(2,1)} async-done(((bf16[256,1024]{1,0:T(8,128)(2,1)}), bf16[2048,1024]{1,0:T(8,128)(2,1)}) %all-gather.3.cloned.1.call-update) | async-done | bytes 4194320 | tf_op jit(solution)/shard_map/all_gather | solution.py:166
  78.7 3.5 %fusion.11 = bf16[128,1024]{0,1:T(8,128)(2,1)S(1)} fusion(bf16[2048,1024]{1,0:T(8,128)(2,1)} %all-gather.3.cloned.1.call-done, bf16[1,128,2048]{2,1,0:T(8,128)(2,1)S(1)} %copy-done), kind=kOutput, calls=%fused_computation.22 | convolution fusion | flops 537001984 | bytes 4980736 | tf_op jit(solution)/shard_map/dot_general | solution.py:164
  82.2 0.8 copy.44
  83.0 0.0 all-to-all-done.4
  83.0 3.3 %all-to-all-start = ((bf16[128,4,128]{2,0,1:T(8,128)(2,1)}), bf16[128,4,128]{2,0,1:T(8,128)(2,1)S(1)}, u32[]{:S(2)}, u32[]{:S(2)}) async-start(bf16[128,4,128]{2,0,1:T(8,128)(2,1)} %copy.44), calls=%async_computation | async-start | bytes 262144 | tf_op jit(solution)/shard_map/all_to_all | solution.py:181
  86.3 0.2 fusion.13
  86.5 0.3 copy.47
  86.8 0.3 copy.54
  87.1 0.8 copy.48
  87.9 4.8 %all-to-all-done = bf16[128,4,128]{2,0,1:T(8,128)(2,1)S(1)} async-done(((bf16[128,4,128]{2,0,1:T(8,128)(2,1)}), bf16[128,4,128]{2,0,1:T(8,128)(2,1)S(1)}, u32[]{:S(2)}, u32[]{:S(2)}) %all-to-all-start) | async-done | bytes 131104 | tf_op jit(solution)/shard_map/all_to_all | solution.py:181
  92.7 3.3 %all-to-all-start.2 = ((bf16[128,4,128]{2,0,1:T(8,128)(2,1)}), bf16[128,4,128]{2,0,1:T(8,128)(2,1)S(1)}, u32[]{:S(2)}, u32[]{:S(2)}) async-start(bf16[128,4,128]{2,0,1:T(8,128)(2,1)} %copy.48), calls=%async_computation.2 | async-start | bytes 262144 | tf_op jit(solution)/shard_map/all_to_all | solution.py:182
  96.0 0.9 fusion.3
  96.9 1.0 select_reduce_fusion
  98.0 0.9 fusion.10
  99.0 0.0 copy-done.1
  99.0 1.2 copy.60
  100.2 1.8 all-to-all-done.2
  101.9 3.5 %all-to-all-start.7 = ((bf16[512,4,128]{2,1,0:T(4,128)(2,1)}), bf16[512,4,128]{2,1,0:T(4,128)(2,1)S(1)}, u32[]{:S(2)}, u32[]{:S(2)}) async-start(bf16[512,4,128]{2,1,0:T(4,128)(2,1)} %copy.60), calls=%async_computation.7 | async-start | bytes 1048576 | tf_op jit(solution)/shard_map/all_to_all | solution.py:205
  105.4 3.9 %fusion.12 = (f32[4,512]{1,0:T(4,128)S(1)}, bf16[4,512,128]{2,1,0:T(8,128)(2,1)S(1)}) fusion(bf16[4,128,4,128]{3,1,0,2:T(8,128)(2,1)S(1)} %copy.54, bf16[512,128]{1,0:T(8,128)(2,1)S(1)} %bitcast.111, f32[4,512,512]{2,1,0:T(8,128)} %copy-done.1, f32[4,512]{1,0:T(4,128)S(1)} %log_add_fusion, pred[512,512]{0,1:T(8,128)(4,1)S(1)} %fusion.13), kind=kOutput, calls=%fused_computation.24 | convolution fusion | flops 273938432 | bytes 5652480 | tf_op jit(solution)/shard_map/while/body/eval_jaxpr/while/body/hqk,khd->qhd/dot_general | solution.py:77
  109.3 0.0 copy-done.2
  109.3 1.4 fusion
  110.8 0.7 fusion.8
  111.5 0.6 copy-done.4
  112.1 1.2 copy.58
  113.3 5.2 %all-to-all-done.7 = bf16[512,4,128]{2,1,0:T(4,128)(2,1)S(1)} async-done(((bf16[512,4,128]{2,1,0:T(4,128)(2,1)}), bf16[512,4,128]{2,1,0:T(4,128)(2,1)S(1)}, u32[]{:S(2)}, u32[]{:S(2)}) %all-to-all-start.7) | async-done | bytes 524320 | tf_op jit(solution)/shard_map/all_to_all | solution.py:205
  118.5 3.5 %all-to-all-start.6 = ((bf16[512,4,128]{2,1,0:T(4,128)(2,1)}), bf16[512,4,128]{2,1,0:T(4,128)(2,1)S(1)}, u32[]{:S(2)}, u32[]{:S(2)}) async-start(bf16[512,4,128]{2,1,0:T(4,128)(2,1)} %copy.58), calls=%async_computation.6 | async-start | bytes 1048576 | tf_op jit(solution)/shard_map/all_to_all | solution.py:204
  122.0 0.2 reduce-scatter.2.cloned.1.call-start
  122.2 0.7 reduce_sum.48
  122.9 0.1 copy.61
  123.0 12.3 %all-to-all-done.6 = bf16[512,4,128]{2,1,0:T(4,128)(2,1)S(1)} async-done(((bf16[512,4,128]{2,1,0:T(4,128)(2,1)}), bf16[512,4,128]{2,1,0:T(4,128)(2,1)S(1)}, u32[]{:S(2)}, u32[]{:S(2)}) %all-to-all-start.6) | async-done | bytes 524320 | tf_op jit(solution)/shard_map/all_to_all | solution.py:204
  135.3 0.7 reduce_sum.45
  136.0 0.1 copy.59
  136.1 3.2 %convert_bitcast_fusion = bf16[2048,1024]{0,1:T(8,128)(2,1)} fusion(bf16[1,128,2048]{2,1,0:T(8,128)(2,1)S(1)} %copy-done, bf16[128,512]{0,1:T(8,128)(2,1)S(1)} %bitcast.98, bf16[128,512]{0,1:T(8,128)(2,1)S(1)} %bitcast.100), kind=kOutput, calls=%fused_computation.6 | convolution fusion | flops 539492352 | bytes 4980736 | tf_op jit(solution)/shard_map/dot_general | solution.py:229
  139.3 0.0 reduce-scatter.2.cloned.1.call-update
  139.4 1.2 copy.50
  140.6 3.5 %all-to-all-start.3 = ((bf16[512,4,128]{2,1,0:T(4,128)(2,1)}), bf16[512,4,128]{2,1,0:T(4,128)(2,1)S(1)}, u32[]{:S(2)}, u32[]{:S(2)}) async-start(bf16[512,4,128]{2,1,0:T(4,128)(2,1)} %copy.50), calls=%async_computation.3 | async-start | bytes 1048576 | tf_op jit(solution)/shard_map/all_to_all | solution.py:189
  144.1 0.9 fusion.9
  145.0 1.2 copy.56
  146.2 19.1 %all-to-all-done.3 = bf16[512,4,128]{2,1,0:T(4,128)(2,1)S(1)} async-done(((bf16[512,4,128]{2,1,0:T(4,128)(2,1)}), bf16[512,4,128]{2,1,0:T(4,128)(2,1)S(1)}, u32[]{:S(2)}, u32[]{:S(2)}) %all-to-all-start.3) | async-done | bytes 524320 | tf_op jit(solution)/shard_map/all_to_all | solution.py:189
  165.3 4.3 %all-to-all-start.5 = ((bf16[512,4,128]{2,1,0:T(4,128)(2,1)}), bf16[512,4,128]{2,1,0:T(4,128)(2,1)S(1)}, u32[]{:S(2)}, u32[]{:S(2)}) async-start(bf16[512,4,128]{2,1,0:T(4,128)(2,1)} %copy.56), calls=%async_computation.5 | async-start | bytes 1048576 | tf_op jit(solution)/shard_map/all_to_all | solution.py:203
  169.6 34.6 %reduce-scatter.2.cloned.1.call-done = bf16[256,1024]{0,1:T(8,128)(2,1)} async-done(((bf16[2048,1024]{0,1:T(8,128)(2,1)}), bf16[256,1024]{0,1:T(8,128)(2,1)}) %reduce-scatter.2.cloned.1.call-update) | async-done | bytes 524304 | tf_op jit(solution)/shard_map/reduce_scatter | solution.py:228
  204.2 0.0 all-reduce.2.cloned.1.call-update
  204.2 0.2 copy.51
  204.4 1.2 reshape.232
  205.6 0.0 all-to-all-done.5
  205.6 0.2 copy.57
  205.8 1.2 reshape.233
  207.0 4.5 %fusion.5 = bf16[1,128,2048]{2,1,0:T(8,128)(2,1)} fusion(bf16[2048,1024]{1,0:T(8,128)(2,1)} %all-gather.3.cloned.1.call-done, bf16[128,512]{0,1:T(8,128)(2,1)S(1)} %bitcast.99, bf16[128,512]{0,1:T(8,128)(2,1)S(1)} %bitcast.101), kind=kOutput, calls=%fused_computation.11 | convolution fusion | flops 537657344 | bytes 4980736 | tf_op jit(solution)/shard_map/dot_general | solution.py:220
  211.5 27.7 %all-reduce.2.cloned.1.call-done = bf16[256,1024]{0,1:T(8,128)(2,1)} async-done(((bf16[256,1024]{0,1:T(8,128)(2,1)}), bf16[256,1024]{0,1:T(8,128)(2,1)}) %all-reduce.2.cloned.1.call-update) | async-done | bytes 524304 | tf_op jit(solution)/shard_map/psum | solution.py:236
  239.2 1.1 fusion.25
  240.2 0.8 copy.63
  241.1 0.8 copy.62
  (10 shorter events, 0.1 us)
Async XLA Ops:
  7.2 71.5 %copy-start = (bf16[1,128,2048]{2,1,0:T(8,128)(2,1)S(1)}, bf16[1,128,2048]{2,1,0:T(8,128)(2,1)}, u32[]{:S(2)}) copy-start(bf16[1,128,2048]{2,1,0:T(8,128)(2,1)} %param.6) | copy-start | bytes 1572868
  7.2 40.7 %copy-start.3 = (s32[1,128]{1,0:T(1,128)S(1)}, s32[1,128]{1,0:T(1,128)}, u32[]{:S(2)}) copy-start(s32[1,128]{1,0:T(1,128)} %param.10) | copy-start | bytes 1540
  7.2 71.5 %all-gather.3.cloned.1.call-start = ((), (), s32[]{:S(2)}) async-start(), calls=%async_computation.9 | async-start | bytes 4718592 | tf_op jit(solution)/shard_map/all_gather | solution.py:166
  11.2 33.0 %all-to-all-start.1 = ((bf16[128,16,128]{0,2,1:T(8,128)(2,1)}), bf16[128,16,128]{0,2,1:T(8,128)(2,1)S(1)}, u32[]{:S(2)}, u32[]{:S(2)}) async-start(bf16[128,16,128]{0,2,1:T(8,128)(2,1)} %bitcast.9), calls=%async_computation.1 | async-start | bytes 1048576 | tf_op jit(solution)/shard_map/all_to_all | solution.py:180
  44.2 38.7 %all-to-all-start.4 = ((bf16[128,16,128]{0,2,1:T(8,128)(2,1)}), bf16[128,16,128]{0,2,1:T(8,128)(2,1)S(1)}, u32[]{:S(2)}, u32[]{:S(2)}) async-start(bf16[128,16,128]{0,2,1:T(8,128)(2,1)} %bitcast.22), calls=%async_computation.4 | async-start | bytes 1048576 | tf_op jit(solution)/shard_map/all_to_all | solution.py:192
  83.0 9.7 %all-to-all-start = ((bf16[128,4,128]{2,0,1:T(8,128)(2,1)}), bf16[128,4,128]{2,0,1:T(8,128)(2,1)S(1)}, u32[]{:S(2)}, u32[]{:S(2)}) async-start(bf16[128,4,128]{2,0,1:T(8,128)(2,1)} %copy.44), calls=%async_computation | async-start | bytes 262144 | tf_op jit(solution)/shard_map/all_to_all | solution.py:181
  92.7 9.2 %all-to-all-start.2 = ((bf16[128,4,128]{2,0,1:T(8,128)(2,1)}), bf16[128,4,128]{2,0,1:T(8,128)(2,1)S(1)}, u32[]{:S(2)}, u32[]{:S(2)}) async-start(bf16[128,4,128]{2,0,1:T(8,128)(2,1)} %copy.48), calls=%async_computation.2 | async-start | bytes 262144 | tf_op jit(solution)/shard_map/all_to_all | solution.py:182
  96.9 2.0 copy-start.1
  101.9 16.6 %all-to-all-start.7 = ((bf16[512,4,128]{2,1,0:T(4,128)(2,1)}), bf16[512,4,128]{2,1,0:T(4,128)(2,1)S(1)}, u32[]{:S(2)}, u32[]{:S(2)}) async-start(bf16[512,4,128]{2,1,0:T(4,128)(2,1)} %copy.60), calls=%async_computation.7 | async-start | bytes 1048576 | tf_op jit(solution)/shard_map/all_to_all | solution.py:205
  105.4 3.9 %copy-start.2 = (f32[4,512,512]{2,1,0:T(8,128)S(1)}, f32[4,512,512]{2,1,0:T(8,128)}, u32[]{:S(2)}) copy-start(f32[4,512,512]{2,1,0:T(8,128)} %copy-done.1) | copy-start | bytes 12582916
  110.7 1.4 copy-start.4
  118.5 16.8 %all-to-all-start.6 = ((bf16[512,4,128]{2,1,0:T(4,128)(2,1)}), bf16[512,4,128]{2,1,0:T(4,128)(2,1)S(1)}, u32[]{:S(2)}, u32[]{:S(2)}) async-start(bf16[512,4,128]{2,1,0:T(4,128)(2,1)} %copy.58), calls=%async_computation.6 | async-start | bytes 1048576 | tf_op jit(solution)/shard_map/all_to_all | solution.py:204
  122.0 82.2 %reduce-scatter.2.cloned.1.call-start = ((), (), s32[]{:S(2)}) async-start(), calls=%async_computation.10 | async-start | bytes 4718592 | tf_op jit(solution)/shard_map/reduce_scatter | solution.py:228
  139.3 4.7 %copy-start.5 = (bf16[4,512,512]{1,2,0:T(8,128)(2,1)S(1)}, bf16[4,512,512]{1,2,0:T(8,128)(2,1)}, u32[]{:S(2)}) copy-start(bf16[4,512,512]{1,2,0:T(8,128)(2,1)} %copy-done.4) | copy-start | bytes 6291460
  140.6 24.7 %all-to-all-start.3 = ((bf16[512,4,128]{2,1,0:T(4,128)(2,1)}), bf16[512,4,128]{2,1,0:T(4,128)(2,1)S(1)}, u32[]{:S(2)}, u32[]{:S(2)}) async-start(bf16[512,4,128]{2,1,0:T(4,128)(2,1)} %copy.50), calls=%async_computation.3 | async-start | bytes 1048576 | tf_op jit(solution)/shard_map/all_to_all | solution.py:189
  165.3 40.3 %all-to-all-start.5 = ((bf16[512,4,128]{2,1,0:T(4,128)(2,1)}), bf16[512,4,128]{2,1,0:T(4,128)(2,1)S(1)}, u32[]{:S(2)}, u32[]{:S(2)}) async-start(bf16[512,4,128]{2,1,0:T(4,128)(2,1)} %copy.56), calls=%async_computation.5 | async-start | bytes 1048576 | tf_op jit(solution)/shard_map/all_to_all | solution.py:203
  169.6 69.6 %all-reduce.2.cloned.1.call-start = ((), (), s32[]{:S(2)}) async-start(), calls=%async_computation.11 | async-start | bytes 1048576 | tf_op jit(solution)/shard_map/psum | solution.py:236
Sparse Core Ops, SparseCore 0:
  10.2 68.4 all-gather.2
  139.5 64.6 reduce-scatter.1
  206.5 32.6 all-reduce.1
where the time goes:
time: 249 us; the launch traced here: 248 us
  waiting for transfers between devices  139 us (56%)
  starting transfers between devices  31.6 us (13%)
  blocking collectives  21.7 us (9%)
  matrix products  19.9 us (8%)
  local copies, waits for them, and re-layouts  17.4 us (7%)
  between operations  14 us (6%)
  other arithmetic  4.52 us (2%)
    reduce_scatter x1, waiting for transfers between devices, body(): lax.psum_scatter(lax.dot_general(columns, grad_kv, (((0,), (0,)), ((), ()...  34.6 us
    psum x1, waiting for transfers between devices, body(): grad_total = lax.psum(grad_shard, 'rep').astype(jnp.bfloat16)  27.7 us
    all_to_all x1, waiting for transfers between devices, body(): lax.all_to_all(sent[0], 'seq', split_axis=1, concat_axis=0, tiled=True)  24.7 us
    all_gather x1, blocking collectives, body(): seg_all = lax.all_gather(segment_ids[0], 'seq', axis=0, tiled=True)  21.7 us
    all_to_all x1, waiting for transfers between devices, body(): lax.all_to_all(out_part, 'seq', split_axis=0, concat_axis=1, tiled=True)  19.1 us
    all_to_all x1, waiting for transfers between devices, body(): lax.all_to_all(key_back, 'seq', split_axis=0, concat_axis=1, tiled=True)  12.3 us
    all_gather x1, waiting for transfers between devices, body(): lax.all_gather(stacked, ('seq', 'fsdp'), axis=0, tiled=True)  9.14 us
    unnamed x16, local copies, waits for them, and re-layouts  6.44 us
  transfers between devices with their start and end apart: 11, of which 9 were waited for; matrix products, arithmetic and copies ran while one was open for 13% of the time, Pallas kernels for 0%

commit v1 on v0

v1 whole, which is shorter than its diff:
```python
import functools
import math

import jax
import jax.numpy as jnp
from jax import lax
from jax.experimental import pallas as pl
from jax.experimental.pallas import tpu as pltpu
from jax.sharding import PartitionSpec as P

HEADS = 16
KV_HEADS = 4
HEAD_DIM = 128
KV_WIDTH = KV_HEADS * HEAD_DIM
GROUP = HEADS // KV_HEADS
LOG2E = 1.4426950408889634
MASKED = -1e30
VMEM_LIMIT = 56 * 1024 * 1024


def params(**kw):
    return pltpu.CompilerParams(vmem_limit_bytes=VMEM_LIMIT, **kw)


def vspec():
    return pl.BlockSpec(memory_space=pltpu.VMEM)


def sspec():
    return pl.BlockSpec(memory_space=pltpu.SMEM)


def assemble(full_ref, own_ref, other_ref, place, count, rows):
    z, c = place[0], place[1]
    for k in range(count):
        src = lax.rem(z - k + count, count)
        for ref, core in ((own_ref, c), (other_ref, 1 - c)):
            start = pl.multiple_of((src * 2 + core) * rows, rows)
            full_ref[pl.ds(start, rows), :] = ref[k * rows : (k + 1) * rows, :]


def project_kernel(place, x_own, x_next, w_own, w_other, out_own, out_next, full, *, count, rows):
    assemble(full, w_own, w_other, place, count, rows)
    w = full[...]
    out_own[...] = jnp.dot(x_own[...], w, preferred_element_type=jnp.float32).astype(jnp.bfloat16)
    out_next[...] = jnp.dot(x_next[...], w, preferred_element_type=jnp.float32).astype(jnp.bfloat16)


def project(place, x_own, x_next, w_own, w_other, count, rows):
    width = w_own.shape[1]
    out = jax.ShapeDtypeStruct((x_own.shape[0], width), jnp.bfloat16)
    return pl.pallas_call(
        functools.partial(project_kernel, count=count, rows=rows),
        in_specs=[sspec()] + [vspec()] * 4,
        out_specs=[vspec()] * 2,
        out_shape=[out, out],
        scratch_shapes=[pltpu.VMEM((2 * count * rows, width), jnp.bfloat16)],
        compiler_params=params(),
        name="project",
    )(place, x_own, x_next, w_own, w_other)


def nt(a, b):
    return lax.dot_general(a, b, (((1,), (1,)), ((), ())), preferred_element_type=jnp.float32)


def tn(a, b):
    return lax.dot_general(a, b, (((0,), (0,)), ((), ())), preferred_element_type=jnp.float32)


def attend_kernel(place, q_ref, do_ref, seg_col, seg_rows, *refs, count, block):
    same, cross = refs[:count], refs[count : 2 * count]
    ctx_ref, dq_ref = refs[2 * count : 2 * count + 2]
    dk_refs = refs[2 * count + 2 : 3 * count + 2]
    dv_refs = refs[3 * count + 2 : 4 * count + 2]
    bias = refs[4 * count + 2]
    inv_root = 1.0 / math.sqrt(HEAD_DIM)
    length = count * block

    @pl.when(pl.program_id(0) == 0)
    def _():
        cols = lax.broadcasted_iota(jnp.int32, (block, length), 1)
        rows = lax.broadcasted_iota(jnp.int32, (block, length), 0)
        ok = (seg_rows[...] == seg_col[...]) & ((cols <= rows) | (cols >= block))
        bias[...] = jnp.where(ok, 0.0, MASKED)

    even = place[2] == 0
    first = jnp.concatenate([r[...] for r in same], axis=0)
    second = jnp.concatenate([r[...] for r in cross], axis=0)
    key = jnp.where(even, first, second)
    value = jnp.where(even, second, first)

    def stack(ref):
        return jnp.concatenate(
            [ref[:, h * HEAD_DIM : (h + 1) * HEAD_DIM] for h in range(GROUP)], axis=0
        )

    def unstack(ref, val):
        for h in range(GROUP):
            ref[:, h * HEAD_DIM : (h + 1) * HEAD_DIM] = val[h * block : (h + 1) * block, :]

    q, do = stack(q_ref), stack(do_ref)
    s = nt(q, key) * (inv_root * LOG2E)
    s = (s.reshape(GROUP, block, length) + bias[...][None]).reshape(GROUP * block, length)
    e = jnp.exp2(s - jnp.max(s, axis=1, keepdims=True))
    p = e * (1.0 / jnp.sum(e, axis=1, keepdims=True))
    p_low = p.astype(jnp.bfloat16)
    ctx = jnp.dot(p_low, value, preferred_element_type=jnp.float32).astype(jnp.bfloat16)
    unstack(ctx_ref, ctx)
    dots = jnp.sum(do.astype(jnp.float32) * ctx.astype(jnp.float32), axis=1, keepdims=True)
    ds = (p * (nt(do, value) - dots)).astype(jnp.bfloat16)
    dq = jnp.dot(ds, key, preferred_element_type=jnp.float32) * inv_root
    unstack(dq_ref, dq.astype(jnp.bfloat16))
    dv = tn(p_low, do)
    dk = tn(ds, q) * inv_root
    for k in range(count):
        dk_refs[k][...] = dk[k * block : (k + 1) * block, :].astype(dk_refs[k].dtype)
        dv_refs[k][...] = dv[k * block : (k + 1) * block, :].astype(dv_refs[k].dtype)


def attend(place, q, do, seg_col, seg_rows, same, cross):
    block, width = q.shape
    count = len(same)
    wide = pl.BlockSpec((block, GROUP * HEAD_DIM), lambda g: (0, g))
    head = pl.BlockSpec((block, HEAD_DIM), lambda g: (0, g))
    rows = jax.ShapeDtypeStruct((block, width), jnp.bfloat16)
    own = jax.ShapeDtypeStruct((block, KV_WIDTH), jnp.float32)
    sent = jax.ShapeDtypeStruct((block, KV_WIDTH), jnp.bfloat16)
    parts = [own] + [sent] * (count - 1)
    outs = pl.pallas_call(
        functools.partial(attend_kernel, count=count, block=block),
        grid=(KV_HEADS,),
        in_specs=[
            sspec(),
            wide,
            wide,
            pl.BlockSpec((block, 1), lambda g: (0, 0)),
            pl.BlockSpec((1, count * block), lambda g: (0, 0)),
        ]
        + [head] * (2 * count),
        out_specs=[wide, wide] + [head] * (2 * count),
        out_shape=[rows, rows] + parts + parts,
        scratch_shapes=[pltpu.VMEM((block, count * block), jnp.float32)],
        compiler_params=params(dimension_semantics=("arbitrary",)),
        name="attend",
    )(place, q, do, seg_col, seg_rows, *same, *cross)
    return outs[0], outs[1], outs[2 : 2 + count], outs[2 + count :]


def input_grad_kernel(place, gk, gv, a_own, a_other, b_own, b_other, out, fa, fb, *, count, rows):
    assemble(fa, a_own, a_other, place, count, rows)
    assemble(fb, b_own, b_other, place, count, rows)
    even = place[2] == 0
    ga = jnp.where(even, gk[...], gv[...])
    gb = jnp.where(even, gv[...], gk[...])
    out[...] = (nt(ga, fa[...]) + nt(gb, fb[...])).astype(jnp.bfloat16)


def input_grad_of(place, gk, gv, a_own, a_other, b_own, b_other, count, rows):
    full = pltpu.VMEM((2 * count * rows, KV_WIDTH), jnp.bfloat16)
    return pl.pallas_call(
        functools.partial(input_grad_kernel, count=count, rows=rows),
        in_specs=[sspec()] + [vspec()] * 6,
        out_specs=vspec(),
        out_shape=jax.ShapeDtypeStruct((gk.shape[0], 2 * count * rows), jnp.bfloat16),
        scratch_shapes=[full, full],
        compiler_params=params(),
        name="input_grad",
    )(place, gk, gv, a_own, a_other, b_own, b_other)


def weight_grad_kernel(x_own, x_other, g_own, g_other, out):
    out[...] = (tn(x_own[...], g_own[...]) + tn(x_other[...], g_other[...])).astype(jnp.bfloat16)


def weight_grad_of(x_own, x_other, g_own, g_other):
    return pl.pallas_call(
        weight_grad_kernel,
        in_specs=[vspec()] * 4,
        out_specs=vspec(),
        out_shape=jax.ShapeDtypeStruct((x_own.shape[1], g_own.shape[1]), jnp.bfloat16),
        compiler_params=params(),
        name="weight_grad",
    )(x_own, x_other, g_own, g_other)


def body(activations, queries, key_weight, value_weight, segment_ids, out_grad):
    inputs = activations[0]
    block, width = inputs.shape
    rows = key_weight.shape[0]
    n = lax.axis_size("seq")
    reps = lax.axis_size("rep")
    z, r, c = lax.axis_index("seq"), lax.axis_index("rep"), lax.axis_index("fsdp")
    odd = lax.rem(r, 2)
    place = jnp.stack([z, c, odd]).astype(jnp.int32)

    def around(x, k):
        return lax.ppermute(x, "seq", [(i, (i + k) % n) for i in range(n)])

    def up(x, k):
        return lax.ppermute(x, "seq", [(i, i + k) for i in range(n - k)])

    def down(x, k):
        return lax.ppermute(x, "seq", [(i, i - k) for i in range(k, n)])

    def cross_up(x, k):
        pairs = [
            (i * reps + j, (i + k) * reps + (j ^ 1)) for i in range(n - k) for j in range(reps)
        ]
        return lax.ppermute(x, ("seq", "rep"), pairs)

    def partner(x):
        return lax.ppermute(x, "rep", [(j, j ^ 1) for j in range(reps)])

    def core(x):
        return lax.ppermute(x, "fsdp", [(0, 1), (1, 0)])

    half = jnp.where(odd == 0, key_weight, value_weight)
    w_own = jnp.concatenate([half] + [around(half, k) for k in range(1, n)], axis=0)
    w_other = core(w_own)
    x_next = partner(inputs)
    seg = segment_ids[0] + 1
    seg_rows = jnp.concatenate([seg] + [up(seg, k) for k in range(1, n)], axis=0)[None, :]
    seg_col = seg[:, None]

    columns = inputs.reshape(block, n, 2, rows)
    x_mine = lax.dynamic_index_in_dim(columns, c, 2, keepdims=False)
    x_theirs = core(lax.dynamic_index_in_dim(columns, 1 - c, 2, keepdims=False))
    x_both = jnp.concatenate([x_mine, x_theirs], axis=0)

    proj_own, proj_next = project(place, inputs, x_next, w_own, w_other, n, rows)
    same = [proj_own] + [up(proj_own, k) for k in range(1, n)]
    cross = [cross_up(proj_next, k) for k in range(n)]

    def take(k):
        return lax.dynamic_index_in_dim(x_both, lax.rem(z + k + n, n), 1, keepdims=False)

    x_low, _ = lax.optimization_barrier((x_both, proj_own))
    x_pieces = {0: take(0)}

    def piece(source, k):
        return lax.dynamic_index_in_dim(source, lax.rem(z + k + n, n), 1, keepdims=False)

    low = {k: down(piece(x_low, -k), k) for k in range(1, n)}

    context, query_grad, dk, dv = attend(
        place, queries[0], out_grad[0], seg_col, seg_rows, same, cross
    )
    back = [
        down(jnp.concatenate([dk[k], dv[k]], axis=1), k) for k in range(1, n)
    ]
    x_high, _ = lax.optimization_barrier((x_both, dk[1]))
    high = {k: up(piece(x_high, k), k) for k in range(1, n)}

    w_late, _ = lax.optimization_barrier((w_own, same[1]))
    b_own = partner(w_late)
    b_other = core(b_own)

    total = jnp.concatenate([dk[0], dv[0]], axis=1)
    for b in back:
        total = total + b.astype(jnp.float32)
    grad_kv = total.astype(jnp.bfloat16)
    g_own = jnp.concatenate([grad_kv] + [around(grad_kv, k) for k in range(1, n)], axis=0)
    g_other = core(g_own)
    input_grad = input_grad_of(
        place, grad_kv[:, :KV_WIDTH], grad_kv[:, KV_WIDTH:], w_own, w_other, b_own, b_other, n, rows
    )

    own_x, other_x = [x_pieces[0][:block]], [x_pieces[0][block:]]
    for k in range(1, n):
        got = jnp.where(z >= k, high[k], low[n - k])
        own_x.append(got[:block])
        other_x.append(got[block:])
    partial = weight_grad_of(
        jnp.concatenate(own_x, axis=0), jnp.concatenate(other_x, axis=0), g_own, g_other
    )
    if reps == 2:
        grad = partial.astype(jnp.float32) + partner(partial).astype(jnp.float32)
    else:
        grad = lax.psum(partial.astype(jnp.float32), "rep")
    grad = grad.astype(jnp.bfloat16)
    return (
        context[None],
        query_grad[None],
        input_grad[None],
        grad[:, :KV_WIDTH],
        grad[:, KV_WIDTH:],
    )


def solution(mesh):
    return jax.shard_map(
        body,
        mesh=mesh,
        in_specs=(
            P(("groups", "rep", "fsdp"), "seq", None),
            P(("groups", "rep", "fsdp"), "seq", None),
            P(("seq", "fsdp"), None),
            P(("seq", "fsdp"), None),
            P(("groups", "rep", "fsdp"), "seq"),
            P(("groups", "rep", "fsdp"), "seq", None),
        ),
        out_specs=(
            P(("groups", "rep", "fsdp"), "seq", None),
            P(("groups", "rep", "fsdp"), "seq", None),
            P(("groups", "rep", "fsdp"), "seq", None),
            P(("groups", "seq", "fsdp"), None),
            P(("groups", "seq", "fsdp"), None),
        ),
        check_vma=False,
    )
```

time: 249 us -> 189 us (0.76)
  the two profiles are of different devices: /device:TPU:0 before, /device:TPU:8 now
where the time goes in v1:
time: 189 us
  waiting for transfers between devices  105 us (56%)
  starting transfers between devices  46.6 us (25%)
  Pallas kernels  19.9 us (11%)
  local copies, waits for them, and re-layouts  9.2 us (5%)
  other arithmetic  6.75 us (4%)
    ppermute x6, waiting for transfers between devices, around(): return lax.ppermute(x, 'seq', [(i, (i + k) % n) for i in range(n)])  34.7 us
    ppermute x3, waiting for transfers between devices, partner(): return lax.ppermute(x, 'rep', [(j, j ^ 1) for j in range(reps)])  30.8 us
    ppermute x6, waiting for transfers between devices, down(): return lax.ppermute(x, 'seq', [(i, i - k) for i in range(k, n)])  25.1 us
    ppermute x9, starting transfers between devices, up(): return lax.ppermute(x, 'seq', [(i, i + k) for i in range(n - k)])  18.4 us
    ppermute x4, starting transfers between devices, cross_up(): return lax.ppermute(x, ('seq', 'rep'), pairs)  10.2 us
    pallas_call x1, Pallas kernels, attend(): pl.pallas_call(functools.partial(attend_kernel, count=count, block=block)...  8.49 us
    ppermute x6, starting transfers between devices, down(): return lax.ppermute(x, 'seq', [(i, i - k) for i in range(k, n)])  7.89 us
    ppermute x6, starting transfers between devices, around(): return lax.ppermute(x, 'seq', [(i, (i + k) % n) for i in range(n)])  7.63 us
  transfers between devices with their start and end apart: 32, of which 15 were waited for; matrix products, arithmetic and copies ran while one was open for 5% of the time, Pallas kernels for 4%

profile of v1, /device:TPU:8, one launch (start us, length us, event | category | flops | bytes accessed | tf_op | source)
XLA Modules:
  0.0 188.7 jit_solution(3068965552107293334)
XLA Ops:
  0.6 1.0 broadcast_select_fusion
  1.7 3.0 %collective-permute-start.5 = (bf16[256,512]{1,0:T(8,128)(2,1)S(1)}, bf16[256,512]{1,0:T(8,128)(2,1)S(1)}, u32[]{:S(2)}, u32[]{:S(2)}) collective-permute-start(bf16[256,512]{1,0:T(8,128)(2,1)S(1)} %broadcast_select_fusion), channel_id=1, source_target_pairs={{0,8},{4,12},{8,0},{12,4},{1,9},{5,13},{9,1},{13,5},{2,10},{6,14},... | collective-permute-start | bytes 786440 | tf_op jit(solution)/shard_map/ppermute | solution.py:198
  4.7 2.5 %collective-permute-start.4 = (bf16[256,512]{1,0:T(8,128)(2,1)S(1)}, bf16[256,512]{1,0:T(8,128)(2,1)S(1)}, u32[]{:S(2)}, u32[]{:S(2)}) collective-permute-start(bf16[256,512]{1,0:T(8,128)(2,1)S(1)} %broadcast_select_fusion), channel_id=1, source_target_pairs={{0,4},{4,8},{8,12},{12,0},{1,5},{5,9},{9,13},{13,1},{2,6},{6,10},{... | collective-permute-start | bytes 786440 | tf_op jit(solution)/shard_map/ppermute | solution.py:198
  7.2 14.9 %collective-permute-done.6 = bf16[256,512]{1,0:T(8,128)(2,1)S(1)} collective-permute-done((bf16[256,512]{1,0:T(8,128)(2,1)S(1)}, bf16[256,512]{1,0:T(8,128)(2,1)S(1)}, u32[]{:S(2)}, u32[]{:S(2)}) %collective-permute-start.6) | collective-permute-done | bytes 262176 | tf_op jit(solution)/shard_map/ppermute | solution.py:198
  22.2 4.7 %collective-permute-done.4 = bf16[256,512]{1,0:T(8,128)(2,1)S(1)} collective-permute-done((bf16[256,512]{1,0:T(8,128)(2,1)S(1)}, bf16[256,512]{1,0:T(8,128)(2,1)S(1)}, u32[]{:S(2)}, u32[]{:S(2)}) %collective-permute-start.4) | collective-permute-done | bytes 262176 | tf_op jit(solution)/shard_map/ppermute | solution.py:198
  27.0 0.1 collective-permute-start.7
  27.1 1.6 collective-permute-start.3
  28.6 0.4 reshape_squeeze.3
  29.0 1.9 constant_dynamic-slice_fusion.1
  30.9 0.8 copy.18
  31.7 0.2 collective-permute-start.20
  31.9 0.7 pad_add_fusion.1.place
  32.5 9.0 %collective-permute-done.3.x_next = bf16[128,2048]{1,0:T(8,128)(2,1)} collective-permute-done((bf16[128,2048]{1,0:T(8,128)(2,1)S(1)}, bf16[128,2048]{1,0:T(8,128)(2,1)}, u32[]{:S(2)}, u32[]{:S(2)}) %collective-permute-start.3) | collective-permute-done | bytes 524320 | tf_op jit(solution)/shard_map/ppermute | solution.py:213
  41.5 1.0 copy-done.2
  42.5 3.4 %project.1 = (bf16[128,512]{1,0:T(8,128)(2,1)}, bf16[128,512]{1,0:T(8,128)(2,1)}) custom-call(s32[3]{0:T(128)} %pad_add_fusion.1.place, bf16[128,2048]{1,0:T(8,128)(2,1)} %bitcast.38, bf16[128,2048]{1,0:T(8,128)(2,1)} %collective-permute-done.3.x_next, bf16[1024,512]{1,0:T(8,128)(2,1)} %copy-done, bf16[1024,512]{1,0:T(8,128)(2,1)} %copy-done.2), custom_call_target="tpu_custom_call" | custom-call | tf_op jit(solution)/shard_map/project/pallas_call | solution.py:52
  45.9 4.4 %collective-permute-start.8 = (bf16[128,512]{1,0:T(8,128)(2,1)}, bf16[128,512]{1,0:T(8,128)(2,1)S(1)}, u32[]{:S(2)}, u32[]{:S(2)}) collective-permute-start(bf16[128,512]{1,0:T(8,128)(2,1)} %get-tuple-element.20.refs_0_), channel_id=1, source_target_pairs={{0,4},{4,8},{8,12},{1,5},{5,9},{9,13},{2,6},{6,10},{10,14},{3,7},{... | collective-permute-start | bytes 393224 | tf_op jit(solution)/shard_map/ppermute | solution.py:201
  50.3 1.3 collective-permute-start.9
  51.6 0.7 collective-permute-start.2
  52.3 1.3 collective-permute-start.1
  53.6 0.7 copy.11.seg_col
  54.4 1.9 %collective-permute-start = (s32[128]{0:T(128)S(1)}, s32[128]{0:T(128)S(1)}, u32[]{:S(2)}, u32[]{:S(2)}) collective-permute-start(s32[128]{0:T(128)S(1)} %get-tuple-element.55), channel_id=1, source_target_pairs={{0,4},{4,8},{8,12},{1,5},{5,9},{9,13},{2,6},{6,10},{10,14},{3,7},{... | collective-permute-start | bytes 1544 | tf_op jit(solution)/shard_map/ppermute | solution.py:201
  56.3 0.1 copy.19
  56.4 2.4 %collective-permute-done.1 = s32[128]{0:T(128)S(1)} collective-permute-done((s32[128]{0:T(128)S(1)}, s32[128]{0:T(128)S(1)}, u32[]{:S(2)}, u32[]{:S(2)}) %collective-permute-start.1) | collective-permute-done | bytes 544 | tf_op jit(solution)/shard_map/ppermute | solution.py:201
  58.8 0.7 collective-permute-start.10
  59.5 0.4 collective-permute-done
  59.9 1.5 collective-permute-start.11
  61.4 5.1 %collective-permute-start.12 = (bf16[128,512]{1,0:T(8,128)(2,1)}, bf16[128,512]{1,0:T(8,128)(2,1)S(1)}, u32[]{:S(2)}, u32[]{:S(2)}) collective-permute-start(bf16[128,512]{1,0:T(8,128)(2,1)} %get-tuple-element.21), channel_id=1, source_target_pairs={{0,6},{2,4},{4,10},{6,8},{8,14},{10,12},{1,7},{3,5},{5,11},{7,9},{... | collective-permute-start | bytes 393224 | tf_op jit(solution)/shard_map/ppermute | solution.py:210
  66.5 3.0 %collective-permute-start.13 = (bf16[128,512]{1,0:T(8,128)(2,1)}, bf16[128,512]{1,0:T(8,128)(2,1)S(1)}, u32[]{:S(2)}, u32[]{:S(2)}) collective-permute-start(bf16[128,512]{1,0:T(8,128)(2,1)} %get-tuple-element.21), channel_id=1, source_target_pairs={{0,10},{2,8},{4,14},{6,12},{1,11},{3,9},{5,15},{7,13},{16,26},{18,... | collective-permute-start | bytes 393224 | tf_op jit(solution)/shard_map/ppermute | solution.py:210
  69.5 0.7 collective-permute-start.14
  70.2 0.6 pad_add_fusion
  70.8 3.1 %collective-permute-done.12.refs_5_ = bf16[128,512]{1,0:T(8,128)(2,1)S(1)} collective-permute-done((bf16[128,512]{1,0:T(8,128)(2,1)}, bf16[128,512]{1,0:T(8,128)(2,1)S(1)}, u32[]{:S(2)}, u32[]{:S(2)}) %collective-permute-start.12) | collective-permute-done | bytes 131104 | tf_op jit(solution)/shard_map/ppermute | solution.py:210
  73.9 4.2 %collective-permute-done.13.refs_6_ = bf16[128,512]{1,0:T(8,128)(2,1)S(1)} collective-permute-done((bf16[128,512]{1,0:T(8,128)(2,1)}, bf16[128,512]{1,0:T(8,128)(2,1)S(1)}, u32[]{:S(2)}, u32[]{:S(2)}) %collective-permute-start.13) | collective-permute-done | bytes 131104 | tf_op jit(solution)/shard_map/ppermute | solution.py:210
  78.1 0.6 copy-done.16
  78.8 8.5 %attend.1 = (bf16[128,2048]{1,0:T(8,128)(2,1)}, bf16[128,2048]{1,0:T(8,128)(2,1)}, f32[128,512]{1,0:T(8,128)}, bf16[128,512]{1,0:T(8,128)(2,1)}, bf16[128,512]{1...) custom-call(s32[3]{0:T(128)} %pad_add_fusion.1.place, ...), custom_call_target="tpu_custom_call" | custom-call | tf_op jit(solution)/shard_map/attend/pallas_call | solution.py:130
  87.3 1.0 pad_maximum_fusion.5
  88.3 0.7 collective-permute-start.17
  89.0 1.0 pad_maximum_fusion.4
  90.0 1.3 collective-permute-start.16
  91.4 2.1 %collective-permute-start.15 = (bf16[128,1024]{1,0:T(8,128)(2,1)S(1)}, bf16[128,1024]{1,0:T(8,128)(2,1)S(1)}, u32[]{:S(2)}, u32[]{:S(2)}) collective-permute-start(bf16[128,1024]{1,0:T(8,128)(2,1)S(1)} %pad_maximum_fusion.3), channel_id=1, source_target_pairs={{4,0},{8,4},{12,8},{5,1},{9,5},{13,9},{6,2},{10,6},{14,10},{7,3},{... | collective-permute-start | bytes 786440 | tf_op jit(solution)/shard_map/ppermute | solution.py:204
  93.5 1.9 %collective-permute-start.26 = (bf16[256,256]{1,0:T(8,128)(2,1)S(1)}, bf16[256,256]{1,0:T(8,128)(2,1)S(1)}, u32[]{:S(2)}, u32[]{:S(2)}) collective-permute-start(bf16[256,256]{1,0:T(8,128)(2,1)S(1)} %get-tuple-element.38), channel_id=1, source_target_pairs={{4,0},{8,4},{12,8},{5,1},{9,5},{13,9},{6,2},{10,6},{14,10},{7,3},{... | collective-permute-start | bytes 393224 | tf_op jit(solution)/shard_map/ppermute | solution.py:204
  95.5 0.7 collective-permute-start.25
  96.2 10.5 %collective-permute-done.16 = bf16[128,1024]{1,0:T(8,128)(2,1)S(1)} collective-permute-done((bf16[128,1024]{1,0:T(8,128)(2,1)S(1)}, bf16[128,1024]{1,0:T(8,128)(2,1)S(1)}, u32[]{:S(2)}, u32[]{:S(2)}) %collective-permute-start.16) | collective-permute-done | bytes 262176 | tf_op jit(solution)/shard_map/ppermute | solution.py:204
  106.6 8.6 %collective-permute-done.15 = bf16[128,1024]{1,0:T(8,128)(2,1)S(1)} collective-permute-done((bf16[128,1024]{1,0:T(8,128)(2,1)S(1)}, bf16[128,1024]{1,0:T(8,128)(2,1)S(1)}, u32[]{:S(2)}, u32[]{:S(2)}) %collective-permute-start.15) | collective-permute-done | bytes 262176 | tf_op jit(solution)/shard_map/ppermute | solution.py:204
  115.3 0.1 fusion.2
  115.5 1.0 collective-permute-start.28
  116.5 1.0 collective-permute-start.27
  117.5 6.0 %collective-permute-done.26 = bf16[256,256]{1,0:T(8,128)(2,1)S(1)} collective-permute-done((bf16[256,256]{1,0:T(8,128)(2,1)S(1)}, bf16[256,256]{1,0:T(8,128)(2,1)S(1)}, u32[]{:S(2)}, u32[]{:S(2)}) %collective-permute-start.26) | collective-permute-done | bytes 131104 | tf_op jit(solution)/shard_map/ppermute | solution.py:204
  123.5 1.3 collective-permute-start.24
  124.8 0.7 collective-permute-start.22
  125.5 15.0 %collective-permute-done.29 = bf16[128,1024]{1,0:T(8,128)(2,1)S(1)} collective-permute-done((bf16[128,1024]{1,0:T(8,128)(2,1)S(1)}, bf16[128,1024]{1,0:T(8,128)(2,1)S(1)}, u32[]{:S(2)}, u32[]{:S(2)}) %collective-permute-start.29) | collective-permute-done | bytes 262176 | tf_op jit(solution)/shard_map/ppermute | solution.py:198
  140.6 1.3 collective-permute-start.23
  141.9 6.2 %collective-permute-start.21 = (bf16[256,256]{1,0:T(8,128)(2,1)S(1)}, bf16[256,256]{1,0:T(8,128)(2,1)S(1)}, u32[]{:S(2)}, u32[]{:S(2)}) collective-permute-start(bf16[256,256]{1,0:T(8,128)(2,1)S(1)} %get-tuple-element.40), channel_id=1, source_target_pairs={{0,4},{4,8},{8,12},{1,5},{5,9},{9,13},{2,6},{6,10},{10,14},{3,7},{... | collective-permute-start | bytes 393224 | tf_op jit(solution)/shard_map/ppermute | solution.py:201
  148.3 4.2 %collective-permute-done.21 = bf16[256,256]{1,0:T(8,128)(2,1)S(1)} collective-permute-done((bf16[256,256]{1,0:T(8,128)(2,1)S(1)}, bf16[256,256]{1,0:T(8,128)(2,1)S(1)}, u32[]{:S(2)}, u32[]{:S(2)}) %collective-permute-start.21) | collective-permute-done | bytes 131104 | tf_op jit(solution)/shard_map/ppermute | solution.py:201
  152.6 8.6 %collective-permute-done.18.b_own = bf16[1024,512]{1,0:T(8,128)(2,1)S(1)} collective-permute-done((bf16[1024,512]{1,0:T(8,128)(2,1)S(1)}, bf16[1024,512]{1,0:T(8,128)(2,1)S(1)}, u32[]{:S(2)}, u32[]{:S(2)}) %collective-permute-start.18) | collective-permute-done | bytes 1048608 | tf_op jit(solution)/shard_map/ppermute | solution.py:213
  161.2 0.9 pad_maximum_fusion.6
  162.1 1.0 copy-done.7
  163.1 3.2 %weight_grad.1 = bf16[256,1024]{1,0:T(8,128)(2,1)} custom-call(bf16[512,256]{1,0:T(8,128)(2,1)} %get-tuple-element.57.x_own, bf16[512,256]{1,0:T(8,128)(2,1)} %get-tuple-element.58.x_other, bf16[512,1024]{1,0:T(8,128)(2,1)} %copy-done.3, bf16[512,1024]{1,0:T(8,128)(2,1)} %copy-done.7), custom_call_target="tpu_custom_call" | custom-call | tf_op jit(solution)/shard_map/weight_grad/pallas_call | solution.py:177
  166.4 0.6 collective-permute-start.31
  167.0 0.7 fusion.5
  167.7 13.1 %collective-permute-done.31 = bf16[256,1024]{1,0:T(8,128)(2,1)S(1)} collective-permute-done((bf16[256,1024]{1,0:T(8,128)(2,1)}, bf16[256,1024]{1,0:T(8,128)(2,1)S(1)}, u32[]{:S(2)}, u32[]{:S(2)}) %collective-permute-start.31) | collective-permute-done | bytes 524320 | tf_op jit(solution)/shard_map/ppermute | solution.py:213
  180.9 1.2 add_convert_fusion
  182.1 0.8 fusion.4
  182.9 1.0 copy-done.8
  183.9 4.8 %input_grad.1 = bf16[128,2048]{1,0:T(8,128)(2,1)} custom-call(s32[3]{0:T(128)} %pad_add_fusion.1.place, bf16[128,512]{1,0:T(8,128)(2,1)} %get-tuple-element.46.gk, bf16[128,512]{1,0:T(8,128)(2,1)} %get-tuple-element.45.gv, bf16[1024,512]{1,0:T(8,128)(2,1)} %copy-done, bf16[1024,512]{1,0:T(8,128)(2,1)} %copy-done.2, bf16[1024,512]{1,0:T(8,128)(2,1)} %copy-done.6, ...), custom_call_target="tpu_custom_call" | custom-call | tf_op jit(solution)/shard_map/input_grad/pallas_call | solution.py:161
  (76 shorter events, 0.8 us)
Async XLA Ops:
  1.6 25.4 %copy-start.4 = (bf16[1,128,2048]{2,1,0:T(8,128)(2,1)S(1)}, bf16[1,128,2048]{2,1,0:T(8,128)(2,1)}, u32[]{:S(2)}) copy-start(bf16[1,128,2048]{2,1,0:T(8,128)(2,1)} %param.6) | copy-start | bytes 1572868
  1.6 20.5 %collective-permute-start.6 = (bf16[256,512]{1,0:T(8,128)(2,1)S(1)}, bf16[256,512]{1,0:T(8,128)(2,1)S(1)}, u32[]{:S(2)}, u32[]{:S(2)}) collective-permute-start(bf16[256,512]{1,0:T(8,128)(2,1)S(1)} %broadcast_select_fusion), channel_id=1, source_target_pairs={{0,12},{4,0},{8,4},{12,8},{1,13},{5,1},{9,5},{13,9},{2,14},{6,2},{... | collective-permute-start | bytes 786440 | tf_op jit(solution)/shard_map/ppermute | solution.py:198
  1.7 20.5 %collective-permute-start.5 = (bf16[256,512]{1,0:T(8,128)(2,1)S(1)}, bf16[256,512]{1,0:T(8,128)(2,1)S(1)}, u32[]{:S(2)}, u32[]{:S(2)}) collective-permute-start(bf16[256,512]{1,0:T(8,128)(2,1)S(1)} %broadcast_select_fusion), channel_id=1, source_target_pairs={{0,8},{4,12},{8,0},{12,4},{1,9},{5,13},{9,1},{13,5},{2,10},{6,14},... | collective-permute-start | bytes 786440 | tf_op jit(solution)/shard_map/ppermute | solution.py:198
  4.7 22.2 %collective-permute-start.4 = (bf16[256,512]{1,0:T(8,128)(2,1)S(1)}, bf16[256,512]{1,0:T(8,128)(2,1)S(1)}, u32[]{:S(2)}, u32[]{:S(2)}) collective-permute-start(bf16[256,512]{1,0:T(8,128)(2,1)S(1)} %broadcast_select_fusion), channel_id=1, source_target_pairs={{0,4},{4,8},{8,12},{12,0},{1,5},{5,9},{9,13},{13,1},{2,6},{6,10},{... | collective-permute-start | bytes 786440 | tf_op jit(solution)/shard_map/ppermute | solution.py:198
  27.0 3.9 %copy-start = (bf16[1024,512]{1,0:T(8,128)(2,1)}, bf16[1024,512]{1,0:T(8,128)(2,1)S(1)}, u32[]{:S(2)}) copy-start(bf16[1024,512]{1,0:T(8,128)(2,1)S(1)} %pad_maximum_fusion.w_own.a_own) | copy-start | bytes 3145732
  27.0 14.5 %collective-permute-start.7 = (bf16[1024,512]{1,0:T(8,128)(2,1)S(1)}, bf16[1024,512]{1,0:T(8,128)(2,1)S(1)}, u32[]{:S(2)}, u32[]{:S(2)}) collective-permute-start(bf16[1024,512]{1,0:T(8,128)(2,1)S(1)} %pad_maximum_fusion.w_own.a_own), channel_id=1, source_target_pairs={{0,1},{1,0},{2,3},{3,2},{4,5},{5,4},{6,7},{7,6},{8,9},{9,8},{10,11... | collective-permute-start | bytes 3145736 | tf_op jit(solution)/shard_map/ppermute | solution.py:216
  27.1 14.4 %collective-permute-start.3 = (bf16[128,2048]{1,0:T(8,128)(2,1)S(1)}, bf16[128,2048]{1,0:T(8,128)(2,1)}, u32[]{:S(2)}, u32[]{:S(2)}) collective-permute-start(bf16[128,2048]{1,0:T(8,128)(2,1)S(1)} %bitcast.39), channel_id=1, source_target_pairs={{0,2},{2,0},{1,3},{3,1},{4,6},{6,4},{5,7},{7,5},{8,10},{10,8},{9,1... | collective-permute-start | bytes 1572872 | tf_op jit(solution)/shard_map/ppermute | solution.py:213
  31.7 29.7 %collective-permute-start.20 = (bf16[128,4,256]{2,0,1:T(8,128)(2,1)}, bf16[128,4,256]{2,0,1:T(8,128)(2,1)S(1)}, u32[]{:S(2)}, u32[]{:S(2)}) collective-permute-start(bf16[128,4,256]{2,0,1:T(8,128)(2,1)} %bitcast.34), channel_id=1, source_target_pairs={{0,1},{1,0},{2,3},{3,2},{4,5},{5,4},{6,7},{7,6},{8,9},{9,8},{10,11... | collective-permute-start | bytes 786440 | tf_op jit(solution)/shard_map/ppermute | solution.py:216
  32.5 19.1 %copy-start.20 = (s32[1,128]{1,0:T(1,128)S(1)}, s32[1,128]{1,0:T(1,128)}, u32[]{:S(2)}) copy-start(s32[1,128]{1,0:T(1,128)} %param.10) | copy-start | bytes 1540
  32.5 23.8 %copy-start.5 = (bf16[128,4,1,256]{3,2,1,0:T(2,128)(2,1)S(1)}, bf16[128,4,1,256]{3,2,1,0:T(2,128)(2,1)}, u32[]{:S(2)}) copy-start(bf16[128,4,1,256]{3,2,1,0:T(2,128)(2,1)} %get-tuple-element.43) | copy-start | bytes 786436
  41.5 1.0 copy-start.2
  45.9 20.6 %collective-permute-start.8 = (bf16[128,512]{1,0:T(8,128)(2,1)}, bf16[128,512]{1,0:T(8,128)(2,1)S(1)}, u32[]{:S(2)}, u32[]{:S(2)}) collective-permute-start(bf16[128,512]{1,0:T(8,128)(2,1)} %get-tuple-element.20.refs_0_), channel_id=1, source_target_pairs={{0,4},{4,8},{8,12},{1,5},{5,9},{9,13},{2,6},{6,10},{10,14},{3,7},{... | collective-permute-start | bytes 393224 | tf_op jit(solution)/shard_map/ppermute | solution.py:201
  50.3 19.2 %collective-permute-start.9 = (bf16[128,512]{1,0:T(8,128)(2,1)}, bf16[128,512]{1,0:T(8,128)(2,1)S(1)}, u32[]{:S(2)}, u32[]{:S(2)}) collective-permute-start(bf16[128,512]{1,0:T(8,128)(2,1)} %get-tuple-element.20.refs_0_), channel_id=1, source_target_pairs={{0,8},{4,12},{1,9},{5,13},{2,10},{6,14},{3,11},{7,15},{16,24},{20,... | collective-permute-start | bytes 393224 | tf_op jit(solution)/shard_map/ppermute | solution.py:201
  51.6 2.7 %collective-permute-start.2 = (s32[128]{0:T(128)S(1)}, s32[128]{0:T(128)S(1)}, u32[]{:S(2)}, u32[]{:S(2)}) collective-permute-start(s32[128]{0:T(128)S(1)} %get-tuple-element.55), channel_id=1, source_target_pairs={{0,12},{1,13},{2,14},{3,15},{16,28},{17,29},{18,30},{19,31}} | collective-permute-start | bytes 1544 | tf_op jit(solution)/shard_map/ppermute | solution.py:201
  52.3 6.5 %collective-permute-start.1 = (s32[128]{0:T(128)S(1)}, s32[128]{0:T(128)S(1)}, u32[]{:S(2)}, u32[]{:S(2)}) collective-permute-start(s32[128]{0:T(128)S(1)} %get-tuple-element.55), channel_id=1, source_target_pairs={{0,8},{4,12},{1,9},{5,13},{2,10},{6,14},{3,11},{7,15},{16,24},{20,... | collective-permute-start | bytes 1544 | tf_op jit(solution)/shard_map/ppermute | solution.py:201
  54.4 5.5 %collective-permute-start = (s32[128]{0:T(128)S(1)}, s32[128]{0:T(128)S(1)}, u32[]{:S(2)}, u32[]{:S(2)}) collective-permute-start(s32[128]{0:T(128)S(1)} %get-tuple-element.55), channel_id=1, source_target_pairs={{0,4},{4,8},{8,12},{1,5},{5,9},{9,13},{2,6},{6,10},{10,14},{3,7},{... | collective-permute-start | bytes 1544 | tf_op jit(solution)/shard_map/ppermute | solution.py:201
  58.8 12.0 %collective-permute-start.10 = (bf16[128,512]{1,0:T(8,128)(2,1)}, bf16[128,512]{1,0:T(8,128)(2,1)S(1)}, u32[]{:S(2)}, u32[]{:S(2)}) collective-permute-start(bf16[128,512]{1,0:T(8,128)(2,1)} %get-tuple-element.20.refs_0_), channel_id=1, source_target_pairs={{0,12},{1,13},{2,14},{3,15},{16,28},{17,29},{18,30},{19,31}} | collective-permute-start | bytes 393224 | tf_op jit(solution)/shard_map/ppermute | solution.py:201
  59.9 10.9 %collective-permute-start.11 = (bf16[128,512]{1,0:T(8,128)(2,1)}, bf16[128,512]{1,0:T(8,128)(2,1)S(1)}, u32[]{:S(2)}, u32[]{:S(2)}) collective-permute-start(bf16[128,512]{1,0:T(8,128)(2,1)} %get-tuple-element.21), channel_id=1, source_target_pairs={{0,2},{2,0},{4,6},{6,4},{8,10},{10,8},{12,14},{14,12},{1,3},{3,1},... | collective-permute-start | bytes 393224 | tf_op jit(solution)/shard_map/ppermute | solution.py:210
  61.4 12.5 %collective-permute-start.12 = (bf16[128,512]{1,0:T(8,128)(2,1)}, bf16[128,512]{1,0:T(8,128)(2,1)S(1)}, u32[]{:S(2)}, u32[]{:S(2)}) collective-permute-start(bf16[128,512]{1,0:T(8,128)(2,1)} %get-tuple-element.21), channel_id=1, source_target_pairs={{0,6},{2,4},{4,10},{6,8},{8,14},{10,12},{1,7},{3,5},{5,11},{7,9},{... | collective-permute-start | bytes 393224 | tf_op jit(solution)/shard_map/ppermute | solution.py:210
  66.5 11.6 %copy-start.11 = (bf16[128,512]{1,0:T(8,128)(2,1)}, bf16[128,512]{1,0:T(8,128)(2,1)S(1)}, u32[]{:S(2)}) copy-start(bf16[128,512]{1,0:T(8,128)(2,1)S(1)} %collective-permute-done.8.refs_1_) | copy-start | bytes 393220
  66.5 11.6 %collective-permute-start.13 = (bf16[128,512]{1,0:T(8,128)(2,1)}, bf16[128,512]{1,0:T(8,128)(2,1)S(1)}, u32[]{:S(2)}, u32[]{:S(2)}) collective-permute-start(bf16[128,512]{1,0:T(8,128)(2,1)} %get-tuple-element.21), channel_id=1, source_target_pairs={{0,10},{2,8},{4,14},{6,12},{1,11},{3,9},{5,15},{7,13},{16,26},{18,... | collective-permute-start | bytes 393224 | tf_op jit(solution)/shard_map/ppermute | solution.py:210
  69.5 8.6 %copy-start.12 = (bf16[128,512]{1,0:T(8,128)(2,1)}, bf16[128,512]{1,0:T(8,128)(2,1)S(1)}, u32[]{:S(2)}) copy-start(bf16[128,512]{1,0:T(8,128)(2,1)S(1)} %collective-permute-done.9.refs_2_) | copy-start | bytes 393220
  69.5 8.6 %collective-permute-start.14 = (bf16[128,512]{1,0:T(8,128)(2,1)}, bf16[128,512]{1,0:T(8,128)(2,1)S(1)}, u32[]{:S(2)}, u32[]{:S(2)}) collective-permute-start(bf16[128,512]{1,0:T(8,128)(2,1)} %get-tuple-element.21), channel_id=1, source_target_pairs={{0,14},{2,12},{1,15},{3,13},{16,30},{18,28},{17,31},{19,29}} | collective-permute-start | bytes 393224 | tf_op jit(solution)/shard_map/ppermute | solution.py:210
  70.8 7.3 %copy-start.13 = (bf16[128,512]{1,0:T(8,128)(2,1)}, bf16[128,512]{1,0:T(8,128)(2,1)S(1)}, u32[]{:S(2)}) copy-start(bf16[128,512]{1,0:T(8,128)(2,1)S(1)} %collective-permute-done.10.refs_3_) | copy-start | bytes 393220
  70.8 7.3 %copy-start.14 = (bf16[128,512]{1,0:T(8,128)(2,1)}, bf16[128,512]{1,0:T(8,128)(2,1)S(1)}, u32[]{:S(2)}) copy-start(bf16[128,512]{1,0:T(8,128)(2,1)S(1)} %collective-permute-done.11.refs_4_) | copy-start | bytes 393220
  73.9 4.2 %copy-start.15 = (bf16[128,512]{1,0:T(8,128)(2,1)}, bf16[128,512]{1,0:T(8,128)(2,1)S(1)}, u32[]{:S(2)}) copy-start(bf16[128,512]{1,0:T(8,128)(2,1)S(1)} %collective-permute-done.12.refs_5_) | copy-start | bytes 393220
  78.1 0.6 copy-start.16
  78.1 0.7 copy-start.17
  87.3 4.0 %copy-start.18 = (bf16[128,512]{1,0:T(8,128)(2,1)S(1)}, bf16[128,512]{1,0:T(8,128)(2,1)}, u32[]{:S(2)}) copy-start(bf16[128,512]{1,0:T(8,128)(2,1)} %get-tuple-element.26) | copy-start | bytes 393220
  87.3 4.0 %copy-start.19 = (bf16[128,512]{1,0:T(8,128)(2,1)S(1)}, bf16[128,512]{1,0:T(8,128)(2,1)}, u32[]{:S(2)}) copy-start(bf16[128,512]{1,0:T(8,128)(2,1)} %get-tuple-element.27) | copy-start | bytes 393220
  88.3 7.8 %collective-permute-start.17 = (bf16[128,1024]{1,0:T(8,128)(2,1)S(1)}, bf16[128,1024]{1,0:T(8,128)(2,1)S(1)}, u32[]{:S(2)}, u32[]{:S(2)}) collective-permute-start(bf16[128,1024]{1,0:T(8,128)(2,1)S(1)} %pad_maximum_fusion.5), channel_id=1, source_target_pairs={{12,0},{13,1},{14,2},{15,3},{28,16},{29,17},{30,18},{31,19}} | collective-permute-start | bytes 786440 | tf_op jit(solution)/shard_map/ppermute | solution.py:204
  90.0 16.6 %collective-permute-start.16 = (bf16[128,1024]{1,0:T(8,128)(2,1)S(1)}, bf16[128,1024]{1,0:T(8,128)(2,1)S(1)}, u32[]{:S(2)}, u32[]{:S(2)}) collective-permute-start(bf16[128,1024]{1,0:T(8,128)(2,1)S(1)} %pad_maximum_fusion.4), channel_id=1, source_target_pairs={{8,0},{12,4},{9,1},{13,5},{10,2},{14,6},{11,3},{15,7},{24,16},{28,... | collective-permute-start | bytes 786440 | tf_op jit(solution)/shard_map/ppermute | solution.py:204
  91.4 23.9 %copy-start.9 = (f32[128,512]{1,0:T(8,128)S(1)}, f32[128,512]{1,0:T(8,128)}, u32[]{:S(2)}) copy-start(f32[128,512]{1,0:T(8,128)} %get-tuple-element.24) | copy-start | bytes 786436
  91.4 23.9 %copy-start.10 = (f32[128,512]{1,0:T(8,128)S(1)}, f32[128,512]{1,0:T(8,128)}, u32[]{:S(2)}) copy-start(f32[128,512]{1,0:T(8,128)} %get-tuple-element.25) | copy-start | bytes 786436
  91.4 23.9 %collective-permute-start.15 = (bf16[128,1024]{1,0:T(8,128)(2,1)S(1)}, bf16[128,1024]{1,0:T(8,128)(2,1)S(1)}, u32[]{:S(2)}, u32[]{:S(2)}) collective-permute-start(bf16[128,1024]{1,0:T(8,128)(2,1)S(1)} %pad_maximum_fusion.3), channel_id=1, source_target_pairs={{4,0},{8,4},{12,8},{5,1},{9,5},{13,9},{6,2},{10,6},{14,10},{7,3},{... | collective-permute-start | bytes 786440 | tf_op jit(solution)/shard_map/ppermute | solution.py:204
  93.5 30.0 %collective-permute-start.26 = (bf16[256,256]{1,0:T(8,128)(2,1)S(1)}, bf16[256,256]{1,0:T(8,128)(2,1)S(1)}, u32[]{:S(2)}, u32[]{:S(2)}) collective-permute-start(bf16[256,256]{1,0:T(8,128)(2,1)S(1)} %get-tuple-element.38), channel_id=1, source_target_pairs={{4,0},{8,4},{12,8},{5,1},{9,5},{13,9},{6,2},{10,6},{14,10},{7,3},{... | collective-permute-start | bytes 393224 | tf_op jit(solution)/shard_map/ppermute | solution.py:204
  95.5 29.3 %collective-permute-start.25 = (bf16[256,256]{1,0:T(8,128)(2,1)S(1)}, bf16[256,256]{1,0:T(8,128)(2,1)S(1)}, u32[]{:S(2)}, u32[]{:S(2)}) collective-permute-start(bf16[256,256]{1,0:T(8,128)(2,1)S(1)} %get-tuple-element.41), channel_id=1, source_target_pairs={{0,12},{1,13},{2,14},{3,15},{16,28},{17,29},{18,30},{19,31}} | collective-permute-start | bytes 393224 | tf_op jit(solution)/shard_map/ppermute | solution.py:201
  115.3 25.3 %copy-start.1 = (bf16[1024,512]{1,0:T(8,128)(2,1)S(1)}, bf16[1024,512]{1,0:T(8,128)(2,1)}, u32[]{:S(2)}) copy-start(bf16[1024,512]{1,0:T(8,128)(2,1)} %copy-done) | copy-start | bytes 3145732
  115.4 25.1 %collective-permute-start.29 = (bf16[128,1024]{1,0:T(8,128)(2,1)S(1)}, bf16[128,1024]{1,0:T(8,128)(2,1)S(1)}, u32[]{:S(2)}, u32[]{:S(2)}) collective-permute-start(bf16[128,1024]{1,0:T(8,128)(2,1)S(1)} %fusion.2), channel_id=1, source_target_pairs={{0,12},{4,0},{8,4},{12,8},{1,13},{5,1},{9,5},{13,9},{2,14},{6,2},{... | collective-permute-start | bytes 786440 | tf_op jit(solution)/shard_map/ppermute | solution.py:198
  115.5 25.1 %collective-permute-start.28 = (bf16[128,1024]{1,0:T(8,128)(2,1)S(1)}, bf16[128,1024]{1,0:T(8,128)(2,1)S(1)}, u32[]{:S(2)}, u32[]{:S(2)}) collective-permute-start(bf16[128,1024]{1,0:T(8,128)(2,1)S(1)} %fusion.2), channel_id=1, source_target_pairs={{0,8},{4,12},{8,0},{12,4},{1,9},{5,13},{9,1},{13,5},{2,10},{6,14},... | collective-permute-start | bytes 786440 | tf_op jit(solution)/shard_map/ppermute | solution.py:198
  116.5 25.4 %collective-permute-start.27 = (bf16[128,1024]{1,0:T(8,128)(2,1)S(1)}, bf16[128,1024]{1,0:T(8,128)(2,1)S(1)}, u32[]{:S(2)}, u32[]{:S(2)}) collective-permute-start(bf16[128,1024]{1,0:T(8,128)(2,1)S(1)} %fusion.2), channel_id=1, source_target_pairs={{0,4},{4,8},{8,12},{12,0},{1,5},{5,9},{9,13},{13,1},{2,6},{6,10},{... | collective-permute-start | bytes 786440 | tf_op jit(solution)/shard_map/ppermute | solution.py:198
  123.5 24.7 %collective-permute-start.24 = (bf16[256,256]{1,0:T(8,128)(2,1)S(1)}, bf16[256,256]{1,0:T(8,128)(2,1)S(1)}, u32[]{:S(2)}, u32[]{:S(2)}) collective-permute-start(bf16[256,256]{1,0:T(8,128)(2,1)S(1)} %get-tuple-element.39), channel_id=1, source_target_pairs={{8,0},{12,4},{9,1},{13,5},{10,2},{14,6},{11,3},{15,7},{24,16},{28,... | collective-permute-start | bytes 393224 | tf_op jit(solution)/shard_map/ppermute | solution.py:204
  124.8 23.5 %collective-permute-start.22 = (bf16[256,256]{1,0:T(8,128)(2,1)S(1)}, bf16[256,256]{1,0:T(8,128)(2,1)S(1)}, u32[]{:S(2)}, u32[]{:S(2)}) collective-permute-start(bf16[256,256]{1,0:T(8,128)(2,1)S(1)} %get-tuple-element.37), channel_id=1, source_target_pairs={{12,0},{13,1},{14,2},{15,3},{28,16},{29,17},{30,18},{31,19}} | collective-permute-start | bytes 393224 | tf_op jit(solution)/shard_map/ppermute | solution.py:204
  140.6 20.7 %collective-permute-start.18 = (bf16[1024,512]{1,0:T(8,128)(2,1)S(1)}, bf16[1024,512]{1,0:T(8,128)(2,1)S(1)}, u32[]{:S(2)}, u32[]{:S(2)}) collective-permute-start(bf16[1024,512]{1,0:T(8,128)(2,1)S(1)} %copy-done.1), channel_id=1, source_target_pairs={{0,2},{2,0},{1,3},{3,1},{4,6},{6,4},{5,7},{7,5},{8,10},{10,8},{9,1... | collective-permute-start | bytes 3145736 | tf_op jit(solution)/shard_map/ppermute | solution.py:213
  140.6 7.7 %collective-permute-start.23 = (bf16[256,256]{1,0:T(8,128)(2,1)S(1)}, bf16[256,256]{1,0:T(8,128)(2,1)S(1)}, u32[]{:S(2)}, u32[]{:S(2)}) collective-permute-start(bf16[256,256]{1,0:T(8,128)(2,1)S(1)} %get-tuple-element.42), channel_id=1, source_target_pairs={{0,8},{4,12},{1,9},{5,13},{2,10},{6,14},{3,11},{7,15},{16,24},{20,... | collective-permute-start | bytes 393224 | tf_op jit(solution)/shard_map/ppermute | solution.py:201
  141.9 10.7 %collective-permute-start.21 = (bf16[256,256]{1,0:T(8,128)(2,1)S(1)}, bf16[256,256]{1,0:T(8,128)(2,1)S(1)}, u32[]{:S(2)}, u32[]{:S(2)}) collective-permute-start(bf16[256,256]{1,0:T(8,128)(2,1)S(1)} %get-tuple-element.40), channel_id=1, source_target_pairs={{0,4},{4,8},{8,12},{1,5},{5,9},{9,13},{2,6},{6,10},{10,14},{3,7},{... | collective-permute-start | bytes 393224 | tf_op jit(solution)/shard_map/ppermute | solution.py:201
  148.2 14.0 %copy-start.3 = (bf16[512,1024]{1,0:T(8,128)(2,1)}, bf16[512,1024]{1,0:T(8,128)(2,1)S(1)}, u32[]{:S(2)}) copy-start(bf16[512,1024]{1,0:T(8,128)(2,1)S(1)} %pad_maximum_fusion.1.g_own) | copy-start | bytes 3145732
  148.2 14.0 %collective-permute-start.30 = (bf16[512,1024]{1,0:T(8,128)(2,1)S(1)}, bf16[512,1024]{1,0:T(8,128)(2,1)S(1)}, u32[]{:S(2)}, u32[]{:S(2)}) collective-permute-start(bf16[512,1024]{1,0:T(8,128)(2,1)S(1)} %pad_maximum_fusion.1.g_own), channel_id=1, source_target_pairs={{0,1},{1,0},{2,3},{3,2},{4,5},{5,4},{6,7},{7,6},{8,9},{9,8},{10,11... | collective-permute-start | bytes 3145736 | tf_op jit(solution)/shard_map/ppermute | solution.py:216
  161.2 5.2 %copy-start.6 = (bf16[1024,512]{1,0:T(8,128)(2,1)}, bf16[1024,512]{1,0:T(8,128)(2,1)S(1)}, u32[]{:S(2)}) copy-start(bf16[1024,512]{1,0:T(8,128)(2,1)S(1)} %collective-permute-done.18.b_own) | copy-start | bytes 3145732
  161.2 21.7 %collective-permute-start.19 = (bf16[1024,512]{1,0:T(8,128)(2,1)S(1)}, bf16[1024,512]{1,0:T(8,128)(2,1)S(1)}, u32[]{:S(2)}, u32[]{:S(2)}) collective-permute-start(bf16[1024,512]{1,0:T(8,128)(2,1)S(1)} %collective-permute-done.18.b_own), channel_id=1, source_target_pairs={{0,1},{1,0},{2,3},{3,2},{4,5},{5,4},{6,7},{7,6},{8,9},{9,8},{10,11... | collective-permute-start | bytes 3145736 | tf_op jit(solution)/shard_map/ppermute | solution.py:216
  162.1 1.0 copy-start.7
  166.4 14.5 %collective-permute-start.31 = (bf16[256,1024]{1,0:T(8,128)(2,1)}, bf16[256,1024]{1,0:T(8,128)(2,1)S(1)}, u32[]{:S(2)}, u32[]{:S(2)}) collective-permute-start(bf16[256,1024]{1,0:T(8,128)(2,1)} %weight_grad.1), channel_id=1, source_target_pairs={{0,2},{2,0},{1,3},{3,1},{4,6},{6,4},{5,7},{7,5},{8,10},{10,8},{9,1... | collective-permute-start | bytes 1572872 | tf_op jit(solution)/shard_map/ppermute | solution.py:213
  182.9 1.0 copy-start.8

commit v2 on v1

v2 whole, which is shorter than its diff:
```python
import functools
import math

import jax
import jax.numpy as jnp
from jax import lax
from jax.experimental import pallas as pl
from jax.experimental.pallas import tpu as pltpu
from jax.sharding import PartitionSpec as P

HEADS = 16
KV_HEADS = 4
HEAD_DIM = 128
KV_WIDTH = KV_HEADS * HEAD_DIM
GROUP = HEADS // KV_HEADS
PARTS = 2
LOG2E = 1.4426950408889634
MASKED = -1e30
EXTRA = 16
VMEM_LIMIT = 56 * 1024 * 1024


def params(**kw):
    return pltpu.CompilerParams(vmem_limit_bytes=VMEM_LIMIT, **kw)


def vspec():
    return pl.BlockSpec(memory_space=pltpu.VMEM)


def sspec():
    return pl.BlockSpec(memory_space=pltpu.SMEM)


def assemble(full_ref, own_ref, other_ref, place, count, rows):
    z, c = place[0], place[1]
    for k in range(count):
        src = lax.rem(z - k + count, count)
        for ref, core in ((own_ref, c), (other_ref, 1 - c)):
            start = pl.multiple_of((src * 2 + core) * rows, rows)
            full_ref[pl.ds(start, rows), :] = ref[k * rows : (k + 1) * rows, :]


def project_kernel(
    place, seg, x_own, x_next, w_own, w_other, out_own, out_next, full, *, count, rows
):
    assemble(full, w_own, w_other, place, count, rows)
    w = full[...]
    block = x_own.shape[0]
    out_own[:block, :] = jnp.dot(x_own[...], w, preferred_element_type=jnp.float32).astype(
        jnp.bfloat16
    )
    ids = (seg[...] + 1).astype(jnp.float32)
    wide = jnp.concatenate([jnp.broadcast_to(ids, (EXTRA, block))] * (KV_WIDTH // block), axis=1)
    out_own[block:, :] = wide.astype(jnp.bfloat16)
    out_next[...] = jnp.dot(x_next[...], w, preferred_element_type=jnp.float32).astype(jnp.bfloat16)


def project(place, seg, x_own, x_next, w_own, w_other, count, rows):
    width = w_own.shape[1]
    block = x_own.shape[0]
    return pl.pallas_call(
        functools.partial(project_kernel, count=count, rows=rows),
        in_specs=[sspec()] + [vspec()] * 5,
        out_specs=[vspec()] * 2,
        out_shape=[
            jax.ShapeDtypeStruct((block + EXTRA, width), jnp.bfloat16),
            jax.ShapeDtypeStruct((block, width), jnp.bfloat16),
        ],
        scratch_shapes=[pltpu.VMEM((2 * count * rows, width), jnp.bfloat16)],
        compiler_params=params(),
        name="project",
    )(place, seg, x_own, x_next, w_own, w_other)


def pack_kernel(place, own, mate, *refs, count):
    cols, outs = refs[: count - 1], refs[count - 1 :]
    block, width = mate.shape
    half = width // PARTS
    first = jnp.concatenate([own[:block, :half], mate[:, :half]], axis=1)
    tail = own[block:, :]
    outs[0][:block, :] = first
    outs[0][block:, :] = tail
    outs[1][...] = jnp.concatenate([own[:block, half:], mate[:, half:]], axis=1)
    for k in range(1, count):
        goes_up = place[0] + k < count
        outs[k + 1][:block, :] = jnp.where(goes_up, first, cols[k - 1][...])
        outs[k + 1][block:, :] = jnp.where(goes_up, tail, jnp.zeros_like(tail))


def pack(place, own, mate, cols):
    count = len(cols) + 1
    tall = jax.ShapeDtypeStruct(own.shape, own.dtype)
    outs = pl.pallas_call(
        functools.partial(pack_kernel, count=count),
        in_specs=[sspec()] + [vspec()] * (count + 1),
        out_specs=[vspec()] * (count + 1),
        out_shape=[tall, jax.ShapeDtypeStruct(mate.shape, mate.dtype)] + [tall] * (count - 1),
        compiler_params=params(),
        name="pack",
    )(place, own, mate, *cols)
    return outs[0], outs[1], outs[2:]


def nt(a, b):
    return lax.dot_general(a, b, (((1,), (1,)), ((), ())), preferred_element_type=jnp.float32)


def tn(a, b):
    return lax.dot_general(a, b, (((0,), (0,)), ((), ())), preferred_element_type=jnp.float32)


def attend_kernel(place, q_ref, do_ref, *refs, count, block, opening):
    first, second = refs[:count], refs[count : 2 * count]
    refs = refs[2 * count :]
    if opening:
        seg_refs, cols = refs[:count], refs[count : 2 * count - 1]
        ctx_ref, dq_ref, bias = refs[2 * count - 1 : 2 * count + 2]
        grads, own_grad = refs[2 * count + 2 : 3 * count + 1], refs[-1]
    else:
        bias = refs[0]
        ctx_ref, dq_ref = refs[3:5]
        grads, own_grad = refs[5:-1], refs[-1]
    inv_root = 1.0 / math.sqrt(HEAD_DIM)
    length = count * block

    if opening:

        @pl.when(pl.program_id(0) == 0)
        def _():
            ids = [r[:1, :].astype(jnp.float32) for r in seg_refs]
            mine = jnp.broadcast_to(ids[0], (block, block)).T
            rows = lax.broadcasted_iota(jnp.int32, (block, block), 0)
            cols_here = lax.broadcasted_iota(jnp.int32, (block, block), 1)
            for k in range(count):
                ok = mine == jnp.broadcast_to(ids[k], (block, block))
                if k == 0:
                    ok = ok & (cols_here <= rows)
                bias[:, k * block : (k + 1) * block] = jnp.where(ok, 0.0, MASKED)

    even = place[2] == 0
    a = jnp.concatenate([r[...] for r in first], axis=0)
    b = jnp.concatenate([r[...] for r in second], axis=0)
    key = jnp.where(even, a, b)
    value = jnp.where(even, b, a)

    def stack(ref):
        return jnp.concatenate(
            [ref[:, h * HEAD_DIM : (h + 1) * HEAD_DIM] for h in range(GROUP)], axis=0
        )

    def unstack(ref, val):
        for h in range(GROUP):
            ref[:, h * HEAD_DIM : (h + 1) * HEAD_DIM] = val[h * block : (h + 1) * block, :]

    q, do = stack(q_ref), stack(do_ref)
    s = nt(q, key) * (inv_root * LOG2E)
    s = (s.reshape(GROUP, block, length) + bias[...][None]).reshape(GROUP * block, length)
    e = jnp.exp2(s - jnp.max(s, axis=1, keepdims=True))
    p = e * (1.0 / jnp.sum(e, axis=1, keepdims=True))
    p_low = p.astype(jnp.bfloat16)
    ctx = jnp.dot(p_low, value, preferred_element_type=jnp.float32).astype(jnp.bfloat16)
    unstack(ctx_ref, ctx)
    dots = jnp.sum(do.astype(jnp.float32) * ctx.astype(jnp.float32), axis=1, keepdims=True)
    ds = (p * (nt(do, value) - dots)).astype(jnp.bfloat16)
    dq = jnp.dot(ds, key, preferred_element_type=jnp.float32) * inv_root
    unstack(dq_ref, dq.astype(jnp.bfloat16))
    dv = tn(p_low, do)
    dk = tn(ds, q) * inv_root
    at_key = pl.multiple_of(pl.program_id(0) * HEAD_DIM, HEAD_DIM)
    at_value = pl.multiple_of(at_key + KV_WIDTH // PARTS, HEAD_DIM)
    own_grad[:, pl.ds(at_key, HEAD_DIM)] = dk[:block]
    own_grad[:, pl.ds(at_value, HEAD_DIM)] = dv[:block]
    for k in range(1, count):
        piece = slice(k * block, (k + 1) * block)
        for at, grad in ((at_key, dk), (at_value, dv)):
            sent = grad[piece].astype(jnp.bfloat16)
            if opening:
                sent = jnp.where(place[0] >= k, sent, cols[k - 1][:, pl.ds(at, HEAD_DIM)])
            grads[k - 1][:, pl.ds(at, HEAD_DIM)] = sent


def attend(place, q, do, pairs, part, cols, before):
    block, width = q.shape
    count = len(pairs)
    steps = KV_HEADS // PARTS
    opening = not before
    wide = pl.BlockSpec((block, GROUP * HEAD_DIM), lambda g: (0, part * steps + g))
    first = pl.BlockSpec((block, HEAD_DIM), lambda g: (0, g))
    second = pl.BlockSpec((block, HEAD_DIM), lambda g: (0, steps + g))
    both = 2 * KV_WIDTH // PARTS
    held = pl.BlockSpec((block, both), lambda g: (0, 0))
    bias = pl.BlockSpec((block, count * block), lambda g: (0, 0))
    seg = pl.BlockSpec((EXTRA, block), lambda g: (block // EXTRA, 0))
    rows = jax.ShapeDtypeStruct((block, width), jnp.bfloat16)
    own = jax.ShapeDtypeStruct((block, both), jnp.float32)
    sent = jax.ShapeDtypeStruct((block, both), jnp.bfloat16)
    operands = [place, q, do, *pairs, *pairs]
    in_specs = [sspec(), wide, wide] + [first] * count + [second] * count
    if opening:
        operands += [*pairs, *cols]
        in_specs += [seg] * count + [held] * (count - 1)
        out_specs = [wide, wide, bias] + [held] * count
        out_shape = [rows, rows, jax.ShapeDtypeStruct((block, count * block), jnp.float32)]
        aliases = {}
    else:
        context, query_grad, mask = before
        aliases = {len(operands) + 1: 0, len(operands) + 2: 1}
        operands += [mask, context, query_grad]
        in_specs += [bias] + [pl.BlockSpec(memory_space=pl.ANY)] * 2
        out_specs = [wide, wide] + [held] * count
        out_shape = [rows, rows]
    outs = pl.pallas_call(
        functools.partial(attend_kernel, count=count, block=block, opening=opening),
        grid=(steps,),
        in_specs=in_specs,
        out_specs=out_specs,
        out_shape=out_shape + [sent] * (count - 1) + [own],
        input_output_aliases=aliases,
        compiler_params=params(dimension_semantics=("arbitrary",)),
        name="attend",
    )(*operands)
    return outs[: len(outs) - count], outs[len(outs) - count : -1], outs[-1]


def input_grad_kernel(place, *refs, count, rows):
    grads = refs[:PARTS]
    a_own, a_other, b_own, b_other, out, fa, fb = refs[PARTS:]
    assemble(fa, a_own, a_other, place, count, rows)
    assemble(fb, b_own, b_other, place, count, rows)
    even = place[2] == 0
    half = KV_WIDTH // PARTS
    gk = jnp.concatenate([g[:, :half] for g in grads], axis=1)
    gv = jnp.concatenate([g[:, half:] for g in grads], axis=1)
    ga = jnp.where(even, gk, gv)
    gb = jnp.where(even, gv, gk)
    out[...] = (nt(ga, fa[...]) + nt(gb, fb[...])).astype(jnp.bfloat16)


def input_grad_of(place, grads, a_own, a_other, b_own, b_other, count, rows):
    full = pltpu.VMEM((2 * count * rows, KV_WIDTH), jnp.bfloat16)
    return pl.pallas_call(
        functools.partial(input_grad_kernel, count=count, rows=rows),
        in_specs=[sspec()] + [vspec()] * (4 + len(grads)),
        out_specs=vspec(),
        out_shape=jax.ShapeDtypeStruct((grads[0].shape[0], 2 * count * rows), jnp.bfloat16),
        scratch_shapes=[full, full],
        compiler_params=params(),
        name="input_grad",
    )(place, *grads, a_own, a_other, b_own, b_other)


def turn_kernel(place, here, *refs, count, rows):
    wrapped, returned, out = refs[: count - 1], refs[count - 1 : 2 * count - 2], refs[-1]
    block = here.shape[0]
    for k in range(count):
        if k == 0:
            got = here[...]
        else:
            got = jnp.where(place[0] >= k, returned[count - k - 1][...], wrapped[k - 1][:block, :])
        for core in range(2):
            at = (2 * k + core) * block
            out[:, at : at + block] = got[:, core * rows : (core + 1) * rows].T


def turn(place, here, wrapped, returned, rows):
    count = len(wrapped) + 1
    return pl.pallas_call(
        functools.partial(turn_kernel, count=count, rows=rows),
        in_specs=[sspec()] + [vspec()] * (2 * count - 1),
        out_specs=vspec(),
        out_shape=jax.ShapeDtypeStruct((rows, 2 * count * here.shape[0]), here.dtype),
        compiler_params=params(),
        name="turn",
    )(place, here, *wrapped, *returned)


def weight_grad_kernel(x_turned, g_own, g_other, out, *, count):
    size = g_own.shape[0] // count
    pieces = []
    for k in range(count):
        pieces += [g_own[k * size : (k + 1) * size, :], g_other[k * size : (k + 1) * size, :]]
    grads = jnp.concatenate(pieces, axis=0)
    out[...] = jnp.dot(x_turned[...], grads, preferred_element_type=jnp.float32).astype(jnp.bfloat16)


def weight_grad_of(x_turned, g_own, g_other, count):
    return pl.pallas_call(
        functools.partial(weight_grad_kernel, count=count),
        in_specs=[vspec()] * 3,
        out_specs=vspec(),
        out_shape=jax.ShapeDtypeStruct((x_turned.shape[0], g_own.shape[1]), jnp.bfloat16),
        compiler_params=params(),
        name="weight_grad",
    )(x_turned, g_own, g_other)


def finish_kernel(*refs):
    pairs, outs = refs[:-2], refs[-2:]
    half = KV_WIDTH // PARTS
    for part in range(PARTS):
        a, b = pairs[2 * part], pairs[2 * part + 1]
        grad = (a[...].astype(jnp.float32) + b[...].astype(jnp.float32)).astype(jnp.bfloat16)
        outs[0][:, part * half : (part + 1) * half] = grad[:, :half]
        outs[1][:, part * half : (part + 1) * half] = grad[:, half:]


def finish(*partials):
    out = jax.ShapeDtypeStruct((partials[0].shape[0], KV_WIDTH), jnp.bfloat16)
    return pl.pallas_call(
        finish_kernel,
        in_specs=[vspec()] * len(partials),
        out_specs=[vspec()] * 2,
        out_shape=[out, out],
        compiler_params=params(),
        name="finish",
    )(*partials)


def body(activations, queries, key_weight, value_weight, segment_ids, out_grad):
    inputs = activations[0]
    block, width = inputs.shape
    rows = key_weight.shape[0]
    n = lax.axis_size("seq")
    reps = lax.axis_size("rep")
    z, r, c = lax.axis_index("seq"), lax.axis_index("rep"), lax.axis_index("fsdp")
    odd = lax.rem(r, 2)
    place = jnp.stack([z, c, odd]).astype(jnp.int32)
    shifts = range(1, n)

    def around(x, k):
        return lax.ppermute(x, "seq", [(i, (i + k) % n) for i in range(n)])

    def up(x, k):
        return lax.ppermute(x, "seq", [(i, i + k) for i in range(n - k)])

    def down(x, k):
        return lax.ppermute(x, "seq", [(i, i - k) for i in range(k, n)])

    def partner(x):
        return lax.ppermute(x, "rep", [(j, j ^ 1) for j in range(reps)])

    def core(x):
        return lax.ppermute(x, "fsdp", [(0, 1), (1, 0)])

    half = jnp.where(odd == 0, key_weight, value_weight)
    gathered = [half] + [around(half, k) for k in shifts]
    x_next = partner(inputs)

    late, gathered[1] = lax.optimization_barrier((inputs, gathered[1]))
    columns = late.reshape(block, n, 2, rows)
    x_mine = lax.dynamic_index_in_dim(columns, c, 2, keepdims=False)
    x_theirs = core(lax.dynamic_index_in_dim(columns, 1 - c, 2, keepdims=False))
    x_both = jnp.concatenate([x_mine, x_theirs], axis=2).transpose(1, 0, 2)
    x_both = jnp.pad(x_both, ((0, 0), (0, 0), (0, KV_WIDTH - 2 * rows)))
    x_for = [
        lax.dynamic_index_in_dim(x_both, lax.rem(z + k, n), 0, keepdims=False) for k in range(n)
    ]
    gathered, x_next, x_for = lax.optimization_barrier((gathered, x_next, x_for))

    w_own = jnp.concatenate(gathered, axis=0)
    w_other = core(w_own)
    own, other = project(place, segment_ids, inputs, x_next, w_own, w_other, n, rows)
    pair_a, pair_b, loads = pack(place, own, partner(other), x_for[1:])
    carried = [around(x, k) for k, x in zip(shifts, loads)]
    pairs = [[pair_a] + carried, [pair_b] + [up(pair_b, k) for k in shifts]]

    w_late, _ = lax.optimization_barrier((w_own, carried[0]))
    b_own = partner(w_late)
    b_other = core(b_own)

    before, sums = [], []
    for part in range(PARTS):
        before, sent, total = attend(
            place, queries[0], out_grad[0], pairs[part], part, x_for[:0:-1], before
        )
        if part == 0:
            back = [around(x, n - k) for k, x in zip(shifts, sent)]
            returned = back
            back = [jnp.where(z + k < n, x, jnp.zeros_like(x)) for k, x in zip(shifts, back)]
        else:
            back = [down(x, k) for k, x in zip(shifts, sent)]
        for x in back:
            total = total + x.astype(jnp.float32)
        sums.append(total.astype(jnp.bfloat16))
    context, query_grad = before[:2]
    x_turned = turn(place, x_for[0], carried, returned, rows)

    input_grad = input_grad_of(place, sums, w_own, w_other, b_own, b_other, n, rows)
    partials = []
    for part in range(PARTS):
        g_own = jnp.concatenate([sums[part]] + [around(sums[part], k) for k in shifts], axis=0)
        g_other = core(g_own)
        if part == PARTS - 1:
            g_other, input_grad = lax.optimization_barrier((g_other, input_grad))
        partials.append(weight_grad_of(x_turned, g_own, g_other, n))
    if reps == 2:
        grads = finish(*[x for p in partials for x in (p, partner(p))])
    else:
        totals = [lax.psum(p.astype(jnp.float32), "rep").astype(jnp.bfloat16) for p in partials]
        grads = finish(*[x for p in totals for x in (p, jnp.zeros_like(p))])
    return context[None], query_grad[None], input_grad[None], grads[0], grads[1]


def solution(mesh):
    return jax.shard_map(
        body,
        mesh=mesh,
        in_specs=(
            P(("groups", "rep", "fsdp"), "seq", None),
            P(("groups", "rep", "fsdp"), "seq", None),
            P(("seq", "fsdp"), None),
            P(("seq", "fsdp"), None),
            P(("groups", "rep", "fsdp"), "seq"),
            P(("groups", "rep", "fsdp"), "seq", None),
        ),
        out_specs=(
            P(("groups", "rep", "fsdp"), "seq", None),
            P(("groups", "rep", "fsdp"), "seq", None),
            P(("groups", "rep", "fsdp"), "seq", None),
            P(("groups", "seq", "fsdp"), None),
            P(("groups", "seq", "fsdp"), None),
        ),
        check_vma=False,
    )
```

time: 189 us -> 158 us (0.84)
  the two profiles are of different devices: /device:TPU:8 before, /device:TPU:0 now
where the time goes in v2:
time: 158 us; the launch traced here: 157 us
  starting transfers between devices  56.9 us (36%)
  waiting for transfers between devices  56.4 us (36%)
  Pallas kernels  30.7 us (19%)
  local copies, waits for them, and re-layouts  9.34 us (6%)
  other arithmetic  2.82 us (2%)
    ppermute x15, waiting for transfers between devices, around(): return lax.ppermute(x, 'seq', [(i, (i + k) % n) for i in range(n)])  38.6 us
    ppermute x15, starting transfers between devices, around(): return lax.ppermute(x, 'seq', [(i, (i + k) % n) for i in range(n)])  32.5 us
    ppermute x3, starting transfers between devices, up(): return lax.ppermute(x, 'seq', [(i, i + k) for i in range(n - k)])  13.7 us
    ppermute x5, waiting for transfers between devices, partner(): return lax.ppermute(x, 'rep', [(j, j ^ 1) for j in range(reps)])  11.3 us
    pallas_call x2, Pallas kernels, attend(): pl.pallas_call(functools.partial(attend_kernel, count=count, block=block,...  11 us
    unnamed x55, local copies, waits for them, and re-layouts  7.7 us
    ppermute x5, starting transfers between devices, partner(): return lax.ppermute(x, 'rep', [(j, j ^ 1) for j in range(reps)])  6.51 us
    pallas_call x2, Pallas kernels, weight_grad_of(): pl.pallas_call(functools.partial(weight_grad_kernel, count=count), in_spe...  5 us
  transfers between devices with their start and end apart: 31, of which 13 were waited for; matrix products, arithmetic and copies ran while one was open for 2% of the time, Pallas kernels for 15%

profile of v2, /device:TPU:0, one launch (start us, length us, event | category | flops | bytes accessed | tf_op | source)
XLA Modules:
  0.0 157.3 jit_solution(12530704482310360821)
XLA Ops:
  0.7 1.0 broadcast_select_fusion
  1.7 3.1 %collective-permute-start = (bf16[256,512]{1,0:T(8,128)(2,1)S(1)}, bf16[256,512]{1,0:T(8,128)(2,1)S(1)}, u32[]{:S(2)}, u32[]{:S(2)}) collective-permute-start(bf16[256,512]{1,0:T(8,128)(2,1)S(1)} %broadcast_select_fusion), channel_id=1, source_target_pairs={{0,4},{4,8},{8,12},{12,0},{1,5},{5,9},{9,13},{13,1},{2,6},{6,10},{... | collective-permute-start | bytes 786440 | tf_op jit(solution)/shard_map/ppermute | solution.py:332
  4.8 1.5 collective-permute-start.3
  6.3 6.8 %collective-permute-done = bf16[256,512]{1,0:T(8,128)(2,1)S(1)} collective-permute-done((bf16[256,512]{1,0:T(8,128)(2,1)S(1)}, bf16[256,512]{1,0:T(8,128)(2,1)S(1)}, u32[]{:S(2)}, u32[]{:S(2)}) %collective-permute-start) | collective-permute-done | bytes 262176 | tf_op jit(solution)/shard_map/ppermute | solution.py:332
  13.1 0.4 reshape.21
  13.5 1.1 constant_dynamic-slice_fusion
  14.6 0.1 copy.17
  14.7 0.1 collective-permute-start.4
  14.7 0.8 collective-permute-start.1
  15.5 1.3 collective-permute-start.2
  16.9 0.1 copy.18
  17.0 0.8 fusion.1
  17.8 11.4 %collective-permute-done.1 = bf16[256,512]{1,0:T(8,128)(2,1)S(1)} collective-permute-done((bf16[256,512]{1,0:T(8,128)(2,1)S(1)}, bf16[256,512]{1,0:T(8,128)(2,1)S(1)}, u32[]{:S(2)}, u32[]{:S(2)}) %collective-permute-start.1) | collective-permute-done | bytes 262176 | tf_op jit(solution)/shard_map/ppermute | solution.py:332
  29.2 0.3 collective-permute-done.2
  29.6 0.7 copy-done.17
  30.4 0.1 collective-permute-start.5
  30.5 0.7 pad_add_fusion.place
  31.2 1.9 %collective-permute-done.5.w_other.refs_3_ = bf16[1024,512]{1,0:T(8,128)(2,1)S(1)} collective-permute-done((bf16[1024,512]{1,0:T(8,128)(2,1)S(1)}, bf16[1024,512]{1,0:T(8,128)(2,1)S(1)}, u32[]{:S(2)}, u32[]{:S(2)}) %collective-permute-start.5) | collective-permute-done | bytes 1048608 | tf_op jit(solution)/shard_map/ppermute | solution.py:344
  33.1 1.0 copy-done.1
  34.1 3.4 %project.1 = (bf16[144,512]{1,0:T(8,128)(2,1)}, bf16[128,512]{1,0:T(8,128)(2,1)}) custom-call(s32[3]{0:T(128)} %pad_add_fusion.place, s32[1,128]{1,0:T(1,128)} %seg.1, bf16[128,2048]{1,0:T(8,128)(2,1)} %bitcast.23, bf16[128,2048]{1,0:T(8,128)(2,1)} %copy-done.17, bf16[1024,512]{1,0:T(8,128)(2,1)} %copy-done, bf16[1024,512]{1,0:T(8,128)(2,1)} %copy-done.1), custom_call_target="tpu_custom_call" | custom-call | tf_op jit(solution)/shard_map/project/pallas_call | solution.py:62
  37.5 1.5 collective-permute-start.6
  39.0 4.3 %collective-permute-done.6.mate = bf16[128,512]{1,0:T(8,128)(2,1)S(1)} collective-permute-done((bf16[128,512]{1,0:T(8,128)(2,1)}, bf16[128,512]{1,0:T(8,128)(2,1)S(1)}, u32[]{:S(2)}, u32[]{:S(2)}) %collective-permute-start.6) | collective-permute-done | bytes 131104 | tf_op jit(solution)/shard_map/ppermute | solution.py:341
  43.3 0.6 copy-done.25
  43.9 2.0 %pack.1 = (bf16[144,512]{1,0:T(8,128)(2,1)}, bf16[128,512]{1,0:T(8,128)(2,1)}, bf16[144,512]{1,0:T(8,128)(2,1)}, bf16[144,512]{1,0:T(8,128)(2,1)}, bf16[144,512]{1,0:T(8,128)(2,1)}) custom-call(s32[3]{0:T(128)} %pad_add_fusion.place, bf16[144,512]{1,0:T(8,128)(2,1)} %get-tuple-element.48.own, bf16[128,512]{1,0:T(8,128)(2,1)} %copy-done.25, ...), custom_call_target="tpu_custom_call" | custom-call | tf_op jit(solution)/shard_map/pack/pallas_call | solution.py:94
  46.0 5.8 %collective-permute-start.10 = (bf16[144,512]{1,0:T(8,128)(2,1)}, bf16[144,512]{1,0:T(8,128)(2,1)S(1)}, u32[]{:S(2)}, u32[]{:S(2)}) collective-permute-start(bf16[144,512]{1,0:T(8,128)(2,1)} %get-tuple-element.55), channel_id=1, source_target_pairs={{0,4},{4,8},{8,12},{12,0},{1,5},{5,9},{9,13},{13,1},{2,6},{6,10},{... | collective-permute-start | bytes 442376 | tf_op jit(solution)/shard_map/ppermute | solution.py:332
  51.8 5.4 %collective-permute-done.10.refs_1_.refs_5_.refs_9_.refs_0_ = bf16[144,512]{1,0:T(8,128)(2,1)S(1)} collective-permute-done((bf16[144,512]{1,0:T(8,128)(2,1)}, bf16[144,512]{1,0:T(8,128)(2,1)S(1)}, u32[]{:S(2)}, u32[]{:S(2)}) %collective-permute-start.10) | collective-permute-done | bytes 147488 | tf_op jit(solution)/shard_map/ppermute | solution.py:332
  57.2 1.5 collective-permute-start.23
  58.7 2.3 %collective-permute-start.12 = (bf16[144,512]{1,0:T(8,128)(2,1)}, bf16[144,512]{1,0:T(8,128)(2,1)S(1)}, u32[]{:S(2)}, u32[]{:S(2)}) collective-permute-start(bf16[144,512]{1,0:T(8,128)(2,1)} %get-tuple-element.57), channel_id=1, source_target_pairs={{0,12},{4,0},{8,4},{12,8},{1,13},{5,1},{9,5},{13,9},{2,14},{6,2},{... | collective-permute-start | bytes 442376 | tf_op jit(solution)/shard_map/ppermute | solution.py:332
  61.0 2.0 %collective-permute-start.7 = (bf16[128,512]{1,0:T(8,128)(2,1)}, bf16[128,512]{1,0:T(8,128)(2,1)S(1)}, u32[]{:S(2)}, u32[]{:S(2)}) collective-permute-start(bf16[128,512]{1,0:T(8,128)(2,1)} %get-tuple-element.53.refs_0_.refs_4_), channel_id=1, source_target_pairs={{0,4},{4,8},{8,12},{1,5},{5,9},{9,13},{2,6},{6,10},{10,14},{3,7},{... | collective-permute-start | bytes 393224 | tf_op jit(solution)/shard_map/ppermute | solution.py:335
  63.0 4.5 %collective-permute-start.8 = (bf16[128,512]{1,0:T(8,128)(2,1)}, bf16[128,512]{1,0:T(8,128)(2,1)S(1)}, u32[]{:S(2)}, u32[]{:S(2)}) collective-permute-start(bf16[128,512]{1,0:T(8,128)(2,1)} %get-tuple-element.53.refs_0_.refs_4_), channel_id=1, source_target_pairs={{0,8},{4,12},{1,9},{5,13},{2,10},{6,14},{3,11},{7,15},{16,24},{20,... | collective-permute-start | bytes 393224 | tf_op jit(solution)/shard_map/ppermute | solution.py:335
  67.4 0.1 collective-permute-done.11.refs_2_.refs_6_.refs_10_.refs_1_
  67.6 7.3 %collective-permute-start.9 = (bf16[128,512]{1,0:T(8,128)(2,1)}, bf16[128,512]{1,0:T(8,128)(2,1)S(1)}, u32[]{:S(2)}, u32[]{:S(2)}) collective-permute-start(bf16[128,512]{1,0:T(8,128)(2,1)} %get-tuple-element.53.refs_0_.refs_4_), channel_id=1, source_target_pairs={{0,12},{1,13},{2,14},{3,15},{16,28},{17,29},{18,30},{19,31}} | collective-permute-start | bytes 393224 | tf_op jit(solution)/shard_map/ppermute | solution.py:335
  74.9 0.6 copy-done.4
  75.6 5.7 %attend.2 = (bf16[128,2048]{1,0:T(8,128)(2,1)}, bf16[128,2048]{1,0:T(8,128)(2,1)}, f32[128,512]{1,0:T(8,128)}, bf16[128,512]{1,0:T(8,128)(2,1)}, bf16[128,512]{1...) custom-call(s32[3]{0:T(128)} %pad_add_fusion.place, bf16[128,2048]{1,0:T(8,128)(2,1)} %bitcast.26, ...), custom_call_target="tpu_custom_call" | custom-call | tf_op jit(solution)/shard_map/attend/pallas_call | solution.py:213
  81.4 3.8 %collective-permute-start.20 = (bf16[128,512]{1,0:T(8,128)(2,1)}, bf16[128,512]{1,0:T(8,128)(2,1)S(1)}, u32[]{:S(2)}, u32[]{:S(2)}) collective-permute-start(bf16[128,512]{1,0:T(8,128)(2,1)} %get-tuple-element.68), channel_id=1, source_target_pairs={{0,12},{4,0},{8,4},{12,8},{1,13},{5,1},{9,5},{13,9},{2,14},{6,2},{... | collective-permute-start | bytes 393224 | tf_op jit(solution)/shard_map/ppermute | solution.py:332
  85.2 0.6 copy-done.16
  85.9 5.4 %attend.3 = (bf16[128,2048]{1,0:T(8,128)(2,1)}, bf16[128,2048]{1,0:T(8,128)(2,1)}, bf16[128,512]{1,0:T(8,128)(2,1)}, bf16[128,512]{1,0:T(8,128)(2,1)}, bf16[128,512]{1,0:T(8,128)(2,1)}, /*index=5*/f32[128,512]{1,0:T(8,128)}) custom-call(s32[3]{0:T(128)} %pad_add_fusion.place, ...), custom_call_target="tpu_custom_call", output_to_operand_aliasing={{0}: (12, {}), {1}: (13, {})} | custom-call | tf_op jit(solution)/shard_map/attend/pallas_call | solution.py:213
  91.2 1.3 collective-permute-start.15
  92.5 1.3 collective-permute-start.14
  93.8 0.3 collective-permute-done.21.refs_4_
  94.1 1.3 collective-permute-start.13
  95.5 0.1 add_convert_fusion.refs_0_
  95.7 0.6 copy-done.20
  96.3 5.4 %collective-permute-start.27 = (bf16[128,512]{1,0:T(8,128)(2,1)S(1)}, bf16[128,512]{1,0:T(8,128)(2,1)S(1)}, u32[]{:S(2)}, u32[]{:S(2)}) collective-permute-start(bf16[128,512]{1,0:T(8,128)(2,1)S(1)} %add_convert_fusion.refs_0_), channel_id=1, source_target_pairs={{0,12},{4,0},{8,4},{12,8},{1,13},{5,1},{9,5},{13,9},{2,14},{6,2},{... | collective-permute-start | bytes 393224 | tf_op jit(solution)/shard_map/ppermute | solution.py:332
  101.7 3.7 %collective-permute-done.14 = bf16[128,512]{1,0:T(8,128)(2,1)S(1)} collective-permute-done((bf16[128,512]{1,0:T(8,128)(2,1)}, bf16[128,512]{1,0:T(8,128)(2,1)S(1)}, u32[]{:S(2)}, u32[]{:S(2)}) %collective-permute-start.14) | collective-permute-done | bytes 131104 | tf_op jit(solution)/shard_map/ppermute | solution.py:338
  105.4 0.9 collective-permute-done.13
  106.4 2.9 %collective-permute-start.18 = (bf16[128,512]{1,0:T(8,128)(2,1)S(1)}, bf16[128,512]{1,0:T(8,128)(2,1)S(1)}, u32[]{:S(2)}, u32[]{:S(2)}) collective-permute-start(bf16[128,512]{1,0:T(8,128)(2,1)S(1)} %add_convert_fusion.1.refs_1_), channel_id=1, source_target_pairs={{0,12},{4,0},{8,4},{12,8},{1,13},{5,1},{9,5},{13,9},{2,14},{6,2},{... | collective-permute-start | bytes 393224 | tf_op jit(solution)/shard_map/ppermute | solution.py:332
  109.3 6.8 %collective-permute-start.17 = (bf16[128,512]{1,0:T(8,128)(2,1)S(1)}, bf16[128,512]{1,0:T(8,128)(2,1)S(1)}, u32[]{:S(2)}, u32[]{:S(2)}) collective-permute-start(bf16[128,512]{1,0:T(8,128)(2,1)S(1)} %add_convert_fusion.1.refs_1_), channel_id=1, source_target_pairs={{0,8},{4,12},{8,0},{12,4},{1,9},{5,13},{9,1},{13,5},{2,10},{6,14},... | collective-permute-start | bytes 393224 | tf_op jit(solution)/shard_map/ppermute | solution.py:332
  116.1 3.3 %collective-permute-done.26 = bf16[128,512]{1,0:T(8,128)(2,1)S(1)} collective-permute-done((bf16[128,512]{1,0:T(8,128)(2,1)S(1)}, bf16[128,512]{1,0:T(8,128)(2,1)S(1)}, u32[]{:S(2)}, u32[]{:S(2)}) %collective-permute-start.26) | collective-permute-done | bytes 131104 | tf_op jit(solution)/shard_map/ppermute | solution.py:332
  119.5 0.1 collective-permute-start.28
  119.6 11.0 %collective-permute-done.17 = bf16[128,512]{1,0:T(8,128)(2,1)S(1)} collective-permute-done((bf16[128,512]{1,0:T(8,128)(2,1)S(1)}, bf16[128,512]{1,0:T(8,128)(2,1)S(1)}, u32[]{:S(2)}, u32[]{:S(2)}) %collective-permute-start.17) | collective-permute-done | bytes 131104 | tf_op jit(solution)/shard_map/ppermute | solution.py:332
  130.6 0.1 collective-permute-start.19
  130.7 2.4 %turn.1.x_turned = bf16[256,1024]{1,0:T(8,128)(2,1)} custom-call(s32[3]{0:T(128)} %pad_add_fusion.place, bf16[128,512]{1,0:T(8,128)(2,1)} %get-tuple-element.73.here, bf16[144,512]{1,0:T(8,128)(2,1)} %copy-done.2, bf16[144,512]{1,0:T(8,128)(2,1)} %copy-done.3, bf16[144,512]{1,0:T(8,128)(2,1)} %copy-done.4, bf16[128,512]{1,0:T(8,128)(2,1)} %copy-done.20, ...), custom_call_target="tpu_custom_call" | custom-call | tf_op jit(solution)/shard_map/turn/pallas_call | solution.py:268
  133.1 0.8 copy-done.13
  133.9 2.5 %weight_grad.2.refs_0_ = bf16[256,512]{1,0:T(8,128)(2,1)} custom-call(bf16[256,1024]{1,0:T(8,128)(2,1)} %turn.1.x_turned, bf16[512,512]{1,0:T(8,128)(2,1)} %copy-done.6, bf16[512,512]{1,0:T(8,128)(2,1)} %copy-done.13), custom_call_target="tpu_custom_call" | custom-call | tf_op jit(solution)/shard_map/weight_grad/pallas_call | solution.py:288
  136.4 0.6 collective-permute-start.29
  137.0 1.0 copy-done.11
  138.0 4.8 %input_grad.1 = bf16[128,2048]{1,0:T(8,128)(2,1)} custom-call(s32[3]{0:T(128)} %pad_add_fusion.place, bf16[128,512]{1,0:T(8,128)(2,1)} %copy-done.8, bf16[128,512]{1,0:T(8,128)(2,1)} %copy-done.9, bf16[1024,512]{1,0:T(8,128)(2,1)} %copy-done, bf16[1024,512]{1,0:T(8,128)(2,1)} %copy-done.1, bf16[1024,512]{1,0:T(8,128)(2,1)} %copy-done.10, ...), custom_call_target="tpu_custom_call" | custom-call | tf_op jit(solution)/shard_map/input_grad/pallas_call | solution.py:242
  142.8 0.8 copy-done.12
  143.6 2.5 %weight_grad.3.refs_2_ = bf16[256,512]{1,0:T(8,128)(2,1)} custom-call(bf16[256,1024]{1,0:T(8,128)(2,1)} %turn.1.x_turned, bf16[512,512]{1,0:T(8,128)(2,1)} %copy-done.5, bf16[512,512]{1,0:T(8,128)(2,1)} %copy-done.12), custom_call_target="tpu_custom_call" | custom-call | tf_op jit(solution)/shard_map/weight_grad/pallas_call | solution.py:288
  146.1 1.5 collective-permute-start.30
  147.5 7.0 %collective-permute-done.30.refs_3_ = bf16[256,512]{1,0:T(8,128)(2,1)S(1)} collective-permute-done((bf16[256,512]{1,0:T(8,128)(2,1)}, bf16[256,512]{1,0:T(8,128)(2,1)S(1)}, u32[]{:S(2)}, u32[]{:S(2)}) %collective-permute-start.30) | collective-permute-done | bytes 262176 | tf_op jit(solution)/shard_map/ppermute | solution.py:341
  154.6 0.7 copy-done.24
  155.3 2.1 %finish.1 = (bf16[256,512]{1,0:T(8,128)(2,1)}, bf16[256,512]{1,0:T(8,128)(2,1)}) custom-call(bf16[256,512]{1,0:T(8,128)(2,1)} %weight_grad.2.refs_0_, bf16[256,512]{1,0:T(8,128)(2,1)} %copy-done.23, bf16[256,512]{1,0:T(8,128)(2,1)} %weight_grad.3.refs_2_, bf16[256,512]{1,0:T(8,128)(2,1)} %copy-done.24), custom_call_target="tpu_custom_call" | custom-call | tf_op jit(solution)/shard_map/finish/pallas_call | solution.py:310
  (74 shorter events, 0.6 us)
Async XLA Ops:
  0.6 4.1 %copy-start.7 = (bf16[1,128,2048]{2,1,0:T(8,128)(2,1)S(1)}, bf16[1,128,2048]{2,1,0:T(8,128)(2,1)}, u32[]{:S(2)}) copy-start(bf16[1,128,2048]{2,1,0:T(8,128)(2,1)} %param.6) | copy-start | bytes 1572868
  1.7 11.4 %collective-permute-start = (bf16[256,512]{1,0:T(8,128)(2,1)S(1)}, bf16[256,512]{1,0:T(8,128)(2,1)S(1)}, u32[]{:S(2)}, u32[]{:S(2)}) collective-permute-start(bf16[256,512]{1,0:T(8,128)(2,1)S(1)} %broadcast_select_fusion), channel_id=1, source_target_pairs={{0,4},{4,8},{8,12},{12,0},{1,5},{5,9},{9,13},{13,1},{2,6},{6,10},{... | collective-permute-start | bytes 786440 | tf_op jit(solution)/shard_map/ppermute | solution.py:332
  4.8 24.8 %collective-permute-start.3 = (bf16[128,2048]{1,0:T(8,128)(2,1)S(1)}, bf16[128,2048]{1,0:T(8,128)(2,1)S(1)}, u32[]{:S(2)}, u32[]{:S(2)}) collective-permute-start(bf16[128,2048]{1,0:T(8,128)(2,1)S(1)} %bitcast.24), channel_id=1, source_target_pairs={{0,2},{2,0},{1,3},{3,1},{4,6},{6,4},{5,7},{7,5},{8,10},{10,8},{9,1... | collective-permute-start | bytes 1572872 | tf_op jit(solution)/shard_map/ppermute | solution.py:341
  14.7 2.3 %collective-permute-start.4 = (bf16[128,4,256]{2,0,1:T(8,128)(2,1)S(1)}, bf16[128,4,256]{2,0,1:T(8,128)(2,1)S(1)}, u32[]{:S(2)}, u32[]{:S(2)}) collective-permute-start(bf16[128,4,256]{2,0,1:T(8,128)(2,1)S(1)} %bitcast.34), channel_id=1, source_target_pairs={{0,1},{1,0},{2,3},{3,2},{4,5},{5,4},{6,7},{7,6},{8,9},{9,8},{10,11... | collective-permute-start | bytes 786440 | tf_op jit(solution)/shard_map/ppermute | solution.py:344
  14.7 14.5 %collective-permute-start.1 = (bf16[256,512]{1,0:T(8,128)(2,1)S(1)}, bf16[256,512]{1,0:T(8,128)(2,1)S(1)}, u32[]{:S(2)}, u32[]{:S(2)}) collective-permute-start(bf16[256,512]{1,0:T(8,128)(2,1)S(1)} %broadcast_select_fusion), channel_id=1, source_target_pairs={{0,8},{4,12},{8,0},{12,4},{1,9},{5,13},{9,1},{13,5},{2,10},{6,14},... | collective-permute-start | bytes 786440 | tf_op jit(solution)/shard_map/ppermute | solution.py:332
  15.5 14.0 %collective-permute-start.2 = (bf16[256,512]{1,0:T(8,128)(2,1)S(1)}, bf16[256,512]{1,0:T(8,128)(2,1)S(1)}, u32[]{:S(2)}, u32[]{:S(2)}) collective-permute-start(bf16[256,512]{1,0:T(8,128)(2,1)S(1)} %broadcast_select_fusion), channel_id=1, source_target_pairs={{0,12},{4,0},{8,4},{12,8},{1,13},{5,1},{9,5},{13,9},{2,14},{6,2},{... | collective-permute-start | bytes 786440 | tf_op jit(solution)/shard_map/ppermute | solution.py:332
  29.5 0.8 copy-start.17
  30.4 2.7 %copy-start = (bf16[1024,512]{1,0:T(8,128)(2,1)}, bf16[1024,512]{1,0:T(8,128)(2,1)S(1)}, u32[]{:S(2)}) copy-start(bf16[1024,512]{1,0:T(8,128)(2,1)S(1)} %constant_dynamic-update-slice_fusion.w_own.refs_2_) | copy-start | bytes 3145732
  30.4 2.7 %collective-permute-start.5 = (bf16[1024,512]{1,0:T(8,128)(2,1)S(1)}, bf16[1024,512]{1,0:T(8,128)(2,1)S(1)}, u32[]{:S(2)}, u32[]{:S(2)}) collective-permute-start(bf16[1024,512]{1,0:T(8,128)(2,1)S(1)} %constant_dynamic-update-slice_fusion.w_own.refs_2_), channel_id=1, source_target_pairs={{0,1},{1,0},{2,3},{3,2},{4,5},{5,4},{6,7},{7,6},{8,9},{9,8},{10,11... | collective-permute-start | bytes 3145736 | tf_op jit(solution)/shard_map/ppermute | solution.py:344
  33.1 1.0 copy-start.1
  37.5 5.7 %collective-permute-start.6 = (bf16[128,512]{1,0:T(8,128)(2,1)}, bf16[128,512]{1,0:T(8,128)(2,1)S(1)}, u32[]{:S(2)}, u32[]{:S(2)}) collective-permute-start(bf16[128,512]{1,0:T(8,128)(2,1)} %get-tuple-element.49), channel_id=1, source_target_pairs={{0,2},{2,0},{1,3},{3,1},{4,6},{6,4},{5,7},{7,5},{8,10},{10,8},{9,1... | collective-permute-start | bytes 393224 | tf_op jit(solution)/shard_map/ppermute | solution.py:341
  43.3 0.6 copy-start.25
  46.0 11.2 %collective-permute-start.10 = (bf16[144,512]{1,0:T(8,128)(2,1)}, bf16[144,512]{1,0:T(8,128)(2,1)S(1)}, u32[]{:S(2)}, u32[]{:S(2)}) collective-permute-start(bf16[144,512]{1,0:T(8,128)(2,1)} %get-tuple-element.55), channel_id=1, source_target_pairs={{0,4},{4,8},{8,12},{12,0},{1,5},{5,9},{9,13},{13,1},{2,6},{6,10},{... | collective-permute-start | bytes 442376 | tf_op jit(solution)/shard_map/ppermute | solution.py:332
  57.2 17.7 %copy-start.2 = (bf16[144,512]{1,0:T(8,128)(2,1)}, bf16[144,512]{1,0:T(8,128)(2,1)S(1)}, u32[]{:S(2)}) copy-start(bf16[144,512]{1,0:T(8,128)(2,1)S(1)} %collective-permute-done.10.refs_1_.refs_5_.refs_9_.refs_0_) | copy-start | bytes 442372
  57.2 38.2 %collective-permute-start.23 = (bf16[1024,512]{1,0:T(8,128)(2,1)}, bf16[1024,512]{1,0:T(8,128)(2,1)S(1)}, u32[]{:S(2)}, u32[]{:S(2)}) collective-permute-start(bf16[1024,512]{1,0:T(8,128)(2,1)} %copy-done), channel_id=1, source_target_pairs={{0,2},{2,0},{1,3},{3,1},{4,6},{6,4},{5,7},{7,5},{8,10},{10,8},{9,1... | collective-permute-start | bytes 3145736 | tf_op jit(solution)/shard_map/ppermute | solution.py:341
  58.7 8.9 %collective-permute-start.11 = (bf16[144,512]{1,0:T(8,128)(2,1)}, bf16[144,512]{1,0:T(8,128)(2,1)S(1)}, u32[]{:S(2)}, u32[]{:S(2)}) collective-permute-start(bf16[144,512]{1,0:T(8,128)(2,1)} %get-tuple-element.56), channel_id=1, source_target_pairs={{0,8},{4,12},{8,0},{12,4},{1,9},{5,13},{9,1},{13,5},{2,10},{6,14},... | collective-permute-start | bytes 442376 | tf_op jit(solution)/shard_map/ppermute | solution.py:332
  58.7 16.2 %collective-permute-start.12 = (bf16[144,512]{1,0:T(8,128)(2,1)}, bf16[144,512]{1,0:T(8,128)(2,1)S(1)}, u32[]{:S(2)}, u32[]{:S(2)}) collective-permute-start(bf16[144,512]{1,0:T(8,128)(2,1)} %get-tuple-element.57), channel_id=1, source_target_pairs={{0,12},{4,0},{8,4},{12,8},{1,13},{5,1},{9,5},{13,9},{2,14},{6,2},{... | collective-permute-start | bytes 442376 | tf_op jit(solution)/shard_map/ppermute | solution.py:332
  61.0 20.3 %collective-permute-start.7 = (bf16[128,512]{1,0:T(8,128)(2,1)}, bf16[128,512]{1,0:T(8,128)(2,1)S(1)}, u32[]{:S(2)}, u32[]{:S(2)}) collective-permute-start(bf16[128,512]{1,0:T(8,128)(2,1)} %get-tuple-element.53.refs_0_.refs_4_), channel_id=1, source_target_pairs={{0,4},{4,8},{8,12},{1,5},{5,9},{9,13},{2,6},{6,10},{10,14},{3,7},{... | collective-permute-start | bytes 393224 | tf_op jit(solution)/shard_map/ppermute | solution.py:335
  63.0 18.4 %collective-permute-start.8 = (bf16[128,512]{1,0:T(8,128)(2,1)}, bf16[128,512]{1,0:T(8,128)(2,1)S(1)}, u32[]{:S(2)}, u32[]{:S(2)}) collective-permute-start(bf16[128,512]{1,0:T(8,128)(2,1)} %get-tuple-element.53.refs_0_.refs_4_), channel_id=1, source_target_pairs={{0,8},{4,12},{1,9},{5,13},{2,10},{6,14},{3,11},{7,15},{16,24},{20,... | collective-permute-start | bytes 393224 | tf_op jit(solution)/shard_map/ppermute | solution.py:335
  67.6 7.3 %copy-start.3 = (bf16[144,512]{1,0:T(8,128)(2,1)}, bf16[144,512]{1,0:T(8,128)(2,1)S(1)}, u32[]{:S(2)}) copy-start(bf16[144,512]{1,0:T(8,128)(2,1)S(1)} %collective-permute-done.11.refs_2_.refs_6_.refs_10_.refs_1_) | copy-start | bytes 442372
  67.6 17.6 %collective-permute-start.9 = (bf16[128,512]{1,0:T(8,128)(2,1)}, bf16[128,512]{1,0:T(8,128)(2,1)S(1)}, u32[]{:S(2)}, u32[]{:S(2)}) collective-permute-start(bf16[128,512]{1,0:T(8,128)(2,1)} %get-tuple-element.53.refs_0_.refs_4_), channel_id=1, source_target_pairs={{0,12},{1,13},{2,14},{3,15},{16,28},{17,29},{18,30},{19,31}} | collective-permute-start | bytes 393224 | tf_op jit(solution)/shard_map/ppermute | solution.py:335
  74.9 0.7 copy-start.4
  81.2 11.3 %collective-permute-start.22 = (bf16[128,512]{1,0:T(8,128)(2,1)}, bf16[128,512]{1,0:T(8,128)(2,1)S(1)}, u32[]{:S(2)}, u32[]{:S(2)}) collective-permute-start(bf16[128,512]{1,0:T(8,128)(2,1)} %get-tuple-element.70), channel_id=1, source_target_pairs={{0,4},{4,8},{8,12},{12,0},{1,5},{5,9},{9,13},{13,1},{2,6},{6,10},{... | collective-permute-start | bytes 393224 | tf_op jit(solution)/shard_map/ppermute | solution.py:332
  81.3 3.9 %copy-start.14 = (bf16[128,512]{1,0:T(8,128)(2,1)}, bf16[128,512]{1,0:T(8,128)(2,1)S(1)}, u32[]{:S(2)}) copy-start(bf16[128,512]{1,0:T(8,128)(2,1)S(1)} %collective-permute-done.7.refs_1_.refs_5_) | copy-start | bytes 393220
  81.3 12.8 %collective-permute-start.21 = (bf16[128,512]{1,0:T(8,128)(2,1)}, bf16[128,512]{1,0:T(8,128)(2,1)S(1)}, u32[]{:S(2)}, u32[]{:S(2)}) collective-permute-start(bf16[128,512]{1,0:T(8,128)(2,1)} %get-tuple-element.69), channel_id=1, source_target_pairs={{0,8},{4,12},{8,0},{12,4},{1,9},{5,13},{9,1},{13,5},{2,10},{6,14},... | collective-permute-start | bytes 393224 | tf_op jit(solution)/shard_map/ppermute | solution.py:332
  81.4 3.8 %copy-start.15 = (bf16[128,512]{1,0:T(8,128)(2,1)}, bf16[128,512]{1,0:T(8,128)(2,1)S(1)}, u32[]{:S(2)}) copy-start(bf16[128,512]{1,0:T(8,128)(2,1)S(1)} %collective-permute-done.8.refs_2_.refs_6_) | copy-start | bytes 393220
  81.4 14.1 %collective-permute-start.20 = (bf16[128,512]{1,0:T(8,128)(2,1)}, bf16[128,512]{1,0:T(8,128)(2,1)S(1)}, u32[]{:S(2)}, u32[]{:S(2)}) collective-permute-start(bf16[128,512]{1,0:T(8,128)(2,1)} %get-tuple-element.68), channel_id=1, source_target_pairs={{0,12},{4,0},{8,4},{12,8},{1,13},{5,1},{9,5},{13,9},{2,14},{6,2},{... | collective-permute-start | bytes 393224 | tf_op jit(solution)/shard_map/ppermute | solution.py:332
  85.2 0.7 copy-start.16
  85.9 9.7 %copy-start.22 = (f32[128,512]{1,0:T(8,128)S(1)}, f32[128,512]{1,0:T(8,128)}, u32[]{:S(2)}) copy-start(f32[128,512]{1,0:T(8,128)} %get-tuple-element.67) | copy-start | bytes 786436
  91.2 10.5 %collective-permute-start.15 = (bf16[128,512]{1,0:T(8,128)(2,1)}, bf16[128,512]{1,0:T(8,128)(2,1)S(1)}, u32[]{:S(2)}, u32[]{:S(2)}) collective-permute-start(bf16[128,512]{1,0:T(8,128)(2,1)} %get-tuple-element.66), channel_id=1, source_target_pairs={{12,0},{13,1},{14,2},{15,3},{28,16},{29,17},{30,18},{31,19}} | collective-permute-start | bytes 393224 | tf_op jit(solution)/shard_map/ppermute | solution.py:338
  92.5 3.1 %copy-start.18 = (bf16[128,512]{1,0:T(8,128)(2,1)}, bf16[128,512]{1,0:T(8,128)(2,1)S(1)}, u32[]{:S(2)}) copy-start(bf16[128,512]{1,0:T(8,128)(2,1)S(1)} %collective-permute-done.22.refs_5_) | copy-start | bytes 393220
  92.5 12.8 %collective-permute-start.14 = (bf16[128,512]{1,0:T(8,128)(2,1)}, bf16[128,512]{1,0:T(8,128)(2,1)S(1)}, u32[]{:S(2)}, u32[]{:S(2)}) collective-permute-start(bf16[128,512]{1,0:T(8,128)(2,1)} %get-tuple-element.65), channel_id=1, source_target_pairs={{8,0},{12,4},{9,1},{13,5},{10,2},{14,6},{11,3},{15,7},{24,16},{28,... | collective-permute-start | bytes 393224 | tf_op jit(solution)/shard_map/ppermute | solution.py:338
  94.1 1.5 copy-start.19
  94.1 12.2 %collective-permute-start.13 = (bf16[128,512]{1,0:T(8,128)(2,1)}, bf16[128,512]{1,0:T(8,128)(2,1)S(1)}, u32[]{:S(2)}, u32[]{:S(2)}) collective-permute-start(bf16[128,512]{1,0:T(8,128)(2,1)} %get-tuple-element.64), channel_id=1, source_target_pairs={{4,0},{8,4},{12,8},{5,1},{9,5},{13,9},{6,2},{10,6},{14,10},{7,3},{... | collective-permute-start | bytes 393224 | tf_op jit(solution)/shard_map/ppermute | solution.py:338
  95.4 24.1 %copy-start.10 = (bf16[1024,512]{1,0:T(8,128)(2,1)}, bf16[1024,512]{1,0:T(8,128)(2,1)S(1)}, u32[]{:S(2)}) copy-start(bf16[1024,512]{1,0:T(8,128)(2,1)S(1)} %collective-permute-done.23.refs_4_) | copy-start | bytes 3145732
  95.4 41.6 %collective-permute-start.24 = (bf16[1024,512]{1,0:T(8,128)(2,1)S(1)}, bf16[1024,512]{1,0:T(8,128)(2,1)S(1)}, u32[]{:S(2)}, u32[]{:S(2)}) collective-permute-start(bf16[1024,512]{1,0:T(8,128)(2,1)S(1)} %collective-permute-done.23.refs_4_), channel_id=1, source_target_pairs={{0,1},{1,0},{2,3},{3,2},{4,5},{5,4},{6,7},{7,6},{8,9},{9,8},{10,11... | collective-permute-start | bytes 3145736 | tf_op jit(solution)/shard_map/ppermute | solution.py:344
  95.5 0.8 copy-start.20
  95.5 10.8 %copy-start.21 = (f32[128,512]{1,0:T(8,128)S(1)}, f32[128,512]{1,0:T(8,128)}, u32[]{:S(2)}) copy-start(f32[128,512]{1,0:T(8,128)} %get-tuple-element.63) | copy-start | bytes 786436
  96.3 23.1 %copy-start.8 = (bf16[128,512]{1,0:T(8,128)(2,1)}, bf16[128,512]{1,0:T(8,128)(2,1)S(1)}, u32[]{:S(2)}) copy-start(bf16[128,512]{1,0:T(8,128)(2,1)S(1)} %add_convert_fusion.refs_0_) | copy-start | bytes 393220
  96.3 13.1 %collective-permute-start.27 = (bf16[128,512]{1,0:T(8,128)(2,1)S(1)}, bf16[128,512]{1,0:T(8,128)(2,1)S(1)}, u32[]{:S(2)}, u32[]{:S(2)}) collective-permute-start(bf16[128,512]{1,0:T(8,128)(2,1)S(1)} %add_convert_fusion.refs_0_), channel_id=1, source_target_pairs={{0,12},{4,0},{8,4},{12,8},{1,13},{5,1},{9,5},{13,9},{2,14},{6,2},{... | collective-permute-start | bytes 393224 | tf_op jit(solution)/shard_map/ppermute | solution.py:332
  101.7 17.7 %collective-permute-start.26 = (bf16[128,512]{1,0:T(8,128)(2,1)S(1)}, bf16[128,512]{1,0:T(8,128)(2,1)S(1)}, u32[]{:S(2)}, u32[]{:S(2)}) collective-permute-start(bf16[128,512]{1,0:T(8,128)(2,1)S(1)} %add_convert_fusion.refs_0_), channel_id=1, source_target_pairs={{0,8},{4,12},{8,0},{12,4},{1,9},{5,13},{9,1},{13,5},{2,10},{6,14},... | collective-permute-start | bytes 393224 | tf_op jit(solution)/shard_map/ppermute | solution.py:332
  105.4 14.0 %collective-permute-start.25 = (bf16[128,512]{1,0:T(8,128)(2,1)S(1)}, bf16[128,512]{1,0:T(8,128)(2,1)S(1)}, u32[]{:S(2)}, u32[]{:S(2)}) collective-permute-start(bf16[128,512]{1,0:T(8,128)(2,1)S(1)} %add_convert_fusion.refs_0_), channel_id=1, source_target_pairs={{0,4},{4,8},{8,12},{12,0},{1,5},{5,9},{9,13},{13,1},{2,6},{6,10},{... | collective-permute-start | bytes 393224 | tf_op jit(solution)/shard_map/ppermute | solution.py:332
  106.4 24.2 %copy-start.9 = (bf16[128,512]{1,0:T(8,128)(2,1)}, bf16[128,512]{1,0:T(8,128)(2,1)S(1)}, u32[]{:S(2)}) copy-start(bf16[128,512]{1,0:T(8,128)(2,1)S(1)} %add_convert_fusion.1.refs_1_) | copy-start | bytes 393220
  106.4 13.2 %collective-permute-start.18 = (bf16[128,512]{1,0:T(8,128)(2,1)S(1)}, bf16[128,512]{1,0:T(8,128)(2,1)S(1)}, u32[]{:S(2)}, u32[]{:S(2)}) collective-permute-start(bf16[128,512]{1,0:T(8,128)(2,1)S(1)} %add_convert_fusion.1.refs_1_), channel_id=1, source_target_pairs={{0,12},{4,0},{8,4},{12,8},{1,13},{5,1},{9,5},{13,9},{2,14},{6,2},{... | collective-permute-start | bytes 393224 | tf_op jit(solution)/shard_map/ppermute | solution.py:332
  109.3 21.2 %collective-permute-start.17 = (bf16[128,512]{1,0:T(8,128)(2,1)S(1)}, bf16[128,512]{1,0:T(8,128)(2,1)S(1)}, u32[]{:S(2)}, u32[]{:S(2)}) collective-permute-start(bf16[128,512]{1,0:T(8,128)(2,1)S(1)} %add_convert_fusion.1.refs_1_), channel_id=1, source_target_pairs={{0,8},{4,12},{8,0},{12,4},{1,9},{5,13},{9,1},{13,5},{2,10},{6,14},... | collective-permute-start | bytes 393224 | tf_op jit(solution)/shard_map/ppermute | solution.py:332
  119.4 11.1 %collective-permute-start.16 = (bf16[128,512]{1,0:T(8,128)(2,1)S(1)}, bf16[128,512]{1,0:T(8,128)(2,1)S(1)}, u32[]{:S(2)}, u32[]{:S(2)}) collective-permute-start(bf16[128,512]{1,0:T(8,128)(2,1)S(1)} %add_convert_fusion.1.refs_1_), channel_id=1, source_target_pairs={{0,4},{4,8},{8,12},{12,0},{1,5},{5,9},{9,13},{13,1},{2,6},{6,10},{... | collective-permute-start | bytes 393224 | tf_op jit(solution)/shard_map/ppermute | solution.py:332
  119.5 11.1 %copy-start.6 = (bf16[512,512]{1,0:T(8,128)(2,1)}, bf16[512,512]{1,0:T(8,128)(2,1)S(1)}, u32[]{:S(2)}) copy-start(bf16[512,512]{1,0:T(8,128)(2,1)S(1)} %pad_maximum_fusion.1.g_own) | copy-start | bytes 1572868
  119.5 13.6 %collective-permute-start.28 = (bf16[512,512]{1,0:T(8,128)(2,1)S(1)}, bf16[512,512]{1,0:T(8,128)(2,1)S(1)}, u32[]{:S(2)}, u32[]{:S(2)}) collective-permute-start(bf16[512,512]{1,0:T(8,128)(2,1)S(1)} %pad_maximum_fusion.1.g_own), channel_id=1, source_target_pairs={{0,1},{1,0},{2,3},{3,2},{4,5},{5,4},{6,7},{7,6},{8,9},{9,8},{10,11... | collective-permute-start | bytes 1572872 | tf_op jit(solution)/shard_map/ppermute | solution.py:344
  130.6 2.5 %copy-start.5 = (bf16[512,512]{1,0:T(8,128)(2,1)}, bf16[512,512]{1,0:T(8,128)(2,1)S(1)}, u32[]{:S(2)}) copy-start(bf16[512,512]{1,0:T(8,128)(2,1)S(1)} %pad_maximum_fusion.g_own) | copy-start | bytes 1572868
  130.6 12.1 %collective-permute-start.19 = (bf16[512,512]{1,0:T(8,128)(2,1)S(1)}, bf16[512,512]{1,0:T(8,128)(2,1)S(1)}, u32[]{:S(2)}, u32[]{:S(2)}) collective-permute-start(bf16[512,512]{1,0:T(8,128)(2,1)S(1)} %pad_maximum_fusion.g_own), channel_id=1, source_target_pairs={{0,1},{1,0},{2,3},{3,2},{4,5},{5,4},{6,7},{7,6},{8,9},{9,8},{10,11... | collective-permute-start | bytes 1572872 | tf_op jit(solution)/shard_map/ppermute | solution.py:344
  133.1 0.8 copy-start.13
  136.4 11.1 %collective-permute-start.29 = (bf16[256,512]{1,0:T(8,128)(2,1)}, bf16[256,512]{1,0:T(8,128)(2,1)S(1)}, u32[]{:S(2)}, u32[]{:S(2)}) collective-permute-start(bf16[256,512]{1,0:T(8,128)(2,1)} %weight_grad.2.refs_0_), channel_id=1, source_target_pairs={{0,2},{2,0},{1,3},{3,1},{4,6},{6,4},{5,7},{7,5},{8,10},{10,8},{9,1... | collective-permute-start | bytes 786440 | tf_op jit(solution)/shard_map/ppermute | solution.py:341
  137.0 1.0 copy-start.11
  142.7 0.8 copy-start.12
  146.1 8.5 %collective-permute-start.30 = (bf16[256,512]{1,0:T(8,128)(2,1)}, bf16[256,512]{1,0:T(8,128)(2,1)S(1)}, u32[]{:S(2)}, u32[]{:S(2)}) collective-permute-start(bf16[256,512]{1,0:T(8,128)(2,1)} %weight_grad.3.refs_2_), channel_id=1, source_target_pairs={{0,2},{2,0},{1,3},{3,1},{4,6},{6,4},{5,7},{7,5},{8,10},{10,8},{9,1... | collective-permute-start | bytes 786440 | tf_op jit(solution)/shard_map/ppermute | solution.py:341
  147.5 7.0 %copy-start.23 = (bf16[256,512]{1,0:T(8,128)(2,1)}, bf16[256,512]{1,0:T(8,128)(2,1)S(1)}, u32[]{:S(2)}) copy-start(bf16[256,512]{1,0:T(8,128)(2,1)S(1)} %collective-permute-done.29.refs_1_) | copy-start | bytes 786436
  154.6 0.7 copy-start.24

commit v3 on v2

--- a/solution.py
+++ b/solution.py
@@ -365,37 +365,39 @@
     carried = [around(x, k) for k, x in zip(shifts, loads)]
     pairs = [[pair_a] + carried, [pair_b] + [up(pair_b, k) for k in shifts]]
 
-    w_late, _ = lax.optimization_barrier((w_own, carried[0]))
-    b_own = partner(w_late)
-    b_other = core(b_own)
-
-    before, sums = [], []
-    for part in range(PARTS):
-        before, sent, total = attend(
-            place, queries[0], out_grad[0], pairs[part], part, x_for[:0:-1], before
-        )
-        if part == 0:
-            back = [around(x, n - k) for k, x in zip(shifts, sent)]
-            returned = back
-            back = [jnp.where(z + k < n, x, jnp.zeros_like(x)) for k, x in zip(shifts, back)]
-        else:
-            back = [down(x, k) for k, x in zip(shifts, sent)]
+    queries, out_grad = queries[0], out_grad[0]
+    before, sent_a, own_a = attend(place, queries, out_grad, pairs[0], 0, x_for[:0:-1], [])
+    returned = [around(x, n - k) for k, x in zip(shifts, sent_a)]
+    before, sent_b, own_b = attend(place, queries, out_grad, pairs[1], 1, [], before)
+    back_b = [down(x, k) for k, x in zip(shifts, sent_b)]
+    returned, _ = lax.optimization_barrier((returned, sent_b))
+    back_a = [jnp.where(z + k < n, x, jnp.zeros_like(x)) for k, x in zip(shifts, returned)]
+    sums = []
+    for total, back in ((own_a, back_a), (own_b, back_b)):
         for x in back:
             total = total + x.astype(jnp.float32)
         sums.append(total.astype(jnp.bfloat16))
     context, query_grad = before[:2]
     x_turned = turn(place, x_for[0], carried, returned, rows)
 
-    input_grad = input_grad_of(place, sums, w_own, w_other, b_own, b_other, n, rows)
+    w_late, _ = lax.optimization_barrier((w_own, sums[1]))
+    b_own = partner(w_late)
+    b_other = core(b_own)
     partials = []
     for part in range(PARTS):
-        g_own = jnp.concatenate([sums[part]] + [around(sums[part], k) for k in shifts], axis=0)
-        g_other = core(g_own)
+        pieces = [sums[part]] + [around(sums[part], k) for k in shifts]
+        if part == 0:
+            pieces, _ = lax.optimization_barrier((pieces, sums[1]))
         if part == PARTS - 1:
-            g_other, input_grad = lax.optimization_barrier((g_other, input_grad))
-        partials.append(weight_grad_of(x_turned, g_own, g_other, n))
+            pieces, partials = lax.optimization_barrier((pieces, partials))
+        g_own = jnp.concatenate(pieces, axis=0)
+        partials.append(weight_grad_of(x_turned, g_own, core(g_own), n))
+    sums, _ = lax.optimization_barrier((sums, partials[-1]))
+    input_grad = input_grad_of(place, sums, w_own, w_other, b_own, b_other, n, rows)
     if reps == 2:
-        grads = finish(*[x for p in partials for x in (p, partner(p))])
+        others = [partner(p) for p in partials]
+        others, input_grad = lax.optimization_barrier((others, input_grad))
+        grads = finish(*[x for p in zip(partials, others) for x in p])
     else:
         totals = [lax.psum(p.astype(jnp.float32), "rep").astype(jnp.bfloat16) for p in partials]
         grads = finish(*[x for p in totals for x in (p, jnp.zeros_like(p))])

time: 158 us -> 143 us (0.905)
  waiting for transfers between devices: 56.4 us -> 43.8 us
  starting transfers between devices: 56.9 us -> 53.5 us
    ppermute x15, waiting for transfers between devices: 38.6 us -> 30.9 us  [around(): return lax.ppermute(x, 'seq', [(i, (i + k) % n) for i in range(n)])]
    ppermute x3, starting transfers between devices: 13.7 us -> 7.08 us  [up(): return lax.ppermute(x, 'seq', [(i, i + k) for i in range(n - k)])]
    ppermute x5, waiting for transfers between devices: 11.3 us -> 5.56 us  [partner(): return lax.ppermute(x, 'rep', [(j, j ^ 1) for j in range(reps)])]
    unnamed x55 -> x63, local copies, waits for them, and re-layouts: 7.7 us -> 8.36 us
  transfers between devices with their start and end apart: 31 -> 31, of which waited for: 13 -> 12; matrix products, arithmetic and copies ran while one was open for 2% -> 3% of each run, Pallas kernels for 15% -> 16%
where the time goes in v3:
time: 143 us
  starting transfers between devices  53.5 us (37%)
  waiting for transfers between devices  43.8 us (31%)
  Pallas kernels  30.6 us (21%)
  local copies, waits for them, and re-layouts  10 us (7%)
  other arithmetic  3.77 us (3%)
    ppermute x15, starting transfers between devices, around(): return lax.ppermute(x, 'seq', [(i, (i + k) % n) for i in range(n)])  34 us
    ppermute x15, waiting for transfers between devices, around(): return lax.ppermute(x, 'seq', [(i, (i + k) % n) for i in range(n)])  30.9 us
    pallas_call x2, Pallas kernels, attend(): pl.pallas_call(functools.partial(attend_kernel, count=count, block=block,...  11 us
    unnamed x63, local copies, waits for them, and re-layouts  8.36 us
    ppermute x5, starting transfers between devices, partner(): return lax.ppermute(x, 'rep', [(j, j ^ 1) for j in range(reps)])  7.62 us
    ppermute x3, starting transfers between devices, up(): return lax.ppermute(x, 'seq', [(i, i + k) for i in range(n - k)])  7.08 us
    ppermute x5, waiting for transfers between devices, partner(): return lax.ppermute(x, 'rep', [(j, j ^ 1) for j in range(reps)])  5.56 us
    pallas_call x2, Pallas kernels, weight_grad_of(): pl.pallas_call(functools.partial(weight_grad_kernel, count=count), in_spe...  5.03 us
  transfers between devices with their start and end apart: 31, of which 12 were waited for; matrix products, arithmetic and copies ran while one was open for 3% of the time, Pallas kernels for 16%

profile of v3, /device:TPU:0, one launch (start us, length us, event | category | flops | bytes accessed | tf_op | source)
XLA Modules:
  0.0 142.9 jit_solution(972957901558293134)
XLA Ops:
  0.7 1.0 broadcast_select_fusion
  1.7 3.1 %collective-permute-start = (bf16[256,512]{1,0:T(8,128)(2,1)S(1)}, bf16[256,512]{1,0:T(8,128)(2,1)S(1)}, u32[]{:S(2)}, u32[]{:S(2)}) collective-permute-start(bf16[256,512]{1,0:T(8,128)(2,1)S(1)} %broadcast_select_fusion), channel_id=1, source_target_pairs={{0,4},{4,8},{8,12},{12,0},{1,5},{5,9},{9,13},{13,1},{2,6},{6,10},{... | collective-permute-start | bytes 786440 | tf_op jit(solution)/shard_map/ppermute | solution.py:332
  4.8 1.5 %collective-permute-start.3 = (bf16[128,2048]{1,0:T(8,128)(2,1)S(1)}, bf16[128,2048]{1,0:T(8,128)(2,1)S(1)}, u32[]{:S(2)}, u32[]{:S(2)}) collective-permute-start(bf16[128,2048]{1,0:T(8,128)(2,1)S(1)} %bitcast.24), channel_id=1, source_target_pairs={{0,2},{2,0},{1,3},{3,1},{4,6},{6,4},{5,7},{7,5},{8,10},{10,8},{9,1... | collective-permute-start | bytes 1572872 | tf_op jit(solution)/shard_map/ppermute | solution.py:341
  6.3 6.8 %collective-permute-done = bf16[256,512]{1,0:T(8,128)(2,1)S(1)} collective-permute-done((bf16[256,512]{1,0:T(8,128)(2,1)S(1)}, bf16[256,512]{1,0:T(8,128)(2,1)S(1)}, u32[]{:S(2)}, u32[]{:S(2)}) %collective-permute-start) | collective-permute-done | bytes 262176 | tf_op jit(solution)/shard_map/ppermute | solution.py:332
  13.1 0.4 reshape.21
  13.5 1.1 constant_dynamic-slice_fusion
  14.6 0.1 copy.17
  14.7 0.1 collective-permute-start.4
  14.7 1.8 %collective-permute-start.2 = (bf16[256,512]{1,0:T(8,128)(2,1)S(1)}, bf16[256,512]{1,0:T(8,128)(2,1)S(1)}, u32[]{:S(2)}, u32[]{:S(2)}) collective-permute-start(bf16[256,512]{1,0:T(8,128)(2,1)S(1)} %broadcast_select_fusion), channel_id=1, source_target_pairs={{0,12},{4,0},{8,4},{12,8},{1,13},{5,1},{9,5},{13,9},{2,14},{6,2},{... | collective-permute-start | bytes 786440 | tf_op jit(solution)/shard_map/ppermute | solution.py:332
  16.5 0.1 copy.18
  16.6 0.8 fusion.1
  17.5 7.1 %collective-permute-done.2 = bf16[256,512]{1,0:T(8,128)(2,1)S(1)} collective-permute-done((bf16[256,512]{1,0:T(8,128)(2,1)S(1)}, bf16[256,512]{1,0:T(8,128)(2,1)S(1)}, u32[]{:S(2)}, u32[]{:S(2)}) %collective-permute-start.2) | collective-permute-done | bytes 262176 | tf_op jit(solution)/shard_map/ppermute | solution.py:332
  24.6 9.3 %collective-permute-done.1 = bf16[256,512]{1,0:T(8,128)(2,1)S(1)} collective-permute-done((bf16[256,512]{1,0:T(8,128)(2,1)S(1)}, bf16[256,512]{1,0:T(8,128)(2,1)S(1)}, u32[]{:S(2)}, u32[]{:S(2)}) %collective-permute-start.1) | collective-permute-done | bytes 262176 | tf_op jit(solution)/shard_map/ppermute | solution.py:332
  33.9 0.7 copy-done.19
  34.7 0.1 collective-permute-start.5
  34.8 0.8 pad_add_fusion.place
  35.6 1.8 %collective-permute-done.5.w_other.refs_3_ = bf16[1024,512]{1,0:T(8,128)(2,1)S(1)} collective-permute-done((bf16[1024,512]{1,0:T(8,128)(2,1)S(1)}, bf16[1024,512]{1,0:T(8,128)(2,1)S(1)}, u32[]{:S(2)}, u32[]{:S(2)}) %collective-permute-start.5) | collective-permute-done | bytes 1048608 | tf_op jit(solution)/shard_map/ppermute | solution.py:344
  37.4 1.0 copy-done.2
  38.4 3.4 %project.1 = (bf16[144,512]{1,0:T(8,128)(2,1)}, bf16[128,512]{1,0:T(8,128)(2,1)}) custom-call(s32[3]{0:T(128)} %pad_add_fusion.place, s32[1,128]{1,0:T(1,128)} %seg.1, bf16[128,2048]{1,0:T(8,128)(2,1)} %bitcast.23, bf16[128,2048]{1,0:T(8,128)(2,1)} %copy-done.19, bf16[1024,512]{1,0:T(8,128)(2,1)} %copy-done, bf16[1024,512]{1,0:T(8,128)(2,1)} %copy-done.2), custom_call_target="tpu_custom_call" | custom-call | tf_op jit(solution)/shard_map/project/pallas_call | solution.py:62
  41.8 1.5 %collective-permute-start.6 = (bf16[128,512]{1,0:T(8,128)(2,1)}, bf16[128,512]{1,0:T(8,128)(2,1)S(1)}, u32[]{:S(2)}, u32[]{:S(2)}) collective-permute-start(bf16[128,512]{1,0:T(8,128)(2,1)} %get-tuple-element.64), channel_id=1, source_target_pairs={{0,2},{2,0},{1,3},{3,1},{4,6},{6,4},{5,7},{7,5},{8,10},{10,8},{9,1... | collective-permute-start | bytes 393224 | tf_op jit(solution)/shard_map/ppermute | solution.py:341
  43.3 4.3 %collective-permute-done.6.mate = bf16[128,512]{1,0:T(8,128)(2,1)S(1)} collective-permute-done((bf16[128,512]{1,0:T(8,128)(2,1)}, bf16[128,512]{1,0:T(8,128)(2,1)S(1)}, u32[]{:S(2)}, u32[]{:S(2)}) %collective-permute-start.6) | collective-permute-done | bytes 131104 | tf_op jit(solution)/shard_map/ppermute | solution.py:341
  47.6 0.6 copy-done.26
  48.2 2.0 %pack.1 = (bf16[144,512]{1,0:T(8,128)(2,1)}, bf16[128,512]{1,0:T(8,128)(2,1)}, bf16[144,512]{1,0:T(8,128)(2,1)}, bf16[144,512]{1,0:T(8,128)(2,1)}, bf16[144,512]{1,0:T(8,128)(2,1)}) custom-call(s32[3]{0:T(128)} %pad_add_fusion.place, bf16[144,512]{1,0:T(8,128)(2,1)} %get-tuple-element.63.own, bf16[128,512]{1,0:T(8,128)(2,1)} %copy-done.26, ...), custom_call_target="tpu_custom_call" | custom-call | tf_op jit(solution)/shard_map/pack/pallas_call | solution.py:94
  50.3 0.8 collective-permute-start.10
  51.1 3.4 %collective-permute-start.11 = (bf16[144,512]{1,0:T(8,128)(2,1)}, bf16[144,512]{1,0:T(8,128)(2,1)S(1)}, u32[]{:S(2)}, u32[]{:S(2)}) collective-permute-start(bf16[144,512]{1,0:T(8,128)(2,1)} %get-tuple-element.71), channel_id=1, source_target_pairs={{0,8},{4,12},{8,0},{12,4},{1,9},{5,13},{9,1},{13,5},{2,10},{6,14},... | collective-permute-start | bytes 442376 | tf_op jit(solution)/shard_map/ppermute | solution.py:332
  54.5 3.4 %collective-permute-start.9 = (bf16[128,512]{1,0:T(8,128)(2,1)}, bf16[128,512]{1,0:T(8,128)(2,1)S(1)}, u32[]{:S(2)}, u32[]{:S(2)}) collective-permute-start(bf16[128,512]{1,0:T(8,128)(2,1)} %get-tuple-element.68.refs_0_.refs_4_), channel_id=1, source_target_pairs={{0,12},{1,13},{2,14},{3,15},{16,28},{17,29},{18,30},{19,31}} | collective-permute-start | bytes 393224 | tf_op jit(solution)/shard_map/ppermute | solution.py:335
  57.9 1.3 collective-permute-start.8
  59.2 2.4 %collective-permute-start.7 = (bf16[128,512]{1,0:T(8,128)(2,1)}, bf16[128,512]{1,0:T(8,128)(2,1)S(1)}, u32[]{:S(2)}, u32[]{:S(2)}) collective-permute-start(bf16[128,512]{1,0:T(8,128)(2,1)} %get-tuple-element.68.refs_0_.refs_4_), channel_id=1, source_target_pairs={{0,4},{4,8},{8,12},{1,5},{5,9},{9,13},{2,6},{6,10},{10,14},{3,7},{... | collective-permute-start | bytes 393224 | tf_op jit(solution)/shard_map/ppermute | solution.py:335
  61.7 2.2 %collective-permute-done.11.refs_2_.refs_6_.refs_10_.refs_1_ = bf16[144,512]{1,0:T(8,128)(2,1)S(1)} collective-permute-done((bf16[144,512]{1,0:T(8,128)(2,1)}, bf16[144,512]{1,0:T(8,128)(2,1)S(1)}, u32[]{:S(2)}, u32[]{:S(2)}) %collective-permute-start.11) | collective-permute-done | bytes 147488 | tf_op jit(solution)/shard_map/ppermute | solution.py:332
  63.9 0.6 copy-done.4
  64.6 5.7 %attend.2 = (bf16[128,2048]{1,0:T(8,128)(2,1)}, bf16[128,2048]{1,0:T(8,128)(2,1)}, f32[128,512]{1,0:T(8,128)}, bf16[128,512]{1,0:T(8,128)(2,1)}, bf16[128,512]{1...) custom-call(s32[3]{0:T(128)} %pad_add_fusion.place, bf16[128,2048]{1,0:T(8,128)(2,1)} %bitcast.26, ...), custom_call_target="tpu_custom_call" | custom-call | tf_op jit(solution)/shard_map/attend/pallas_call | solution.py:213
  70.3 9.7 %collective-permute-start.19 = (bf16[128,512]{1,0:T(8,128)(2,1)}, bf16[128,512]{1,0:T(8,128)(2,1)S(1)}, u32[]{:S(2)}, u32[]{:S(2)}) collective-permute-start(bf16[128,512]{1,0:T(8,128)(2,1)} %get-tuple-element.83), channel_id=1, source_target_pairs={{0,12},{4,0},{8,4},{12,8},{1,13},{5,1},{9,5},{13,9},{2,14},{6,2},{... | collective-permute-start | bytes 393224 | tf_op jit(solution)/shard_map/ppermute | solution.py:332
  80.0 0.6 collective-permute-start.21
  80.7 0.6 copy-done.17
  81.3 5.4 %attend.3 = (bf16[128,2048]{1,0:T(8,128)(2,1)}, bf16[128,2048]{1,0:T(8,128)(2,1)}, bf16[128,512]{1,0:T(8,128)(2,1)}, bf16[128,512]{1,0:T(8,128)(2,1)}, bf16[128,512]{1,0:T(8,128)(2,1)}, /*index=5*/f32[128,512]{1,0:T(8,128)}) custom-call(s32[3]{0:T(128)} %pad_add_fusion.place, ...), custom_call_target="tpu_custom_call", output_to_operand_aliasing={{0}: (12, {}), {1}: (13, {})} | custom-call | tf_op jit(solution)/shard_map/attend/pallas_call | solution.py:213
  86.7 1.4 collective-permute-start.13
  88.1 1.3 collective-permute-start.14
  89.5 1.3 collective-permute-start.15
  90.8 0.1 add_convert_fusion.refs_0_
  90.9 0.5 copy-done.21
  91.5 6.5 %collective-permute-start.24 = (bf16[128,512]{1,0:T(8,128)(2,1)S(1)}, bf16[128,512]{1,0:T(8,128)(2,1)S(1)}, u32[]{:S(2)}, u32[]{:S(2)}) collective-permute-start(bf16[128,512]{1,0:T(8,128)(2,1)S(1)} %add_convert_fusion.refs_0_), channel_id=1, source_target_pairs={{0,12},{4,0},{8,4},{12,8},{1,13},{5,1},{9,5},{13,9},{2,14},{6,2},{... | collective-permute-start | bytes 393224 | tf_op jit(solution)/shard_map/ppermute | solution.py:332
  98.0 6.0 %collective-permute-start.22 = (bf16[128,512]{1,0:T(8,128)(2,1)S(1)}, bf16[128,512]{1,0:T(8,128)(2,1)S(1)}, u32[]{:S(2)}, u32[]{:S(2)}) collective-permute-start(bf16[128,512]{1,0:T(8,128)(2,1)S(1)} %add_convert_fusion.refs_0_), channel_id=1, source_target_pairs={{0,4},{4,8},{8,12},{12,0},{1,5},{5,9},{9,13},{13,1},{2,6},{6,10},{... | collective-permute-start | bytes 393224 | tf_op jit(solution)/shard_map/ppermute | solution.py:332
  104.0 4.7 %collective-permute-done.14 = bf16[128,512]{1,0:T(8,128)(2,1)S(1)} collective-permute-done((bf16[128,512]{1,0:T(8,128)(2,1)}, bf16[128,512]{1,0:T(8,128)(2,1)S(1)}, u32[]{:S(2)}, u32[]{:S(2)}) %collective-permute-start.14) | collective-permute-done | bytes 131104 | tf_op jit(solution)/shard_map/ppermute | solution.py:338
  108.7 1.0 add_convert_fusion.1.refs_1_
  109.8 1.6 %collective-permute-start.29 = (bf16[1024,512]{1,0:T(8,128)(2,1)S(1)}, bf16[1024,512]{1,0:T(8,128)(2,1)S(1)}, u32[]{:S(2)}, u32[]{:S(2)}) collective-permute-start(bf16[1024,512]{1,0:T(8,128)(2,1)S(1)} %copy-done.1), channel_id=1, source_target_pairs={{0,2},{2,0},{1,3},{3,1},{4,6},{6,4},{5,7},{7,5},{8,10},{10,8},{9,1... | collective-permute-start | bytes 3145736 | tf_op jit(solution)/shard_map/ppermute | solution.py:341
  111.3 0.2 collective-permute-done.23
  111.8 0.6 collective-permute-start.17
  112.4 1.4 collective-permute-start.16
  113.8 2.3 %turn.1.x_turned = bf16[256,1024]{1,0:T(8,128)(2,1)} custom-call(s32[3]{0:T(128)} %pad_add_fusion.place, bf16[128,512]{1,0:T(8,128)(2,1)} %get-tuple-element.82.here, bf16[144,512]{1,0:T(8,128)(2,1)} %copy-done.3, bf16[144,512]{1,0:T(8,128)(2,1)} %copy-done.4, bf16[144,512]{1,0:T(8,128)(2,1)} %copy-done.5, bf16[128,512]{1,0:T(8,128)(2,1)} %copy-done.20, ...), custom_call_target="tpu_custom_call" | custom-call | tf_op jit(solution)/shard_map/turn/pallas_call | solution.py:268
  116.1 0.8 copy-done.14
  116.9 2.5 %weight_grad.2.refs_0_ = bf16[256,512]{1,0:T(8,128)(2,1)} custom-call(bf16[256,1024]{1,0:T(8,128)(2,1)} %turn.1.x_turned, bf16[512,512]{1,0:T(8,128)(2,1)} %copy-done.13, bf16[512,512]{1,0:T(8,128)(2,1)} %copy-done.14), custom_call_target="tpu_custom_call" | custom-call | tf_op jit(solution)/shard_map/weight_grad/pallas_call | solution.py:288
  119.4 5.2 %collective-permute-done.17 = bf16[128,512]{1,0:T(8,128)(2,1)S(1)} collective-permute-done((bf16[128,512]{1,0:T(8,128)(2,1)S(1)}, bf16[128,512]{1,0:T(8,128)(2,1)S(1)}, u32[]{:S(2)}, u32[]{:S(2)}) %collective-permute-start.17) | collective-permute-done | bytes 131104 | tf_op jit(solution)/shard_map/ppermute | solution.py:332
  124.8 0.6 collective-permute-start.27
  125.4 0.5 copy-done.11
  125.9 1.5 %collective-permute-start.26 = (bf16[256,512]{1,0:T(8,128)(2,1)S(1)}, bf16[256,512]{1,0:T(8,128)(2,1)S(1)}, u32[]{:S(2)}, u32[]{:S(2)}) collective-permute-start(bf16[256,512]{1,0:T(8,128)(2,1)S(1)} %copy-done.11), channel_id=1, source_target_pairs={{0,2},{2,0},{1,3},{3,1},{4,6},{6,4},{5,7},{7,5},{8,10},{10,8},{9,1... | collective-permute-start | bytes 786440 | tf_op jit(solution)/shard_map/ppermute | solution.py:341
  127.4 0.7 collective-permute-done.27.g_other
  128.1 0.8 copy-done.15
  129.0 2.5 %weight_grad.3.refs_2_ = bf16[256,512]{1,0:T(8,128)(2,1)} custom-call(bf16[256,1024]{1,0:T(8,128)(2,1)} %turn.1.x_turned, bf16[512,512]{1,0:T(8,128)(2,1)} %copy-done.12, bf16[512,512]{1,0:T(8,128)(2,1)} %copy-done.15), custom_call_target="tpu_custom_call" | custom-call | tf_op jit(solution)/shard_map/weight_grad/pallas_call | solution.py:288
  131.5 1.5 %collective-permute-start.28 = (bf16[256,512]{1,0:T(8,128)(2,1)}, bf16[256,512]{1,0:T(8,128)(2,1)S(1)}, u32[]{:S(2)}, u32[]{:S(2)}) collective-permute-start(bf16[256,512]{1,0:T(8,128)(2,1)} %weight_grad.3.refs_2_), channel_id=1, source_target_pairs={{0,2},{2,0},{1,3},{3,1},{4,6},{6,4},{5,7},{7,5},{8,10},{10,8},{9,1... | collective-permute-start | bytes 786440 | tf_op jit(solution)/shard_map/ppermute | solution.py:341
  133.0 1.0 copy-done.10
  134.0 4.8 %input_grad.1 = bf16[128,2048]{1,0:T(8,128)(2,1)} custom-call(s32[3]{0:T(128)} %pad_add_fusion.place, bf16[128,512]{1,0:T(8,128)(2,1)} %copy-done.7, bf16[128,512]{1,0:T(8,128)(2,1)} %copy-done.8, bf16[1024,512]{1,0:T(8,128)(2,1)} %copy-done, bf16[1024,512]{1,0:T(8,128)(2,1)} %copy-done.2, bf16[1024,512]{1,0:T(8,128)(2,1)} %copy-done.9, ...), custom_call_target="tpu_custom_call" | custom-call | tf_op jit(solution)/shard_map/input_grad/pallas_call | solution.py:242
  138.8 1.3 collective-permute-done.28.refs_3_
  140.1 0.7 copy-done.25
  140.8 2.1 %finish.1 = (bf16[256,512]{1,0:T(8,128)(2,1)}, bf16[256,512]{1,0:T(8,128)(2,1)}) custom-call(bf16[256,512]{1,0:T(8,128)(2,1)} %weight_grad.2.refs_0_, bf16[256,512]{1,0:T(8,128)(2,1)} %copy-done.24, bf16[256,512]{1,0:T(8,128)(2,1)} %weight_grad.3.refs_2_, bf16[256,512]{1,0:T(8,128)(2,1)} %copy-done.25), custom_call_target="tpu_custom_call" | custom-call | tf_op jit(solution)/shard_map/finish/pallas_call | solution.py:310
  (82 shorter events, 0.7 us)
Async XLA Ops:
  0.6 4.1 %copy-start.6 = (bf16[1,128,2048]{2,1,0:T(8,128)(2,1)S(1)}, bf16[1,128,2048]{2,1,0:T(8,128)(2,1)}, u32[]{:S(2)}) copy-start(bf16[1,128,2048]{2,1,0:T(8,128)(2,1)} %param.6) | copy-start | bytes 1572868
  1.7 11.4 %collective-permute-start = (bf16[256,512]{1,0:T(8,128)(2,1)S(1)}, bf16[256,512]{1,0:T(8,128)(2,1)S(1)}, u32[]{:S(2)}, u32[]{:S(2)}) collective-permute-start(bf16[256,512]{1,0:T(8,128)(2,1)S(1)} %broadcast_select_fusion), channel_id=1, source_target_pairs={{0,4},{4,8},{8,12},{12,0},{1,5},{5,9},{9,13},{13,1},{2,6},{6,10},{... | collective-permute-start | bytes 786440 | tf_op jit(solution)/shard_map/ppermute | solution.py:332
  4.8 29.1 %collective-permute-start.3 = (bf16[128,2048]{1,0:T(8,128)(2,1)S(1)}, bf16[128,2048]{1,0:T(8,128)(2,1)S(1)}, u32[]{:S(2)}, u32[]{:S(2)}) collective-permute-start(bf16[128,2048]{1,0:T(8,128)(2,1)S(1)} %bitcast.24), channel_id=1, source_target_pairs={{0,2},{2,0},{1,3},{3,1},{4,6},{6,4},{5,7},{7,5},{8,10},{10,8},{9,1... | collective-permute-start | bytes 1572872 | tf_op jit(solution)/shard_map/ppermute | solution.py:341
  14.7 2.0 %collective-permute-start.4 = (bf16[128,4,256]{2,0,1:T(8,128)(2,1)S(1)}, bf16[128,4,256]{2,0,1:T(8,128)(2,1)S(1)}, u32[]{:S(2)}, u32[]{:S(2)}) collective-permute-start(bf16[128,4,256]{2,0,1:T(8,128)(2,1)S(1)} %bitcast.34), channel_id=1, source_target_pairs={{0,1},{1,0},{2,3},{3,2},{4,5},{5,4},{6,7},{7,6},{8,9},{9,8},{10,11... | collective-permute-start | bytes 786440 | tf_op jit(solution)/shard_map/ppermute | solution.py:344
  14.7 9.8 %collective-permute-start.2 = (bf16[256,512]{1,0:T(8,128)(2,1)S(1)}, bf16[256,512]{1,0:T(8,128)(2,1)S(1)}, u32[]{:S(2)}, u32[]{:S(2)}) collective-permute-start(bf16[256,512]{1,0:T(8,128)(2,1)S(1)} %broadcast_select_fusion), channel_id=1, source_target_pairs={{0,12},{4,0},{8,4},{12,8},{1,13},{5,1},{9,5},{13,9},{2,14},{6,2},{... | collective-permute-start | bytes 786440 | tf_op jit(solution)/shard_map/ppermute | solution.py:332
  16.5 17.3 %collective-permute-start.1 = (bf16[256,512]{1,0:T(8,128)(2,1)S(1)}, bf16[256,512]{1,0:T(8,128)(2,1)S(1)}, u32[]{:S(2)}, u32[]{:S(2)}) collective-permute-start(bf16[256,512]{1,0:T(8,128)(2,1)S(1)} %broadcast_select_fusion), channel_id=1, source_target_pairs={{0,8},{4,12},{8,0},{12,4},{1,9},{5,13},{9,1},{13,5},{2,10},{6,14},... | collective-permute-start | bytes 786440 | tf_op jit(solution)/shard_map/ppermute | solution.py:332
  33.8 0.8 copy-start.19
  34.7 2.7 %copy-start = (bf16[1024,512]{1,0:T(8,128)(2,1)}, bf16[1024,512]{1,0:T(8,128)(2,1)S(1)}, u32[]{:S(2)}) copy-start(bf16[1024,512]{1,0:T(8,128)(2,1)S(1)} %constant_dynamic-update-slice_fusion.w_own.refs_2_) | copy-start | bytes 3145732
  34.7 2.7 %collective-permute-start.5 = (bf16[1024,512]{1,0:T(8,128)(2,1)S(1)}, bf16[1024,512]{1,0:T(8,128)(2,1)S(1)}, u32[]{:S(2)}, u32[]{:S(2)}) collective-permute-start(bf16[1024,512]{1,0:T(8,128)(2,1)S(1)} %constant_dynamic-update-slice_fusion.w_own.refs_2_), channel_id=1, source_target_pairs={{0,1},{1,0},{2,3},{3,2},{4,5},{5,4},{6,7},{7,6},{8,9},{9,8},{10,11... | collective-permute-start | bytes 3145736 | tf_op jit(solution)/shard_map/ppermute | solution.py:344
  37.4 1.0 copy-start.2
  41.8 5.7 %collective-permute-start.6 = (bf16[128,512]{1,0:T(8,128)(2,1)}, bf16[128,512]{1,0:T(8,128)(2,1)S(1)}, u32[]{:S(2)}, u32[]{:S(2)}) collective-permute-start(bf16[128,512]{1,0:T(8,128)(2,1)} %get-tuple-element.64), channel_id=1, source_target_pairs={{0,2},{2,0},{1,3},{3,1},{4,6},{6,4},{5,7},{7,5},{8,10},{10,8},{9,1... | collective-permute-start | bytes 393224 | tf_op jit(solution)/shard_map/ppermute | solution.py:341
  47.6 0.6 copy-start.26
  50.3 9.0 %collective-permute-start.10 = (bf16[144,512]{1,0:T(8,128)(2,1)}, bf16[144,512]{1,0:T(8,128)(2,1)S(1)}, u32[]{:S(2)}, u32[]{:S(2)}) collective-permute-start(bf16[144,512]{1,0:T(8,128)(2,1)} %get-tuple-element.70), channel_id=1, source_target_pairs={{0,4},{4,8},{8,12},{12,0},{1,5},{5,9},{9,13},{13,1},{2,6},{6,10},{... | collective-permute-start | bytes 442376 | tf_op jit(solution)/shard_map/ppermute | solution.py:332
  51.1 12.8 %collective-permute-start.11 = (bf16[144,512]{1,0:T(8,128)(2,1)}, bf16[144,512]{1,0:T(8,128)(2,1)S(1)}, u32[]{:S(2)}, u32[]{:S(2)}) collective-permute-start(bf16[144,512]{1,0:T(8,128)(2,1)} %get-tuple-element.71), channel_id=1, source_target_pairs={{0,8},{4,12},{8,0},{12,4},{1,9},{5,13},{9,1},{13,5},{2,10},{6,14},... | collective-permute-start | bytes 442376 | tf_op jit(solution)/shard_map/ppermute | solution.py:332
  54.5 9.4 %collective-permute-start.12 = (bf16[144,512]{1,0:T(8,128)(2,1)}, bf16[144,512]{1,0:T(8,128)(2,1)S(1)}, u32[]{:S(2)}, u32[]{:S(2)}) collective-permute-start(bf16[144,512]{1,0:T(8,128)(2,1)} %get-tuple-element.72), channel_id=1, source_target_pairs={{0,12},{4,0},{8,4},{12,8},{1,13},{5,1},{9,5},{13,9},{2,14},{6,2},{... | collective-permute-start | bytes 442376 | tf_op jit(solution)/shard_map/ppermute | solution.py:332
  54.5 25.5 %collective-permute-start.9 = (bf16[128,512]{1,0:T(8,128)(2,1)}, bf16[128,512]{1,0:T(8,128)(2,1)S(1)}, u32[]{:S(2)}, u32[]{:S(2)}) collective-permute-start(bf16[128,512]{1,0:T(8,128)(2,1)} %get-tuple-element.68.refs_0_.refs_4_), channel_id=1, source_target_pairs={{0,12},{1,13},{2,14},{3,15},{16,28},{17,29},{18,30},{19,31}} | collective-permute-start | bytes 393224 | tf_op jit(solution)/shard_map/ppermute | solution.py:335
  57.9 22.8 %collective-permute-start.8 = (bf16[128,512]{1,0:T(8,128)(2,1)}, bf16[128,512]{1,0:T(8,128)(2,1)S(1)}, u32[]{:S(2)}, u32[]{:S(2)}) collective-permute-start(bf16[128,512]{1,0:T(8,128)(2,1)} %get-tuple-element.68.refs_0_.refs_4_), channel_id=1, source_target_pairs={{0,8},{4,12},{1,9},{5,13},{2,10},{6,14},{3,11},{7,15},{16,24},{20,... | collective-permute-start | bytes 393224 | tf_op jit(solution)/shard_map/ppermute | solution.py:335
  59.2 4.6 %copy-start.3 = (bf16[144,512]{1,0:T(8,128)(2,1)}, bf16[144,512]{1,0:T(8,128)(2,1)S(1)}, u32[]{:S(2)}) copy-start(bf16[144,512]{1,0:T(8,128)(2,1)S(1)} %collective-permute-done.10.refs_1_.refs_5_.refs_9_.refs_0_) | copy-start | bytes 442372
  59.2 21.4 %collective-permute-start.7 = (bf16[128,512]{1,0:T(8,128)(2,1)}, bf16[128,512]{1,0:T(8,128)(2,1)S(1)}, u32[]{:S(2)}, u32[]{:S(2)}) collective-permute-start(bf16[128,512]{1,0:T(8,128)(2,1)} %get-tuple-element.68.refs_0_.refs_4_), channel_id=1, source_target_pairs={{0,4},{4,8},{8,12},{1,5},{5,9},{9,13},{2,6},{6,10},{10,14},{3,7},{... | collective-permute-start | bytes 393224 | tf_op jit(solution)/shard_map/ppermute | solution.py:335
  63.9 0.7 copy-start.4
  63.9 0.7 copy-start.5
  70.3 19.2 %collective-permute-start.19 = (bf16[128,512]{1,0:T(8,128)(2,1)}, bf16[128,512]{1,0:T(8,128)(2,1)S(1)}, u32[]{:S(2)}, u32[]{:S(2)}) collective-permute-start(bf16[128,512]{1,0:T(8,128)(2,1)} %get-tuple-element.83), channel_id=1, source_target_pairs={{0,12},{4,0},{8,4},{12,8},{1,13},{5,1},{9,5},{13,9},{2,14},{6,2},{... | collective-permute-start | bytes 393224 | tf_op jit(solution)/shard_map/ppermute | solution.py:332
  80.0 10.8 %collective-permute-start.20 = (bf16[128,512]{1,0:T(8,128)(2,1)}, bf16[128,512]{1,0:T(8,128)(2,1)S(1)}, u32[]{:S(2)}, u32[]{:S(2)}) collective-permute-start(bf16[128,512]{1,0:T(8,128)(2,1)} %get-tuple-element.84), channel_id=1, source_target_pairs={{0,8},{4,12},{8,0},{12,4},{1,9},{5,13},{9,1},{13,5},{2,10},{6,14},... | collective-permute-start | bytes 393224 | tf_op jit(solution)/shard_map/ppermute | solution.py:332
  80.0 0.7 copy-start.16
  80.0 10.8 %collective-permute-start.21 = (bf16[128,512]{1,0:T(8,128)(2,1)}, bf16[128,512]{1,0:T(8,128)(2,1)S(1)}, u32[]{:S(2)}, u32[]{:S(2)}) collective-permute-start(bf16[128,512]{1,0:T(8,128)(2,1)} %get-tuple-element.85), channel_id=1, source_target_pairs={{0,4},{4,8},{8,12},{12,0},{1,5},{5,9},{9,13},{13,1},{2,6},{6,10},{... | collective-permute-start | bytes 393224 | tf_op jit(solution)/shard_map/ppermute | solution.py:332
  80.6 0.6 copy-start.17
  80.6 0.7 copy-start.18
  81.3 9.5 %copy-start.23 = (f32[128,512]{1,0:T(8,128)S(1)}, f32[128,512]{1,0:T(8,128)}, u32[]{:S(2)}) copy-start(f32[128,512]{1,0:T(8,128)} %get-tuple-element.89) | copy-start | bytes 786436
  86.7 23.0 %copy-start.1 = (bf16[1024,512]{1,0:T(8,128)(2,1)S(1)}, bf16[1024,512]{1,0:T(8,128)(2,1)}, u32[]{:S(2)}) copy-start(bf16[1024,512]{1,0:T(8,128)(2,1)} %copy-done) | copy-start | bytes 3145732
  86.7 11.2 %collective-permute-start.13 = (bf16[128,512]{1,0:T(8,128)(2,1)}, bf16[128,512]{1,0:T(8,128)(2,1)S(1)}, u32[]{:S(2)}, u32[]{:S(2)}) collective-permute-start(bf16[128,512]{1,0:T(8,128)(2,1)} %get-tuple-element.79), channel_id=1, source_target_pairs={{4,0},{8,4},{12,8},{5,1},{9,5},{13,9},{6,2},{10,6},{14,10},{7,3},{... | collective-permute-start | bytes 393224 | tf_op jit(solution)/shard_map/ppermute | solution.py:338
  88.1 20.6 %collective-permute-start.14 = (bf16[128,512]{1,0:T(8,128)(2,1)}, bf16[128,512]{1,0:T(8,128)(2,1)S(1)}, u32[]{:S(2)}, u32[]{:S(2)}) collective-permute-start(bf16[128,512]{1,0:T(8,128)(2,1)} %get-tuple-element.80), channel_id=1, source_target_pairs={{8,0},{12,4},{9,1},{13,5},{10,2},{14,6},{11,3},{15,7},{24,16},{28,... | collective-permute-start | bytes 393224 | tf_op jit(solution)/shard_map/ppermute | solution.py:338
  89.5 1.5 %copy-start.20 = (bf16[128,512]{1,0:T(8,128)(2,1)}, bf16[128,512]{1,0:T(8,128)(2,1)S(1)}, u32[]{:S(2)}) copy-start(bf16[128,512]{1,0:T(8,128)(2,1)S(1)} %collective-permute-done.19.refs_3_) | copy-start | bytes 393220
  89.5 19.3 %collective-permute-start.15 = (bf16[128,512]{1,0:T(8,128)(2,1)}, bf16[128,512]{1,0:T(8,128)(2,1)S(1)}, u32[]{:S(2)}, u32[]{:S(2)}) collective-permute-start(bf16[128,512]{1,0:T(8,128)(2,1)} %get-tuple-element.81), channel_id=1, source_target_pairs={{12,0},{13,1},{14,2},{15,3},{28,16},{29,17},{30,18},{31,19}} | collective-permute-start | bytes 393224 | tf_op jit(solution)/shard_map/ppermute | solution.py:338
  90.8 0.7 copy-start.21
  90.8 0.7 copy-start.22
  91.5 20.0 %copy-start.7 = (bf16[128,512]{1,0:T(8,128)(2,1)}, bf16[128,512]{1,0:T(8,128)(2,1)S(1)}, u32[]{:S(2)}) copy-start(bf16[128,512]{1,0:T(8,128)(2,1)S(1)} %add_convert_fusion.refs_0_) | copy-start | bytes 393220
  91.5 19.9 %collective-permute-start.24 = (bf16[128,512]{1,0:T(8,128)(2,1)S(1)}, bf16[128,512]{1,0:T(8,128)(2,1)S(1)}, u32[]{:S(2)}, u32[]{:S(2)}) collective-permute-start(bf16[128,512]{1,0:T(8,128)(2,1)S(1)} %add_convert_fusion.refs_0_), channel_id=1, source_target_pairs={{0,12},{4,0},{8,4},{12,8},{1,13},{5,1},{9,5},{13,9},{2,14},{6,2},{... | collective-permute-start | bytes 393224 | tf_op jit(solution)/shard_map/ppermute | solution.py:332
  97.9 13.6 %collective-permute-start.23 = (bf16[128,512]{1,0:T(8,128)(2,1)S(1)}, bf16[128,512]{1,0:T(8,128)(2,1)S(1)}, u32[]{:S(2)}, u32[]{:S(2)}) collective-permute-start(bf16[128,512]{1,0:T(8,128)(2,1)S(1)} %add_convert_fusion.refs_0_), channel_id=1, source_target_pairs={{0,8},{4,12},{8,0},{12,4},{1,9},{5,13},{9,1},{13,5},{2,10},{6,14},... | collective-permute-start | bytes 393224 | tf_op jit(solution)/shard_map/ppermute | solution.py:332
  98.0 13.6 %collective-permute-start.22 = (bf16[128,512]{1,0:T(8,128)(2,1)S(1)}, bf16[128,512]{1,0:T(8,128)(2,1)S(1)}, u32[]{:S(2)}, u32[]{:S(2)}) collective-permute-start(bf16[128,512]{1,0:T(8,128)(2,1)S(1)} %add_convert_fusion.refs_0_), channel_id=1, source_target_pairs={{0,4},{4,8},{8,12},{12,0},{1,5},{5,9},{9,13},{13,1},{2,6},{6,10},{... | collective-permute-start | bytes 393224 | tf_op jit(solution)/shard_map/ppermute | solution.py:332
  109.7 14.9 %copy-start.8 = (bf16[128,512]{1,0:T(8,128)(2,1)}, bf16[128,512]{1,0:T(8,128)(2,1)S(1)}, u32[]{:S(2)}) copy-start(bf16[128,512]{1,0:T(8,128)(2,1)S(1)} %add_convert_fusion.1.refs_1_) | copy-start | bytes 393220
  109.8 14.9 %collective-permute-start.29 = (bf16[1024,512]{1,0:T(8,128)(2,1)S(1)}, bf16[1024,512]{1,0:T(8,128)(2,1)S(1)}, u32[]{:S(2)}, u32[]{:S(2)}) collective-permute-start(bf16[1024,512]{1,0:T(8,128)(2,1)S(1)} %copy-done.1), channel_id=1, source_target_pairs={{0,2},{2,0},{1,3},{3,1},{4,6},{6,4},{5,7},{7,5},{8,10},{10,8},{9,1... | collective-permute-start | bytes 3145736 | tf_op jit(solution)/shard_map/ppermute | solution.py:341
  111.6 4.4 %copy-start.13 = (bf16[512,512]{1,0:T(8,128)(2,1)}, bf16[512,512]{1,0:T(8,128)(2,1)S(1)}, u32[]{:S(2)}) copy-start(bf16[512,512]{1,0:T(8,128)(2,1)S(1)} %constant_dynamic-update-slice_fusion.4.g_own) | copy-start | bytes 1572868
  111.6 4.4 %collective-permute-start.25 = (bf16[512,512]{1,0:T(8,128)(2,1)S(1)}, bf16[512,512]{1,0:T(8,128)(2,1)S(1)}, u32[]{:S(2)}, u32[]{:S(2)}) collective-permute-start(bf16[512,512]{1,0:T(8,128)(2,1)S(1)} %constant_dynamic-update-slice_fusion.4.g_own), channel_id=1, source_target_pairs={{0,1},{1,0},{2,3},{3,2},{4,5},{5,4},{6,7},{7,6},{8,9},{9,8},{10,11... | collective-permute-start | bytes 1572872 | tf_op jit(solution)/shard_map/ppermute | solution.py:344
  111.7 7.7 %collective-permute-start.18 = (bf16[128,512]{1,0:T(8,128)(2,1)S(1)}, bf16[128,512]{1,0:T(8,128)(2,1)S(1)}, u32[]{:S(2)}, u32[]{:S(2)}) collective-permute-start(bf16[128,512]{1,0:T(8,128)(2,1)S(1)} %add_convert_fusion.1.refs_1_), channel_id=1, source_target_pairs={{0,12},{4,0},{8,4},{12,8},{1,13},{5,1},{9,5},{13,9},{2,14},{6,2},{... | collective-permute-start | bytes 393224 | tf_op jit(solution)/shard_map/ppermute | solution.py:332
  111.8 12.9 %collective-permute-start.17 = (bf16[128,512]{1,0:T(8,128)(2,1)S(1)}, bf16[128,512]{1,0:T(8,128)(2,1)S(1)}, u32[]{:S(2)}, u32[]{:S(2)}) collective-permute-start(bf16[128,512]{1,0:T(8,128)(2,1)S(1)} %add_convert_fusion.1.refs_1_), channel_id=1, source_target_pairs={{0,8},{4,12},{8,0},{12,4},{1,9},{5,13},{9,1},{13,5},{2,10},{6,14},... | collective-permute-start | bytes 393224 | tf_op jit(solution)/shard_map/ppermute | solution.py:332
  112.4 12.2 %collective-permute-start.16 = (bf16[128,512]{1,0:T(8,128)(2,1)S(1)}, bf16[128,512]{1,0:T(8,128)(2,1)S(1)}, u32[]{:S(2)}, u32[]{:S(2)}) collective-permute-start(bf16[128,512]{1,0:T(8,128)(2,1)S(1)} %add_convert_fusion.1.refs_1_), channel_id=1, source_target_pairs={{0,4},{4,8},{8,12},{12,0},{1,5},{5,9},{9,13},{13,1},{2,6},{6,10},{... | collective-permute-start | bytes 393224 | tf_op jit(solution)/shard_map/ppermute | solution.py:332
  116.1 0.8 copy-start.14
  124.7 6.8 %copy-start.9 = (bf16[1024,512]{1,0:T(8,128)(2,1)}, bf16[1024,512]{1,0:T(8,128)(2,1)S(1)}, u32[]{:S(2)}) copy-start(bf16[1024,512]{1,0:T(8,128)(2,1)S(1)} %collective-permute-done.29.refs_4_) | copy-start | bytes 3145732
  124.7 8.3 %collective-permute-start.30 = (bf16[1024,512]{1,0:T(8,128)(2,1)S(1)}, bf16[1024,512]{1,0:T(8,128)(2,1)S(1)}, u32[]{:S(2)}, u32[]{:S(2)}) collective-permute-start(bf16[1024,512]{1,0:T(8,128)(2,1)S(1)} %collective-permute-done.29.refs_4_), channel_id=1, source_target_pairs={{0,1},{1,0},{2,3},{3,2},{4,5},{5,4},{6,7},{7,6},{8,9},{9,8},{10,11... | collective-permute-start | bytes 3145736 | tf_op jit(solution)/shard_map/ppermute | solution.py:344
  124.8 1.1 copy-start.11
  124.8 3.3 %copy-start.12 = (bf16[512,512]{1,0:T(8,128)(2,1)}, bf16[512,512]{1,0:T(8,128)(2,1)S(1)}, u32[]{:S(2)}) copy-start(bf16[512,512]{1,0:T(8,128)(2,1)S(1)} %constant_dynamic-update-slice_fusion.8.g_own) | copy-start | bytes 1572868
  124.8 3.3 %collective-permute-start.27 = (bf16[512,512]{1,0:T(8,128)(2,1)S(1)}, bf16[512,512]{1,0:T(8,128)(2,1)S(1)}, u32[]{:S(2)}, u32[]{:S(2)}) collective-permute-start(bf16[512,512]{1,0:T(8,128)(2,1)S(1)} %constant_dynamic-update-slice_fusion.8.g_own), channel_id=1, source_target_pairs={{0,1},{1,0},{2,3},{3,2},{4,5},{5,4},{6,7},{7,6},{8,9},{9,8},{10,11... | collective-permute-start | bytes 1572872 | tf_op jit(solution)/shard_map/ppermute | solution.py:344
  125.9 12.8 %collective-permute-start.26 = (bf16[256,512]{1,0:T(8,128)(2,1)S(1)}, bf16[256,512]{1,0:T(8,128)(2,1)S(1)}, u32[]{:S(2)}, u32[]{:S(2)}) collective-permute-start(bf16[256,512]{1,0:T(8,128)(2,1)S(1)} %copy-done.11), channel_id=1, source_target_pairs={{0,2},{2,0},{1,3},{3,1},{4,6},{6,4},{5,7},{7,5},{8,10},{10,8},{9,1... | collective-permute-start | bytes 786440 | tf_op jit(solution)/shard_map/ppermute | solution.py:341
  128.1 0.8 copy-start.15
  131.5 8.6 %collective-permute-start.28 = (bf16[256,512]{1,0:T(8,128)(2,1)}, bf16[256,512]{1,0:T(8,128)(2,1)S(1)}, u32[]{:S(2)}, u32[]{:S(2)}) collective-permute-start(bf16[256,512]{1,0:T(8,128)(2,1)} %weight_grad.3.refs_2_), channel_id=1, source_target_pairs={{0,2},{2,0},{1,3},{3,1},{4,6},{6,4},{5,7},{7,5},{8,10},{10,8},{9,1... | collective-permute-start | bytes 786440 | tf_op jit(solution)/shard_map/ppermute | solution.py:341
  133.0 1.0 copy-start.10
  138.8 1.3 copy-start.24
  140.1 0.7 copy-start.25

commit v4 on v3

v4 whole, which is shorter than its diff:
```python
import functools
import math

import jax
import jax.numpy as jnp
from jax import lax
from jax.experimental import pallas as pl
from jax.experimental.pallas import tpu as pltpu
from jax.sharding import PartitionSpec as P

HEADS = 16
KV_HEADS = 4
HEAD_DIM = 128
KV_WIDTH = KV_HEADS * HEAD_DIM
GROUP = HEADS // KV_HEADS
PARTS = 2
LOG2E = 1.4426950408889634
MASKED = -1e30
EXTRA = 16
MIB = 1024 * 1024


def params(mib=16, **kw):
    return pltpu.CompilerParams(vmem_limit_bytes=mib * MIB, **kw)


def vspec():
    return pl.BlockSpec(memory_space=pltpu.VMEM)


def near(*xs):
    return [pltpu.with_memory_space_constraint(x, pltpu.VMEM) for x in xs]


def sspec():
    return pl.BlockSpec(memory_space=pltpu.SMEM)


def assemble(full_ref, own_ref, other_ref, place, count, rows, left=0):
    z, c = place[0], place[1]
    right = left + own_ref.shape[1]
    for k in range(count):
        src = lax.rem(z - k + count, count)
        for ref, core in ((own_ref, c), (other_ref, 1 - c)):
            start = pl.multiple_of((src * 2 + core) * rows, rows)
            full_ref[pl.ds(start, rows), left:right] = ref[k * rows : (k + 1) * rows, :]


def project_kernel(place, seg, x_own, x_next, w_own, w_other, out_own, out_next, full, *, count, rows):
    assemble(full, w_own, w_other, place, count, rows)
    w = full[...]
    block = x_own.shape[0]
    out_next[...] = jnp.dot(x_next[...], w, preferred_element_type=jnp.float32).astype(jnp.bfloat16)
    out_own[:block, :] = jnp.dot(x_own[...], w, preferred_element_type=jnp.float32).astype(
        jnp.bfloat16
    )
    ids = (seg[...] + 1).astype(jnp.float32)
    copies = out_own.shape[1] // block
    wide = jnp.concatenate([jnp.broadcast_to(ids, (EXTRA, block))] * copies, axis=1)
    out_own[block:, :] = wide.astype(jnp.bfloat16)


def project(place, seg, x_own, x_next, w_own, w_other, count, rows):
    width = w_own.shape[1]
    block = x_own.shape[0]
    return pl.pallas_call(
        functools.partial(project_kernel, count=count, rows=rows),
        in_specs=[sspec()] + [vspec()] * 5,
        out_specs=[vspec()] * 2,
        out_shape=[
            pltpu.VMEM((block + EXTRA, width), jnp.bfloat16),
            pltpu.VMEM((block, width), jnp.bfloat16),
        ],
        scratch_shapes=[pltpu.VMEM((2 * count * rows, width), jnp.bfloat16)],
        compiler_params=params(),
        name="project",
    )(place, seg, x_own, *near(x_next, w_own, w_other))


def cut_kernel(place, own, other, *outs, count, rows):
    for k in range(count):
        start = (lax.rem(place[0] + k, count) * 2 + place[1]) * rows
        start = pl.multiple_of(start, rows)
        outs[k][:, :rows] = own[:, pl.ds(start, rows)]
        outs[k][:, rows:] = other[:, pl.ds(start, rows)]


def cut(place, own, other, count, rows):
    block = own.shape[0]
    if rows % 128 or 2 * rows != KV_WIDTH:
        pieces = []
        for k in range(count):
            start = (lax.rem(place[0] + k, count) * 2 + place[1]) * rows
            both = [lax.dynamic_slice_in_dim(x, start, rows, 1) for x in (own, other)]
            wide = jnp.concatenate(both, axis=1)
            pieces.append(jnp.pad(wide, ((0, 0), (0, KV_WIDTH - 2 * rows))))
        return pieces
    return pl.pallas_call(
        functools.partial(cut_kernel, count=count, rows=rows),
        in_specs=[sspec()] + [vspec()] * 2,
        out_specs=[vspec()] * count,
        out_shape=[pltpu.VMEM((block, 2 * rows), own.dtype)] * count,
        compiler_params=params(),
        name="cut",
    )(place, own, *near(other))


def pack_kernel(place, own, mate, *refs, count):
    cols, outs = refs[: count - 1], refs[count - 1 :]
    block, half = mate.shape
    first = jnp.concatenate([own[:block, :], mate[...]], axis=1)
    tail = own[block:, :]
    outs[0][:block, :] = first
    outs[0][block:, :half] = tail
    outs[0][block:, half:] = jnp.zeros_like(tail)
    for k in range(1, count):
        goes_up = place[0] + k < count
        outs[k][:block, :] = jnp.where(goes_up, first, cols[k - 1][...])
        outs[k][block:, :half] = jnp.where(goes_up, tail, jnp.zeros_like(tail))
        outs[k][block:, half:] = jnp.zeros_like(tail)


def pack(place, own, mate, cols):
    count = len(cols) + 1
    tall = pltpu.VMEM((own.shape[0], 2 * own.shape[1]), own.dtype)
    outs = pl.pallas_call(
        functools.partial(pack_kernel, count=count),
        in_specs=[sspec()] + [vspec()] * (count + 1),
        out_specs=[vspec()] * count,
        out_shape=[tall] * count,
        compiler_params=params(),
        name="pack",
    )(place, *near(own, mate, *cols))
    return outs[0], outs[1:]


def nt(a, b):
    return lax.dot_general(a, b, (((1,), (1,)), ((), ())), preferred_element_type=jnp.float32)


def tn(a, b):
    return lax.dot_general(a, b, (((0,), (0,)), ((), ())), preferred_element_type=jnp.float32)


def attend_kernel(place, q_ref, do_ref, *refs, count, block, opening):
    pair_refs, refs = refs[:count], refs[count:]
    if opening:
        cols = refs[: count - 1]
        ctx_ref, dq_ref, bias = refs[count - 1 : count + 2]
        grads, own_grad = refs[count + 2 : -1], refs[-1]
    else:
        bias = refs[0]
        ctx_ref, dq_ref = refs[3:5]
        grads, own_grad = refs[5:-1], refs[-1]
    inv_root = 1.0 / math.sqrt(HEAD_DIM)
    length = count * block

    if opening:

        @pl.when(pl.program_id(0) == 0)
        def _():
            ids = [r[block : block + 1, :block].astype(jnp.float32) for r in pair_refs]
            mine = jnp.broadcast_to(ids[0], (block, block)).T
            rows = lax.broadcasted_iota(jnp.int32, (block, block), 0)
            cols_here = lax.broadcasted_iota(jnp.int32, (block, block), 1)
            for k in range(count):
                ok = mine == jnp.broadcast_to(ids[k], (block, block))
                if k == 0:
                    ok = ok & (cols_here <= rows)
                bias[:, k * block : (k + 1) * block] = jnp.where(ok, 0.0, MASKED)

    even = place[2] == 0
    at_key = pl.multiple_of(pl.program_id(0) * HEAD_DIM, HEAD_DIM)
    at_value = pl.multiple_of(at_key + KV_WIDTH // PARTS, HEAD_DIM)
    a = jnp.concatenate([r[:block, pl.ds(at_key, HEAD_DIM)] for r in pair_refs], axis=0)
    b = jnp.concatenate([r[:block, pl.ds(at_value, HEAD_DIM)] for r in pair_refs], axis=0)
    key = jnp.where(even, a, b)
    value = jnp.where(even, b, a)

    def stack(ref):
        return jnp.concatenate(
            [ref[:, h * HEAD_DIM : (h + 1) * HEAD_DIM] for h in range(GROUP)], axis=0
        )

    def unstack(ref, val):
        for h in range(GROUP):
            ref[:, h * HEAD_DIM : (h + 1) * HEAD_DIM] = val[h * block : (h + 1) * block, :]

    q, do = stack(q_ref), stack(do_ref)
    s = nt(q, key) * (inv_root * LOG2E)
    s = (s.reshape(GROUP, block, length) + bias[...][None]).reshape(GROUP * block, length)
    e = jnp.exp2(s - jnp.max(s, axis=1, keepdims=True))
    p = e * (1.0 / jnp.sum(e, axis=1, keepdims=True))
    p_low = p.astype(jnp.bfloat16)
    ctx = jnp.dot(p_low, value, preferred_element_type=jnp.float32).astype(jnp.bfloat16)
    unstack(ctx_ref, ctx)
    dots = jnp.sum(do.astype(jnp.float32) * ctx.astype(jnp.float32), axis=1, keepdims=True)
    ds = (p * (nt(do, value) - dots)).astype(jnp.bfloat16)
    dq = jnp.dot(ds, key, preferred_element_type=jnp.float32) * inv_root
    unstack(dq_ref, dq.astype(jnp.bfloat16))
    dv = tn(p_low, do)
    dk = tn(ds, q) * inv_root
    own_grad[:, pl.ds(at_key, HEAD_DIM)] = dk[:block]
    own_grad[:, pl.ds(at_value, HEAD_DIM)] = dv[:block]
    for k in range(1, count):
        piece = slice(k * block, (k + 1) * block)
        for at, grad in ((at_key, dk), (at_value, dv)):
            sent = grad[piece].astype(jnp.bfloat16)
            if opening:
                sent = jnp.where(place[0] >= k, sent, cols[k - 1][:, pl.ds(at, HEAD_DIM)])
            grads[k - 1][:, pl.ds(at, HEAD_DIM)] = sent


def attend(place, q, do, pairs, part, cols, before):
    block, width = q.shape
    count = len(pairs)
    steps = KV_HEADS // PARTS
    opening = not before

    def at_part(g, place):
        return (0, (place[3] if part == 0 else 1 - place[3]) * steps + g)

    wide = pl.BlockSpec((block, GROUP * HEAD_DIM), at_part)
    both = 2 * KV_WIDTH // PARTS
    rows = jax.ShapeDtypeStruct((block, width), jnp.bfloat16)
    own = jax.ShapeDtypeStruct((block, both), jnp.float32)
    sent = pltpu.VMEM((block, both), jnp.bfloat16)
    operands = [place, q, do, *near(*pairs)]
    in_specs = [wide, wide] + [vspec()] * count
    if opening:
        operands += near(*cols)
        in_specs += [vspec()] * (count - 1)
        out_specs = [wide, wide, vspec()] + [vspec()] * count
        out_shape = [rows, rows, jax.ShapeDtypeStruct((block, count * block), jnp.float32)]
        aliases = {}
    else:
        context, query_grad, mask = before
        aliases = {len(operands) + 1: 0, len(operands) + 2: 1}
        operands += [mask, context, query_grad]
        in_specs += [vspec()] + [pl.BlockSpec(memory_space=pl.ANY)] * 2
        out_specs = [wide, wide] + [vspec()] * count
        out_shape = [rows, rows]
    outs = pl.pallas_call(
        functools.partial(attend_kernel, count=count, block=block, opening=opening),
        grid_spec=pltpu.PrefetchScalarGridSpec(
            num_scalar_prefetch=1, grid=(steps,), in_specs=in_specs, out_specs=out_specs
        ),
        out_shape=out_shape + [sent] * (count - 1) + [own],
        input_output_aliases=aliases,
        compiler_params=params(4 + 3 * count, dimension_semantics=("arbitrary",)),
        name="attend",
    )(*operands)
    return outs[: len(outs) - count], outs[len(outs) - count : -1], outs[-1]


def input_grad_kernel(place, *refs, count, rows):
    grads = refs[:PARTS]
    own = refs[PARTS : 3 * PARTS]
    late, (out, fa, fb) = refs[3 * PARTS : 5 * PARTS], refs[5 * PARTS :]
    half = KV_WIDTH // PARTS
    for part in range(PARTS):
        assemble(fa, own[2 * part], own[2 * part + 1], place, count, rows, part * half)
        assemble(fb, late[2 * part], late[2 * part + 1], place, count, rows, part * half)
    even = place[2] == 0
    gk = jnp.concatenate([g[:, :half] for g in grads], axis=1)
    gv = jnp.concatenate([g[:, half:] for g in grads], axis=1)
    ga = jnp.where(even, gk, gv)
    gb = jnp.where(even, gv, gk)
    out[...] = (nt(ga, fa[...]) + nt(gb, fb[...])).astype(jnp.bfloat16)


def input_grad_of(place, grads, own, late, count, rows):
    full = pltpu.VMEM((2 * count * rows, KV_WIDTH), jnp.bfloat16)
    operands = [*grads, *own, *late]
    return pl.pallas_call(
        functools.partial(input_grad_kernel, count=count, rows=rows),
        in_specs=[sspec()] + [vspec()] * len(operands),
        out_specs=vspec(),
        out_shape=jax.ShapeDtypeStruct((grads[0].shape[0], 2 * count * rows), jnp.bfloat16),
        scratch_shapes=[full, full],
        compiler_params=params(),
        name="input_grad",
    )(place, *near(*operands))


def turn_kernel(place, here, *refs, count, rows):
    wrapped, returned, out = refs[: count - 1], refs[count - 1 : 2 * count - 2], refs[-1]
    block = here.shape[0]
    for k in range(count):
        if k == 0:
            got = here[...]
        else:
            got = jnp.where(place[0] >= k, returned[count - k - 1][...], wrapped[k - 1][:block, :])
        for core in range(2):
            at = (2 * k + core) * block
            out[:, at : at + block] = got[:, core * rows : (core + 1) * rows].T


def turn(place, here, wrapped, returned, rows):
    count = len(wrapped) + 1
    return pl.pallas_call(
        functools.partial(turn_kernel, count=count, rows=rows),
        in_specs=[sspec()] + [vspec()] * (2 * count - 1),
        out_specs=vspec(),
        out_shape=pltpu.VMEM((rows, 2 * count * here.shape[0]), here.dtype),
        compiler_params=params(),
        name="turn",
    )(place, *near(here, *wrapped, *returned))


def weight_grad_kernel(x_turned, g_own, g_other, out, *, count):
    size = g_own.shape[0] // count
    pieces = []
    for k in range(count):
        pieces += [g_own[k * size : (k + 1) * size, :], g_other[k * size : (k + 1) * size, :]]
    grads = jnp.concatenate(pieces, axis=0)
    out[...] = jnp.dot(x_turned[...], grads, preferred_element_type=jnp.float32).astype(jnp.bfloat16)


def weight_grad_of(x_turned, g_own, g_other, count):
    return pl.pallas_call(
        functools.partial(weight_grad_kernel, count=count),
        in_specs=[vspec()] * 3,
        out_specs=vspec(),
        out_shape=pltpu.VMEM((x_turned.shape[0], g_own.shape[1]), jnp.bfloat16),
        compiler_params=params(),
        name="weight_grad",
    )(*near(x_turned, g_own, g_other))


def finish_kernel(place, *refs):
    pairs, outs = refs[:-2], refs[-2:]
    half = KV_WIDTH // PARTS
    for part in range(PARTS):
        a, b = pairs[2 * part], pairs[2 * part + 1]
        grad = (a[...].astype(jnp.float32) + b[...].astype(jnp.float32)).astype(jnp.bfloat16)
        left = pl.multiple_of((place[3] if part == 0 else 1 - place[3]) * half, half)
        outs[0][:, pl.ds(left, half)] = grad[:, :half]
        outs[1][:, pl.ds(left, half)] = grad[:, half:]


def finish(place, *partials):
    out = jax.ShapeDtypeStruct((partials[0].shape[0], KV_WIDTH), jnp.bfloat16)
    return pl.pallas_call(
        finish_kernel,
        in_specs=[sspec()] + [vspec()] * len(partials),
        out_specs=[vspec()] * 2,
        out_shape=[out, out],
        compiler_params=params(),
        name="finish",
    )(place, *near(*partials))


def body(activations, queries, key_weight, value_weight, segment_ids, out_grad):
    inputs = activations[0]
    block = inputs.shape[0]
    rows = key_weight.shape[0]
    n = lax.axis_size("seq")
    reps = lax.axis_size("rep")
    z, c = lax.axis_index("seq"), lax.axis_index("fsdp")
    odd = lax.rem(lax.axis_index("rep"), 2)
    turned = lax.rem(lax.axis_index("groups"), 2)
    place = jnp.stack([z, c, odd, turned]).astype(jnp.int32)
    shifts = range(1, n)
    cut_at = KV_WIDTH // PARTS

    def around(x, k):
        return lax.ppermute(x, "seq", [(i, (i + k) % n) for i in range(n)])

    def up(x, k):
        return lax.ppermute(x, "seq", [(i, i + k) for i in range(n - k)])

    def down(x, k):
        return lax.ppermute(x, "seq", [(i, i - k) for i in range(k, n)])

    def pairwise(x, axis):
        return lax.ppermute(x, axis, [(j, j ^ 1) for j in range(lax.axis_size(axis))])

    def partner(x):
        return pairwise(x, "rep")

    def core(x):
        return pairwise(x, "fsdp")

    half = jnp.where(odd == 0, key_weight, value_weight)
    half = lax.dynamic_slice_in_dim(half, turned * cut_at, cut_at, 1)
    gathered = [half] + [around(half, k) for k in shifts]
    x_next = partner(inputs)
    x_for = cut(place, inputs, core(inputs), n, rows)
    gathered, x_next, x_for = lax.optimization_barrier((gathered, x_next, x_for))
    w_own = [jnp.concatenate(gathered, axis=0)]
    w_other = [core(w_own[0])]
    w_across = pairwise(w_own[0], "groups")

    own, other = project(place, segment_ids, inputs, x_next, w_own[0], w_other[0], n, rows)
    pair, loads = pack(place, own, partner(other), x_for[1:])
    carried = [around(x, k) for k, x in zip(shifts, loads)]
    w_across, _ = lax.optimization_barrier((w_across, loads[0]))
    w_own.append(w_across)
    w_other.append(core(w_across))
    own_2, other_2 = project(place, segment_ids, inputs, x_next, w_own[1], w_other[1], n, rows)
    mate_2, _ = lax.optimization_barrier((partner(other_2), carried))
    pair_2 = jnp.concatenate([own_2[:block], mate_2], axis=1)
    ups = [up(pair_2, k) for k in shifts]

    w_late, _ = lax.optimization_barrier((w_own, carried[0]))
    b_own = [partner(w) for w in w_late]
    queries, out_grad = queries[0], out_grad[0]
    before, sent_a, own_a = attend(
        place, queries, out_grad, [pair] + carried, 0, x_for[:0:-1], []
    )
    returned = [around(x, n - k) for k, x in zip(shifts, sent_a)]
    before, sent_b, own_b = attend(place, queries, out_grad, [pair_2] + ups, 1, [], before)
    back_b = [down(x, k) for k, x in zip(shifts, sent_b)]
    back_b, b_own = lax.optimization_barrier((back_b, b_own))
    b_other = [core(b) for b in b_own]
    returned, _ = lax.optimization_barrier((returned, sent_b))
    back_a = [jnp.where(z + k < n, x, jnp.zeros_like(x)) for k, x in zip(shifts, returned)]
    sums = []
    for total, back in ((own_a, back_a), (own_b, back_b)):
        for x in back:
            total = total + x.astype(jnp.float32)
        sums.append(total.astype(jnp.bfloat16))
    context, query_grad = before[:2]
    x_turned = turn(place, x_for[0], carried, returned, rows)

    partials = []
    for part in range(PARTS):
        pieces = [sums[part]] + [around(sums[part], k) for k in shifts]
        if part == 0:
            pieces, _ = lax.optimization_barrier((pieces, sums[1]))
        else:
            pieces, partials = lax.optimization_barrier((pieces, partials))
        g_own = jnp.concatenate(pieces, axis=0)
        partials.append(weight_grad_of(x_turned, g_own, core(g_own), n))
    sums, _ = lax.optimization_barrier((sums, partials[-1]))
    own_weights = [w_own[0], w_other[0], w_own[1], w_other[1]]
    input_grad = input_grad_of(place, sums, own_weights, [b_own[0], b_other[0], b_own[1], b_other[1]], n, rows)
    if reps == 2:
        others = [partner(p) for p in partials]
        others, input_grad = lax.optimization_barrier((others, input_grad))
        grads = finish(place, *[x for p in zip(partials, others) for x in p])
    else:
        totals = [lax.psum(p.astype(jnp.float32), "rep").astype(jnp.bfloat16) for p in partials]
        grads = finish(place, *[x for p in totals for x in (p, jnp.zeros_like(p))])
    return context[None], query_grad[None], input_grad[None], grads[0], grads[1]


def solution(mesh):
    return jax.shard_map(
        body,
        mesh=mesh,
        in_specs=(
            P(("groups", "rep", "fsdp"), "seq", None),
            P(("groups", "rep", "fsdp"), "seq", None),
            P(("seq", "fsdp"), None),
            P(("seq", "fsdp"), None),
            P(("groups", "rep", "fsdp"), "seq"),
            P(("groups", "rep", "fsdp"), "seq", None),
        ),
        out_specs=(
            P(("groups", "rep", "fsdp"), "seq", None),
            P(("groups", "rep", "fsdp"), "seq", None),
            P(("groups", "rep", "fsdp"), "seq", None),
            P(("groups", "seq", "fsdp"), None),
            P(("groups", "seq", "fsdp"), None),
        ),
        check_vma=False,
    )
```

time: 143 us -> 134 us (0.937)
  Pallas kernels: 30.6 us -> 19.8 us
  waiting for transfers between devices: 43.8 us -> 52 us
  starting transfers between devices: 53.5 us -> 49.2 us
  other arithmetic: 3.77 us -> 2.29 us
    ppermute x10 -> x15, waiting for transfers between devices: 8.13 us -> 19.3 us  [pairwise(): lax.ppermute(x, axis, [(j, j ^ 1) for j in range(lax.axis_size(axis))])]
    ppermute x15, waiting for transfers between devices: 30.9 us -> 21.7 us  [around(): return lax.ppermute(x, 'seq', [(i, (i + k) % n) for i in range(n)])]
    ppermute x15, starting transfers between devices: 34 us -> 25.2 us  [around(): return lax.ppermute(x, 'seq', [(i, (i + k) % n) for i in range(n)])]
    ppermute x3, waiting for transfers between devices: 4.75 us -> 10.9 us  [down(): return lax.ppermute(x, 'seq', [(i, i - k) for i in range(k, n)])]
    pallas_call x2, Pallas kernels: 5.03 us -> 0.86 us  [weight_grad_of(): pl.pallas_call(functools.partial(weight_grad_kernel, count=count), in_spe...]
    ppermute x3, starting transfers between devices: 7.08 us -> 10.1 us  [up(): return lax.ppermute(x, 'seq', [(i, i + k) for i in range(n - k)])]
    pallas_call x2, Pallas kernels: 11 us -> 9.2 us  [attend(): pl.pallas_call(functools.partial(attend_kernel, count=count, block=block,...]
    ppermute x10 -> x15, starting transfers between devices: 8.46 us -> 10 us  [pairwise(): lax.ppermute(x, axis, [(j, j ^ 1) for j in range(lax.axis_size(axis))])]
  transfers between devices with their start and end apart: 31 -> 36, of which waited for: 12 -> 15; matrix products, arithmetic and copies ran while one was open for 3% -> 2% of each run, Pallas kernels for 16% -> 14%
where the time goes in v4:
time: 134 us; the launch traced here: 133 us
  waiting for transfers between devices  52 us (39%)
  starting transfers between devices  49.2 us (37%)
  Pallas kernels  19.8 us (15%)
  local copies, waits for them, and re-layouts  9.16 us (7%)
  other arithmetic  2.29 us (2%)
    ppermute x15, starting transfers between devices, around(): return lax.ppermute(x, 'seq', [(i, (i + k) % n) for i in range(n)])  25.2 us
    ppermute x15, waiting for transfers between devices, around(): return lax.ppermute(x, 'seq', [(i, (i + k) % n) for i in range(n)])  21.7 us
    ppermute x15, waiting for transfers between devices, pairwise(): lax.ppermute(x, axis, [(j, j ^ 1) for j in range(lax.axis_size(axis))])  19.3 us
    ppermute x3, waiting for transfers between devices, down(): return lax.ppermute(x, 'seq', [(i, i - k) for i in range(k, n)])  10.9 us
    ppermute x3, starting transfers between devices, up(): return lax.ppermute(x, 'seq', [(i, i + k) for i in range(n - k)])  10.1 us
    ppermute x15, starting transfers between devices, pairwise(): lax.ppermute(x, axis, [(j, j ^ 1) for j in range(lax.axis_size(axis))])  10 us
    pallas_call x2, Pallas kernels, attend(): pl.pallas_call(functools.partial(attend_kernel, count=count, block=block,...  9.2 us
    unnamed x55, local copies, waits for them, and re-layouts  9.12 us
  transfers between devices with their start and end apart: 36, of which 15 were waited for; matrix products, arithmetic and copies ran while one was open for 2% of the time, Pallas kernels for 14%

profile of v4, /device:TPU:0, one launch (start us, length us, event | category | flops | bytes accessed | tf_op | source)
XLA Modules:
  0.0 133.4 jit_solution(9884992680304155558)
XLA Ops:
  0.6 0.5 collective-permute-start.4
  1.1 2.6 %collective-permute-start.3 = (bf16[128,2048]{1,0:T(8,128)(2,1)}, bf16[128,2048]{1,0:T(8,128)(2,1)S(1)}, u32[]{:S(2)}, u32[]{:S(2)}) collective-permute-start(bf16[128,2048]{1,0:T(8,128)(2,1)} %bitcast.11), channel_id=1, source_target_pairs={{0,2},{2,0},{1,3},{3,1},{4,6},{6,4},{5,7},{7,5},{8,10},{10,8},{9,1... | collective-permute-start | bytes 1572872 | tf_op jit(solution)/shard_map/ppermute | solution.py:377
  3.7 1.0 dynamic-slice_select_fusion
  4.7 1.6 %collective-permute-start = (bf16[256,256]{1,0:T(8,128)(2,1)S(1)}, bf16[256,256]{1,0:T(8,128)(2,1)S(1)}, u32[]{:S(2)}, u32[]{:S(2)}) collective-permute-start(bf16[256,256]{1,0:T(8,128)(2,1)S(1)} %dynamic-slice_select_fusion), channel_id=1, source_target_pairs={{0,4},{4,8},{8,12},{12,0},{1,5},{5,9},{9,13},{13,1},{2,6},{6,10},{... | collective-permute-start | bytes 393224 | tf_op jit(solution)/shard_map/ppermute | solution.py:368
  6.3 2.6 %collective-permute-start.1 = (bf16[256,256]{1,0:T(8,128)(2,1)S(1)}, bf16[256,256]{1,0:T(8,128)(2,1)S(1)}, u32[]{:S(2)}, u32[]{:S(2)}) collective-permute-start(bf16[256,256]{1,0:T(8,128)(2,1)S(1)} %dynamic-slice_select_fusion), channel_id=1, source_target_pairs={{0,8},{4,12},{8,0},{12,4},{1,9},{5,13},{9,1},{13,5},{2,10},{6,14},... | collective-permute-start | bytes 393224 | tf_op jit(solution)/shard_map/ppermute | solution.py:368
  8.9 1.3 %collective-permute-start.2 = (bf16[256,256]{1,0:T(8,128)(2,1)S(1)}, bf16[256,256]{1,0:T(8,128)(2,1)S(1)}, u32[]{:S(2)}, u32[]{:S(2)}) collective-permute-start(bf16[256,256]{1,0:T(8,128)(2,1)S(1)} %dynamic-slice_select_fusion), channel_id=1, source_target_pairs={{0,12},{4,0},{8,4},{12,8},{1,13},{5,1},{9,5},{13,9},{2,14},{6,2},{... | collective-permute-start | bytes 393224 | tf_op jit(solution)/shard_map/ppermute | solution.py:368
  10.4 1.0 copy-done
  11.4 0.6 cut.1
  12.0 1.0 collective-permute-done
  13.0 4.9 %collective-permute-done.1 = bf16[256,256]{1,0:T(8,128)(2,1)S(1)} collective-permute-done((bf16[256,256]{1,0:T(8,128)(2,1)S(1)}, bf16[256,256]{1,0:T(8,128)(2,1)S(1)}, u32[]{:S(2)}, u32[]{:S(2)}) %collective-permute-start.1) | collective-permute-done | bytes 131104 | tf_op jit(solution)/shard_map/ppermute | solution.py:368
  18.1 1.6 %collective-permute-start.5 = (bf16[1024,256]{1,0:T(8,128)(2,1)S(1)}, bf16[1024,256]{1,0:T(8,128)(2,1)S(1)}, u32[]{:S(2)}, u32[]{:S(2)}) collective-permute-start(bf16[1024,256]{1,0:T(8,128)(2,1)S(1)} %constant_dynamic-update-slice_fusion.w_own.refs_2_), channel_id=1, source_target_pairs={{0,16},{16,0},{1,17},{17,1},{2,18},{18,2},{3,19},{19,3},{4,20},{20... | collective-permute-start | bytes 1572872 | tf_op jit(solution)/shard_map/ppermute | solution.py:377
  20.0 1.1 project.2
  21.1 0.6 collective-permute-start.7
  21.7 3.7 %collective-permute-done.7.mate = bf16[128,256]{1,0:T(8,128)(2,1)S(1)} collective-permute-done((bf16[128,256]{1,0:T(8,128)(2,1)S(1)}, bf16[128,256]{1,0:T(8,128)(2,1)S(1)}, u32[]{:S(2)}, u32[]{:S(2)}) %collective-permute-start.7) | collective-permute-done | bytes 65568 | tf_op jit(solution)/shard_map/ppermute | solution.py:377
  25.4 0.6 pack.1
  26.0 6.4 %collective-permute-done.5.w_own.refs_4_ = bf16[1024,256]{1,0:T(8,128)(2,1)S(1)} collective-permute-done((bf16[1024,256]{1,0:T(8,128)(2,1)S(1)}, bf16[1024,256]{1,0:T(8,128)(2,1)S(1)}, u32[]{:S(2)}, u32[]{:S(2)}) %collective-permute-start.5) | collective-permute-done | bytes 524320 | tf_op jit(solution)/shard_map/ppermute | solution.py:377
  32.5 3.3 %collective-permute-start.10 = (bf16[144,512]{1,0:T(8,128)(2,1)S(1)}, bf16[144,512]{1,0:T(8,128)(2,1)S(1)}, u32[]{:S(2)}, u32[]{:S(2)}) collective-permute-start(bf16[144,512]{1,0:T(8,128)(2,1)S(1)} %get-tuple-element.81), channel_id=1, source_target_pairs={{0,4},{4,8},{8,12},{12,0},{1,5},{5,9},{9,13},{13,1},{2,6},{6,10},{... | collective-permute-start | bytes 442376 | tf_op jit(solution)/shard_map/ppermute | solution.py:368
  35.7 1.6 %collective-permute-start.11 = (bf16[144,512]{1,0:T(8,128)(2,1)S(1)}, bf16[144,512]{1,0:T(8,128)(2,1)S(1)}, u32[]{:S(2)}, u32[]{:S(2)}) collective-permute-start(bf16[144,512]{1,0:T(8,128)(2,1)S(1)} %get-tuple-element.85), channel_id=1, source_target_pairs={{0,8},{4,12},{8,0},{12,4},{1,9},{5,13},{9,1},{13,5},{2,10},{6,14},... | collective-permute-start | bytes 442376 | tf_op jit(solution)/shard_map/ppermute | solution.py:368
  37.4 0.7 collective-permute-start.12
  38.1 1.1 project.3
  39.2 0.6 collective-permute-start.9
  39.8 1.8 %collective-permute-done.10.refs_1_.refs_0_ = bf16[144,512]{1,0:T(8,128)(2,1)S(1)} collective-permute-done((bf16[144,512]{1,0:T(8,128)(2,1)S(1)}, bf16[144,512]{1,0:T(8,128)(2,1)S(1)}, u32[]{:S(2)}, u32[]{:S(2)}) %collective-permute-start.10) | collective-permute-done | bytes 147488 | tf_op jit(solution)/shard_map/ppermute | solution.py:368
  41.6 0.5 collective-permute-start.19
  42.1 1.5 %collective-permute-start.20 = (bf16[1024,256]{1,0:T(8,128)(2,1)S(1)}, bf16[1024,256]{1,0:T(8,128)(2,1)}, u32[]{:S(2)}, u32[]{:S(2)}) collective-permute-start(bf16[1024,256]{1,0:T(8,128)(2,1)S(1)} %collective-permute-done.5.w_own.refs_4_), channel_id=1, source_target_pairs={{0,2},{2,0},{1,3},{3,1},{4,6},{6,4},{5,7},{7,5},{8,10},{10,8},{9,1... | collective-permute-start | bytes 1572872 | tf_op jit(solution)/shard_map/ppermute | solution.py:377
  43.6 4.1 %collective-permute-done.11.refs_2_.refs_1_ = bf16[144,512]{1,0:T(8,128)(2,1)S(1)} collective-permute-done((bf16[144,512]{1,0:T(8,128)(2,1)S(1)}, bf16[144,512]{1,0:T(8,128)(2,1)S(1)}, u32[]{:S(2)}, u32[]{:S(2)}) %collective-permute-start.11) | collective-permute-done | bytes 147488 | tf_op jit(solution)/shard_map/ppermute | solution.py:368
  47.7 5.6 %collective-permute-start.13 = (bf16[128,512]{1,0:T(8,128)(2,1)S(1)}, bf16[128,512]{1,0:T(8,128)(2,1)S(1)}, u32[]{:S(2)}, u32[]{:S(2)}) collective-permute-start(bf16[128,512]{1,0:T(8,128)(2,1)S(1)} %pad_maximum_fusion.refs_0_), channel_id=1, source_target_pairs={{0,4},{4,8},{8,12},{1,5},{5,9},{9,13},{2,6},{6,10},{10,14},{3,7},{... | collective-permute-start | bytes 393224 | tf_op jit(solution)/shard_map/ppermute | solution.py:371
  53.3 3.2 %collective-permute-start.14 = (bf16[128,512]{1,0:T(8,128)(2,1)S(1)}, bf16[128,512]{1,0:T(8,128)(2,1)S(1)}, u32[]{:S(2)}, u32[]{:S(2)}) collective-permute-start(bf16[128,512]{1,0:T(8,128)(2,1)S(1)} %pad_maximum_fusion.refs_0_), channel_id=1, source_target_pairs={{0,8},{4,12},{1,9},{5,13},{2,10},{6,14},{3,11},{7,15},{16,24},{20,... | collective-permute-start | bytes 393224 | tf_op jit(solution)/shard_map/ppermute | solution.py:371
  56.5 1.3 collective-permute-start.15
  57.8 4.7 %attend.2 = (bf16[128,2048]{1,0:T(8,128)(2,1)}, bf16[128,2048]{1,0:T(8,128)(2,1)}, f32[128,512]{1,0:T(8,128)S(1)}, bf16[128,512]{1,0:T(8,128)(2,1)}, bf16[128,51...) custom-call(s32[4]{0:T(128)S(1)} %pad_add_fusion.place, bf16[128,2048]{1,0:T(8,128)(2,1)S(1)} %bitcast.15, ...), custom_call_target="tpu_custom_call" | custom-call | tf_op jit(solution)/shard_map/attend/pallas_call | solution.py:243
  62.6 0.7 copy-done.10
  63.3 0.7 copy-done.12
  64.0 0.6 copy-done.14
  64.7 0.6 copy-done.16
  65.5 0.7 copy-done.18
  66.2 3.6 %collective-permute-start.26 = (bf16[128,512]{1,0:T(8,128)(2,1)}, bf16[128,512]{1,0:T(8,128)(2,1)}, u32[]{:S(2)}, u32[]{:S(2)}) collective-permute-start(bf16[128,512]{1,0:T(8,128)(2,1)} %get-tuple-element.106), channel_id=1, source_target_pairs={{0,4},{4,8},{8,12},{12,0},{1,5},{5,9},{9,13},{13,1},{2,6},{6,10},{... | collective-permute-start | bytes 393224 | tf_op jit(solution)/shard_map/ppermute | solution.py:368
  69.8 0.9 copy-done.9
  70.7 0.9 copy-done.11
  71.6 0.9 copy-done.15
  72.5 0.9 copy-done.17
  73.4 0.9 copy-done.19
  74.3 4.5 %attend.3 = (bf16[128,2048]{1,0:T(8,128)(2,1)}, bf16[128,2048]{1,0:T(8,128)(2,1)}, bf16[128,512]{1,0:T(8,128)(2,1)S(1)}, bf16[128,512]{1,0:T(8,128)(2,1)S(1)}, b...) custom-call(s32[4]{0:T(128)S(1)} %pad_add_fusion.place, ...), custom_call_target="tpu_custom_call", output_to_operand_aliasing={{0}: (8, {}), {1}: (9, {})} | custom-call | tf_op jit(solution)/shard_map/attend/pallas_call | solution.py:243
  78.8 1.3 collective-permute-start.16
  80.1 1.3 collective-permute-start.17
  81.4 1.3 collective-permute-start.18
  82.7 1.1 add_convert_fusion.refs_0_
  83.9 2.0 %collective-permute-start.27 = (bf16[128,512]{1,0:T(8,128)(2,1)S(1)}, bf16[128,512]{1,0:T(8,128)(2,1)S(1)}, u32[]{:S(2)}, u32[]{:S(2)}) collective-permute-start(bf16[128,512]{1,0:T(8,128)(2,1)S(1)} %add_convert_fusion.refs_0_), channel_id=1, source_target_pairs={{0,4},{4,8},{8,12},{12,0},{1,5},{5,9},{9,13},{13,1},{2,6},{6,10},{... | collective-permute-start | bytes 393224 | tf_op jit(solution)/shard_map/ppermute | solution.py:368
  85.9 3.2 %collective-permute-start.28 = (bf16[128,512]{1,0:T(8,128)(2,1)S(1)}, bf16[128,512]{1,0:T(8,128)(2,1)S(1)}, u32[]{:S(2)}, u32[]{:S(2)}) collective-permute-start(bf16[128,512]{1,0:T(8,128)(2,1)S(1)} %add_convert_fusion.refs_0_), channel_id=1, source_target_pairs={{0,8},{4,12},{8,0},{12,4},{1,9},{5,13},{9,1},{13,5},{2,10},{6,14},... | collective-permute-start | bytes 393224 | tf_op jit(solution)/shard_map/ppermute | solution.py:368
  89.1 0.6 collective-permute-start.29
  89.7 10.9 %collective-permute-done.17 = bf16[128,512]{1,0:T(8,128)(2,1)S(1)} collective-permute-done((bf16[128,512]{1,0:T(8,128)(2,1)S(1)}, bf16[128,512]{1,0:T(8,128)(2,1)S(1)}, u32[]{:S(2)}, u32[]{:S(2)}) %collective-permute-start.17) | collective-permute-done | bytes 131104 | tf_op jit(solution)/shard_map/ppermute | solution.py:374
  100.7 2.7 %collective-permute-done.28 = bf16[128,512]{1,0:T(8,128)(2,1)S(1)} collective-permute-done((bf16[128,512]{1,0:T(8,128)(2,1)S(1)}, bf16[128,512]{1,0:T(8,128)(2,1)S(1)}, u32[]{:S(2)}, u32[]{:S(2)}) %collective-permute-start.28) | collective-permute-done | bytes 131104 | tf_op jit(solution)/shard_map/ppermute | solution.py:368
  103.6 2.0 %collective-permute-start.21 = (bf16[128,512]{1,0:T(8,128)(2,1)S(1)}, bf16[128,512]{1,0:T(8,128)(2,1)S(1)}, u32[]{:S(2)}, u32[]{:S(2)}) collective-permute-start(bf16[128,512]{1,0:T(8,128)(2,1)S(1)} %add_convert_fusion.1.refs_1_), channel_id=1, source_target_pairs={{0,4},{4,8},{8,12},{12,0},{1,5},{5,9},{9,13},{13,1},{2,6},{6,10},{... | collective-permute-start | bytes 393224 | tf_op jit(solution)/shard_map/ppermute | solution.py:368
  105.6 2.5 %collective-permute-start.23 = (bf16[128,512]{1,0:T(8,128)(2,1)S(1)}, bf16[128,512]{1,0:T(8,128)(2,1)S(1)}, u32[]{:S(2)}, u32[]{:S(2)}) collective-permute-start(bf16[128,512]{1,0:T(8,128)(2,1)S(1)} %add_convert_fusion.1.refs_1_), channel_id=1, source_target_pairs={{0,12},{4,0},{8,4},{12,8},{1,13},{5,1},{9,5},{13,9},{2,14},{6,2},{... | collective-permute-start | bytes 393224 | tf_op jit(solution)/shard_map/ppermute | solution.py:368
  108.1 1.2 turn.1.x_turned
  109.8 2.1 %collective-permute-done.21 = bf16[128,512]{1,0:T(8,128)(2,1)S(1)} collective-permute-done((bf16[128,512]{1,0:T(8,128)(2,1)S(1)}, bf16[128,512]{1,0:T(8,128)(2,1)S(1)}, u32[]{:S(2)}, u32[]{:S(2)}) %collective-permute-start.21) | collective-permute-done | bytes 131104 | tf_op jit(solution)/shard_map/ppermute | solution.py:368
  111.9 5.1 %collective-permute-done.22 = bf16[128,512]{1,0:T(8,128)(2,1)S(1)} collective-permute-done((bf16[128,512]{1,0:T(8,128)(2,1)S(1)}, bf16[128,512]{1,0:T(8,128)(2,1)S(1)}, u32[]{:S(2)}, u32[]{:S(2)}) %collective-permute-start.22) | collective-permute-done | bytes 131104 | tf_op jit(solution)/shard_map/ppermute | solution.py:368
  117.2 0.5 collective-permute-start.34
  117.7 0.5 collective-permute-start.31
  118.3 0.8 collective-permute-done.32.g_other
  119.5 0.8 collective-permute-start.33
  120.3 0.5 collective-permute-done.35.refs_9_
  120.8 3.7 %input_grad.1 = bf16[128,2048]{1,0:T(8,128)(2,1)} custom-call(s32[4]{0:T(128)S(1)} %pad_add_fusion.place, bf16[128,512]{1,0:T(8,128)(2,1)S(1)} %add_convert_fusion.refs_0_, bf16[128,512]{1,0:T(8,128)(2,1)S(1)} %add_convert_fusion.1.refs_1_, bf16[1024,256]{1,0:T(8,128)(2,1)S(1)} %constant_dynamic-update-slice_fusion.w_own.refs_2_, ...), custom_call_target="tpu_custom_call" | custom-call | tf_op jit(solution)/shard_map/input_grad/pallas_call | solution.py:275
  124.5 2.4 %collective-permute-done.31.refs_1_ = bf16[256,512]{1,0:T(8,128)(2,1)S(1)} collective-permute-done((bf16[256,512]{1,0:T(8,128)(2,1)S(1)}, bf16[256,512]{1,0:T(8,128)(2,1)S(1)}, u32[]{:S(2)}, u32[]{:S(2)}) %collective-permute-start.31) | collective-permute-done | bytes 262176 | tf_op jit(solution)/shard_map/ppermute | solution.py:377
  126.8 5.2 %collective-permute-done.33.refs_3_ = bf16[256,512]{1,0:T(8,128)(2,1)S(1)} collective-permute-done((bf16[256,512]{1,0:T(8,128)(2,1)S(1)}, bf16[256,512]{1,0:T(8,128)(2,1)S(1)}, u32[]{:S(2)}, u32[]{:S(2)}) %collective-permute-start.33) | collective-permute-done | bytes 262176 | tf_op jit(solution)/shard_map/ppermute | solution.py:377
  132.0 1.4 %finish.1 = (bf16[256,512]{1,0:T(8,128)(2,1)}, bf16[256,512]{1,0:T(8,128)(2,1)}) custom-call(s32[4]{0:T(128)S(1)} %pad_add_fusion.place, bf16[256,512]{1,0:T(8,128)(2,1)S(1)} %weight_grad.2.refs_0_, bf16[256,512]{1,0:T(8,128)(2,1)S(1)} %collective-permute-done.31.refs_1_, bf16[256,512]{1,0:T(8,128)(2,1)S(1)} %weight_grad.3.refs_2_, ...), custom_call_target="tpu_custom_call" | custom-call | tf_op jit(solution)/shard_map/finish/pallas_call | solution.py:344
  (83 shorter events, 2.1 us)
Async XLA Ops:
  0.6 9.7 %collective-permute-start.4 = (bf16[128,2048]{1,0:T(8,128)(2,1)}, bf16[128,2048]{1,0:T(8,128)(2,1)S(1)}, u32[]{:S(2)}, u32[]{:S(2)}) collective-permute-start(bf16[128,2048]{1,0:T(8,128)(2,1)} %bitcast.10), channel_id=1, source_target_pairs={{0,1},{1,0},{2,3},{3,2},{4,5},{5,4},{6,7},{7,6},{8,9},{9,8},{10,11... | collective-permute-start | bytes 1572872 | tf_op jit(solution)/shard_map/ppermute | solution.py:377
  1.1 16.8 %collective-permute-start.3 = (bf16[128,2048]{1,0:T(8,128)(2,1)}, bf16[128,2048]{1,0:T(8,128)(2,1)S(1)}, u32[]{:S(2)}, u32[]{:S(2)}) collective-permute-start(bf16[128,2048]{1,0:T(8,128)(2,1)} %bitcast.11), channel_id=1, source_target_pairs={{0,2},{2,0},{1,3},{3,1},{4,6},{6,4},{5,7},{7,5},{8,10},{10,8},{9,1... | collective-permute-start | bytes 1572872 | tf_op jit(solution)/shard_map/ppermute | solution.py:377
  4.7 8.3 %collective-permute-start = (bf16[256,256]{1,0:T(8,128)(2,1)S(1)}, bf16[256,256]{1,0:T(8,128)(2,1)S(1)}, u32[]{:S(2)}, u32[]{:S(2)}) collective-permute-start(bf16[256,256]{1,0:T(8,128)(2,1)S(1)} %dynamic-slice_select_fusion), channel_id=1, source_target_pairs={{0,4},{4,8},{8,12},{12,0},{1,5},{5,9},{9,13},{13,1},{2,6},{6,10},{... | collective-permute-start | bytes 393224 | tf_op jit(solution)/shard_map/ppermute | solution.py:368
  6.3 11.6 %collective-permute-start.1 = (bf16[256,256]{1,0:T(8,128)(2,1)S(1)}, bf16[256,256]{1,0:T(8,128)(2,1)S(1)}, u32[]{:S(2)}, u32[]{:S(2)}) collective-permute-start(bf16[256,256]{1,0:T(8,128)(2,1)S(1)} %dynamic-slice_select_fusion), channel_id=1, source_target_pairs={{0,8},{4,12},{8,0},{12,4},{1,9},{5,13},{9,1},{13,5},{2,10},{6,14},... | collective-permute-start | bytes 393224 | tf_op jit(solution)/shard_map/ppermute | solution.py:368
  8.9 9.0 %collective-permute-start.2 = (bf16[256,256]{1,0:T(8,128)(2,1)S(1)}, bf16[256,256]{1,0:T(8,128)(2,1)S(1)}, u32[]{:S(2)}, u32[]{:S(2)}) collective-permute-start(bf16[256,256]{1,0:T(8,128)(2,1)S(1)} %dynamic-slice_select_fusion), channel_id=1, source_target_pairs={{0,12},{4,0},{8,4},{12,8},{1,13},{5,1},{9,5},{13,9},{2,14},{6,2},{... | collective-permute-start | bytes 393224 | tf_op jit(solution)/shard_map/ppermute | solution.py:368
  10.4 1.0 copy-start
  12.0 5.9 %copy-start.20 = (bf16[128,512]{1,0:T(8,128)(2,1)}, bf16[128,512]{1,0:T(8,128)(2,1)S(1)}, u32[]{:S(2)}) copy-start(bf16[128,512]{1,0:T(8,128)(2,1)S(1)} %get-tuple-element.103.here) | copy-start | bytes 393220
  17.9 2.1 %copy-start.4 = (bf16[128,2048]{1,0:T(8,128)(2,1)}, bf16[128,2048]{1,0:T(8,128)(2,1)S(1)}, u32[]{:S(2)}) copy-start(bf16[128,2048]{1,0:T(8,128)(2,1)S(1)} %collective-permute-done.3.x_next) | copy-start | bytes 1572868
  17.9 2.1 %copy-start.1 = (bf16[1,128,2048]{2,1,0:T(8,128)(2,1)S(1)}, bf16[1,128,2048]{2,1,0:T(8,128)(2,1)}, u32[]{:S(2)}) copy-start(bf16[1,128,2048]{2,1,0:T(8,128)(2,1)} %param.6) | copy-start | bytes 1572868
  18.0 2.0 %copy-start.22 = (s32[1,128]{1,0:T(1,128)S(1)}, s32[1,128]{1,0:T(1,128)}, u32[]{:S(2)}) copy-start(s32[1,128]{1,0:T(1,128)} %seg.3) | copy-start | bytes 1540
  18.0 2.0 %collective-permute-start.6 = (bf16[1024,256]{1,0:T(8,128)(2,1)S(1)}, bf16[1024,256]{1,0:T(8,128)(2,1)S(1)}, u32[]{:S(2)}, u32[]{:S(2)}) collective-permute-start(bf16[1024,256]{1,0:T(8,128)(2,1)S(1)} %constant_dynamic-update-slice_fusion.w_own.refs_2_), channel_id=1, source_target_pairs={{0,1},{1,0},{2,3},{3,2},{4,5},{5,4},{6,7},{7,6},{8,9},{9,8},{10,11... | collective-permute-start | bytes 1572872 | tf_op jit(solution)/shard_map/ppermute | solution.py:377
  18.1 14.3 %collective-permute-start.5 = (bf16[1024,256]{1,0:T(8,128)(2,1)S(1)}, bf16[1024,256]{1,0:T(8,128)(2,1)S(1)}, u32[]{:S(2)}, u32[]{:S(2)}) collective-permute-start(bf16[1024,256]{1,0:T(8,128)(2,1)S(1)} %constant_dynamic-update-slice_fusion.w_own.refs_2_), channel_id=1, source_target_pairs={{0,16},{16,0},{1,17},{17,1},{2,18},{18,2},{3,19},{19,3},{4,20},{20... | collective-permute-start | bytes 1572872 | tf_op jit(solution)/shard_map/ppermute | solution.py:377
  21.1 17.0 %copy-start.5 = (bf16[128,2048]{1,0:T(8,128)(2,1)S(1)}, bf16[128,2048]{1,0:T(8,128)(2,1)}, u32[]{:S(2)}) copy-start(bf16[128,2048]{1,0:T(8,128)(2,1)} %copy-done.4) | copy-start | bytes 1572868
  21.1 4.3 %collective-permute-start.7 = (bf16[128,256]{1,0:T(8,128)(2,1)S(1)}, bf16[128,256]{1,0:T(8,128)(2,1)S(1)}, u32[]{:S(2)}, u32[]{:S(2)}) collective-permute-start(bf16[128,256]{1,0:T(8,128)(2,1)S(1)} %get-tuple-element.77), channel_id=1, source_target_pairs={{0,2},{2,0},{1,3},{3,1},{4,6},{6,4},{5,7},{7,5},{8,10},{10,8},{9,1... | collective-permute-start | bytes 196616 | tf_op jit(solution)/shard_map/ppermute | solution.py:377
  32.5 5.6 %collective-permute-start.8 = (bf16[1024,256]{1,0:T(8,128)(2,1)S(1)}, bf16[1024,256]{1,0:T(8,128)(2,1)S(1)}, u32[]{:S(2)}, u32[]{:S(2)}) collective-permute-start(bf16[1024,256]{1,0:T(8,128)(2,1)S(1)} %collective-permute-done.5.w_own.refs_4_), channel_id=1, source_target_pairs={{0,1},{1,0},{2,3},{3,2},{4,5},{5,4},{6,7},{7,6},{8,9},{9,8},{10,11... | collective-permute-start | bytes 1572872 | tf_op jit(solution)/shard_map/ppermute | solution.py:377
  32.5 9.1 %collective-permute-start.10 = (bf16[144,512]{1,0:T(8,128)(2,1)S(1)}, bf16[144,512]{1,0:T(8,128)(2,1)S(1)}, u32[]{:S(2)}, u32[]{:S(2)}) collective-permute-start(bf16[144,512]{1,0:T(8,128)(2,1)S(1)} %get-tuple-element.81), channel_id=1, source_target_pairs={{0,4},{4,8},{8,12},{12,0},{1,5},{5,9},{9,13},{13,1},{2,6},{6,10},{... | collective-permute-start | bytes 442376 | tf_op jit(solution)/shard_map/ppermute | solution.py:368
  35.7 12.0 %collective-permute-start.11 = (bf16[144,512]{1,0:T(8,128)(2,1)S(1)}, bf16[144,512]{1,0:T(8,128)(2,1)S(1)}, u32[]{:S(2)}, u32[]{:S(2)}) collective-permute-start(bf16[144,512]{1,0:T(8,128)(2,1)S(1)} %get-tuple-element.85), channel_id=1, source_target_pairs={{0,8},{4,12},{8,0},{12,4},{1,9},{5,13},{9,1},{13,5},{2,10},{6,14},... | collective-permute-start | bytes 442376 | tf_op jit(solution)/shard_map/ppermute | solution.py:368
  37.4 10.3 %collective-permute-start.12 = (bf16[144,512]{1,0:T(8,128)(2,1)S(1)}, bf16[144,512]{1,0:T(8,128)(2,1)S(1)}, u32[]{:S(2)}, u32[]{:S(2)}) collective-permute-start(bf16[144,512]{1,0:T(8,128)(2,1)S(1)} %get-tuple-element.86), channel_id=1, source_target_pairs={{0,12},{4,0},{8,4},{12,8},{1,13},{5,1},{9,5},{13,9},{2,14},{6,2},{... | collective-permute-start | bytes 442376 | tf_op jit(solution)/shard_map/ppermute | solution.py:368
  38.1 19.7 %copy-start.2 = (bf16[1,128,2048]{2,1,0:T(8,128)(2,1)S(1)}, bf16[1,128,2048]{2,1,0:T(8,128)(2,1)}, u32[]{:S(2)}) copy-start(bf16[1,128,2048]{2,1,0:T(8,128)(2,1)} %param.7) | copy-start | bytes 1572868
  38.1 19.7 %copy-start.3 = (bf16[1,128,2048]{2,1,0:T(8,128)(2,1)S(1)}, bf16[1,128,2048]{2,1,0:T(8,128)(2,1)}, u32[]{:S(2)}) copy-start(bf16[1,128,2048]{2,1,0:T(8,128)(2,1)} %param.11) | copy-start | bytes 1572868
  39.2 8.5 %collective-permute-start.9 = (bf16[128,256]{1,0:T(8,128)(2,1)S(1)}, bf16[128,256]{1,0:T(8,128)(2,1)S(1)}, u32[]{:S(2)}, u32[]{:S(2)}) collective-permute-start(bf16[128,256]{1,0:T(8,128)(2,1)S(1)} %get-tuple-element.84), channel_id=1, source_target_pairs={{0,2},{2,0},{1,3},{3,1},{4,6},{6,4},{5,7},{7,5},{8,10},{10,8},{9,1... | collective-permute-start | bytes 196616 | tf_op jit(solution)/shard_map/ppermute | solution.py:377
  41.6 42.3 %collective-permute-start.19 = (bf16[1024,256]{1,0:T(8,128)(2,1)S(1)}, bf16[1024,256]{1,0:T(8,128)(2,1)}, u32[]{:S(2)}, u32[]{:S(2)}) collective-permute-start(bf16[1024,256]{1,0:T(8,128)(2,1)S(1)} %constant_dynamic-update-slice_fusion.w_own.refs_2_), channel_id=1, source_target_pairs={{0,2},{2,0},{1,3},{3,1},{4,6},{6,4},{5,7},{7,5},{8,10},{10,8},{9,1... | collective-permute-start | bytes 1572872 | tf_op jit(solution)/shard_map/ppermute | solution.py:377
  42.1 43.8 %collective-permute-start.20 = (bf16[1024,256]{1,0:T(8,128)(2,1)S(1)}, bf16[1024,256]{1,0:T(8,128)(2,1)}, u32[]{:S(2)}, u32[]{:S(2)}) collective-permute-start(bf16[1024,256]{1,0:T(8,128)(2,1)S(1)} %collective-permute-done.5.w_own.refs_4_), channel_id=1, source_target_pairs={{0,2},{2,0},{1,3},{3,1},{4,6},{6,4},{5,7},{7,5},{8,10},{10,8},{9,1... | collective-permute-start | bytes 1572872 | tf_op jit(solution)/shard_map/ppermute | solution.py:377
  47.7 14.9 %copy-start.6 = (bf16[144,512]{1,0:T(8,128)(2,1)}, bf16[144,512]{1,0:T(8,128)(2,1)S(1)}, u32[]{:S(2)}) copy-start(bf16[144,512]{1,0:T(8,128)(2,1)S(1)} %collective-permute-done.12.refs_3_.refs_2_) | copy-start | bytes 442372
  47.7 14.8 %copy-start.8 = (bf16[128,512]{1,0:T(8,128)(2,1)}, bf16[128,512]{1,0:T(8,128)(2,1)S(1)}, u32[]{:S(2)}) copy-start(bf16[128,512]{1,0:T(8,128)(2,1)S(1)} %pad_maximum_fusion.refs_0_) | copy-start | bytes 393220
  47.7 16.3 %collective-permute-start.13 = (bf16[128,512]{1,0:T(8,128)(2,1)S(1)}, bf16[128,512]{1,0:T(8,128)(2,1)S(1)}, u32[]{:S(2)}, u32[]{:S(2)}) collective-permute-start(bf16[128,512]{1,0:T(8,128)(2,1)S(1)} %pad_maximum_fusion.refs_0_), channel_id=1, source_target_pairs={{0,4},{4,8},{8,12},{1,5},{5,9},{9,13},{2,6},{6,10},{10,14},{3,7},{... | collective-permute-start | bytes 393224 | tf_op jit(solution)/shard_map/ppermute | solution.py:371
  53.3 11.3 %collective-permute-start.14 = (bf16[128,512]{1,0:T(8,128)(2,1)S(1)}, bf16[128,512]{1,0:T(8,128)(2,1)S(1)}, u32[]{:S(2)}, u32[]{:S(2)}) collective-permute-start(bf16[128,512]{1,0:T(8,128)(2,1)S(1)} %pad_maximum_fusion.refs_0_), channel_id=1, source_target_pairs={{0,8},{4,12},{1,9},{5,13},{2,10},{6,14},{3,11},{7,15},{16,24},{20,... | collective-permute-start | bytes 393224 | tf_op jit(solution)/shard_map/ppermute | solution.py:371
  56.5 9.0 %collective-permute-start.15 = (bf16[128,512]{1,0:T(8,128)(2,1)S(1)}, bf16[128,512]{1,0:T(8,128)(2,1)S(1)}, u32[]{:S(2)}, u32[]{:S(2)}) collective-permute-start(bf16[128,512]{1,0:T(8,128)(2,1)S(1)} %pad_maximum_fusion.refs_0_), channel_id=1, source_target_pairs={{0,12},{1,13},{2,14},{3,15},{16,28},{17,29},{18,30},{19,31}} | collective-permute-start | bytes 393224 | tf_op jit(solution)/shard_map/ppermute | solution.py:371
  62.6 0.7 copy-start.10
  63.3 0.7 copy-start.12
  64.0 0.6 copy-start.14
  64.6 14.2 %collective-permute-start.24 = (bf16[128,512]{1,0:T(8,128)(2,1)}, bf16[128,512]{1,0:T(8,128)(2,1)}, u32[]{:S(2)}, u32[]{:S(2)}) collective-permute-start(bf16[128,512]{1,0:T(8,128)(2,1)} %get-tuple-element.104), channel_id=1, source_target_pairs={{0,12},{4,0},{8,4},{12,8},{1,13},{5,1},{9,5},{13,9},{2,14},{6,2},{... | collective-permute-start | bytes 393224 | tf_op jit(solution)/shard_map/ppermute | solution.py:368
  64.6 0.7 copy-start.16
  65.3 14.8 %collective-permute-start.25 = (bf16[128,512]{1,0:T(8,128)(2,1)}, bf16[128,512]{1,0:T(8,128)(2,1)}, u32[]{:S(2)}, u32[]{:S(2)}) collective-permute-start(bf16[128,512]{1,0:T(8,128)(2,1)} %get-tuple-element.105), channel_id=1, source_target_pairs={{0,8},{4,12},{8,0},{12,4},{1,9},{5,13},{9,1},{13,5},{2,10},{6,14},... | collective-permute-start | bytes 393224 | tf_op jit(solution)/shard_map/ppermute | solution.py:368
  65.5 0.7 copy-start.18
  66.2 15.2 %collective-permute-start.26 = (bf16[128,512]{1,0:T(8,128)(2,1)}, bf16[128,512]{1,0:T(8,128)(2,1)}, u32[]{:S(2)}, u32[]{:S(2)}) collective-permute-start(bf16[128,512]{1,0:T(8,128)(2,1)} %get-tuple-element.106), channel_id=1, source_target_pairs={{0,4},{4,8},{8,12},{12,0},{1,5},{5,9},{9,13},{13,1},{2,6},{6,10},{... | collective-permute-start | bytes 393224 | tf_op jit(solution)/shard_map/ppermute | solution.py:368
  69.8 0.9 copy-start.9
  70.7 0.9 copy-start.11
  71.6 0.9 copy-start.15
  72.5 0.9 copy-start.17
  73.4 0.9 copy-start.19
  74.3 8.4 %copy-start.13 = (f32[128,512]{1,0:T(8,128)S(1)}, f32[128,512]{1,0:T(8,128)}, u32[]{:S(2)}) copy-start(f32[128,512]{1,0:T(8,128)} %copy-done.12) | copy-start | bytes 786436
  78.8 10.3 %collective-permute-start.16 = (bf16[128,512]{1,0:T(8,128)(2,1)S(1)}, bf16[128,512]{1,0:T(8,128)(2,1)S(1)}, u32[]{:S(2)}, u32[]{:S(2)}) collective-permute-start(bf16[128,512]{1,0:T(8,128)(2,1)S(1)} %get-tuple-element.95), channel_id=1, source_target_pairs={{4,0},{8,4},{12,8},{5,1},{9,5},{13,9},{6,2},{10,6},{14,10},{7,3},{... | collective-permute-start | bytes 393224 | tf_op jit(solution)/shard_map/ppermute | solution.py:374
  80.1 20.5 %collective-permute-start.17 = (bf16[128,512]{1,0:T(8,128)(2,1)S(1)}, bf16[128,512]{1,0:T(8,128)(2,1)S(1)}, u32[]{:S(2)}, u32[]{:S(2)}) collective-permute-start(bf16[128,512]{1,0:T(8,128)(2,1)S(1)} %get-tuple-element.96), channel_id=1, source_target_pairs={{8,0},{12,4},{9,1},{13,5},{10,2},{14,6},{11,3},{15,7},{24,16},{28,... | collective-permute-start | bytes 393224 | tf_op jit(solution)/shard_map/ppermute | solution.py:374
  81.4 19.2 %collective-permute-start.18 = (bf16[128,512]{1,0:T(8,128)(2,1)S(1)}, bf16[128,512]{1,0:T(8,128)(2,1)S(1)}, u32[]{:S(2)}, u32[]{:S(2)}) collective-permute-start(bf16[128,512]{1,0:T(8,128)(2,1)S(1)} %get-tuple-element.97), channel_id=1, source_target_pairs={{12,0},{13,1},{14,2},{15,3},{28,16},{29,17},{30,18},{31,19}} | collective-permute-start | bytes 393224 | tf_op jit(solution)/shard_map/ppermute | solution.py:374
  83.9 16.8 %collective-permute-start.27 = (bf16[128,512]{1,0:T(8,128)(2,1)S(1)}, bf16[128,512]{1,0:T(8,128)(2,1)S(1)}, u32[]{:S(2)}, u32[]{:S(2)}) collective-permute-start(bf16[128,512]{1,0:T(8,128)(2,1)S(1)} %add_convert_fusion.refs_0_), channel_id=1, source_target_pairs={{0,4},{4,8},{8,12},{12,0},{1,5},{5,9},{9,13},{13,1},{2,6},{6,10},{... | collective-permute-start | bytes 393224 | tf_op jit(solution)/shard_map/ppermute | solution.py:368
  85.9 17.5 %collective-permute-start.28 = (bf16[128,512]{1,0:T(8,128)(2,1)S(1)}, bf16[128,512]{1,0:T(8,128)(2,1)S(1)}, u32[]{:S(2)}, u32[]{:S(2)}) collective-permute-start(bf16[128,512]{1,0:T(8,128)(2,1)S(1)} %add_convert_fusion.refs_0_), channel_id=1, source_target_pairs={{0,8},{4,12},{8,0},{12,4},{1,9},{5,13},{9,1},{13,5},{2,10},{6,14},... | collective-permute-start | bytes 393224 | tf_op jit(solution)/shard_map/ppermute | solution.py:368
  89.1 14.3 %collective-permute-start.29 = (bf16[128,512]{1,0:T(8,128)(2,1)S(1)}, bf16[128,512]{1,0:T(8,128)(2,1)S(1)}, u32[]{:S(2)}, u32[]{:S(2)}) collective-permute-start(bf16[128,512]{1,0:T(8,128)(2,1)S(1)} %add_convert_fusion.refs_0_), channel_id=1, source_target_pairs={{0,12},{4,0},{8,4},{12,8},{1,13},{5,1},{9,5},{13,9},{2,14},{6,2},{... | collective-permute-start | bytes 393224 | tf_op jit(solution)/shard_map/ppermute | solution.py:368
  103.4 4.6 %copy-start.21 = (bf16[128,512]{1,0:T(8,128)(2,1)S(1)}, bf16[128,512]{1,0:T(8,128)(2,1)}, u32[]{:S(2)}) copy-start(bf16[128,512]{1,0:T(8,128)(2,1)} %copy-done.20) | copy-start | bytes 393220
  103.5 4.6 %copy-start.7 = (bf16[144,512]{1,0:T(8,128)(2,1)S(1)}, bf16[144,512]{1,0:T(8,128)(2,1)}, u32[]{:S(2)}) copy-start(bf16[144,512]{1,0:T(8,128)(2,1)} %copy-done.6) | copy-start | bytes 442372
  103.5 5.8 %collective-permute-start.30 = (bf16[512,512]{1,0:T(8,128)(2,1)S(1)}, bf16[512,512]{1,0:T(8,128)(2,1)S(1)}, u32[]{:S(2)}, u32[]{:S(2)}) collective-permute-start(bf16[512,512]{1,0:T(8,128)(2,1)S(1)} %constant_dynamic-update-slice_fusion.4.g_own), channel_id=1, source_target_pairs={{0,1},{1,0},{2,3},{3,2},{4,5},{5,4},{6,7},{7,6},{8,9},{9,8},{10,11... | collective-permute-start | bytes 1572872 | tf_op jit(solution)/shard_map/ppermute | solution.py:377
  103.6 8.3 %collective-permute-start.21 = (bf16[128,512]{1,0:T(8,128)(2,1)S(1)}, bf16[128,512]{1,0:T(8,128)(2,1)S(1)}, u32[]{:S(2)}, u32[]{:S(2)}) collective-permute-start(bf16[128,512]{1,0:T(8,128)(2,1)S(1)} %add_convert_fusion.1.refs_1_), channel_id=1, source_target_pairs={{0,4},{4,8},{8,12},{12,0},{1,5},{5,9},{9,13},{13,1},{2,6},{6,10},{... | collective-permute-start | bytes 393224 | tf_op jit(solution)/shard_map/ppermute | solution.py:368
  105.6 11.4 %collective-permute-start.22 = (bf16[128,512]{1,0:T(8,128)(2,1)S(1)}, bf16[128,512]{1,0:T(8,128)(2,1)S(1)}, u32[]{:S(2)}, u32[]{:S(2)}) collective-permute-start(bf16[128,512]{1,0:T(8,128)(2,1)S(1)} %add_convert_fusion.1.refs_1_), channel_id=1, source_target_pairs={{0,8},{4,12},{8,0},{12,4},{1,9},{5,13},{9,1},{13,5},{2,10},{6,14},... | collective-permute-start | bytes 393224 | tf_op jit(solution)/shard_map/ppermute | solution.py:368
  105.6 11.4 %collective-permute-start.23 = (bf16[128,512]{1,0:T(8,128)(2,1)S(1)}, bf16[128,512]{1,0:T(8,128)(2,1)S(1)}, u32[]{:S(2)}, u32[]{:S(2)}) collective-permute-start(bf16[128,512]{1,0:T(8,128)(2,1)S(1)} %add_convert_fusion.1.refs_1_), channel_id=1, source_target_pairs={{0,12},{4,0},{8,4},{12,8},{1,13},{5,1},{9,5},{13,9},{2,14},{6,2},{... | collective-permute-start | bytes 393224 | tf_op jit(solution)/shard_map/ppermute | solution.py:368
  117.1 2.0 %collective-permute-start.32 = (bf16[512,512]{1,0:T(8,128)(2,1)S(1)}, bf16[512,512]{1,0:T(8,128)(2,1)S(1)}, u32[]{:S(2)}, u32[]{:S(2)}) collective-permute-start(bf16[512,512]{1,0:T(8,128)(2,1)S(1)} %constant_dynamic-update-slice_fusion.8.g_own), channel_id=1, source_target_pairs={{0,1},{1,0},{2,3},{3,2},{4,5},{5,4},{6,7},{7,6},{8,9},{9,8},{10,11... | collective-permute-start | bytes 1572872 | tf_op jit(solution)/shard_map/ppermute | solution.py:377
  117.2 3.1 %collective-permute-start.34 = (bf16[1024,256]{1,0:T(8,128)(2,1)}, bf16[1024,256]{1,0:T(8,128)(2,1)S(1)}, u32[]{:S(2)}, u32[]{:S(2)}) collective-permute-start(bf16[1024,256]{1,0:T(8,128)(2,1)} %collective-permute-done.19.refs_6_), channel_id=1, source_target_pairs={{0,1},{1,0},{2,3},{3,2},{4,5},{5,4},{6,7},{7,6},{8,9},{9,8},{10,11... | collective-permute-start | bytes 1572872 | tf_op jit(solution)/shard_map/ppermute | solution.py:377
  117.7 3.1 %collective-permute-start.35 = (bf16[1024,256]{1,0:T(8,128)(2,1)}, bf16[1024,256]{1,0:T(8,128)(2,1)S(1)}, u32[]{:S(2)}, u32[]{:S(2)}) collective-permute-start(bf16[1024,256]{1,0:T(8,128)(2,1)} %collective-permute-done.20.refs_8_), channel_id=1, source_target_pairs={{0,1},{1,0},{2,3},{3,2},{4,5},{5,4},{6,7},{7,6},{8,9},{9,8},{10,11... | collective-permute-start | bytes 1572872 | tf_op jit(solution)/shard_map/ppermute | solution.py:377
  117.7 9.1 %collective-permute-start.31 = (bf16[256,512]{1,0:T(8,128)(2,1)S(1)}, bf16[256,512]{1,0:T(8,128)(2,1)S(1)}, u32[]{:S(2)}, u32[]{:S(2)}) collective-permute-start(bf16[256,512]{1,0:T(8,128)(2,1)S(1)} %weight_grad.2.refs_0_), channel_id=1, source_target_pairs={{0,2},{2,0},{1,3},{3,1},{4,6},{6,4},{5,7},{7,5},{8,10},{10,8},{9,1... | collective-permute-start | bytes 786440 | tf_op jit(solution)/shard_map/ppermute | solution.py:377
  119.5 12.5 %collective-permute-start.33 = (bf16[256,512]{1,0:T(8,128)(2,1)S(1)}, bf16[256,512]{1,0:T(8,128)(2,1)S(1)}, u32[]{:S(2)}, u32[]{:S(2)}) collective-permute-start(bf16[256,512]{1,0:T(8,128)(2,1)S(1)} %weight_grad.3.refs_2_), channel_id=1, source_target_pairs={{0,2},{2,0},{1,3},{3,1},{4,6},{6,4},{5,7},{7,5},{8,10},{10,8},{9,1... | collective-permute-start | bytes 786440 | tf_op jit(solution)/shard_map/ppermute | solution.py:377

commit v5 on v4

--- a/solution.py
+++ b/solution.py
@@ -17,7 +17,12 @@
 LOG2E = 1.4426950408889634
 MASKED = -1e30
 EXTRA = 16
+LIGHT = pl.CostEstimate(flops=0, transcendentals=0, bytes_accessed=0)
 MIB = 1024 * 1024
+
+
+def far(*xs):
+    return [pltpu.with_memory_space_constraint(x, pltpu.HBM) for x in xs]
 
 
 def params(mib=16, **kw):
@@ -198,8 +203,8 @@
     ds = (p * (nt(do, value) - dots)).astype(jnp.bfloat16)
     dq = jnp.dot(ds, key, preferred_element_type=jnp.float32) * inv_root
     unstack(dq_ref, dq.astype(jnp.bfloat16))
-    dv = tn(p_low, do)
-    dk = tn(ds, q) * inv_root
+    dv = tn(do, p_low).T
+    dk = (tn(q, ds) * inv_root).T
     own_grad[:, pl.ds(at_key, HEAD_DIM)] = dk[:block]
     own_grad[:, pl.ds(at_value, HEAD_DIM)] = dv[:block]
     for k in range(1, count):
@@ -223,20 +228,20 @@
     wide = pl.BlockSpec((block, GROUP * HEAD_DIM), at_part)
     both = 2 * KV_WIDTH // PARTS
     rows = jax.ShapeDtypeStruct((block, width), jnp.bfloat16)
-    own = jax.ShapeDtypeStruct((block, both), jnp.float32)
+    own = pltpu.HBM((block, both), jnp.float32)
     sent = pltpu.VMEM((block, both), jnp.bfloat16)
-    operands = [place, q, do, *near(*pairs)]
+    operands = [place, q, do, *(near(*pairs) if opening else far(*pairs))]
     in_specs = [wide, wide] + [vspec()] * count
     if opening:
         operands += near(*cols)
         in_specs += [vspec()] * (count - 1)
         out_specs = [wide, wide, vspec()] + [vspec()] * count
-        out_shape = [rows, rows, jax.ShapeDtypeStruct((block, count * block), jnp.float32)]
+        out_shape = [rows, rows, pltpu.HBM((block, count * block), jnp.float32)]
         aliases = {}
     else:
         context, query_grad, mask = before
         aliases = {len(operands) + 1: 0, len(operands) + 2: 1}
-        operands += [mask, context, query_grad]
+        operands += [*far(mask), context, query_grad]
         in_specs += [vspec()] + [pl.BlockSpec(memory_space=pl.ANY)] * 2
         out_specs = [wide, wide] + [vspec()] * count
         out_shape = [rows, rows]
@@ -256,11 +261,11 @@
 def input_grad_kernel(place, *refs, count, rows):
     grads = refs[:PARTS]
     own = refs[PARTS : 3 * PARTS]
-    late, (out, fa, fb) = refs[3 * PARTS : 5 * PARTS], refs[5 * PARTS :]
+    b_own, b_other, out, fa, fb = refs[3 * PARTS :]
     half = KV_WIDTH // PARTS
     for part in range(PARTS):
         assemble(fa, own[2 * part], own[2 * part + 1], place, count, rows, part * half)
-        assemble(fb, late[2 * part], late[2 * part + 1], place, count, rows, part * half)
+    assemble(fb, b_own, b_other, place, count, rows)
     even = place[2] == 0
     gk = jnp.concatenate([g[:, :half] for g in grads], axis=1)
     gv = jnp.concatenate([g[:, half:] for g in grads], axis=1)
@@ -269,9 +274,9 @@
     out[...] = (nt(ga, fa[...]) + nt(gb, fb[...])).astype(jnp.bfloat16)
 
 
-def input_grad_of(place, grads, own, late, count, rows):
+def input_grad_of(place, grads, own, b_own, b_other, count, rows):
     full = pltpu.VMEM((2 * count * rows, KV_WIDTH), jnp.bfloat16)
-    operands = [*grads, *own, *late]
+    operands = [*grads, *own, b_own, b_other]
     return pl.pallas_call(
         functools.partial(input_grad_kernel, count=count, rows=rows),
         in_specs=[sspec()] + [vspec()] * len(operands),
@@ -403,18 +408,18 @@
     pair_2 = jnp.concatenate([own_2[:block], mate_2], axis=1)
     ups = [up(pair_2, k) for k in shifts]
 
-    w_late, _ = lax.optimization_barrier((w_own, carried[0]))
-    b_own = [partner(w) for w in w_late]
+    w_late, _ = lax.optimization_barrier((w_own, pair_2))
+    b_own = partner(jnp.concatenate(w_late, axis=1))
+    carried, _ = lax.optimization_barrier((carried, pair_2))
     queries, out_grad = queries[0], out_grad[0]
     before, sent_a, own_a = attend(
         place, queries, out_grad, [pair] + carried, 0, x_for[:0:-1], []
     )
     returned = [around(x, n - k) for k, x in zip(shifts, sent_a)]
     before, sent_b, own_b = attend(place, queries, out_grad, [pair_2] + ups, 1, [], before)
+    sent_b, returned, b_own = lax.optimization_barrier((sent_b, returned, b_own))
     back_b = [down(x, k) for k, x in zip(shifts, sent_b)]
-    back_b, b_own = lax.optimization_barrier((back_b, b_own))
-    b_other = [core(b) for b in b_own]
-    returned, _ = lax.optimization_barrier((returned, sent_b))
+    b_other = core(b_own)
     back_a = [jnp.where(z + k < n, x, jnp.zeros_like(x)) for k, x in zip(shifts, returned)]
     sums = []
     for total, back in ((own_a, back_a), (own_b, back_b)):
@@ -435,7 +440,7 @@
         partials.append(weight_grad_of(x_turned, g_own, core(g_own), n))
     sums, _ = lax.optimization_barrier((sums, partials[-1]))
     own_weights = [w_own[0], w_other[0], w_own[1], w_other[1]]
-    input_grad = input_grad_of(place, sums, own_weights, [b_own[0], b_other[0], b_own[1], b_other[1]], n, rows)
+    input_grad = input_grad_of(place, sums, own_weights, b_own, b_other, n, rows)
     if reps == 2:
         others = [partner(p) for p in partials]
         others, input_grad = lax.optimization_barrier((others, input_grad))

time: 134 us -> 133 us (level)
  local copies, waits for them, and re-layouts: 9.16 us -> 1.21 us
  other arithmetic: 2.29 us -> 5 us
  waiting for transfers between devices: 52 us -> 54.4 us
    ppermute x15, waiting for transfers between devices: 21.7 us -> 31.7 us  [around(): return lax.ppermute(x, 'seq', [(i, (i + k) % n) for i in range(n)])]
    unnamed x55 -> x29, local copies, waits for them, and re-layouts: 9.12 us -> 1.17 us
    ppermute x3, waiting for transfers between devices: 10.9 us -> 5.15 us  [down(): return lax.ppermute(x, 'seq', [(i, i - k) for i in range(k, n)])]
    ppermute x15 -> x13, waiting for transfers between devices: 19.3 us -> 17.6 us  [pairwise(): lax.ppermute(x, axis, [(j, j ^ 1) for j in range(lax.axis_size(axis))])]
    ppermute x15 -> x13, starting transfers between devices: 10 us -> 9.79 us  [pairwise(): lax.ppermute(x, axis, [(j, j ^ 1) for j in range(lax.axis_size(axis))])]
  transfers between devices with their start and end apart: 36 -> 34, of which waited for: 15 -> 16; matrix products, arithmetic and copies ran while one was open for 2% -> 2% of each run, Pallas kernels for 14% -> 14%
where the time goes in v5:
time: 133 us; the launch traced here: 132 us
  waiting for transfers between devices  54.4 us (41%)
  starting transfers between devices  50.3 us (38%)
  Pallas kernels  20.1 us (15%)
  other arithmetic  5 us (4%)
    ppermute x15, waiting for transfers between devices, around(): return lax.ppermute(x, 'seq', [(i, (i + k) % n) for i in range(n)])  31.7 us
    ppermute x15, starting transfers between devices, around(): return lax.ppermute(x, 'seq', [(i, (i + k) % n) for i in range(n)])  25.3 us
    ppermute x13, waiting for transfers between devices, pairwise(): lax.ppermute(x, axis, [(j, j ^ 1) for j in range(lax.axis_size(axis))])  17.6 us
    ppermute x3, starting transfers between devices, up(): return lax.ppermute(x, 'seq', [(i, i + k) for i in range(n - k)])  11.4 us
    ppermute x13, starting transfers between devices, pairwise(): lax.ppermute(x, axis, [(j, j ^ 1) for j in range(lax.axis_size(axis))])  9.79 us
    pallas_call x2, Pallas kernels, attend(): pl.pallas_call(functools.partial(attend_kernel, count=count, block=block,...  9.48 us
    ppermute x3, waiting for transfers between devices, down(): return lax.ppermute(x, 'seq', [(i, i - k) for i in range(k, n)])  5.15 us
    ppermute x3, starting transfers between devices, down(): return lax.ppermute(x, 'seq', [(i, i - k) for i in range(k, n)])  3.87 us
  transfers between devices with their start and end apart: 34, of which 16 were waited for; matrix products, arithmetic and copies ran while one was open for 2% of the time, Pallas kernels for 14%

profile of v5, /device:TPU:0, one launch (start us, length us, event | category | flops | bytes accessed | tf_op | source)
XLA Modules:
  0.0 131.9 jit_solution(15841356787669936505)
XLA Ops:
  0.6 0.5 collective-permute-start.4
  1.1 2.6 %collective-permute-start.3 = (bf16[128,2048]{1,0:T(8,128)(2,1)}, bf16[128,2048]{1,0:T(8,128)(2,1)S(1)}, u32[]{:S(2)}, u32[]{:S(2)}) collective-permute-start(bf16[128,2048]{1,0:T(8,128)(2,1)} %bitcast.11), channel_id=1, source_target_pairs={{0,2},{2,0},{1,3},{3,1},{4,6},{6,4},{5,7},{7,5},{8,10},{10,8},{9,1... | collective-permute-start | bytes 1572872 | tf_op jit(solution)/shard_map/ppermute | solution.py:382
  3.7 1.0 dynamic-slice_select_fusion
  4.7 1.6 %collective-permute-start = (bf16[256,256]{1,0:T(8,128)(2,1)S(1)}, bf16[256,256]{1,0:T(8,128)(2,1)S(1)}, u32[]{:S(2)}, u32[]{:S(2)}) collective-permute-start(bf16[256,256]{1,0:T(8,128)(2,1)S(1)} %dynamic-slice_select_fusion), channel_id=1, source_target_pairs={{0,4},{4,8},{8,12},{12,0},{1,5},{5,9},{9,13},{13,1},{2,6},{6,10},{... | collective-permute-start | bytes 393224 | tf_op jit(solution)/shard_map/ppermute | solution.py:373
  6.3 2.6 %collective-permute-start.1 = (bf16[256,256]{1,0:T(8,128)(2,1)S(1)}, bf16[256,256]{1,0:T(8,128)(2,1)S(1)}, u32[]{:S(2)}, u32[]{:S(2)}) collective-permute-start(bf16[256,256]{1,0:T(8,128)(2,1)S(1)} %dynamic-slice_select_fusion), channel_id=1, source_target_pairs={{0,8},{4,12},{8,0},{12,4},{1,9},{5,13},{9,1},{13,5},{2,10},{6,14},... | collective-permute-start | bytes 393224 | tf_op jit(solution)/shard_map/ppermute | solution.py:373
  8.9 1.3 %collective-permute-start.2 = (bf16[256,256]{1,0:T(8,128)(2,1)S(1)}, bf16[256,256]{1,0:T(8,128)(2,1)S(1)}, u32[]{:S(2)}, u32[]{:S(2)}) collective-permute-start(bf16[256,256]{1,0:T(8,128)(2,1)S(1)} %dynamic-slice_select_fusion), channel_id=1, source_target_pairs={{0,12},{4,0},{8,4},{12,8},{1,13},{5,1},{9,5},{13,9},{2,14},{6,2},{... | collective-permute-start | bytes 393224 | tf_op jit(solution)/shard_map/ppermute | solution.py:373
  10.3 0.1 pad_add_fusion.place
  10.4 1.0 copy-done
  11.4 0.6 cut.1
  12.1 0.9 collective-permute-done
  13.0 4.9 %collective-permute-done.1 = bf16[256,256]{1,0:T(8,128)(2,1)S(1)} collective-permute-done((bf16[256,256]{1,0:T(8,128)(2,1)S(1)}, bf16[256,256]{1,0:T(8,128)(2,1)S(1)}, u32[]{:S(2)}, u32[]{:S(2)}) %collective-permute-start.1) | collective-permute-done | bytes 131104 | tf_op jit(solution)/shard_map/ppermute | solution.py:373
  18.0 0.1 collective-permute-start.6
  18.1 1.6 %collective-permute-start.5 = (bf16[1024,256]{1,0:T(8,128)(2,1)S(1)}, bf16[1024,256]{1,0:T(8,128)(2,1)S(1)}, u32[]{:S(2)}, u32[]{:S(2)}) collective-permute-start(bf16[1024,256]{1,0:T(8,128)(2,1)S(1)} %constant_dynamic-update-slice_fusion.w_own.refs_2_), channel_id=1, source_target_pairs={{0,16},{16,0},{1,17},{17,1},{2,18},{18,2},{3,19},{19,3},{4,20},{20... | collective-permute-start | bytes 1572872 | tf_op jit(solution)/shard_map/ppermute | solution.py:382
  19.7 0.3 collective-permute-done.6.w_other.refs_3_
  20.0 1.1 project.2
  21.1 0.6 collective-permute-start.7
  21.7 3.7 %collective-permute-done.7.mate = bf16[128,256]{1,0:T(8,128)(2,1)S(1)} collective-permute-done((bf16[128,256]{1,0:T(8,128)(2,1)S(1)}, bf16[128,256]{1,0:T(8,128)(2,1)S(1)}, u32[]{:S(2)}, u32[]{:S(2)}) %collective-permute-start.7) | collective-permute-done | bytes 65568 | tf_op jit(solution)/shard_map/ppermute | solution.py:382
  25.4 0.6 pack.1
  26.0 6.4 %collective-permute-done.5.w_own.refs_4_ = bf16[1024,256]{1,0:T(8,128)(2,1)S(1)} collective-permute-done((bf16[1024,256]{1,0:T(8,128)(2,1)S(1)}, bf16[1024,256]{1,0:T(8,128)(2,1)S(1)}, u32[]{:S(2)}, u32[]{:S(2)}) %collective-permute-start.5) | collective-permute-done | bytes 524320 | tf_op jit(solution)/shard_map/ppermute | solution.py:382
  32.4 3.3 %collective-permute-start.10 = (bf16[144,512]{1,0:T(8,128)(2,1)S(1)}, bf16[144,512]{1,0:T(8,128)(2,1)S(1)}, u32[]{:S(2)}, u32[]{:S(2)}) collective-permute-start(bf16[144,512]{1,0:T(8,128)(2,1)S(1)} %get-tuple-element.83), channel_id=1, source_target_pairs={{0,4},{4,8},{8,12},{12,0},{1,5},{5,9},{9,13},{13,1},{2,6},{6,10},{... | collective-permute-start | bytes 442376 | tf_op jit(solution)/shard_map/ppermute | solution.py:373
  35.7 1.6 %collective-permute-start.11 = (bf16[144,512]{1,0:T(8,128)(2,1)S(1)}, bf16[144,512]{1,0:T(8,128)(2,1)S(1)}, u32[]{:S(2)}, u32[]{:S(2)}) collective-permute-start(bf16[144,512]{1,0:T(8,128)(2,1)S(1)} %get-tuple-element.87), channel_id=1, source_target_pairs={{0,8},{4,12},{8,0},{12,4},{1,9},{5,13},{9,1},{13,5},{2,10},{6,14},... | collective-permute-start | bytes 442376 | tf_op jit(solution)/shard_map/ppermute | solution.py:373
  37.3 0.7 collective-permute-start.12
  38.1 1.1 project.3
  39.1 0.6 collective-permute-start.9
  39.7 1.8 %collective-permute-done.10.refs_1_.refs_0_ = bf16[144,512]{1,0:T(8,128)(2,1)S(1)} collective-permute-done((bf16[144,512]{1,0:T(8,128)(2,1)S(1)}, bf16[144,512]{1,0:T(8,128)(2,1)S(1)}, u32[]{:S(2)}, u32[]{:S(2)}) %collective-permute-start.10) | collective-permute-done | bytes 147488 | tf_op jit(solution)/shard_map/ppermute | solution.py:373
  41.6 6.1 %collective-permute-done.11.refs_2_.refs_1_ = bf16[144,512]{1,0:T(8,128)(2,1)S(1)} collective-permute-done((bf16[144,512]{1,0:T(8,128)(2,1)S(1)}, bf16[144,512]{1,0:T(8,128)(2,1)S(1)}, u32[]{:S(2)}, u32[]{:S(2)}) %collective-permute-start.11) | collective-permute-done | bytes 147488 | tf_op jit(solution)/shard_map/ppermute | solution.py:373
  47.7 0.7 pad_maximum_fusion.1.refs_0_
  48.4 1.1 pad_maximum_fusion
  49.5 0.5 collective-permute-start.19
  50.0 6.2 %collective-permute-start.13 = (bf16[128,512]{1,0:T(8,128)(2,1)}, bf16[128,512]{1,0:T(8,128)(2,1)}, u32[]{:S(2)}, u32[]{:S(2)}) collective-permute-start(bf16[128,512]{1,0:T(8,128)(2,1)} %pad_maximum_fusion.1.refs_0_), channel_id=1, source_target_pairs={{0,4},{4,8},{8,12},{1,5},{5,9},{9,13},{2,6},{6,10},{10,14},{3,7},{... | collective-permute-start | bytes 393224 | tf_op jit(solution)/shard_map/ppermute | solution.py:376
  56.2 3.2 %collective-permute-start.14 = (bf16[128,512]{1,0:T(8,128)(2,1)}, bf16[128,512]{1,0:T(8,128)(2,1)}, u32[]{:S(2)}, u32[]{:S(2)}) collective-permute-start(bf16[128,512]{1,0:T(8,128)(2,1)} %pad_maximum_fusion.1.refs_0_), channel_id=1, source_target_pairs={{0,8},{4,12},{1,9},{5,13},{2,10},{6,14},{3,11},{7,15},{16,24},{20,... | collective-permute-start | bytes 393224 | tf_op jit(solution)/shard_map/ppermute | solution.py:376
  59.4 1.9 %collective-permute-start.15 = (bf16[128,512]{1,0:T(8,128)(2,1)}, bf16[128,512]{1,0:T(8,128)(2,1)}, u32[]{:S(2)}, u32[]{:S(2)}) collective-permute-start(bf16[128,512]{1,0:T(8,128)(2,1)} %pad_maximum_fusion.1.refs_0_), channel_id=1, source_target_pairs={{0,12},{1,13},{2,14},{3,15},{16,28},{17,29},{18,30},{19,31}} | collective-permute-start | bytes 393224 | tf_op jit(solution)/shard_map/ppermute | solution.py:376
  61.4 4.3 %attend.2 = (bf16[128,2048]{1,0:T(8,128)(2,1)}, bf16[128,2048]{1,0:T(8,128)(2,1)}, f32[128,512]{1,0:T(8,128)}, bf16[128,512]{1,0:T(8,128)(2,1)}, bf16[128,512]{1...) custom-call(s32[4]{0:T(128)S(1)} %pad_add_fusion.place, bf16[128,2048]{1,0:T(8,128)(2,1)S(1)} %bitcast.15, ...), custom_call_target="tpu_custom_call" | custom-call | tf_op jit(solution)/shard_map/attend/pallas_call | solution.py:248
  65.7 0.2 collective-permute-start.17
  65.9 1.9 %collective-permute-start.18 = (bf16[128,512]{1,0:T(8,128)(2,1)}, bf16[128,512]{1,0:T(8,128)(2,1)}, u32[]{:S(2)}, u32[]{:S(2)}) collective-permute-start(bf16[128,512]{1,0:T(8,128)(2,1)} %get-tuple-element.105), channel_id=1, source_target_pairs={{0,4},{4,8},{8,12},{12,0},{1,5},{5,9},{9,13},{13,1},{2,6},{6,10},{... | collective-permute-start | bytes 393224 | tf_op jit(solution)/shard_map/ppermute | solution.py:373
  67.8 5.2 %attend.3 = (bf16[128,2048]{1,0:T(8,128)(2,1)}, bf16[128,2048]{1,0:T(8,128)(2,1)}, bf16[128,512]{1,0:T(8,128)(2,1)S(1)}, bf16[128,512]{1,0:T(8,128)(2,1)S(1)}, b...) custom-call(s32[4]{0:T(128)S(1)} %pad_add_fusion.place, ...), custom_call_target="tpu_custom_call", output_to_operand_aliasing={{0}: (8, {}), {1}: (9, {})} | custom-call | tf_op jit(solution)/shard_map/attend/pallas_call | solution.py:248
  73.0 3.2 %collective-permute-done.17.refs_4_ = bf16[128,512]{1,0:T(8,128)(2,1)} collective-permute-done((bf16[128,512]{1,0:T(8,128)(2,1)}, bf16[128,512]{1,0:T(8,128)(2,1)}, u32[]{:S(2)}, u32[]{:S(2)}) %collective-permute-start.17) | collective-permute-done | bytes 131104 | tf_op jit(solution)/shard_map/ppermute | solution.py:373
  76.2 1.6 %collective-permute-done.18.refs_5_ = bf16[128,512]{1,0:T(8,128)(2,1)} collective-permute-done((bf16[128,512]{1,0:T(8,128)(2,1)}, bf16[128,512]{1,0:T(8,128)(2,1)}, u32[]{:S(2)}, u32[]{:S(2)}) %collective-permute-start.18) | collective-permute-done | bytes 131104 | tf_op jit(solution)/shard_map/ppermute | solution.py:373
  77.8 1.3 collective-permute-start.22
  79.1 1.3 collective-permute-start.21
  80.4 1.3 collective-permute-start.20
  81.7 1.1 add_convert_fusion.refs_0_
  82.8 2.6 %collective-permute-start.26 = (bf16[128,512]{1,0:T(8,128)(2,1)S(1)}, bf16[128,512]{1,0:T(8,128)(2,1)S(1)}, u32[]{:S(2)}, u32[]{:S(2)}) collective-permute-start(bf16[128,512]{1,0:T(8,128)(2,1)S(1)} %add_convert_fusion.refs_0_), channel_id=1, source_target_pairs={{0,4},{4,8},{8,12},{12,0},{1,5},{5,9},{9,13},{13,1},{2,6},{6,10},{... | collective-permute-start | bytes 393224 | tf_op jit(solution)/shard_map/ppermute | solution.py:373
  85.5 2.6 %collective-permute-start.27 = (bf16[128,512]{1,0:T(8,128)(2,1)S(1)}, bf16[128,512]{1,0:T(8,128)(2,1)S(1)}, u32[]{:S(2)}, u32[]{:S(2)}) collective-permute-start(bf16[128,512]{1,0:T(8,128)(2,1)S(1)} %add_convert_fusion.refs_0_), channel_id=1, source_target_pairs={{0,8},{4,12},{8,0},{12,4},{1,9},{5,13},{9,1},{13,5},{2,10},{6,14},... | collective-permute-start | bytes 393224 | tf_op jit(solution)/shard_map/ppermute | solution.py:373
  88.1 1.8 %collective-permute-start.28 = (bf16[128,512]{1,0:T(8,128)(2,1)S(1)}, bf16[128,512]{1,0:T(8,128)(2,1)S(1)}, u32[]{:S(2)}, u32[]{:S(2)}) collective-permute-start(bf16[128,512]{1,0:T(8,128)(2,1)S(1)} %add_convert_fusion.refs_0_), channel_id=1, source_target_pairs={{0,12},{4,0},{8,4},{12,8},{1,13},{5,1},{9,5},{13,9},{2,14},{6,2},{... | collective-permute-start | bytes 393224 | tf_op jit(solution)/shard_map/ppermute | solution.py:373
  89.9 5.1 %collective-permute-done.21 = bf16[128,512]{1,0:T(8,128)(2,1)S(1)} collective-permute-done((bf16[128,512]{1,0:T(8,128)(2,1)S(1)}, bf16[128,512]{1,0:T(8,128)(2,1)S(1)}, u32[]{:S(2)}, u32[]{:S(2)}) %collective-permute-start.21) | collective-permute-done | bytes 131104 | tf_op jit(solution)/shard_map/ppermute | solution.py:379
  95.0 1.0 add_convert_fusion.1.refs_1_
  96.0 6.4 %collective-permute-done.27 = bf16[128,512]{1,0:T(8,128)(2,1)S(1)} collective-permute-done((bf16[128,512]{1,0:T(8,128)(2,1)S(1)}, bf16[128,512]{1,0:T(8,128)(2,1)S(1)}, u32[]{:S(2)}, u32[]{:S(2)}) %collective-permute-start.27) | collective-permute-done | bytes 131104 | tf_op jit(solution)/shard_map/ppermute | solution.py:373
  102.5 0.1 collective-permute-start.29
  102.6 2.5 %collective-permute-start.23 = (bf16[128,512]{1,0:T(8,128)(2,1)S(1)}, bf16[128,512]{1,0:T(8,128)(2,1)S(1)}, u32[]{:S(2)}, u32[]{:S(2)}) collective-permute-start(bf16[128,512]{1,0:T(8,128)(2,1)S(1)} %add_convert_fusion.1.refs_1_), channel_id=1, source_target_pairs={{0,4},{4,8},{8,12},{12,0},{1,5},{5,9},{9,13},{13,1},{2,6},{6,10},{... | collective-permute-start | bytes 393224 | tf_op jit(solution)/shard_map/ppermute | solution.py:373
  105.1 2.5 %collective-permute-start.25 = (bf16[128,512]{1,0:T(8,128)(2,1)S(1)}, bf16[128,512]{1,0:T(8,128)(2,1)S(1)}, u32[]{:S(2)}, u32[]{:S(2)}) collective-permute-start(bf16[128,512]{1,0:T(8,128)(2,1)S(1)} %add_convert_fusion.1.refs_1_), channel_id=1, source_target_pairs={{0,12},{4,0},{8,4},{12,8},{1,13},{5,1},{9,5},{13,9},{2,14},{6,2},{... | collective-permute-start | bytes 393224 | tf_op jit(solution)/shard_map/ppermute | solution.py:373
  107.5 1.2 turn.1.x_turned
  108.9 0.4 weight_grad.2.refs_0_
  109.3 1.6 %collective-permute-done.23 = bf16[128,512]{1,0:T(8,128)(2,1)S(1)} collective-permute-done((bf16[128,512]{1,0:T(8,128)(2,1)S(1)}, bf16[128,512]{1,0:T(8,128)(2,1)S(1)}, u32[]{:S(2)}, u32[]{:S(2)}) %collective-permute-start.23) | collective-permute-done | bytes 131104 | tf_op jit(solution)/shard_map/ppermute | solution.py:373
  110.8 5.1 %collective-permute-done.24 = bf16[128,512]{1,0:T(8,128)(2,1)S(1)} collective-permute-done((bf16[128,512]{1,0:T(8,128)(2,1)S(1)}, bf16[128,512]{1,0:T(8,128)(2,1)S(1)}, u32[]{:S(2)}, u32[]{:S(2)}) %collective-permute-start.24) | collective-permute-done | bytes 131104 | tf_op jit(solution)/shard_map/ppermute | solution.py:373
  116.1 0.1 collective-permute-start.31
  116.1 1.6 %collective-permute-start.30 = (bf16[256,512]{1,0:T(8,128)(2,1)S(1)}, bf16[256,512]{1,0:T(8,128)(2,1)S(1)}, u32[]{:S(2)}, u32[]{:S(2)}) collective-permute-start(bf16[256,512]{1,0:T(8,128)(2,1)S(1)} %weight_grad.2.refs_0_), channel_id=1, source_target_pairs={{0,2},{2,0},{1,3},{3,1},{4,6},{6,4},{5,7},{7,5},{8,10},{10,8},{9,1... | collective-permute-start | bytes 786440 | tf_op jit(solution)/shard_map/ppermute | solution.py:382
  117.7 0.3 collective-permute-done.31.g_other
  118.0 0.4 weight_grad.3.refs_2_
  118.5 1.6 %collective-permute-start.32 = (bf16[256,512]{1,0:T(8,128)(2,1)S(1)}, bf16[256,512]{1,0:T(8,128)(2,1)S(1)}, u32[]{:S(2)}, u32[]{:S(2)}) collective-permute-start(bf16[256,512]{1,0:T(8,128)(2,1)S(1)} %weight_grad.3.refs_2_), channel_id=1, source_target_pairs={{0,2},{2,0},{1,3},{3,1},{4,6},{6,4},{5,7},{7,5},{8,10},{10,8},{9,1... | collective-permute-start | bytes 786440 | tf_op jit(solution)/shard_map/ppermute | solution.py:382
  120.0 3.7 %input_grad.1 = bf16[128,2048]{1,0:T(8,128)(2,1)} custom-call(s32[4]{0:T(128)S(1)} %pad_add_fusion.place, bf16[128,512]{1,0:T(8,128)(2,1)S(1)} %add_convert_fusion.refs_0_, bf16[128,512]{1,0:T(8,128)(2,1)S(1)} %add_convert_fusion.1.refs_1_, bf16[1024,256]{1,0:T(8,128)(2,1)S(1)} %constant_dynamic-update-slice_fusion.w_own.refs_2_, ...), custom_call_target="tpu_custom_call" | custom-call | tf_op jit(solution)/shard_map/input_grad/pallas_call | solution.py:280
  123.8 1.6 %collective-permute-done.30.refs_1_ = bf16[256,512]{1,0:T(8,128)(2,1)S(1)} collective-permute-done((bf16[256,512]{1,0:T(8,128)(2,1)S(1)}, bf16[256,512]{1,0:T(8,128)(2,1)S(1)}, u32[]{:S(2)}, u32[]{:S(2)}) %collective-permute-start.30) | collective-permute-done | bytes 262176 | tf_op jit(solution)/shard_map/ppermute | solution.py:382
  125.3 5.2 %collective-permute-done.32.refs_3_ = bf16[256,512]{1,0:T(8,128)(2,1)S(1)} collective-permute-done((bf16[256,512]{1,0:T(8,128)(2,1)S(1)}, bf16[256,512]{1,0:T(8,128)(2,1)S(1)}, u32[]{:S(2)}, u32[]{:S(2)}) %collective-permute-start.32) | collective-permute-done | bytes 262176 | tf_op jit(solution)/shard_map/ppermute | solution.py:382
  130.5 1.4 %finish.1 = (bf16[256,512]{1,0:T(8,128)(2,1)}, bf16[256,512]{1,0:T(8,128)(2,1)}) custom-call(s32[4]{0:T(128)S(1)} %pad_add_fusion.place, bf16[256,512]{1,0:T(8,128)(2,1)S(1)} %weight_grad.2.refs_0_, bf16[256,512]{1,0:T(8,128)(2,1)S(1)} %collective-permute-done.30.refs_1_, bf16[256,512]{1,0:T(8,128)(2,1)S(1)} %weight_grad.3.refs_2_, ...), custom_call_target="tpu_custom_call" | custom-call | tf_op jit(solution)/shard_map/finish/pallas_call | solution.py:349
  (54 shorter events, 0.3 us)
Async XLA Ops:
  0.6 9.7 %collective-permute-start.4 = (bf16[128,2048]{1,0:T(8,128)(2,1)}, bf16[128,2048]{1,0:T(8,128)(2,1)S(1)}, u32[]{:S(2)}, u32[]{:S(2)}) collective-permute-start(bf16[128,2048]{1,0:T(8,128)(2,1)} %bitcast.10), channel_id=1, source_target_pairs={{0,1},{1,0},{2,3},{3,2},{4,5},{5,4},{6,7},{7,6},{8,9},{9,8},{10,11... | collective-permute-start | bytes 1572872 | tf_op jit(solution)/shard_map/ppermute | solution.py:382
  1.1 16.8 %collective-permute-start.3 = (bf16[128,2048]{1,0:T(8,128)(2,1)}, bf16[128,2048]{1,0:T(8,128)(2,1)S(1)}, u32[]{:S(2)}, u32[]{:S(2)}) collective-permute-start(bf16[128,2048]{1,0:T(8,128)(2,1)} %bitcast.11), channel_id=1, source_target_pairs={{0,2},{2,0},{1,3},{3,1},{4,6},{6,4},{5,7},{7,5},{8,10},{10,8},{9,1... | collective-permute-start | bytes 1572872 | tf_op jit(solution)/shard_map/ppermute | solution.py:382
  4.7 8.3 %collective-permute-start = (bf16[256,256]{1,0:T(8,128)(2,1)S(1)}, bf16[256,256]{1,0:T(8,128)(2,1)S(1)}, u32[]{:S(2)}, u32[]{:S(2)}) collective-permute-start(bf16[256,256]{1,0:T(8,128)(2,1)S(1)} %dynamic-slice_select_fusion), channel_id=1, source_target_pairs={{0,4},{4,8},{8,12},{12,0},{1,5},{5,9},{9,13},{13,1},{2,6},{6,10},{... | collective-permute-start | bytes 393224 | tf_op jit(solution)/shard_map/ppermute | solution.py:373
  6.3 11.6 %collective-permute-start.1 = (bf16[256,256]{1,0:T(8,128)(2,1)S(1)}, bf16[256,256]{1,0:T(8,128)(2,1)S(1)}, u32[]{:S(2)}, u32[]{:S(2)}) collective-permute-start(bf16[256,256]{1,0:T(8,128)(2,1)S(1)} %dynamic-slice_select_fusion), channel_id=1, source_target_pairs={{0,8},{4,12},{8,0},{12,4},{1,9},{5,13},{9,1},{13,5},{2,10},{6,14},... | collective-permute-start | bytes 393224 | tf_op jit(solution)/shard_map/ppermute | solution.py:373
  8.9 9.0 %collective-permute-start.2 = (bf16[256,256]{1,0:T(8,128)(2,1)S(1)}, bf16[256,256]{1,0:T(8,128)(2,1)S(1)}, u32[]{:S(2)}, u32[]{:S(2)}) collective-permute-start(bf16[256,256]{1,0:T(8,128)(2,1)S(1)} %dynamic-slice_select_fusion), channel_id=1, source_target_pairs={{0,12},{4,0},{8,4},{12,8},{1,13},{5,1},{9,5},{13,9},{2,14},{6,2},{... | collective-permute-start | bytes 393224 | tf_op jit(solution)/shard_map/ppermute | solution.py:373
  10.4 1.0 copy-start
  11.4 8.6 %copy-start.1 = (bf16[1,128,2048]{2,1,0:T(8,128)(2,1)S(1)}, bf16[1,128,2048]{2,1,0:T(8,128)(2,1)}, u32[]{:S(2)}) copy-start(bf16[1,128,2048]{2,1,0:T(8,128)(2,1)} %param.6) | copy-start | bytes 1572868
  11.4 8.6 %copy-start.8 = (s32[1,128]{1,0:T(1,128)S(1)}, s32[1,128]{1,0:T(1,128)}, u32[]{:S(2)}) copy-start(s32[1,128]{1,0:T(1,128)} %seg.3) | copy-start | bytes 1540
  12.0 6.0 %copy-start.6 = (bf16[128,512]{1,0:T(8,128)(2,1)}, bf16[128,512]{1,0:T(8,128)(2,1)S(1)}, u32[]{:S(2)}) copy-start(bf16[128,512]{1,0:T(8,128)(2,1)S(1)} %get-tuple-element.111.here) | copy-start | bytes 393220
  18.0 2.0 %collective-permute-start.6 = (bf16[1024,256]{1,0:T(8,128)(2,1)S(1)}, bf16[1024,256]{1,0:T(8,128)(2,1)S(1)}, u32[]{:S(2)}, u32[]{:S(2)}) collective-permute-start(bf16[1024,256]{1,0:T(8,128)(2,1)S(1)} %constant_dynamic-update-slice_fusion.w_own.refs_2_), channel_id=1, source_target_pairs={{0,1},{1,0},{2,3},{3,2},{4,5},{5,4},{6,7},{7,6},{8,9},{9,8},{10,11... | collective-permute-start | bytes 1572872 | tf_op jit(solution)/shard_map/ppermute | solution.py:382
  18.1 14.3 %collective-permute-start.5 = (bf16[1024,256]{1,0:T(8,128)(2,1)S(1)}, bf16[1024,256]{1,0:T(8,128)(2,1)S(1)}, u32[]{:S(2)}, u32[]{:S(2)}) collective-permute-start(bf16[1024,256]{1,0:T(8,128)(2,1)S(1)} %constant_dynamic-update-slice_fusion.w_own.refs_2_), channel_id=1, source_target_pairs={{0,16},{16,0},{1,17},{17,1},{2,18},{18,2},{3,19},{19,3},{4,20},{20... | collective-permute-start | bytes 1572872 | tf_op jit(solution)/shard_map/ppermute | solution.py:382
  21.1 4.3 %collective-permute-start.7 = (bf16[128,256]{1,0:T(8,128)(2,1)S(1)}, bf16[128,256]{1,0:T(8,128)(2,1)S(1)}, u32[]{:S(2)}, u32[]{:S(2)}) collective-permute-start(bf16[128,256]{1,0:T(8,128)(2,1)S(1)} %get-tuple-element.79), channel_id=1, source_target_pairs={{0,2},{2,0},{1,3},{3,1},{4,6},{6,4},{5,7},{7,5},{8,10},{10,8},{9,1... | collective-permute-start | bytes 196616 | tf_op jit(solution)/shard_map/ppermute | solution.py:382
  32.4 5.6 %collective-permute-start.8 = (bf16[1024,256]{1,0:T(8,128)(2,1)S(1)}, bf16[1024,256]{1,0:T(8,128)(2,1)S(1)}, u32[]{:S(2)}, u32[]{:S(2)}) collective-permute-start(bf16[1024,256]{1,0:T(8,128)(2,1)S(1)} %collective-permute-done.5.w_own.refs_4_), channel_id=1, source_target_pairs={{0,1},{1,0},{2,3},{3,2},{4,5},{5,4},{6,7},{7,6},{8,9},{9,8},{10,11... | collective-permute-start | bytes 1572872 | tf_op jit(solution)/shard_map/ppermute | solution.py:382
  32.4 9.1 %collective-permute-start.10 = (bf16[144,512]{1,0:T(8,128)(2,1)S(1)}, bf16[144,512]{1,0:T(8,128)(2,1)S(1)}, u32[]{:S(2)}, u32[]{:S(2)}) collective-permute-start(bf16[144,512]{1,0:T(8,128)(2,1)S(1)} %get-tuple-element.83), channel_id=1, source_target_pairs={{0,4},{4,8},{8,12},{12,0},{1,5},{5,9},{9,13},{13,1},{2,6},{6,10},{... | collective-permute-start | bytes 442376 | tf_op jit(solution)/shard_map/ppermute | solution.py:373
  35.7 12.0 %collective-permute-start.11 = (bf16[144,512]{1,0:T(8,128)(2,1)S(1)}, bf16[144,512]{1,0:T(8,128)(2,1)S(1)}, u32[]{:S(2)}, u32[]{:S(2)}) collective-permute-start(bf16[144,512]{1,0:T(8,128)(2,1)S(1)} %get-tuple-element.87), channel_id=1, source_target_pairs={{0,8},{4,12},{8,0},{12,4},{1,9},{5,13},{9,1},{13,5},{2,10},{6,14},... | collective-permute-start | bytes 442376 | tf_op jit(solution)/shard_map/ppermute | solution.py:373
  37.3 10.3 %collective-permute-start.12 = (bf16[144,512]{1,0:T(8,128)(2,1)S(1)}, bf16[144,512]{1,0:T(8,128)(2,1)S(1)}, u32[]{:S(2)}, u32[]{:S(2)}) collective-permute-start(bf16[144,512]{1,0:T(8,128)(2,1)S(1)} %get-tuple-element.88), channel_id=1, source_target_pairs={{0,12},{4,0},{8,4},{12,8},{1,13},{5,1},{9,5},{13,9},{2,14},{6,2},{... | collective-permute-start | bytes 442376 | tf_op jit(solution)/shard_map/ppermute | solution.py:373
  39.1 8.5 %collective-permute-start.9 = (bf16[128,256]{1,0:T(8,128)(2,1)S(1)}, bf16[128,256]{1,0:T(8,128)(2,1)S(1)}, u32[]{:S(2)}, u32[]{:S(2)}) collective-permute-start(bf16[128,256]{1,0:T(8,128)(2,1)S(1)} %get-tuple-element.86), channel_id=1, source_target_pairs={{0,2},{2,0},{1,3},{3,1},{4,6},{6,4},{5,7},{7,5},{8,10},{10,8},{9,1... | collective-permute-start | bytes 196616 | tf_op jit(solution)/shard_map/ppermute | solution.py:382
  47.7 13.7 %copy-start.4 = (bf16[144,512]{1,0:T(8,128)(2,1)}, bf16[144,512]{1,0:T(8,128)(2,1)S(1)}, u32[]{:S(2)}) copy-start(bf16[144,512]{1,0:T(8,128)(2,1)S(1)} %collective-permute-done.12.refs_3_.refs_2_) | copy-start | bytes 442372
  48.4 13.0 %copy-start.2 = (bf16[1,128,2048]{2,1,0:T(8,128)(2,1)S(1)}, bf16[1,128,2048]{2,1,0:T(8,128)(2,1)}, u32[]{:S(2)}) copy-start(bf16[1,128,2048]{2,1,0:T(8,128)(2,1)} %param.7) | copy-start | bytes 1572868
  48.4 13.0 %copy-start.3 = (bf16[1,128,2048]{2,1,0:T(8,128)(2,1)S(1)}, bf16[1,128,2048]{2,1,0:T(8,128)(2,1)}, u32[]{:S(2)}) copy-start(bf16[1,128,2048]{2,1,0:T(8,128)(2,1)} %param.11) | copy-start | bytes 1572868
  49.5 28.3 %collective-permute-start.19 = (bf16[1024,512]{1,0:T(8,128)(2,1)}, bf16[1024,512]{1,0:T(8,128)(2,1)}, u32[]{:S(2)}, u32[]{:S(2)}) collective-permute-start(bf16[1024,512]{1,0:T(8,128)(2,1)} %pad_maximum_fusion), channel_id=1, source_target_pairs={{0,2},{2,0},{1,3},{3,1},{4,6},{6,4},{5,7},{7,5},{8,10},{10,8},{9,1... | collective-permute-start | bytes 3145736 | tf_op jit(solution)/shard_map/ppermute | solution.py:382
  50.0 15.7 %collective-permute-start.13 = (bf16[128,512]{1,0:T(8,128)(2,1)}, bf16[128,512]{1,0:T(8,128)(2,1)}, u32[]{:S(2)}, u32[]{:S(2)}) collective-permute-start(bf16[128,512]{1,0:T(8,128)(2,1)} %pad_maximum_fusion.1.refs_0_), channel_id=1, source_target_pairs={{0,4},{4,8},{8,12},{1,5},{5,9},{9,13},{2,6},{6,10},{10,14},{3,7},{... | collective-permute-start | bytes 393224 | tf_op jit(solution)/shard_map/ppermute | solution.py:376
  56.2 9.7 %collective-permute-start.14 = (bf16[128,512]{1,0:T(8,128)(2,1)}, bf16[128,512]{1,0:T(8,128)(2,1)}, u32[]{:S(2)}, u32[]{:S(2)}) collective-permute-start(bf16[128,512]{1,0:T(8,128)(2,1)} %pad_maximum_fusion.1.refs_0_), channel_id=1, source_target_pairs={{0,8},{4,12},{1,9},{5,13},{2,10},{6,14},{3,11},{7,15},{16,24},{20,... | collective-permute-start | bytes 393224 | tf_op jit(solution)/shard_map/ppermute | solution.py:376
  59.4 8.4 %collective-permute-start.15 = (bf16[128,512]{1,0:T(8,128)(2,1)}, bf16[128,512]{1,0:T(8,128)(2,1)}, u32[]{:S(2)}, u32[]{:S(2)}) collective-permute-start(bf16[128,512]{1,0:T(8,128)(2,1)} %pad_maximum_fusion.1.refs_0_), channel_id=1, source_target_pairs={{0,12},{1,13},{2,14},{3,15},{16,28},{17,29},{18,30},{19,31}} | collective-permute-start | bytes 393224 | tf_op jit(solution)/shard_map/ppermute | solution.py:376
  65.7 7.3 %collective-permute-start.16 = (bf16[128,512]{1,0:T(8,128)(2,1)}, bf16[128,512]{1,0:T(8,128)(2,1)}, u32[]{:S(2)}, u32[]{:S(2)}) collective-permute-start(bf16[128,512]{1,0:T(8,128)(2,1)} %get-tuple-element.103), channel_id=1, source_target_pairs={{0,12},{4,0},{8,4},{12,8},{1,13},{5,1},{9,5},{13,9},{2,14},{6,2},{... | collective-permute-start | bytes 393224 | tf_op jit(solution)/shard_map/ppermute | solution.py:373
  65.7 10.5 %collective-permute-start.17 = (bf16[128,512]{1,0:T(8,128)(2,1)}, bf16[128,512]{1,0:T(8,128)(2,1)}, u32[]{:S(2)}, u32[]{:S(2)}) collective-permute-start(bf16[128,512]{1,0:T(8,128)(2,1)} %get-tuple-element.104), channel_id=1, source_target_pairs={{0,8},{4,12},{8,0},{12,4},{1,9},{5,13},{9,1},{13,5},{2,10},{6,14},... | collective-permute-start | bytes 393224 | tf_op jit(solution)/shard_map/ppermute | solution.py:373
  65.9 11.8 %collective-permute-start.18 = (bf16[128,512]{1,0:T(8,128)(2,1)}, bf16[128,512]{1,0:T(8,128)(2,1)}, u32[]{:S(2)}, u32[]{:S(2)}) collective-permute-start(bf16[128,512]{1,0:T(8,128)(2,1)} %get-tuple-element.105), channel_id=1, source_target_pairs={{0,4},{4,8},{8,12},{12,0},{1,5},{5,9},{9,13},{13,1},{2,6},{6,10},{... | collective-permute-start | bytes 393224 | tf_op jit(solution)/shard_map/ppermute | solution.py:373
  67.8 13.9 %copy-start.9 = (f32[128,512]{1,0:T(8,128)S(1)}, f32[128,512]{1,0:T(8,128)}, u32[]{:S(2)}) copy-start(f32[128,512]{1,0:T(8,128)} %get-tuple-element.115) | copy-start | bytes 786436
  77.8 10.3 %collective-permute-start.22 = (bf16[128,512]{1,0:T(8,128)(2,1)S(1)}, bf16[128,512]{1,0:T(8,128)(2,1)S(1)}, u32[]{:S(2)}, u32[]{:S(2)}) collective-permute-start(bf16[128,512]{1,0:T(8,128)(2,1)S(1)} %get-tuple-element.110), channel_id=1, source_target_pairs={{12,0},{13,1},{14,2},{15,3},{28,16},{29,17},{30,18},{31,19}} | collective-permute-start | bytes 393224 | tf_op jit(solution)/shard_map/ppermute | solution.py:379
  79.1 15.9 %collective-permute-start.21 = (bf16[128,512]{1,0:T(8,128)(2,1)S(1)}, bf16[128,512]{1,0:T(8,128)(2,1)S(1)}, u32[]{:S(2)}, u32[]{:S(2)}) collective-permute-start(bf16[128,512]{1,0:T(8,128)(2,1)S(1)} %get-tuple-element.109), channel_id=1, source_target_pairs={{8,0},{12,4},{9,1},{13,5},{10,2},{14,6},{11,3},{15,7},{24,16},{28,... | collective-permute-start | bytes 393224 | tf_op jit(solution)/shard_map/ppermute | solution.py:379
  80.4 14.6 %collective-permute-start.20 = (bf16[128,512]{1,0:T(8,128)(2,1)S(1)}, bf16[128,512]{1,0:T(8,128)(2,1)S(1)}, u32[]{:S(2)}, u32[]{:S(2)}) collective-permute-start(bf16[128,512]{1,0:T(8,128)(2,1)S(1)} %get-tuple-element.108), channel_id=1, source_target_pairs={{4,0},{8,4},{12,8},{5,1},{9,5},{13,9},{6,2},{10,6},{14,10},{7,3},{... | collective-permute-start | bytes 393224 | tf_op jit(solution)/shard_map/ppermute | solution.py:379
  82.8 24.7 %copy-start.5 = (bf16[144,512]{1,0:T(8,128)(2,1)S(1)}, bf16[144,512]{1,0:T(8,128)(2,1)}, u32[]{:S(2)}) copy-start(bf16[144,512]{1,0:T(8,128)(2,1)} %copy-done.4) | copy-start | bytes 442372
  82.8 24.7 %copy-start.7 = (bf16[128,512]{1,0:T(8,128)(2,1)S(1)}, bf16[128,512]{1,0:T(8,128)(2,1)}, u32[]{:S(2)}) copy-start(bf16[128,512]{1,0:T(8,128)(2,1)} %copy-done.6) | copy-start | bytes 393220
  82.8 13.2 %collective-permute-start.26 = (bf16[128,512]{1,0:T(8,128)(2,1)S(1)}, bf16[128,512]{1,0:T(8,128)(2,1)S(1)}, u32[]{:S(2)}, u32[]{:S(2)}) collective-permute-start(bf16[128,512]{1,0:T(8,128)(2,1)S(1)} %add_convert_fusion.refs_0_), channel_id=1, source_target_pairs={{0,4},{4,8},{8,12},{12,0},{1,5},{5,9},{9,13},{13,1},{2,6},{6,10},{... | collective-permute-start | bytes 393224 | tf_op jit(solution)/shard_map/ppermute | solution.py:373
  85.5 16.9 %collective-permute-start.27 = (bf16[128,512]{1,0:T(8,128)(2,1)S(1)}, bf16[128,512]{1,0:T(8,128)(2,1)S(1)}, u32[]{:S(2)}, u32[]{:S(2)}) collective-permute-start(bf16[128,512]{1,0:T(8,128)(2,1)S(1)} %add_convert_fusion.refs_0_), channel_id=1, source_target_pairs={{0,8},{4,12},{8,0},{12,4},{1,9},{5,13},{9,1},{13,5},{2,10},{6,14},... | collective-permute-start | bytes 393224 | tf_op jit(solution)/shard_map/ppermute | solution.py:373
  88.1 14.4 %collective-permute-start.28 = (bf16[128,512]{1,0:T(8,128)(2,1)S(1)}, bf16[128,512]{1,0:T(8,128)(2,1)S(1)}, u32[]{:S(2)}, u32[]{:S(2)}) collective-permute-start(bf16[128,512]{1,0:T(8,128)(2,1)S(1)} %add_convert_fusion.refs_0_), channel_id=1, source_target_pairs={{0,12},{4,0},{8,4},{12,8},{1,13},{5,1},{9,5},{13,9},{2,14},{6,2},{... | collective-permute-start | bytes 393224 | tf_op jit(solution)/shard_map/ppermute | solution.py:373
  102.5 6.4 %collective-permute-start.29 = (bf16[512,512]{1,0:T(8,128)(2,1)S(1)}, bf16[512,512]{1,0:T(8,128)(2,1)S(1)}, u32[]{:S(2)}, u32[]{:S(2)}) collective-permute-start(bf16[512,512]{1,0:T(8,128)(2,1)S(1)} %constant_dynamic-update-slice_fusion.4.g_own), channel_id=1, source_target_pairs={{0,1},{1,0},{2,3},{3,2},{4,5},{5,4},{6,7},{7,6},{8,9},{9,8},{10,11... | collective-permute-start | bytes 1572872 | tf_op jit(solution)/shard_map/ppermute | solution.py:382
  102.6 8.3 %collective-permute-start.23 = (bf16[128,512]{1,0:T(8,128)(2,1)S(1)}, bf16[128,512]{1,0:T(8,128)(2,1)S(1)}, u32[]{:S(2)}, u32[]{:S(2)}) collective-permute-start(bf16[128,512]{1,0:T(8,128)(2,1)S(1)} %add_convert_fusion.1.refs_1_), channel_id=1, source_target_pairs={{0,4},{4,8},{8,12},{12,0},{1,5},{5,9},{9,13},{13,1},{2,6},{6,10},{... | collective-permute-start | bytes 393224 | tf_op jit(solution)/shard_map/ppermute | solution.py:373
  105.1 10.9 %collective-permute-start.24 = (bf16[128,512]{1,0:T(8,128)(2,1)S(1)}, bf16[128,512]{1,0:T(8,128)(2,1)S(1)}, u32[]{:S(2)}, u32[]{:S(2)}) collective-permute-start(bf16[128,512]{1,0:T(8,128)(2,1)S(1)} %add_convert_fusion.1.refs_1_), channel_id=1, source_target_pairs={{0,8},{4,12},{8,0},{12,4},{1,9},{5,13},{9,1},{13,5},{2,10},{6,14},... | collective-permute-start | bytes 393224 | tf_op jit(solution)/shard_map/ppermute | solution.py:373
  105.1 10.9 %collective-permute-start.25 = (bf16[128,512]{1,0:T(8,128)(2,1)S(1)}, bf16[128,512]{1,0:T(8,128)(2,1)S(1)}, u32[]{:S(2)}, u32[]{:S(2)}) collective-permute-start(bf16[128,512]{1,0:T(8,128)(2,1)S(1)} %add_convert_fusion.1.refs_1_), channel_id=1, source_target_pairs={{0,12},{4,0},{8,4},{12,8},{1,13},{5,1},{9,5},{13,9},{2,14},{6,2},{... | collective-permute-start | bytes 393224 | tf_op jit(solution)/shard_map/ppermute | solution.py:373
  108.8 11.3 %collective-permute-start.33 = (bf16[1024,512]{1,0:T(8,128)(2,1)}, bf16[1024,512]{1,0:T(8,128)(2,1)S(1)}, u32[]{:S(2)}, u32[]{:S(2)}) collective-permute-start(bf16[1024,512]{1,0:T(8,128)(2,1)} %collective-permute-done.19.refs_6_), channel_id=1, source_target_pairs={{0,1},{1,0},{2,3},{3,2},{4,5},{5,4},{6,7},{7,6},{8,9},{9,8},{10,11... | collective-permute-start | bytes 3145736 | tf_op jit(solution)/shard_map/ppermute | solution.py:382
  116.1 2.0 %collective-permute-start.31 = (bf16[512,512]{1,0:T(8,128)(2,1)S(1)}, bf16[512,512]{1,0:T(8,128)(2,1)S(1)}, u32[]{:S(2)}, u32[]{:S(2)}) collective-permute-start(bf16[512,512]{1,0:T(8,128)(2,1)S(1)} %constant_dynamic-update-slice_fusion.8.g_own), channel_id=1, source_target_pairs={{0,1},{1,0},{2,3},{3,2},{4,5},{5,4},{6,7},{7,6},{8,9},{9,8},{10,11... | collective-permute-start | bytes 1572872 | tf_op jit(solution)/shard_map/ppermute | solution.py:382
  116.1 9.2 %collective-permute-start.30 = (bf16[256,512]{1,0:T(8,128)(2,1)S(1)}, bf16[256,512]{1,0:T(8,128)(2,1)S(1)}, u32[]{:S(2)}, u32[]{:S(2)}) collective-permute-start(bf16[256,512]{1,0:T(8,128)(2,1)S(1)} %weight_grad.2.refs_0_), channel_id=1, source_target_pairs={{0,2},{2,0},{1,3},{3,1},{4,6},{6,4},{5,7},{7,5},{8,10},{10,8},{9,1... | collective-permute-start | bytes 786440 | tf_op jit(solution)/shard_map/ppermute | solution.py:382
  118.5 12.0 %collective-permute-start.32 = (bf16[256,512]{1,0:T(8,128)(2,1)S(1)}, bf16[256,512]{1,0:T(8,128)(2,1)S(1)}, u32[]{:S(2)}, u32[]{:S(2)}) collective-permute-start(bf16[256,512]{1,0:T(8,128)(2,1)S(1)} %weight_grad.3.refs_2_), channel_id=1, source_target_pairs={{0,2},{2,0},{1,3},{3,1},{4,6},{6,4},{5,7},{7,5},{8,10},{10,8},{9,1... | collective-permute-start | bytes 786440 | tf_op jit(solution)/shard_map/ppermute | solution.py:382

commit v6 on v5

--- a/solution.py
+++ b/solution.py
@@ -41,14 +41,13 @@
     return pl.BlockSpec(memory_space=pltpu.SMEM)
 
 
-def assemble(full_ref, own_ref, other_ref, place, count, rows, left=0):
+def assemble(full_ref, own_ref, other_ref, place, count, rows):
     z, c = place[0], place[1]
-    right = left + own_ref.shape[1]
     for k in range(count):
         src = lax.rem(z - k + count, count)
         for ref, core in ((own_ref, c), (other_ref, 1 - c)):
             start = pl.multiple_of((src * 2 + core) * rows, rows)
-            full_ref[pl.ds(start, rows), left:right] = ref[k * rows : (k + 1) * rows, :]
+            full_ref[pl.ds(start, rows), :] = ref[k * rows : (k + 1) * rows, :]
 
 
 def project_kernel(place, seg, x_own, x_next, w_own, w_other, out_own, out_next, full, *, count, rows):
@@ -79,7 +78,7 @@
         scratch_shapes=[pltpu.VMEM((2 * count * rows, width), jnp.bfloat16)],
         compiler_params=params(),
         name="project",
-    )(place, seg, x_own, *near(x_next, w_own, w_other))
+    )(place, seg, x_own, x_next, *near(w_own, w_other))
 
 
 def cut_kernel(place, own, other, *outs, count, rows):
@@ -112,31 +111,31 @@
 
 def pack_kernel(place, own, mate, *refs, count):
     cols, outs = refs[: count - 1], refs[count - 1 :]
-    block, half = mate.shape
-    first = jnp.concatenate([own[:block, :], mate[...]], axis=1)
+    block, width = mate.shape
+    half = width // PARTS
+    first = jnp.concatenate([own[:block, :half], mate[:, :half]], axis=1)
     tail = own[block:, :]
     outs[0][:block, :] = first
-    outs[0][block:, :half] = tail
-    outs[0][block:, half:] = jnp.zeros_like(tail)
+    outs[0][block:, :] = tail
+    outs[1][...] = jnp.concatenate([own[:block, half:], mate[:, half:]], axis=1)
     for k in range(1, count):
         goes_up = place[0] + k < count
-        outs[k][:block, :] = jnp.where(goes_up, first, cols[k - 1][...])
-        outs[k][block:, :half] = jnp.where(goes_up, tail, jnp.zeros_like(tail))
-        outs[k][block:, half:] = jnp.zeros_like(tail)
+        outs[k + 1][:block, :] = jnp.where(goes_up, first, cols[k - 1][...])
+        outs[k + 1][block:, :] = jnp.where(goes_up, tail, jnp.zeros_like(tail))
 
 
 def pack(place, own, mate, cols):
     count = len(cols) + 1
-    tall = pltpu.VMEM((own.shape[0], 2 * own.shape[1]), own.dtype)
+    tall = pltpu.VMEM(own.shape, own.dtype)
     outs = pl.pallas_call(
         functools.partial(pack_kernel, count=count),
         in_specs=[sspec()] + [vspec()] * (count + 1),
-        out_specs=[vspec()] * count,
-        out_shape=[tall] * count,
+        out_specs=[vspec()] * (count + 1),
+        out_shape=[tall, pltpu.VMEM(mate.shape, mate.dtype)] + [tall] * (count - 1),
         compiler_params=params(),
         name="pack",
     )(place, *near(own, mate, *cols))
-    return outs[0], outs[1:]
+    return outs[0], outs[1], outs[2:]
 
 
 def nt(a, b):
@@ -223,7 +222,7 @@
     opening = not before
 
     def at_part(g, place):
-        return (0, (place[3] if part == 0 else 1 - place[3]) * steps + g)
+        return (0, part * steps + g)
 
     wide = pl.BlockSpec((block, GROUP * HEAD_DIM), at_part)
     both = 2 * KV_WIDTH // PARTS
@@ -260,11 +259,9 @@
 
 def input_grad_kernel(place, *refs, count, rows):
     grads = refs[:PARTS]
-    own = refs[PARTS : 3 * PARTS]
-    b_own, b_other, out, fa, fb = refs[3 * PARTS :]
+    a_own, a_other, b_own, b_other, out, fa, fb = refs[PARTS:]
     half = KV_WIDTH // PARTS
-    for part in range(PARTS):
-        assemble(fa, own[2 * part], own[2 * part + 1], place, count, rows, part * half)
+    assemble(fa, a_own, a_other, place, count, rows)
     assemble(fb, b_own, b_other, place, count, rows)
     even = place[2] == 0
     gk = jnp.concatenate([g[:, :half] for g in grads], axis=1)
@@ -274,9 +271,9 @@
     out[...] = (nt(ga, fa[...]) + nt(gb, fb[...])).astype(jnp.bfloat16)
 
 
-def input_grad_of(place, grads, own, b_own, b_other, count, rows):
+def input_grad_of(place, grads, a_own, a_other, b_own, b_other, count, rows):
     full = pltpu.VMEM((2 * count * rows, KV_WIDTH), jnp.bfloat16)
-    operands = [*grads, *own, b_own, b_other]
+    operands = [*grads, a_own, a_other, b_own, b_other]
     return pl.pallas_call(
         functools.partial(input_grad_kernel, count=count, rows=rows),
         in_specs=[sspec()] + [vspec()] * len(operands),
@@ -339,9 +336,8 @@
     for part in range(PARTS):
         a, b = pairs[2 * part], pairs[2 * part + 1]
         grad = (a[...].astype(jnp.float32) + b[...].astype(jnp.float32)).astype(jnp.bfloat16)
-        left = pl.multiple_of((place[3] if part == 0 else 1 - place[3]) * half, half)
-        outs[0][:, pl.ds(left, half)] = grad[:, :half]
-        outs[1][:, pl.ds(left, half)] = grad[:, half:]
+        outs[0][:, part * half : (part + 1) * half] = grad[:, :half]
+        outs[1][:, part * half : (part + 1) * half] = grad[:, half:]
 
 
 def finish(place, *partials):
@@ -364,10 +360,8 @@
     reps = lax.axis_size("rep")
     z, c = lax.axis_index("seq"), lax.axis_index("fsdp")
     odd = lax.rem(lax.axis_index("rep"), 2)
-    turned = lax.rem(lax.axis_index("groups"), 2)
-    place = jnp.stack([z, c, odd, turned]).astype(jnp.int32)
+    place = jnp.stack([z, c, odd]).astype(jnp.int32)
     shifts = range(1, n)
-    cut_at = KV_WIDTH // PARTS
 
     def around(x, k):
         return lax.ppermute(x, "seq", [(i, (i + k) % n) for i in range(n)])
@@ -388,38 +382,27 @@
         return pairwise(x, "fsdp")
 
     half = jnp.where(odd == 0, key_weight, value_weight)
-    half = lax.dynamic_slice_in_dim(half, turned * cut_at, cut_at, 1)
     gathered = [half] + [around(half, k) for k in shifts]
     x_next = partner(inputs)
     x_for = cut(place, inputs, core(inputs), n, rows)
     gathered, x_next, x_for = lax.optimization_barrier((gathered, x_next, x_for))
-    w_own = [jnp.concatenate(gathered, axis=0)]
-    w_other = [core(w_own[0])]
-    w_across = pairwise(w_own[0], "groups")
-
-    own, other = project(place, segment_ids, inputs, x_next, w_own[0], w_other[0], n, rows)
-    pair, loads = pack(place, own, partner(other), x_for[1:])
+    w_own = jnp.concatenate(gathered, axis=0)
+    w_other = core(w_own)
+    own, other = project(place, segment_ids, inputs, x_next, w_own, w_other, n, rows)
+    pair, pair_2, loads = pack(place, own, partner(other), x_for[1:])
     carried = [around(x, k) for k, x in zip(shifts, loads)]
-    w_across, _ = lax.optimization_barrier((w_across, loads[0]))
-    w_own.append(w_across)
-    w_other.append(core(w_across))
-    own_2, other_2 = project(place, segment_ids, inputs, x_next, w_own[1], w_other[1], n, rows)
-    mate_2, _ = lax.optimization_barrier((partner(other_2), carried))
-    pair_2 = jnp.concatenate([own_2[:block], mate_2], axis=1)
     ups = [up(pair_2, k) for k in shifts]
 
-    w_late, _ = lax.optimization_barrier((w_own, pair_2))
-    b_own = partner(jnp.concatenate(w_late, axis=1))
-    carried, _ = lax.optimization_barrier((carried, pair_2))
     queries, out_grad = queries[0], out_grad[0]
     before, sent_a, own_a = attend(
         place, queries, out_grad, [pair] + carried, 0, x_for[:0:-1], []
     )
     returned = [around(x, n - k) for k, x in zip(shifts, sent_a)]
     before, sent_b, own_b = attend(place, queries, out_grad, [pair_2] + ups, 1, [], before)
-    sent_b, returned, b_own = lax.optimization_barrier((sent_b, returned, b_own))
+    sent_b, returned = lax.optimization_barrier((sent_b, returned))
+    w_late, _ = lax.optimization_barrier((w_own, sent_b))
+    b_own = partner(w_late)
     back_b = [down(x, k) for k, x in zip(shifts, sent_b)]
-    b_other = core(b_own)
     back_a = [jnp.where(z + k < n, x, jnp.zeros_like(x)) for k, x in zip(shifts, returned)]
     sums = []
     for total, back in ((own_a, back_a), (own_b, back_b)):
@@ -435,12 +418,12 @@
         if part == 0:
             pieces, _ = lax.optimization_barrier((pieces, sums[1]))
         else:
-            pieces, partials = lax.optimization_barrier((pieces, partials))
+            pieces, partials, b_own = lax.optimization_barrier((pieces, partials, b_own))
+            b_other = core(b_own)
         g_own = jnp.concatenate(pieces, axis=0)
         partials.append(weight_grad_of(x_turned, g_own, core(g_own), n))
     sums, _ = lax.optimization_barrier((sums, partials[-1]))
-    own_weights = [w_own[0], w_other[0], w_own[1], w_other[1]]
-    input_grad = input_grad_of(place, sums, own_weights, b_own, b_other, n, rows)
+    input_grad = input_grad_of(place, sums, w_own, w_other, b_own, b_other, n, rows)
     if reps == 2:
         others = [partner(p) for p in partials]
         others, input_grad = lax.optimization_barrier((others, input_grad))

time: 133 us -> 131 us (0.985)
  starting transfers between devices: 50.3 us -> 56.2 us
  waiting for transfers between devices: 54.4 us -> 50.3 us
  other arithmetic: 5 us -> 2.29 us
    ppermute x15, starting transfers between devices: 25.3 us -> 37.2 us  [around(): return lax.ppermute(x, 'seq', [(i, (i + k) % n) for i in range(n)])]
    ppermute x15, waiting for transfers between devices: 31.7 us -> 26 us  [around(): return lax.ppermute(x, 'seq', [(i, (i + k) % n) for i in range(n)])]
    ppermute x13 -> x10, starting transfers between devices: 9.79 us -> 6.09 us  [pairwise(): lax.ppermute(x, axis, [(j, j ^ 1) for j in range(lax.axis_size(axis))])]
    ppermute x3, starting transfers between devices: 11.4 us -> 8.99 us  [up(): return lax.ppermute(x, 'seq', [(i, i + k) for i in range(n - k)])]
    ppermute x3, waiting for transfers between devices: 5.15 us -> 7.3 us  [down(): return lax.ppermute(x, 'seq', [(i, i - k) for i in range(k, n)])]
    concatenate x2 -> x0, other arithmetic: 1.78 us -> none  [the longest x1 1.07 us: body(): b_own = partner(jnp.concatenate(w_late, axis=1))]
    ppermute x13 -> x10, waiting for transfers between devices: 17.6 us -> 17 us  [pairwise(): lax.ppermute(x, axis, [(j, j ^ 1) for j in range(lax.axis_size(axis))])]
  transfers between devices with their start and end apart: 34 -> 31, of which waited for: 16 -> 12; matrix products, arithmetic and copies ran while one was open for 2% -> 2% of each run, Pallas kernels for 14% -> 12%
where the time goes in v6:
time: 131 us
  starting transfers between devices  56.2 us (43%)
  waiting for transfers between devices  50.3 us (38%)
  Pallas kernels  19.3 us (15%)
  other arithmetic  2.29 us (2%)
  local copies, waits for them, and re-layouts  1.65 us (1%)
    ppermute x15, starting transfers between devices, around(): return lax.ppermute(x, 'seq', [(i, (i + k) % n) for i in range(n)])  37.2 us
    ppermute x15, waiting for transfers between devices, around(): return lax.ppermute(x, 'seq', [(i, (i + k) % n) for i in range(n)])  26 us
    ppermute x10, waiting for transfers between devices, pairwise(): lax.ppermute(x, axis, [(j, j ^ 1) for j in range(lax.axis_size(axis))])  17 us
    pallas_call x2, Pallas kernels, attend(): pl.pallas_call(functools.partial(attend_kernel, count=count, block=block,...  9.42 us
    ppermute x3, starting transfers between devices, up(): return lax.ppermute(x, 'seq', [(i, i + k) for i in range(n - k)])  8.99 us
    ppermute x3, waiting for transfers between devices, down(): return lax.ppermute(x, 'seq', [(i, i - k) for i in range(k, n)])  7.3 us
    ppermute x10, starting transfers between devices, pairwise(): lax.ppermute(x, axis, [(j, j ^ 1) for j in range(lax.axis_size(axis))])  6.09 us
    ppermute x3, starting transfers between devices, down(): return lax.ppermute(x, 'seq', [(i, i - k) for i in range(k, n)])  3.87 us
  transfers between devices with their start and end apart: 31, of which 12 were waited for; matrix products, arithmetic and copies ran while one was open for 2% of the time, Pallas kernels for 12%

profile of v6, /device:TPU:0, one launch (start us, length us, event | category | flops | bytes accessed | tf_op | source)
XLA Modules:
  0.0 130.6 jit_solution(6466365709060975002)
XLA Ops:
  0.6 0.5 collective-permute-start.4
  1.2 2.6 %collective-permute-start.3 = (bf16[128,2048]{1,0:T(8,128)(2,1)}, bf16[128,2048]{1,0:T(8,128)(2,1)S(1)}, u32[]{:S(2)}, u32[]{:S(2)}) collective-permute-start(bf16[128,2048]{1,0:T(8,128)(2,1)} %bitcast.14), channel_id=1, source_target_pairs={{0,2},{2,0},{1,3},{3,1},{4,6},{6,4},{5,7},{7,5},{8,10},{10,8},{9,1... | collective-permute-start | bytes 1572872 | tf_op jit(solution)/shard_map/ppermute | solution.py:376
  3.7 1.0 broadcast_select_fusion
  4.7 1.6 %collective-permute-start = (bf16[256,512]{1,0:T(8,128)(2,1)S(1)}, bf16[256,512]{1,0:T(8,128)(2,1)S(1)}, u32[]{:S(2)}, u32[]{:S(2)}) collective-permute-start(bf16[256,512]{1,0:T(8,128)(2,1)S(1)} %broadcast_select_fusion), channel_id=1, source_target_pairs={{0,4},{4,8},{8,12},{12,0},{1,5},{5,9},{9,13},{13,1},{2,6},{6,10},{... | collective-permute-start | bytes 786440 | tf_op jit(solution)/shard_map/ppermute | solution.py:367
  6.3 2.6 %collective-permute-start.1 = (bf16[256,512]{1,0:T(8,128)(2,1)S(1)}, bf16[256,512]{1,0:T(8,128)(2,1)S(1)}, u32[]{:S(2)}, u32[]{:S(2)}) collective-permute-start(bf16[256,512]{1,0:T(8,128)(2,1)S(1)} %broadcast_select_fusion), channel_id=1, source_target_pairs={{0,8},{4,12},{8,0},{12,4},{1,9},{5,13},{9,1},{13,5},{2,10},{6,14},... | collective-permute-start | bytes 786440 | tf_op jit(solution)/shard_map/ppermute | solution.py:367
  8.9 1.3 %collective-permute-start.2 = (bf16[256,512]{1,0:T(8,128)(2,1)S(1)}, bf16[256,512]{1,0:T(8,128)(2,1)S(1)}, u32[]{:S(2)}, u32[]{:S(2)}) collective-permute-start(bf16[256,512]{1,0:T(8,128)(2,1)S(1)} %broadcast_select_fusion), channel_id=1, source_target_pairs={{0,12},{4,0},{8,4},{12,8},{1,13},{5,1},{9,5},{13,9},{2,14},{6,2},{... | collective-permute-start | bytes 786440 | tf_op jit(solution)/shard_map/ppermute | solution.py:367
  10.3 0.1 pad_add_fusion.place
  10.4 0.0 collective-permute-done.4.other
  10.4 0.6 cut.1
  11.0 0.6 copy-done.7
  11.6 4.2 %collective-permute-done = bf16[256,512]{1,0:T(8,128)(2,1)S(1)} collective-permute-done((bf16[256,512]{1,0:T(8,128)(2,1)S(1)}, bf16[256,512]{1,0:T(8,128)(2,1)S(1)}, u32[]{:S(2)}, u32[]{:S(2)}) %collective-permute-start) | collective-permute-done | bytes 262176 | tf_op jit(solution)/shard_map/ppermute | solution.py:367
  15.8 10.5 %collective-permute-done.1 = bf16[256,512]{1,0:T(8,128)(2,1)S(1)} collective-permute-done((bf16[256,512]{1,0:T(8,128)(2,1)S(1)}, bf16[256,512]{1,0:T(8,128)(2,1)S(1)}, u32[]{:S(2)}, u32[]{:S(2)}) %collective-permute-start.1) | collective-permute-done | bytes 262176 | tf_op jit(solution)/shard_map/ppermute | solution.py:367
  26.4 0.0 collective-permute-done.2
  26.4 0.0 collective-permute-done.3.x_next
  26.4 0.8 copy-done.5
  27.2 0.0 copy-start.6
  27.3 0.0 copy-start.9
  27.3 0.1 collective-permute-start.5
  27.4 2.6 %collective-permute-done.5.w_other.refs_3_ = bf16[1024,512]{1,0:T(8,128)(2,1)S(1)} collective-permute-done((bf16[1024,512]{1,0:T(8,128)(2,1)S(1)}, bf16[1024,512]{1,0:T(8,128)(2,1)S(1)}, u32[]{:S(2)}, u32[]{:S(2)}) %collective-permute-start.5) | collective-permute-done | bytes 1048608 | tf_op jit(solution)/shard_map/ppermute | solution.py:376
  30.0 1.4 %project.1 = (bf16[144,512]{1,0:T(8,128)(2,1)S(1)}, bf16[128,512]{1,0:T(8,128)(2,1)S(1)}) custom-call(s32[3]{0:T(128)S(1)} %pad_add_fusion.place, s32[1,128]{1,0:T(1,128)S(1)} %copy-done.9, bf16[128,2048]{1,0:T(8,128)(2,1)S(1)} %bitcast.16, bf16[128,2048]{1,0:T(8,128)(2,1)S(1)} %copy-done.6, ...), custom_call_target="tpu_custom_call" | custom-call | tf_op jit(solution)/shard_map/project/pallas_call | solution.py:70
  31.5 0.0 copy-start
  31.5 0.6 collective-permute-start.6
  32.1 5.0 %collective-permute-done.6.mate = bf16[128,512]{1,0:T(8,128)(2,1)S(1)} collective-permute-done((bf16[128,512]{1,0:T(8,128)(2,1)S(1)}, bf16[128,512]{1,0:T(8,128)(2,1)S(1)}, u32[]{:S(2)}, u32[]{:S(2)}) %collective-permute-start.6) | collective-permute-done | bytes 131104 | tf_op jit(solution)/shard_map/ppermute | solution.py:376
  37.1 1.2 pack.1
  38.3 6.1 %collective-permute-start.10 = (bf16[144,512]{1,0:T(8,128)(2,1)S(1)}, bf16[144,512]{1,0:T(8,128)(2,1)S(1)}, u32[]{:S(2)}, u32[]{:S(2)}) collective-permute-start(bf16[144,512]{1,0:T(8,128)(2,1)S(1)} %get-tuple-element.78), channel_id=1, source_target_pairs={{0,4},{4,8},{8,12},{12,0},{1,5},{5,9},{9,13},{13,1},{2,6},{6,10},{... | collective-permute-start | bytes 442376 | tf_op jit(solution)/shard_map/ppermute | solution.py:367
  44.4 1.6 %collective-permute-start.11 = (bf16[144,512]{1,0:T(8,128)(2,1)S(1)}, bf16[144,512]{1,0:T(8,128)(2,1)S(1)}, u32[]{:S(2)}, u32[]{:S(2)}) collective-permute-start(bf16[144,512]{1,0:T(8,128)(2,1)S(1)} %get-tuple-element.79), channel_id=1, source_target_pairs={{0,8},{4,12},{8,0},{12,4},{1,9},{5,13},{9,1},{13,5},{2,10},{6,14},... | collective-permute-start | bytes 442376 | tf_op jit(solution)/shard_map/ppermute | solution.py:367
  46.0 0.8 collective-permute-start.12
  46.8 3.8 %collective-permute-start.7 = (bf16[128,512]{1,0:T(8,128)(2,1)}, bf16[128,512]{1,0:T(8,128)(2,1)}, u32[]{:S(2)}, u32[]{:S(2)}) collective-permute-start(bf16[128,512]{1,0:T(8,128)(2,1)} %get-tuple-element.76.refs_0_), channel_id=1, source_target_pairs={{0,4},{4,8},{8,12},{1,5},{5,9},{9,13},{2,6},{6,10},{10,14},{3,7},{... | collective-permute-start | bytes 393224 | tf_op jit(solution)/shard_map/ppermute | solution.py:370
  50.6 3.3 %collective-permute-start.8 = (bf16[128,512]{1,0:T(8,128)(2,1)}, bf16[128,512]{1,0:T(8,128)(2,1)}, u32[]{:S(2)}, u32[]{:S(2)}) collective-permute-start(bf16[128,512]{1,0:T(8,128)(2,1)} %get-tuple-element.76.refs_0_), channel_id=1, source_target_pairs={{0,8},{4,12},{1,9},{5,13},{2,10},{6,14},{3,11},{7,15},{16,24},{20,... | collective-permute-start | bytes 393224 | tf_op jit(solution)/shard_map/ppermute | solution.py:370
  53.8 1.9 %collective-permute-start.9 = (bf16[128,512]{1,0:T(8,128)(2,1)}, bf16[128,512]{1,0:T(8,128)(2,1)}, u32[]{:S(2)}, u32[]{:S(2)}) collective-permute-start(bf16[128,512]{1,0:T(8,128)(2,1)} %get-tuple-element.76.refs_0_), channel_id=1, source_target_pairs={{0,12},{1,13},{2,14},{3,15},{16,28},{17,29},{18,30},{19,31}} | collective-permute-start | bytes 393224 | tf_op jit(solution)/shard_map/ppermute | solution.py:370
  55.8 4.3 %attend.2 = (bf16[128,2048]{1,0:T(8,128)(2,1)}, bf16[128,2048]{1,0:T(8,128)(2,1)}, f32[128,512]{1,0:T(8,128)}, bf16[128,512]{1,0:T(8,128)(2,1)}, bf16[128,512]{1...) custom-call(s32[3]{0:T(128)S(1)} %pad_add_fusion.place, bf16[128,2048]{1,0:T(8,128)(2,1)S(1)} %bitcast.9, ...), custom_call_target="tpu_custom_call" | custom-call | tf_op jit(solution)/shard_map/attend/pallas_call | solution.py:247
  60.1 12.3 %collective-permute-start.13 = (bf16[128,512]{1,0:T(8,128)(2,1)}, bf16[128,512]{1,0:T(8,128)(2,1)}, u32[]{:S(2)}, u32[]{:S(2)}) collective-permute-start(bf16[128,512]{1,0:T(8,128)(2,1)} %get-tuple-element.90), channel_id=1, source_target_pairs={{0,12},{4,0},{8,4},{12,8},{1,13},{5,1},{9,5},{13,9},{2,14},{6,2},{... | collective-permute-start | bytes 393224 | tf_op jit(solution)/shard_map/ppermute | solution.py:367
  72.4 0.6 collective-permute-start.15
  73.1 5.1 %attend.3 = (bf16[128,2048]{1,0:T(8,128)(2,1)}, bf16[128,2048]{1,0:T(8,128)(2,1)}, bf16[128,512]{1,0:T(8,128)(2,1)S(1)}, bf16[128,512]{1,0:T(8,128)(2,1)S(1)}, b...) custom-call(s32[3]{0:T(128)S(1)} %pad_add_fusion.place, ...), custom_call_target="tpu_custom_call", output_to_operand_aliasing={{0}: (8, {}), {1}: (9, {})} | custom-call | tf_op jit(solution)/shard_map/attend/pallas_call | solution.py:247
  78.2 2.2 %collective-permute-done.14.refs_4_ = bf16[128,512]{1,0:T(8,128)(2,1)} collective-permute-done((bf16[128,512]{1,0:T(8,128)(2,1)}, bf16[128,512]{1,0:T(8,128)(2,1)}, u32[]{:S(2)}, u32[]{:S(2)}) %collective-permute-start.14) | collective-permute-done | bytes 131104 | tf_op jit(solution)/shard_map/ppermute | solution.py:367
  80.4 1.3 collective-permute-start.16
  81.7 1.3 collective-permute-start.17
  83.0 1.3 collective-permute-start.18
  84.3 0.0 copy-start.10
  84.3 1.2 add_convert_fusion.refs_0_
  85.5 2.0 %collective-permute-start.22 = (bf16[128,512]{1,0:T(8,128)(2,1)S(1)}, bf16[128,512]{1,0:T(8,128)(2,1)S(1)}, u32[]{:S(2)}, u32[]{:S(2)}) collective-permute-start(bf16[128,512]{1,0:T(8,128)(2,1)S(1)} %add_convert_fusion.refs_0_), channel_id=1, source_target_pairs={{0,4},{4,8},{8,12},{12,0},{1,5},{5,9},{9,13},{13,1},{2,6},{6,10},{... | collective-permute-start | bytes 393224 | tf_op jit(solution)/shard_map/ppermute | solution.py:367
  87.5 3.2 %collective-permute-start.23 = (bf16[128,512]{1,0:T(8,128)(2,1)S(1)}, bf16[128,512]{1,0:T(8,128)(2,1)S(1)}, u32[]{:S(2)}, u32[]{:S(2)}) collective-permute-start(bf16[128,512]{1,0:T(8,128)(2,1)S(1)} %add_convert_fusion.refs_0_), channel_id=1, source_target_pairs={{0,8},{4,12},{8,0},{12,4},{1,9},{5,13},{9,1},{13,5},{2,10},{6,14},... | collective-permute-start | bytes 393224 | tf_op jit(solution)/shard_map/ppermute | solution.py:367
  90.6 0.6 collective-permute-start.24
  91.2 7.3 %collective-permute-done.17 = bf16[128,512]{1,0:T(8,128)(2,1)S(1)} collective-permute-done((bf16[128,512]{1,0:T(8,128)(2,1)S(1)}, bf16[128,512]{1,0:T(8,128)(2,1)S(1)}, u32[]{:S(2)}, u32[]{:S(2)}) %collective-permute-start.17) | collective-permute-done | bytes 131104 | tf_op jit(solution)/shard_map/ppermute | solution.py:373
  98.5 0.5 collective-permute-start.26
  99.1 0.1 add_convert_fusion.1.refs_1_
  99.1 1.9 %collective-permute-done.23 = bf16[128,512]{1,0:T(8,128)(2,1)S(1)} collective-permute-done((bf16[128,512]{1,0:T(8,128)(2,1)S(1)}, bf16[128,512]{1,0:T(8,128)(2,1)S(1)}, u32[]{:S(2)}, u32[]{:S(2)}) %collective-permute-start.23) | collective-permute-done | bytes 131104 | tf_op jit(solution)/shard_map/ppermute | solution.py:367
  101.1 0.1 collective-permute-start.25
  101.2 2.0 %collective-permute-start.19 = (bf16[128,512]{1,0:T(8,128)(2,1)S(1)}, bf16[128,512]{1,0:T(8,128)(2,1)S(1)}, u32[]{:S(2)}, u32[]{:S(2)}) collective-permute-start(bf16[128,512]{1,0:T(8,128)(2,1)S(1)} %add_convert_fusion.1.refs_1_), channel_id=1, source_target_pairs={{0,4},{4,8},{8,12},{12,0},{1,5},{5,9},{9,13},{13,1},{2,6},{6,10},{... | collective-permute-start | bytes 393224 | tf_op jit(solution)/shard_map/ppermute | solution.py:367
  103.2 2.5 %collective-permute-start.21 = (bf16[128,512]{1,0:T(8,128)(2,1)S(1)}, bf16[128,512]{1,0:T(8,128)(2,1)S(1)}, u32[]{:S(2)}, u32[]{:S(2)}) collective-permute-start(bf16[128,512]{1,0:T(8,128)(2,1)S(1)} %add_convert_fusion.1.refs_1_), channel_id=1, source_target_pairs={{0,12},{4,0},{8,4},{12,8},{1,13},{5,1},{9,5},{13,9},{2,14},{6,2},{... | collective-permute-start | bytes 393224 | tf_op jit(solution)/shard_map/ppermute | solution.py:367
  105.6 1.2 turn.1.x_turned
  106.9 0.4 weight_grad.2.refs_0_
  107.3 2.1 %collective-permute-done.19 = bf16[128,512]{1,0:T(8,128)(2,1)S(1)} collective-permute-done((bf16[128,512]{1,0:T(8,128)(2,1)S(1)}, bf16[128,512]{1,0:T(8,128)(2,1)S(1)}, u32[]{:S(2)}, u32[]{:S(2)}) %collective-permute-start.19) | collective-permute-done | bytes 131104 | tf_op jit(solution)/shard_map/ppermute | solution.py:367
  109.5 5.1 %collective-permute-done.20 = bf16[128,512]{1,0:T(8,128)(2,1)S(1)} collective-permute-done((bf16[128,512]{1,0:T(8,128)(2,1)S(1)}, bf16[128,512]{1,0:T(8,128)(2,1)S(1)}, u32[]{:S(2)}, u32[]{:S(2)}) %collective-permute-start.20) | collective-permute-done | bytes 131104 | tf_op jit(solution)/shard_map/ppermute | solution.py:367
  114.6 0.1 collective-permute-start.30
  114.8 0.6 collective-permute-start.28
  115.3 0.5 collective-permute-start.27
  115.8 2.3 %collective-permute-done.28.g_other = bf16[512,512]{1,0:T(8,128)(2,1)S(1)} collective-permute-done((bf16[512,512]{1,0:T(8,128)(2,1)S(1)}, bf16[512,512]{1,0:T(8,128)(2,1)S(1)}, u32[]{:S(2)}, u32[]{:S(2)}) %collective-permute-start.28) | collective-permute-done | bytes 524320 | tf_op jit(solution)/shard_map/ppermute | solution.py:376
  118.1 0.4 weight_grad.3.refs_2_
  118.5 0.6 collective-permute-start.29
  119.1 3.0 %input_grad.1 = bf16[128,2048]{1,0:T(8,128)(2,1)} custom-call(s32[3]{0:T(128)S(1)} %pad_add_fusion.place, bf16[128,512]{1,0:T(8,128)(2,1)S(1)} %add_convert_fusion.refs_0_, bf16[128,512]{1,0:T(8,128)(2,1)S(1)} %add_convert_fusion.1.refs_1_, bf16[1024,512]{1,0:T(8,128)(2,1)S(1)} %constant_dynamic-update-slice_fusion.w_own.refs_2_, ...), custom_call_target="tpu_custom_call" | custom-call | tf_op jit(solution)/shard_map/input_grad/pallas_call | solution.py:277
  122.2 2.3 %collective-permute-done.27.refs_1_ = bf16[256,512]{1,0:T(8,128)(2,1)S(1)} collective-permute-done((bf16[256,512]{1,0:T(8,128)(2,1)S(1)}, bf16[256,512]{1,0:T(8,128)(2,1)S(1)}, u32[]{:S(2)}, u32[]{:S(2)}) %collective-permute-start.27) | collective-permute-done | bytes 262176 | tf_op jit(solution)/shard_map/ppermute | solution.py:376
  124.5 4.7 %collective-permute-done.29.refs_3_ = bf16[256,512]{1,0:T(8,128)(2,1)S(1)} collective-permute-done((bf16[256,512]{1,0:T(8,128)(2,1)S(1)}, bf16[256,512]{1,0:T(8,128)(2,1)S(1)}, u32[]{:S(2)}, u32[]{:S(2)}) %collective-permute-start.29) | collective-permute-done | bytes 262176 | tf_op jit(solution)/shard_map/ppermute | solution.py:376
  129.2 1.4 %finish.1 = (bf16[256,512]{1,0:T(8,128)(2,1)}, bf16[256,512]{1,0:T(8,128)(2,1)}) custom-call(s32[3]{0:T(128)S(1)} %pad_add_fusion.place, bf16[256,512]{1,0:T(8,128)(2,1)S(1)} %weight_grad.2.refs_0_, bf16[256,512]{1,0:T(8,128)(2,1)S(1)} %collective-permute-done.27.refs_1_, bf16[256,512]{1,0:T(8,128)(2,1)S(1)} %weight_grad.3.refs_2_, ...), custom_call_target="tpu_custom_call" | custom-call | tf_op jit(solution)/shard_map/finish/pallas_call | solution.py:345
  (48 shorter events, 0.2 us)
Async XLA Ops:
  0.6 9.7 %copy-start.2 = (bf16[1,128,2048]{2,1,0:T(8,128)(2,1)S(1)}, bf16[1,128,2048]{2,1,0:T(8,128)(2,1)}, u32[]{:S(2)}) copy-start(bf16[1,128,2048]{2,1,0:T(8,128)(2,1)} %param.6) | copy-start | bytes 1572868
  0.6 9.7 %collective-permute-start.4 = (bf16[128,2048]{1,0:T(8,128)(2,1)}, bf16[128,2048]{1,0:T(8,128)(2,1)S(1)}, u32[]{:S(2)}, u32[]{:S(2)}) collective-permute-start(bf16[128,2048]{1,0:T(8,128)(2,1)} %bitcast.13), channel_id=1, source_target_pairs={{0,1},{1,0},{2,3},{3,2},{4,5},{5,4},{6,7},{7,6},{8,9},{9,8},{10,11... | collective-permute-start | bytes 1572872 | tf_op jit(solution)/shard_map/ppermute | solution.py:376
  1.2 25.2 %collective-permute-start.3 = (bf16[128,2048]{1,0:T(8,128)(2,1)}, bf16[128,2048]{1,0:T(8,128)(2,1)S(1)}, u32[]{:S(2)}, u32[]{:S(2)}) collective-permute-start(bf16[128,2048]{1,0:T(8,128)(2,1)} %bitcast.14), channel_id=1, source_target_pairs={{0,2},{2,0},{1,3},{3,1},{4,6},{6,4},{5,7},{7,5},{8,10},{10,8},{9,1... | collective-permute-start | bytes 1572872 | tf_op jit(solution)/shard_map/ppermute | solution.py:376
  4.7 11.1 %collective-permute-start = (bf16[256,512]{1,0:T(8,128)(2,1)S(1)}, bf16[256,512]{1,0:T(8,128)(2,1)S(1)}, u32[]{:S(2)}, u32[]{:S(2)}) collective-permute-start(bf16[256,512]{1,0:T(8,128)(2,1)S(1)} %broadcast_select_fusion), channel_id=1, source_target_pairs={{0,4},{4,8},{8,12},{12,0},{1,5},{5,9},{9,13},{13,1},{2,6},{6,10},{... | collective-permute-start | bytes 786440 | tf_op jit(solution)/shard_map/ppermute | solution.py:367
  6.3 20.0 %collective-permute-start.1 = (bf16[256,512]{1,0:T(8,128)(2,1)S(1)}, bf16[256,512]{1,0:T(8,128)(2,1)S(1)}, u32[]{:S(2)}, u32[]{:S(2)}) collective-permute-start(bf16[256,512]{1,0:T(8,128)(2,1)S(1)} %broadcast_select_fusion), channel_id=1, source_target_pairs={{0,8},{4,12},{8,0},{12,4},{1,9},{5,13},{9,1},{13,5},{2,10},{6,14},... | collective-permute-start | bytes 786440 | tf_op jit(solution)/shard_map/ppermute | solution.py:367
  8.9 17.4 %collective-permute-start.2 = (bf16[256,512]{1,0:T(8,128)(2,1)S(1)}, bf16[256,512]{1,0:T(8,128)(2,1)S(1)}, u32[]{:S(2)}, u32[]{:S(2)}) collective-permute-start(bf16[256,512]{1,0:T(8,128)(2,1)S(1)} %broadcast_select_fusion), channel_id=1, source_target_pairs={{0,12},{4,0},{8,4},{12,8},{1,13},{5,1},{9,5},{13,9},{2,14},{6,2},{... | collective-permute-start | bytes 786440 | tf_op jit(solution)/shard_map/ppermute | solution.py:367
  11.0 0.7 copy-start.7
  26.4 0.8 copy-start.5
  27.2 2.8 %copy-start.6 = (bf16[128,2048]{1,0:T(8,128)(2,1)S(1)}, bf16[128,2048]{1,0:T(8,128)(2,1)}, u32[]{:S(2)}) copy-start(bf16[128,2048]{1,0:T(8,128)(2,1)} %copy-done.5) | copy-start | bytes 1572868
  27.3 2.8 %copy-start.9 = (s32[1,128]{1,0:T(1,128)S(1)}, s32[1,128]{1,0:T(1,128)}, u32[]{:S(2)}) copy-start(s32[1,128]{1,0:T(1,128)} %seg.1) | copy-start | bytes 1540
  27.3 2.7 %collective-permute-start.5 = (bf16[1024,512]{1,0:T(8,128)(2,1)S(1)}, bf16[1024,512]{1,0:T(8,128)(2,1)S(1)}, u32[]{:S(2)}, u32[]{:S(2)}) collective-permute-start(bf16[1024,512]{1,0:T(8,128)(2,1)S(1)} %constant_dynamic-update-slice_fusion.w_own.refs_2_), channel_id=1, source_target_pairs={{0,1},{1,0},{2,3},{3,2},{4,5},{5,4},{6,7},{7,6},{8,9},{9,8},{10,11... | collective-permute-start | bytes 3145736 | tf_op jit(solution)/shard_map/ppermute | solution.py:376
  30.0 25.8 %copy-start.1 = (bf16[1,128,2048]{2,1,0:T(8,128)(2,1)S(1)}, bf16[1,128,2048]{2,1,0:T(8,128)(2,1)}, u32[]{:S(2)}) copy-start(bf16[1,128,2048]{2,1,0:T(8,128)(2,1)} %param.11) | copy-start | bytes 1572868
  31.5 24.3 %copy-start = (bf16[1,128,2048]{2,1,0:T(8,128)(2,1)S(1)}, bf16[1,128,2048]{2,1,0:T(8,128)(2,1)}, u32[]{:S(2)}) copy-start(bf16[1,128,2048]{2,1,0:T(8,128)(2,1)} %param.7) | copy-start | bytes 1572868
  31.5 5.6 %collective-permute-start.6 = (bf16[128,512]{1,0:T(8,128)(2,1)S(1)}, bf16[128,512]{1,0:T(8,128)(2,1)S(1)}, u32[]{:S(2)}, u32[]{:S(2)}) collective-permute-start(bf16[128,512]{1,0:T(8,128)(2,1)S(1)} %get-tuple-element.72), channel_id=1, source_target_pairs={{0,2},{2,0},{1,3},{3,1},{4,6},{6,4},{5,7},{7,5},{8,10},{10,8},{9,1... | collective-permute-start | bytes 393224 | tf_op jit(solution)/shard_map/ppermute | solution.py:376
  38.3 15.5 %collective-permute-start.10 = (bf16[144,512]{1,0:T(8,128)(2,1)S(1)}, bf16[144,512]{1,0:T(8,128)(2,1)S(1)}, u32[]{:S(2)}, u32[]{:S(2)}) collective-permute-start(bf16[144,512]{1,0:T(8,128)(2,1)S(1)} %get-tuple-element.78), channel_id=1, source_target_pairs={{0,4},{4,8},{8,12},{12,0},{1,5},{5,9},{9,13},{13,1},{2,6},{6,10},{... | collective-permute-start | bytes 442376 | tf_op jit(solution)/shard_map/ppermute | solution.py:367
  44.4 11.4 %collective-permute-start.11 = (bf16[144,512]{1,0:T(8,128)(2,1)S(1)}, bf16[144,512]{1,0:T(8,128)(2,1)S(1)}, u32[]{:S(2)}, u32[]{:S(2)}) collective-permute-start(bf16[144,512]{1,0:T(8,128)(2,1)S(1)} %get-tuple-element.79), channel_id=1, source_target_pairs={{0,8},{4,12},{8,0},{12,4},{1,9},{5,13},{9,1},{13,5},{2,10},{6,14},... | collective-permute-start | bytes 442376 | tf_op jit(solution)/shard_map/ppermute | solution.py:367
  46.0 9.8 %collective-permute-start.12 = (bf16[144,512]{1,0:T(8,128)(2,1)S(1)}, bf16[144,512]{1,0:T(8,128)(2,1)S(1)}, u32[]{:S(2)}, u32[]{:S(2)}) collective-permute-start(bf16[144,512]{1,0:T(8,128)(2,1)S(1)} %get-tuple-element.80), channel_id=1, source_target_pairs={{0,12},{4,0},{8,4},{12,8},{1,13},{5,1},{9,5},{13,9},{2,14},{6,2},{... | collective-permute-start | bytes 442376 | tf_op jit(solution)/shard_map/ppermute | solution.py:367
  46.8 25.6 %collective-permute-start.7 = (bf16[128,512]{1,0:T(8,128)(2,1)}, bf16[128,512]{1,0:T(8,128)(2,1)}, u32[]{:S(2)}, u32[]{:S(2)}) collective-permute-start(bf16[128,512]{1,0:T(8,128)(2,1)} %get-tuple-element.76.refs_0_), channel_id=1, source_target_pairs={{0,4},{4,8},{8,12},{1,5},{5,9},{9,13},{2,6},{6,10},{10,14},{3,7},{... | collective-permute-start | bytes 393224 | tf_op jit(solution)/shard_map/ppermute | solution.py:370
  50.6 22.5 %collective-permute-start.8 = (bf16[128,512]{1,0:T(8,128)(2,1)}, bf16[128,512]{1,0:T(8,128)(2,1)}, u32[]{:S(2)}, u32[]{:S(2)}) collective-permute-start(bf16[128,512]{1,0:T(8,128)(2,1)} %get-tuple-element.76.refs_0_), channel_id=1, source_target_pairs={{0,8},{4,12},{1,9},{5,13},{2,10},{6,14},{3,11},{7,15},{16,24},{20,... | collective-permute-start | bytes 393224 | tf_op jit(solution)/shard_map/ppermute | solution.py:370
  53.8 19.2 %collective-permute-start.9 = (bf16[128,512]{1,0:T(8,128)(2,1)}, bf16[128,512]{1,0:T(8,128)(2,1)}, u32[]{:S(2)}, u32[]{:S(2)}) collective-permute-start(bf16[128,512]{1,0:T(8,128)(2,1)} %get-tuple-element.76.refs_0_), channel_id=1, source_target_pairs={{0,12},{1,13},{2,14},{3,15},{16,28},{17,29},{18,30},{19,31}} | collective-permute-start | bytes 393224 | tf_op jit(solution)/shard_map/ppermute | solution.py:370
  55.8 4.3 %copy-start.3 = (bf16[144,512]{1,0:T(8,128)(2,1)}, bf16[144,512]{1,0:T(8,128)(2,1)S(1)}, u32[]{:S(2)}) copy-start(bf16[144,512]{1,0:T(8,128)(2,1)S(1)} %collective-permute-done.12.refs_3_.refs_2_) | copy-start | bytes 442372
  60.1 18.1 %collective-permute-start.13 = (bf16[128,512]{1,0:T(8,128)(2,1)}, bf16[128,512]{1,0:T(8,128)(2,1)}, u32[]{:S(2)}, u32[]{:S(2)}) collective-permute-start(bf16[128,512]{1,0:T(8,128)(2,1)} %get-tuple-element.90), channel_id=1, source_target_pairs={{0,12},{4,0},{8,4},{12,8},{1,13},{5,1},{9,5},{13,9},{2,14},{6,2},{... | collective-permute-start | bytes 393224 | tf_op jit(solution)/shard_map/ppermute | solution.py:367
  72.4 8.0 %collective-permute-start.14 = (bf16[128,512]{1,0:T(8,128)(2,1)}, bf16[128,512]{1,0:T(8,128)(2,1)}, u32[]{:S(2)}, u32[]{:S(2)}) collective-permute-start(bf16[128,512]{1,0:T(8,128)(2,1)} %get-tuple-element.91), channel_id=1, source_target_pairs={{0,8},{4,12},{8,0},{12,4},{1,9},{5,13},{9,1},{13,5},{2,10},{6,14},... | collective-permute-start | bytes 393224 | tf_op jit(solution)/shard_map/ppermute | solution.py:367
  72.4 8.0 %collective-permute-start.15 = (bf16[128,512]{1,0:T(8,128)(2,1)}, bf16[128,512]{1,0:T(8,128)(2,1)}, u32[]{:S(2)}, u32[]{:S(2)}) collective-permute-start(bf16[128,512]{1,0:T(8,128)(2,1)} %get-tuple-element.92), channel_id=1, source_target_pairs={{0,4},{4,8},{8,12},{12,0},{1,5},{5,9},{9,13},{13,1},{2,6},{6,10},{... | collective-permute-start | bytes 393224 | tf_op jit(solution)/shard_map/ppermute | solution.py:367
  73.1 11.2 %copy-start.11 = (f32[128,512]{1,0:T(8,128)S(1)}, f32[128,512]{1,0:T(8,128)}, u32[]{:S(2)}) copy-start(f32[128,512]{1,0:T(8,128)} %get-tuple-element.100) | copy-start | bytes 786436
  80.4 10.3 %collective-permute-start.16 = (bf16[128,512]{1,0:T(8,128)(2,1)S(1)}, bf16[128,512]{1,0:T(8,128)(2,1)S(1)}, u32[]{:S(2)}, u32[]{:S(2)}) collective-permute-start(bf16[128,512]{1,0:T(8,128)(2,1)S(1)} %get-tuple-element.93), channel_id=1, source_target_pairs={{4,0},{8,4},{12,8},{5,1},{9,5},{13,9},{6,2},{10,6},{14,10},{7,3},{... | collective-permute-start | bytes 393224 | tf_op jit(solution)/shard_map/ppermute | solution.py:373
  81.7 16.9 %collective-permute-start.17 = (bf16[128,512]{1,0:T(8,128)(2,1)S(1)}, bf16[128,512]{1,0:T(8,128)(2,1)S(1)}, u32[]{:S(2)}, u32[]{:S(2)}) collective-permute-start(bf16[128,512]{1,0:T(8,128)(2,1)S(1)} %get-tuple-element.94), channel_id=1, source_target_pairs={{8,0},{12,4},{9,1},{13,5},{10,2},{14,6},{11,3},{15,7},{24,16},{28,... | collective-permute-start | bytes 393224 | tf_op jit(solution)/shard_map/ppermute | solution.py:373
  83.0 16.1 %collective-permute-start.18 = (bf16[128,512]{1,0:T(8,128)(2,1)S(1)}, bf16[128,512]{1,0:T(8,128)(2,1)S(1)}, u32[]{:S(2)}, u32[]{:S(2)}) collective-permute-start(bf16[128,512]{1,0:T(8,128)(2,1)S(1)} %get-tuple-element.95), channel_id=1, source_target_pairs={{12,0},{13,1},{14,2},{15,3},{28,16},{29,17},{30,18},{31,19}} | collective-permute-start | bytes 393224 | tf_op jit(solution)/shard_map/ppermute | solution.py:373
  84.3 14.8 %copy-start.10 = (f32[128,512]{1,0:T(8,128)S(1)}, f32[128,512]{1,0:T(8,128)}, u32[]{:S(2)}) copy-start(f32[128,512]{1,0:T(8,128)} %get-tuple-element.86) | copy-start | bytes 786436
  85.5 13.7 %collective-permute-start.22 = (bf16[128,512]{1,0:T(8,128)(2,1)S(1)}, bf16[128,512]{1,0:T(8,128)(2,1)S(1)}, u32[]{:S(2)}, u32[]{:S(2)}) collective-permute-start(bf16[128,512]{1,0:T(8,128)(2,1)S(1)} %add_convert_fusion.refs_0_), channel_id=1, source_target_pairs={{0,4},{4,8},{8,12},{12,0},{1,5},{5,9},{9,13},{13,1},{2,6},{6,10},{... | collective-permute-start | bytes 393224 | tf_op jit(solution)/shard_map/ppermute | solution.py:367
  87.5 13.5 %collective-permute-start.23 = (bf16[128,512]{1,0:T(8,128)(2,1)S(1)}, bf16[128,512]{1,0:T(8,128)(2,1)S(1)}, u32[]{:S(2)}, u32[]{:S(2)}) collective-permute-start(bf16[128,512]{1,0:T(8,128)(2,1)S(1)} %add_convert_fusion.refs_0_), channel_id=1, source_target_pairs={{0,8},{4,12},{8,0},{12,4},{1,9},{5,13},{9,1},{13,5},{2,10},{6,14},... | collective-permute-start | bytes 393224 | tf_op jit(solution)/shard_map/ppermute | solution.py:367
  90.6 10.4 %collective-permute-start.24 = (bf16[128,512]{1,0:T(8,128)(2,1)S(1)}, bf16[128,512]{1,0:T(8,128)(2,1)S(1)}, u32[]{:S(2)}, u32[]{:S(2)}) collective-permute-start(bf16[128,512]{1,0:T(8,128)(2,1)S(1)} %add_convert_fusion.refs_0_), channel_id=1, source_target_pairs={{0,12},{4,0},{8,4},{12,8},{1,13},{5,1},{9,5},{13,9},{2,14},{6,2},{... | collective-permute-start | bytes 393224 | tf_op jit(solution)/shard_map/ppermute | solution.py:367
  98.5 16.1 %collective-permute-start.26 = (bf16[1024,512]{1,0:T(8,128)(2,1)S(1)}, bf16[1024,512]{1,0:T(8,128)(2,1)S(1)}, u32[]{:S(2)}, u32[]{:S(2)}) collective-permute-start(bf16[1024,512]{1,0:T(8,128)(2,1)S(1)} %constant_dynamic-update-slice_fusion.w_own.refs_2_), channel_id=1, source_target_pairs={{0,2},{2,0},{1,3},{3,1},{4,6},{6,4},{5,7},{7,5},{8,10},{10,8},{9,1... | collective-permute-start | bytes 3145736 | tf_op jit(solution)/shard_map/ppermute | solution.py:376
  101.0 4.6 %copy-start.8 = (bf16[128,512]{1,0:T(8,128)(2,1)S(1)}, bf16[128,512]{1,0:T(8,128)(2,1)}, u32[]{:S(2)}) copy-start(bf16[128,512]{1,0:T(8,128)(2,1)} %copy-done.7) | copy-start | bytes 393220
  101.1 4.6 %copy-start.4 = (bf16[144,512]{1,0:T(8,128)(2,1)S(1)}, bf16[144,512]{1,0:T(8,128)(2,1)}, u32[]{:S(2)}) copy-start(bf16[144,512]{1,0:T(8,128)(2,1)} %copy-done.3) | copy-start | bytes 442372
  101.1 5.8 %collective-permute-start.25 = (bf16[512,512]{1,0:T(8,128)(2,1)S(1)}, bf16[512,512]{1,0:T(8,128)(2,1)S(1)}, u32[]{:S(2)}, u32[]{:S(2)}) collective-permute-start(bf16[512,512]{1,0:T(8,128)(2,1)S(1)} %constant_dynamic-update-slice_fusion.4.g_own), channel_id=1, source_target_pairs={{0,1},{1,0},{2,3},{3,2},{4,5},{5,4},{6,7},{7,6},{8,9},{9,8},{10,11... | collective-permute-start | bytes 1572872 | tf_op jit(solution)/shard_map/ppermute | solution.py:376
  101.2 8.3 %collective-permute-start.19 = (bf16[128,512]{1,0:T(8,128)(2,1)S(1)}, bf16[128,512]{1,0:T(8,128)(2,1)S(1)}, u32[]{:S(2)}, u32[]{:S(2)}) collective-permute-start(bf16[128,512]{1,0:T(8,128)(2,1)S(1)} %add_convert_fusion.1.refs_1_), channel_id=1, source_target_pairs={{0,4},{4,8},{8,12},{12,0},{1,5},{5,9},{9,13},{13,1},{2,6},{6,10},{... | collective-permute-start | bytes 393224 | tf_op jit(solution)/shard_map/ppermute | solution.py:367
  103.2 11.4 %collective-permute-start.20 = (bf16[128,512]{1,0:T(8,128)(2,1)S(1)}, bf16[128,512]{1,0:T(8,128)(2,1)S(1)}, u32[]{:S(2)}, u32[]{:S(2)}) collective-permute-start(bf16[128,512]{1,0:T(8,128)(2,1)S(1)} %add_convert_fusion.1.refs_1_), channel_id=1, source_target_pairs={{0,8},{4,12},{8,0},{12,4},{1,9},{5,13},{9,1},{13,5},{2,10},{6,14},... | collective-permute-start | bytes 393224 | tf_op jit(solution)/shard_map/ppermute | solution.py:367
  103.2 11.4 %collective-permute-start.21 = (bf16[128,512]{1,0:T(8,128)(2,1)S(1)}, bf16[128,512]{1,0:T(8,128)(2,1)S(1)}, u32[]{:S(2)}, u32[]{:S(2)}) collective-permute-start(bf16[128,512]{1,0:T(8,128)(2,1)S(1)} %add_convert_fusion.1.refs_1_), channel_id=1, source_target_pairs={{0,12},{4,0},{8,4},{12,8},{1,13},{5,1},{9,5},{13,9},{2,14},{6,2},{... | collective-permute-start | bytes 393224 | tf_op jit(solution)/shard_map/ppermute | solution.py:367
  114.6 4.5 %collective-permute-start.30 = (bf16[1024,512]{1,0:T(8,128)(2,1)S(1)}, bf16[1024,512]{1,0:T(8,128)(2,1)S(1)}, u32[]{:S(2)}, u32[]{:S(2)}) collective-permute-start(bf16[1024,512]{1,0:T(8,128)(2,1)S(1)} %collective-permute-done.26.refs_4_), channel_id=1, source_target_pairs={{0,1},{1,0},{2,3},{3,2},{4,5},{5,4},{6,7},{7,6},{8,9},{9,8},{10,11... | collective-permute-start | bytes 3145736 | tf_op jit(solution)/shard_map/ppermute | solution.py:376
  114.8 3.3 %collective-permute-start.28 = (bf16[512,512]{1,0:T(8,128)(2,1)S(1)}, bf16[512,512]{1,0:T(8,128)(2,1)S(1)}, u32[]{:S(2)}, u32[]{:S(2)}) collective-permute-start(bf16[512,512]{1,0:T(8,128)(2,1)S(1)} %constant_dynamic-update-slice_fusion.8.g_own), channel_id=1, source_target_pairs={{0,1},{1,0},{2,3},{3,2},{4,5},{5,4},{6,7},{7,6},{8,9},{9,8},{10,11... | collective-permute-start | bytes 1572872 | tf_op jit(solution)/shard_map/ppermute | solution.py:376
  115.3 9.2 %collective-permute-start.27 = (bf16[256,512]{1,0:T(8,128)(2,1)S(1)}, bf16[256,512]{1,0:T(8,128)(2,1)S(1)}, u32[]{:S(2)}, u32[]{:S(2)}) collective-permute-start(bf16[256,512]{1,0:T(8,128)(2,1)S(1)} %weight_grad.2.refs_0_), channel_id=1, source_target_pairs={{0,2},{2,0},{1,3},{3,1},{4,6},{6,4},{5,7},{7,5},{8,10},{10,8},{9,1... | collective-permute-start | bytes 786440 | tf_op jit(solution)/shard_map/ppermute | solution.py:376
  118.5 10.7 %collective-permute-start.29 = (bf16[256,512]{1,0:T(8,128)(2,1)S(1)}, bf16[256,512]{1,0:T(8,128)(2,1)S(1)}, u32[]{:S(2)}, u32[]{:S(2)}) collective-permute-start(bf16[256,512]{1,0:T(8,128)(2,1)S(1)} %weight_grad.3.refs_2_), channel_id=1, source_target_pairs={{0,2},{2,0},{1,3},{3,1},{4,6},{6,4},{5,7},{7,5},{8,10},{10,8},{9,1... | collective-permute-start | bytes 786440 | tf_op jit(solution)/shard_map/ppermute | solution.py:376

commit v7 on v6

--- a/solution.py
+++ b/solution.py
@@ -412,25 +412,27 @@
     context, query_grad = before[:2]
     x_turned = turn(place, x_for[0], carried, returned, rows)
 
-    partials = []
+    def over_reps(x):
+        if reps == 2:
+            return [x, partner(x)]
+        return [lax.psum(x.astype(jnp.float32), "rep").astype(x.dtype), jnp.zeros_like(x)]
+
+    finals = []
     for part in range(PARTS):
         pieces = [sums[part]] + [around(sums[part], k) for k in shifts]
         if part == 0:
             pieces, _ = lax.optimization_barrier((pieces, sums[1]))
         else:
-            pieces, partials, b_own = lax.optimization_barrier((pieces, partials, b_own))
+            pieces, b_own = lax.optimization_barrier((pieces, b_own))
             b_other = core(b_own)
         g_own = jnp.concatenate(pieces, axis=0)
-        partials.append(weight_grad_of(x_turned, g_own, core(g_own), n))
-    sums, _ = lax.optimization_barrier((sums, partials[-1]))
+        g_own, finals = lax.optimization_barrier((g_own, finals))
+        partial = weight_grad_of(x_turned, g_own, core(g_own), n)
+        finals += over_reps(partial)
+    sums, _ = lax.optimization_barrier((sums, partial))
     input_grad = input_grad_of(place, sums, w_own, w_other, b_own, b_other, n, rows)
-    if reps == 2:
-        others = [partner(p) for p in partials]
-        others, input_grad = lax.optimization_barrier((others, input_grad))
-        grads = finish(place, *[x for p in zip(partials, others) for x in p])
-    else:
-        totals = [lax.psum(p.astype(jnp.float32), "rep").astype(jnp.bfloat16) for p in partials]
-        grads = finish(place, *[x for p in totals for x in (p, jnp.zeros_like(p))])
+    finals, input_grad = lax.optimization_barrier((finals, input_grad))
+    grads = finish(place, *finals)
     return context[None], query_grad[None], input_grad[None], grads[0], grads[1]
 
 

time: 131 us -> 131 us (level)
  starting transfers between devices: 56.2 us -> 54.5 us
  waiting for transfers between devices: 50.3 us -> 51.8 us
    ppermute x15, waiting for transfers between devices: 26 us -> 28.6 us  [around(): return lax.ppermute(x, 'seq', [(i, (i + k) % n) for i in range(n)])]
  transfers between devices with their start and end apart: 31 -> 31, of which waited for: 12 -> 13; matrix products, arithmetic and copies ran while one was open for 2% -> 2% of each run, Pallas kernels for 12% -> 12%
where the time goes in v7:
time: 131 us; the launch traced here: 130 us
  starting transfers between devices  54.5 us (42%)
  waiting for transfers between devices  51.8 us (40%)
  Pallas kernels  19.3 us (15%)
  other arithmetic  2.35 us (2%)
  local copies, waits for them, and re-layouts  1.56 us (1%)
    ppermute x15, starting transfers between devices, around(): return lax.ppermute(x, 'seq', [(i, (i + k) % n) for i in range(n)])  36 us
    ppermute x15, waiting for transfers between devices, around(): return lax.ppermute(x, 'seq', [(i, (i + k) % n) for i in range(n)])  28.6 us
    ppermute x10, waiting for transfers between devices, pairwise(): lax.ppermute(x, axis, [(j, j ^ 1) for j in range(lax.axis_size(axis))])  15.8 us
    pallas_call x2, Pallas kernels, attend(): pl.pallas_call(functools.partial(attend_kernel, count=count, block=block,...  9.42 us
    ppermute x3, starting transfers between devices, up(): return lax.ppermute(x, 'seq', [(i, i + k) for i in range(n - k)])  8.99 us
    ppermute x3, waiting for transfers between devices, down(): return lax.ppermute(x, 'seq', [(i, i - k) for i in range(k, n)])  7.37 us
    ppermute x10, starting transfers between devices, pairwise(): lax.ppermute(x, axis, [(j, j ^ 1) for j in range(lax.axis_size(axis))])  5.57 us
    ppermute x3, starting transfers between devices, down(): return lax.ppermute(x, 'seq', [(i, i - k) for i in range(k, n)])  3.87 us
  transfers between devices with their start and end apart: 31, of which 13 were waited for; matrix products, arithmetic and copies ran while one was open for 2% of the time, Pallas kernels for 12%

profile of v7, /device:TPU:0, one launch (start us, length us, event | category | flops | bytes accessed | tf_op | source)
XLA Modules:
  0.0 130.4 jit_solution(1480252760589152996)
XLA Ops:
  0.6 0.5 collective-permute-start.4
  1.2 2.6 %collective-permute-start.3 = (bf16[128,2048]{1,0:T(8,128)(2,1)}, bf16[128,2048]{1,0:T(8,128)(2,1)S(1)}, u32[]{:S(2)}, u32[]{:S(2)}) collective-permute-start(bf16[128,2048]{1,0:T(8,128)(2,1)} %bitcast.14), channel_id=1, source_target_pairs={{0,2},{2,0},{1,3},{3,1},{4,6},{6,4},{5,7},{7,5},{8,10},{10,8},{9,1... | collective-permute-start | bytes 1572872 | tf_op jit(solution)/shard_map/ppermute | solution.py:376
  3.7 1.0 broadcast_select_fusion
  4.7 1.6 %collective-permute-start = (bf16[256,512]{1,0:T(8,128)(2,1)S(1)}, bf16[256,512]{1,0:T(8,128)(2,1)S(1)}, u32[]{:S(2)}, u32[]{:S(2)}) collective-permute-start(bf16[256,512]{1,0:T(8,128)(2,1)S(1)} %broadcast_select_fusion), channel_id=1, source_target_pairs={{0,4},{4,8},{8,12},{12,0},{1,5},{5,9},{9,13},{13,1},{2,6},{6,10},{... | collective-permute-start | bytes 786440 | tf_op jit(solution)/shard_map/ppermute | solution.py:367
  6.3 2.6 %collective-permute-start.1 = (bf16[256,512]{1,0:T(8,128)(2,1)S(1)}, bf16[256,512]{1,0:T(8,128)(2,1)S(1)}, u32[]{:S(2)}, u32[]{:S(2)}) collective-permute-start(bf16[256,512]{1,0:T(8,128)(2,1)S(1)} %broadcast_select_fusion), channel_id=1, source_target_pairs={{0,8},{4,12},{8,0},{12,4},{1,9},{5,13},{9,1},{13,5},{2,10},{6,14},... | collective-permute-start | bytes 786440 | tf_op jit(solution)/shard_map/ppermute | solution.py:367
  8.9 1.3 %collective-permute-start.2 = (bf16[256,512]{1,0:T(8,128)(2,1)S(1)}, bf16[256,512]{1,0:T(8,128)(2,1)S(1)}, u32[]{:S(2)}, u32[]{:S(2)}) collective-permute-start(bf16[256,512]{1,0:T(8,128)(2,1)S(1)} %broadcast_select_fusion), channel_id=1, source_target_pairs={{0,12},{4,0},{8,4},{12,8},{1,13},{5,1},{9,5},{13,9},{2,14},{6,2},{... | collective-permute-start | bytes 786440 | tf_op jit(solution)/shard_map/ppermute | solution.py:367
  10.3 0.1 pad_add_fusion.place
  10.4 0.0 collective-permute-done.4.other
  10.4 0.6 cut.1
  11.0 0.6 copy-done.7
  11.6 4.2 %collective-permute-done = bf16[256,512]{1,0:T(8,128)(2,1)S(1)} collective-permute-done((bf16[256,512]{1,0:T(8,128)(2,1)S(1)}, bf16[256,512]{1,0:T(8,128)(2,1)S(1)}, u32[]{:S(2)}, u32[]{:S(2)}) %collective-permute-start) | collective-permute-done | bytes 262176 | tf_op jit(solution)/shard_map/ppermute | solution.py:367
  15.8 10.5 %collective-permute-done.1 = bf16[256,512]{1,0:T(8,128)(2,1)S(1)} collective-permute-done((bf16[256,512]{1,0:T(8,128)(2,1)S(1)}, bf16[256,512]{1,0:T(8,128)(2,1)S(1)}, u32[]{:S(2)}, u32[]{:S(2)}) %collective-permute-start.1) | collective-permute-done | bytes 262176 | tf_op jit(solution)/shard_map/ppermute | solution.py:367
  26.4 0.0 collective-permute-done.2
  26.4 0.0 collective-permute-done.3.x_next
  26.4 0.8 copy-done.5
  27.2 0.0 copy-start.6
  27.3 0.0 copy-start.9
  27.3 0.1 collective-permute-start.5
  27.4 2.6 %collective-permute-done.5.w_other.refs_3_ = bf16[1024,512]{1,0:T(8,128)(2,1)S(1)} collective-permute-done((bf16[1024,512]{1,0:T(8,128)(2,1)S(1)}, bf16[1024,512]{1,0:T(8,128)(2,1)S(1)}, u32[]{:S(2)}, u32[]{:S(2)}) %collective-permute-start.5) | collective-permute-done | bytes 1048608 | tf_op jit(solution)/shard_map/ppermute | solution.py:376
  30.0 1.4 %project.1 = (bf16[144,512]{1,0:T(8,128)(2,1)S(1)}, bf16[128,512]{1,0:T(8,128)(2,1)S(1)}) custom-call(s32[3]{0:T(128)S(1)} %pad_add_fusion.place, s32[1,128]{1,0:T(1,128)S(1)} %copy-done.9, bf16[128,2048]{1,0:T(8,128)(2,1)S(1)} %bitcast.16, bf16[128,2048]{1,0:T(8,128)(2,1)S(1)} %copy-done.6, ...), custom_call_target="tpu_custom_call" | custom-call | tf_op jit(solution)/shard_map/project/pallas_call | solution.py:70
  31.5 0.0 copy-start
  31.5 0.6 collective-permute-start.6
  32.1 5.0 %collective-permute-done.6.mate = bf16[128,512]{1,0:T(8,128)(2,1)S(1)} collective-permute-done((bf16[128,512]{1,0:T(8,128)(2,1)S(1)}, bf16[128,512]{1,0:T(8,128)(2,1)S(1)}, u32[]{:S(2)}, u32[]{:S(2)}) %collective-permute-start.6) | collective-permute-done | bytes 131104 | tf_op jit(solution)/shard_map/ppermute | solution.py:376
  37.1 1.2 pack.1
  38.3 6.1 %collective-permute-start.10 = (bf16[144,512]{1,0:T(8,128)(2,1)S(1)}, bf16[144,512]{1,0:T(8,128)(2,1)S(1)}, u32[]{:S(2)}, u32[]{:S(2)}) collective-permute-start(bf16[144,512]{1,0:T(8,128)(2,1)S(1)} %get-tuple-element.82), channel_id=1, source_target_pairs={{0,4},{4,8},{8,12},{12,0},{1,5},{5,9},{9,13},{13,1},{2,6},{6,10},{... | collective-permute-start | bytes 442376 | tf_op jit(solution)/shard_map/ppermute | solution.py:367
  44.4 1.6 %collective-permute-start.11 = (bf16[144,512]{1,0:T(8,128)(2,1)S(1)}, bf16[144,512]{1,0:T(8,128)(2,1)S(1)}, u32[]{:S(2)}, u32[]{:S(2)}) collective-permute-start(bf16[144,512]{1,0:T(8,128)(2,1)S(1)} %get-tuple-element.83), channel_id=1, source_target_pairs={{0,8},{4,12},{8,0},{12,4},{1,9},{5,13},{9,1},{13,5},{2,10},{6,14},... | collective-permute-start | bytes 442376 | tf_op jit(solution)/shard_map/ppermute | solution.py:367
  46.0 0.8 collective-permute-start.12
  46.8 3.8 %collective-permute-start.7 = (bf16[128,512]{1,0:T(8,128)(2,1)}, bf16[128,512]{1,0:T(8,128)(2,1)}, u32[]{:S(2)}, u32[]{:S(2)}) collective-permute-start(bf16[128,512]{1,0:T(8,128)(2,1)} %get-tuple-element.80.refs_0_), channel_id=1, source_target_pairs={{0,4},{4,8},{8,12},{1,5},{5,9},{9,13},{2,6},{6,10},{10,14},{3,7},{... | collective-permute-start | bytes 393224 | tf_op jit(solution)/shard_map/ppermute | solution.py:370
  50.6 3.3 %collective-permute-start.8 = (bf16[128,512]{1,0:T(8,128)(2,1)}, bf16[128,512]{1,0:T(8,128)(2,1)}, u32[]{:S(2)}, u32[]{:S(2)}) collective-permute-start(bf16[128,512]{1,0:T(8,128)(2,1)} %get-tuple-element.80.refs_0_), channel_id=1, source_target_pairs={{0,8},{4,12},{1,9},{5,13},{2,10},{6,14},{3,11},{7,15},{16,24},{20,... | collective-permute-start | bytes 393224 | tf_op jit(solution)/shard_map/ppermute | solution.py:370
  53.8 1.9 %collective-permute-start.9 = (bf16[128,512]{1,0:T(8,128)(2,1)}, bf16[128,512]{1,0:T(8,128)(2,1)}, u32[]{:S(2)}, u32[]{:S(2)}) collective-permute-start(bf16[128,512]{1,0:T(8,128)(2,1)} %get-tuple-element.80.refs_0_), channel_id=1, source_target_pairs={{0,12},{1,13},{2,14},{3,15},{16,28},{17,29},{18,30},{19,31}} | collective-permute-start | bytes 393224 | tf_op jit(solution)/shard_map/ppermute | solution.py:370
  55.8 0.0 collective-permute-done.11.refs_2_.refs_1_
  55.8 4.3 %attend.2 = (bf16[128,2048]{1,0:T(8,128)(2,1)}, bf16[128,2048]{1,0:T(8,128)(2,1)}, f32[128,512]{1,0:T(8,128)}, bf16[128,512]{1,0:T(8,128)(2,1)}, bf16[128,512]{1...) custom-call(s32[3]{0:T(128)S(1)} %pad_add_fusion.place, bf16[128,2048]{1,0:T(8,128)(2,1)S(1)} %bitcast.9, ...), custom_call_target="tpu_custom_call" | custom-call | tf_op jit(solution)/shard_map/attend/pallas_call | solution.py:247
  60.1 12.3 %collective-permute-start.13 = (bf16[128,512]{1,0:T(8,128)(2,1)}, bf16[128,512]{1,0:T(8,128)(2,1)}, u32[]{:S(2)}, u32[]{:S(2)}) collective-permute-start(bf16[128,512]{1,0:T(8,128)(2,1)} %get-tuple-element.94), channel_id=1, source_target_pairs={{0,12},{4,0},{8,4},{12,8},{1,13},{5,1},{9,5},{13,9},{2,14},{6,2},{... | collective-permute-start | bytes 393224 | tf_op jit(solution)/shard_map/ppermute | solution.py:367
  72.4 0.0 collective-permute-start.14
  72.4 0.6 collective-permute-start.15
  73.1 5.1 %attend.3 = (bf16[128,2048]{1,0:T(8,128)(2,1)}, bf16[128,2048]{1,0:T(8,128)(2,1)}, bf16[128,512]{1,0:T(8,128)(2,1)S(1)}, bf16[128,512]{1,0:T(8,128)(2,1)S(1)}, b...) custom-call(s32[3]{0:T(128)S(1)} %pad_add_fusion.place, ...), custom_call_target="tpu_custom_call", output_to_operand_aliasing={{0}: (8, {}), {1}: (9, {})} | custom-call | tf_op jit(solution)/shard_map/attend/pallas_call | solution.py:247
  78.2 2.2 %collective-permute-done.14.refs_4_ = bf16[128,512]{1,0:T(8,128)(2,1)} collective-permute-done((bf16[128,512]{1,0:T(8,128)(2,1)}, bf16[128,512]{1,0:T(8,128)(2,1)}, u32[]{:S(2)}, u32[]{:S(2)}) %collective-permute-start.14) | collective-permute-done | bytes 131104 | tf_op jit(solution)/shard_map/ppermute | solution.py:367
  80.4 1.3 collective-permute-start.16
  81.7 1.3 collective-permute-start.17
  83.0 1.3 collective-permute-start.18
  84.3 0.6 collective-permute-start.22
  84.9 1.2 add_convert_fusion.refs_0_
  86.0 2.0 %collective-permute-start.23 = (bf16[128,512]{1,0:T(8,128)(2,1)S(1)}, bf16[128,512]{1,0:T(8,128)(2,1)S(1)}, u32[]{:S(2)}, u32[]{:S(2)}) collective-permute-start(bf16[128,512]{1,0:T(8,128)(2,1)S(1)} %add_convert_fusion.refs_0_), channel_id=1, source_target_pairs={{0,4},{4,8},{8,12},{12,0},{1,5},{5,9},{9,13},{13,1},{2,6},{6,10},{... | collective-permute-start | bytes 393224 | tf_op jit(solution)/shard_map/ppermute | solution.py:367
  88.0 3.2 %collective-permute-start.24 = (bf16[128,512]{1,0:T(8,128)(2,1)S(1)}, bf16[128,512]{1,0:T(8,128)(2,1)S(1)}, u32[]{:S(2)}, u32[]{:S(2)}) collective-permute-start(bf16[128,512]{1,0:T(8,128)(2,1)S(1)} %add_convert_fusion.refs_0_), channel_id=1, source_target_pairs={{0,8},{4,12},{8,0},{12,4},{1,9},{5,13},{9,1},{13,5},{2,10},{6,14},... | collective-permute-start | bytes 393224 | tf_op jit(solution)/shard_map/ppermute | solution.py:367
  91.2 7.4 %collective-permute-done.17 = bf16[128,512]{1,0:T(8,128)(2,1)S(1)} collective-permute-done((bf16[128,512]{1,0:T(8,128)(2,1)S(1)}, bf16[128,512]{1,0:T(8,128)(2,1)S(1)}, u32[]{:S(2)}, u32[]{:S(2)}) %collective-permute-start.17) | collective-permute-done | bytes 131104 | tf_op jit(solution)/shard_map/ppermute | solution.py:373
  98.6 0.1 add_convert_fusion.1.refs_1_
  98.7 2.3 %collective-permute-done.24 = bf16[128,512]{1,0:T(8,128)(2,1)S(1)} collective-permute-done((bf16[128,512]{1,0:T(8,128)(2,1)S(1)}, bf16[128,512]{1,0:T(8,128)(2,1)S(1)}, u32[]{:S(2)}, u32[]{:S(2)}) %collective-permute-start.24) | collective-permute-done | bytes 131104 | tf_op jit(solution)/shard_map/ppermute | solution.py:367
  101.0 2.5 %collective-permute-done.25 = bf16[128,512]{1,0:T(8,128)(2,1)S(1)} collective-permute-done((bf16[128,512]{1,0:T(8,128)(2,1)S(1)}, bf16[128,512]{1,0:T(8,128)(2,1)S(1)}, u32[]{:S(2)}, u32[]{:S(2)}) %collective-permute-start.25) | collective-permute-done | bytes 131104 | tf_op jit(solution)/shard_map/ppermute | solution.py:367
  103.6 0.1 collective-permute-start.26
  103.7 0.1 collective-permute-start.19
  103.7 2.4 %collective-permute-start.20 = (bf16[128,512]{1,0:T(8,128)(2,1)S(1)}, bf16[128,512]{1,0:T(8,128)(2,1)S(1)}, u32[]{:S(2)}, u32[]{:S(2)}) collective-permute-start(bf16[128,512]{1,0:T(8,128)(2,1)S(1)} %add_convert_fusion.1.refs_1_), channel_id=1, source_target_pairs={{0,8},{4,12},{8,0},{12,4},{1,9},{5,13},{9,1},{13,5},{2,10},{6,14},... | collective-permute-start | bytes 393224 | tf_op jit(solution)/shard_map/ppermute | solution.py:367
  106.1 1.5 %collective-permute-start.21 = (bf16[128,512]{1,0:T(8,128)(2,1)S(1)}, bf16[128,512]{1,0:T(8,128)(2,1)S(1)}, u32[]{:S(2)}, u32[]{:S(2)}) collective-permute-start(bf16[128,512]{1,0:T(8,128)(2,1)S(1)} %add_convert_fusion.1.refs_1_), channel_id=1, source_target_pairs={{0,12},{4,0},{8,4},{12,8},{1,13},{5,1},{9,5},{13,9},{2,14},{6,2},{... | collective-permute-start | bytes 393224 | tf_op jit(solution)/shard_map/ppermute | solution.py:367
  107.5 1.2 turn.1.x_turned
  108.8 0.4 weight_grad.2.refs_0_
  109.2 0.6 collective-permute-start.27
  109.8 2.1 %collective-permute-done.19 = bf16[128,512]{1,0:T(8,128)(2,1)S(1)} collective-permute-done((bf16[128,512]{1,0:T(8,128)(2,1)S(1)}, bf16[128,512]{1,0:T(8,128)(2,1)S(1)}, u32[]{:S(2)}, u32[]{:S(2)}) %collective-permute-start.19) | collective-permute-done | bytes 131104 | tf_op jit(solution)/shard_map/ppermute | solution.py:367
  112.0 4.7 %collective-permute-done.20 = bf16[128,512]{1,0:T(8,128)(2,1)S(1)} collective-permute-done((bf16[128,512]{1,0:T(8,128)(2,1)S(1)}, bf16[128,512]{1,0:T(8,128)(2,1)S(1)}, u32[]{:S(2)}, u32[]{:S(2)}) %collective-permute-start.20) | collective-permute-done | bytes 131104 | tf_op jit(solution)/shard_map/ppermute | solution.py:367
  116.7 0.7 collective-permute-done.27.refs_1_
  117.4 2.7 %collective-permute-done.28.g_other = bf16[512,512]{1,0:T(8,128)(2,1)S(1)} collective-permute-done((bf16[512,512]{1,0:T(8,128)(2,1)S(1)}, bf16[512,512]{1,0:T(8,128)(2,1)S(1)}, u32[]{:S(2)}, u32[]{:S(2)}) %collective-permute-start.28) | collective-permute-done | bytes 524320 | tf_op jit(solution)/shard_map/ppermute | solution.py:376
  120.1 0.4 weight_grad.3.refs_2_
  120.5 0.6 collective-permute-start.29
  121.1 3.0 %input_grad.1 = bf16[128,2048]{1,0:T(8,128)(2,1)} custom-call(s32[3]{0:T(128)S(1)} %pad_add_fusion.place, bf16[128,512]{1,0:T(8,128)(2,1)S(1)} %add_convert_fusion.refs_0_, bf16[128,512]{1,0:T(8,128)(2,1)S(1)} %add_convert_fusion.1.refs_1_, bf16[1024,512]{1,0:T(8,128)(2,1)S(1)} %constant_dynamic-update-slice_fusion.w_own.refs_2_, ...), custom_call_target="tpu_custom_call" | custom-call | tf_op jit(solution)/shard_map/input_grad/pallas_call | solution.py:277
  124.2 4.8 %collective-permute-done.29.refs_3_ = bf16[256,512]{1,0:T(8,128)(2,1)S(1)} collective-permute-done((bf16[256,512]{1,0:T(8,128)(2,1)S(1)}, bf16[256,512]{1,0:T(8,128)(2,1)S(1)}, u32[]{:S(2)}, u32[]{:S(2)}) %collective-permute-start.29) | collective-permute-done | bytes 262176 | tf_op jit(solution)/shard_map/ppermute | solution.py:376
  129.0 1.4 %finish.1 = (bf16[256,512]{1,0:T(8,128)(2,1)}, bf16[256,512]{1,0:T(8,128)(2,1)}) custom-call(s32[3]{0:T(128)S(1)} %pad_add_fusion.place, bf16[256,512]{1,0:T(8,128)(2,1)S(1)} %weight_grad.2.refs_0_, bf16[256,512]{1,0:T(8,128)(2,1)S(1)} %collective-permute-done.27.refs_1_, bf16[256,512]{1,0:T(8,128)(2,1)S(1)} %weight_grad.3.refs_2_, ...), custom_call_target="tpu_custom_call" | custom-call | tf_op jit(solution)/shard_map/finish/pallas_call | solution.py:345
  (42 shorter events, 0.2 us)
Async XLA Ops:
  0.6 9.7 %copy-start.2 = (bf16[1,128,2048]{2,1,0:T(8,128)(2,1)S(1)}, bf16[1,128,2048]{2,1,0:T(8,128)(2,1)}, u32[]{:S(2)}) copy-start(bf16[1,128,2048]{2,1,0:T(8,128)(2,1)} %param.6) | copy-start | bytes 1572868
  0.6 9.7 %collective-permute-start.4 = (bf16[128,2048]{1,0:T(8,128)(2,1)}, bf16[128,2048]{1,0:T(8,128)(2,1)S(1)}, u32[]{:S(2)}, u32[]{:S(2)}) collective-permute-start(bf16[128,2048]{1,0:T(8,128)(2,1)} %bitcast.13), channel_id=1, source_target_pairs={{0,1},{1,0},{2,3},{3,2},{4,5},{5,4},{6,7},{7,6},{8,9},{9,8},{10,11... | collective-permute-start | bytes 1572872 | tf_op jit(solution)/shard_map/ppermute | solution.py:376
  1.2 25.2 %collective-permute-start.3 = (bf16[128,2048]{1,0:T(8,128)(2,1)}, bf16[128,2048]{1,0:T(8,128)(2,1)S(1)}, u32[]{:S(2)}, u32[]{:S(2)}) collective-permute-start(bf16[128,2048]{1,0:T(8,128)(2,1)} %bitcast.14), channel_id=1, source_target_pairs={{0,2},{2,0},{1,3},{3,1},{4,6},{6,4},{5,7},{7,5},{8,10},{10,8},{9,1... | collective-permute-start | bytes 1572872 | tf_op jit(solution)/shard_map/ppermute | solution.py:376
  4.7 11.1 %collective-permute-start = (bf16[256,512]{1,0:T(8,128)(2,1)S(1)}, bf16[256,512]{1,0:T(8,128)(2,1)S(1)}, u32[]{:S(2)}, u32[]{:S(2)}) collective-permute-start(bf16[256,512]{1,0:T(8,128)(2,1)S(1)} %broadcast_select_fusion), channel_id=1, source_target_pairs={{0,4},{4,8},{8,12},{12,0},{1,5},{5,9},{9,13},{13,1},{2,6},{6,10},{... | collective-permute-start | bytes 786440 | tf_op jit(solution)/shard_map/ppermute | solution.py:367
  6.3 20.0 %collective-permute-start.1 = (bf16[256,512]{1,0:T(8,128)(2,1)S(1)}, bf16[256,512]{1,0:T(8,128)(2,1)S(1)}, u32[]{:S(2)}, u32[]{:S(2)}) collective-permute-start(bf16[256,512]{1,0:T(8,128)(2,1)S(1)} %broadcast_select_fusion), channel_id=1, source_target_pairs={{0,8},{4,12},{8,0},{12,4},{1,9},{5,13},{9,1},{13,5},{2,10},{6,14},... | collective-permute-start | bytes 786440 | tf_op jit(solution)/shard_map/ppermute | solution.py:367
  8.9 17.4 %collective-permute-start.2 = (bf16[256,512]{1,0:T(8,128)(2,1)S(1)}, bf16[256,512]{1,0:T(8,128)(2,1)S(1)}, u32[]{:S(2)}, u32[]{:S(2)}) collective-permute-start(bf16[256,512]{1,0:T(8,128)(2,1)S(1)} %broadcast_select_fusion), channel_id=1, source_target_pairs={{0,12},{4,0},{8,4},{12,8},{1,13},{5,1},{9,5},{13,9},{2,14},{6,2},{... | collective-permute-start | bytes 786440 | tf_op jit(solution)/shard_map/ppermute | solution.py:367
  11.0 0.7 copy-start.7
  26.4 0.8 copy-start.5
  27.2 2.8 %copy-start.6 = (bf16[128,2048]{1,0:T(8,128)(2,1)S(1)}, bf16[128,2048]{1,0:T(8,128)(2,1)}, u32[]{:S(2)}) copy-start(bf16[128,2048]{1,0:T(8,128)(2,1)} %copy-done.5) | copy-start | bytes 1572868
  27.3 2.8 %copy-start.9 = (s32[1,128]{1,0:T(1,128)S(1)}, s32[1,128]{1,0:T(1,128)}, u32[]{:S(2)}) copy-start(s32[1,128]{1,0:T(1,128)} %seg.1) | copy-start | bytes 1540
  27.3 2.7 %collective-permute-start.5 = (bf16[1024,512]{1,0:T(8,128)(2,1)S(1)}, bf16[1024,512]{1,0:T(8,128)(2,1)S(1)}, u32[]{:S(2)}, u32[]{:S(2)}) collective-permute-start(bf16[1024,512]{1,0:T(8,128)(2,1)S(1)} %constant_dynamic-update-slice_fusion.w_own.refs_2_), channel_id=1, source_target_pairs={{0,1},{1,0},{2,3},{3,2},{4,5},{5,4},{6,7},{7,6},{8,9},{9,8},{10,11... | collective-permute-start | bytes 3145736 | tf_op jit(solution)/shard_map/ppermute | solution.py:376
  30.0 25.8 %copy-start.1 = (bf16[1,128,2048]{2,1,0:T(8,128)(2,1)S(1)}, bf16[1,128,2048]{2,1,0:T(8,128)(2,1)}, u32[]{:S(2)}) copy-start(bf16[1,128,2048]{2,1,0:T(8,128)(2,1)} %param.11) | copy-start | bytes 1572868
  31.5 24.3 %copy-start = (bf16[1,128,2048]{2,1,0:T(8,128)(2,1)S(1)}, bf16[1,128,2048]{2,1,0:T(8,128)(2,1)}, u32[]{:S(2)}) copy-start(bf16[1,128,2048]{2,1,0:T(8,128)(2,1)} %param.7) | copy-start | bytes 1572868
  31.5 5.6 %collective-permute-start.6 = (bf16[128,512]{1,0:T(8,128)(2,1)S(1)}, bf16[128,512]{1,0:T(8,128)(2,1)S(1)}, u32[]{:S(2)}, u32[]{:S(2)}) collective-permute-start(bf16[128,512]{1,0:T(8,128)(2,1)S(1)} %get-tuple-element.76), channel_id=1, source_target_pairs={{0,2},{2,0},{1,3},{3,1},{4,6},{6,4},{5,7},{7,5},{8,10},{10,8},{9,1... | collective-permute-start | bytes 393224 | tf_op jit(solution)/shard_map/ppermute | solution.py:376
  38.3 15.5 %collective-permute-start.10 = (bf16[144,512]{1,0:T(8,128)(2,1)S(1)}, bf16[144,512]{1,0:T(8,128)(2,1)S(1)}, u32[]{:S(2)}, u32[]{:S(2)}) collective-permute-start(bf16[144,512]{1,0:T(8,128)(2,1)S(1)} %get-tuple-element.82), channel_id=1, source_target_pairs={{0,4},{4,8},{8,12},{12,0},{1,5},{5,9},{9,13},{13,1},{2,6},{6,10},{... | collective-permute-start | bytes 442376 | tf_op jit(solution)/shard_map/ppermute | solution.py:367
  44.4 11.4 %collective-permute-start.11 = (bf16[144,512]{1,0:T(8,128)(2,1)S(1)}, bf16[144,512]{1,0:T(8,128)(2,1)S(1)}, u32[]{:S(2)}, u32[]{:S(2)}) collective-permute-start(bf16[144,512]{1,0:T(8,128)(2,1)S(1)} %get-tuple-element.83), channel_id=1, source_target_pairs={{0,8},{4,12},{8,0},{12,4},{1,9},{5,13},{9,1},{13,5},{2,10},{6,14},... | collective-permute-start | bytes 442376 | tf_op jit(solution)/shard_map/ppermute | solution.py:367
  46.0 9.8 %collective-permute-start.12 = (bf16[144,512]{1,0:T(8,128)(2,1)S(1)}, bf16[144,512]{1,0:T(8,128)(2,1)S(1)}, u32[]{:S(2)}, u32[]{:S(2)}) collective-permute-start(bf16[144,512]{1,0:T(8,128)(2,1)S(1)} %get-tuple-element.84), channel_id=1, source_target_pairs={{0,12},{4,0},{8,4},{12,8},{1,13},{5,1},{9,5},{13,9},{2,14},{6,2},{... | collective-permute-start | bytes 442376 | tf_op jit(solution)/shard_map/ppermute | solution.py:367
  46.8 25.6 %collective-permute-start.7 = (bf16[128,512]{1,0:T(8,128)(2,1)}, bf16[128,512]{1,0:T(8,128)(2,1)}, u32[]{:S(2)}, u32[]{:S(2)}) collective-permute-start(bf16[128,512]{1,0:T(8,128)(2,1)} %get-tuple-element.80.refs_0_), channel_id=1, source_target_pairs={{0,4},{4,8},{8,12},{1,5},{5,9},{9,13},{2,6},{6,10},{10,14},{3,7},{... | collective-permute-start | bytes 393224 | tf_op jit(solution)/shard_map/ppermute | solution.py:370
  50.6 22.5 %collective-permute-start.8 = (bf16[128,512]{1,0:T(8,128)(2,1)}, bf16[128,512]{1,0:T(8,128)(2,1)}, u32[]{:S(2)}, u32[]{:S(2)}) collective-permute-start(bf16[128,512]{1,0:T(8,128)(2,1)} %get-tuple-element.80.refs_0_), channel_id=1, source_target_pairs={{0,8},{4,12},{1,9},{5,13},{2,10},{6,14},{3,11},{7,15},{16,24},{20,... | collective-permute-start | bytes 393224 | tf_op jit(solution)/shard_map/ppermute | solution.py:370
  53.8 19.2 %collective-permute-start.9 = (bf16[128,512]{1,0:T(8,128)(2,1)}, bf16[128,512]{1,0:T(8,128)(2,1)}, u32[]{:S(2)}, u32[]{:S(2)}) collective-permute-start(bf16[128,512]{1,0:T(8,128)(2,1)} %get-tuple-element.80.refs_0_), channel_id=1, source_target_pairs={{0,12},{1,13},{2,14},{3,15},{16,28},{17,29},{18,30},{19,31}} | collective-permute-start | bytes 393224 | tf_op jit(solution)/shard_map/ppermute | solution.py:370
  55.8 4.3 %copy-start.3 = (bf16[144,512]{1,0:T(8,128)(2,1)}, bf16[144,512]{1,0:T(8,128)(2,1)S(1)}, u32[]{:S(2)}) copy-start(bf16[144,512]{1,0:T(8,128)(2,1)S(1)} %collective-permute-done.12.refs_3_.refs_2_) | copy-start | bytes 442372
  60.1 18.1 %collective-permute-start.13 = (bf16[128,512]{1,0:T(8,128)(2,1)}, bf16[128,512]{1,0:T(8,128)(2,1)}, u32[]{:S(2)}, u32[]{:S(2)}) collective-permute-start(bf16[128,512]{1,0:T(8,128)(2,1)} %get-tuple-element.94), channel_id=1, source_target_pairs={{0,12},{4,0},{8,4},{12,8},{1,13},{5,1},{9,5},{13,9},{2,14},{6,2},{... | collective-permute-start | bytes 393224 | tf_op jit(solution)/shard_map/ppermute | solution.py:367
  72.4 8.0 %collective-permute-start.14 = (bf16[128,512]{1,0:T(8,128)(2,1)}, bf16[128,512]{1,0:T(8,128)(2,1)}, u32[]{:S(2)}, u32[]{:S(2)}) collective-permute-start(bf16[128,512]{1,0:T(8,128)(2,1)} %get-tuple-element.95), channel_id=1, source_target_pairs={{0,8},{4,12},{8,0},{12,4},{1,9},{5,13},{9,1},{13,5},{2,10},{6,14},... | collective-permute-start | bytes 393224 | tf_op jit(solution)/shard_map/ppermute | solution.py:367
  72.4 8.0 %collective-permute-start.15 = (bf16[128,512]{1,0:T(8,128)(2,1)}, bf16[128,512]{1,0:T(8,128)(2,1)}, u32[]{:S(2)}, u32[]{:S(2)}) collective-permute-start(bf16[128,512]{1,0:T(8,128)(2,1)} %get-tuple-element.96), channel_id=1, source_target_pairs={{0,4},{4,8},{8,12},{12,0},{1,5},{5,9},{9,13},{13,1},{2,6},{6,10},{... | collective-permute-start | bytes 393224 | tf_op jit(solution)/shard_map/ppermute | solution.py:367
  73.1 11.8 %copy-start.11 = (f32[128,512]{1,0:T(8,128)S(1)}, f32[128,512]{1,0:T(8,128)}, u32[]{:S(2)}) copy-start(f32[128,512]{1,0:T(8,128)} %get-tuple-element.109) | copy-start | bytes 786436
  80.4 7.7 %collective-permute-start.16 = (bf16[128,512]{1,0:T(8,128)(2,1)S(1)}, bf16[128,512]{1,0:T(8,128)(2,1)S(1)}, u32[]{:S(2)}, u32[]{:S(2)}) collective-permute-start(bf16[128,512]{1,0:T(8,128)(2,1)S(1)} %get-tuple-element.97), channel_id=1, source_target_pairs={{4,0},{8,4},{12,8},{5,1},{9,5},{13,9},{6,2},{10,6},{14,10},{7,3},{... | collective-permute-start | bytes 393224 | tf_op jit(solution)/shard_map/ppermute | solution.py:373
  81.7 16.9 %collective-permute-start.17 = (bf16[128,512]{1,0:T(8,128)(2,1)S(1)}, bf16[128,512]{1,0:T(8,128)(2,1)S(1)}, u32[]{:S(2)}, u32[]{:S(2)}) collective-permute-start(bf16[128,512]{1,0:T(8,128)(2,1)S(1)} %get-tuple-element.98), channel_id=1, source_target_pairs={{8,0},{12,4},{9,1},{13,5},{10,2},{14,6},{11,3},{15,7},{24,16},{28,... | collective-permute-start | bytes 393224 | tf_op jit(solution)/shard_map/ppermute | solution.py:373
  83.0 15.6 %collective-permute-start.18 = (bf16[128,512]{1,0:T(8,128)(2,1)S(1)}, bf16[128,512]{1,0:T(8,128)(2,1)S(1)}, u32[]{:S(2)}, u32[]{:S(2)}) collective-permute-start(bf16[128,512]{1,0:T(8,128)(2,1)S(1)} %get-tuple-element.99), channel_id=1, source_target_pairs={{12,0},{13,1},{14,2},{15,3},{28,16},{29,17},{30,18},{31,19}} | collective-permute-start | bytes 393224 | tf_op jit(solution)/shard_map/ppermute | solution.py:373
  84.3 32.4 %collective-permute-start.22 = (bf16[1024,512]{1,0:T(8,128)(2,1)S(1)}, bf16[1024,512]{1,0:T(8,128)(2,1)S(1)}, u32[]{:S(2)}, u32[]{:S(2)}) collective-permute-start(bf16[1024,512]{1,0:T(8,128)(2,1)S(1)} %constant_dynamic-update-slice_fusion.w_own.refs_2_), channel_id=1, source_target_pairs={{0,2},{2,0},{1,3},{3,1},{4,6},{6,4},{5,7},{7,5},{8,10},{10,8},{9,1... | collective-permute-start | bytes 3145736 | tf_op jit(solution)/shard_map/ppermute | solution.py:376
  84.9 13.7 %copy-start.10 = (f32[128,512]{1,0:T(8,128)S(1)}, f32[128,512]{1,0:T(8,128)}, u32[]{:S(2)}) copy-start(f32[128,512]{1,0:T(8,128)} %get-tuple-element.90) | copy-start | bytes 786436
  86.0 12.7 %collective-permute-start.23 = (bf16[128,512]{1,0:T(8,128)(2,1)S(1)}, bf16[128,512]{1,0:T(8,128)(2,1)S(1)}, u32[]{:S(2)}, u32[]{:S(2)}) collective-permute-start(bf16[128,512]{1,0:T(8,128)(2,1)S(1)} %add_convert_fusion.refs_0_), channel_id=1, source_target_pairs={{0,4},{4,8},{8,12},{12,0},{1,5},{5,9},{9,13},{13,1},{2,6},{6,10},{... | collective-permute-start | bytes 393224 | tf_op jit(solution)/shard_map/ppermute | solution.py:367
  88.0 13.0 %collective-permute-start.24 = (bf16[128,512]{1,0:T(8,128)(2,1)S(1)}, bf16[128,512]{1,0:T(8,128)(2,1)S(1)}, u32[]{:S(2)}, u32[]{:S(2)}) collective-permute-start(bf16[128,512]{1,0:T(8,128)(2,1)S(1)} %add_convert_fusion.refs_0_), channel_id=1, source_target_pairs={{0,8},{4,12},{8,0},{12,4},{1,9},{5,13},{9,1},{13,5},{2,10},{6,14},... | collective-permute-start | bytes 393224 | tf_op jit(solution)/shard_map/ppermute | solution.py:367
  98.6 5.0 %collective-permute-start.25 = (bf16[128,512]{1,0:T(8,128)(2,1)S(1)}, bf16[128,512]{1,0:T(8,128)(2,1)S(1)}, u32[]{:S(2)}, u32[]{:S(2)}) collective-permute-start(bf16[128,512]{1,0:T(8,128)(2,1)S(1)} %add_convert_fusion.refs_0_), channel_id=1, source_target_pairs={{0,12},{4,0},{8,4},{12,8},{1,13},{5,1},{9,5},{13,9},{2,14},{6,2},{... | collective-permute-start | bytes 393224 | tf_op jit(solution)/shard_map/ppermute | solution.py:367
  98.7 8.9 %copy-start.4 = (bf16[144,512]{1,0:T(8,128)(2,1)S(1)}, bf16[144,512]{1,0:T(8,128)(2,1)}, u32[]{:S(2)}) copy-start(bf16[144,512]{1,0:T(8,128)(2,1)} %copy-done.3) | copy-start | bytes 442372
  98.7 8.9 %copy-start.8 = (bf16[128,512]{1,0:T(8,128)(2,1)S(1)}, bf16[128,512]{1,0:T(8,128)(2,1)}, u32[]{:S(2)}) copy-start(bf16[128,512]{1,0:T(8,128)(2,1)} %copy-done.7) | copy-start | bytes 393220
  103.6 5.2 %collective-permute-start.26 = (bf16[512,512]{1,0:T(8,128)(2,1)S(1)}, bf16[512,512]{1,0:T(8,128)(2,1)S(1)}, u32[]{:S(2)}, u32[]{:S(2)}) collective-permute-start(bf16[512,512]{1,0:T(8,128)(2,1)S(1)} %pad_maximum_fusion.1.g_own), channel_id=1, source_target_pairs={{0,1},{1,0},{2,3},{3,2},{4,5},{5,4},{6,7},{7,6},{8,9},{9,8},{10,11... | collective-permute-start | bytes 1572872 | tf_op jit(solution)/shard_map/ppermute | solution.py:376
  103.7 8.3 %collective-permute-start.19 = (bf16[128,512]{1,0:T(8,128)(2,1)S(1)}, bf16[128,512]{1,0:T(8,128)(2,1)S(1)}, u32[]{:S(2)}, u32[]{:S(2)}) collective-permute-start(bf16[128,512]{1,0:T(8,128)(2,1)S(1)} %add_convert_fusion.1.refs_1_), channel_id=1, source_target_pairs={{0,4},{4,8},{8,12},{12,0},{1,5},{5,9},{9,13},{13,1},{2,6},{6,10},{... | collective-permute-start | bytes 393224 | tf_op jit(solution)/shard_map/ppermute | solution.py:367
  103.7 13.0 %collective-permute-start.20 = (bf16[128,512]{1,0:T(8,128)(2,1)S(1)}, bf16[128,512]{1,0:T(8,128)(2,1)S(1)}, u32[]{:S(2)}, u32[]{:S(2)}) collective-permute-start(bf16[128,512]{1,0:T(8,128)(2,1)S(1)} %add_convert_fusion.1.refs_1_), channel_id=1, source_target_pairs={{0,8},{4,12},{8,0},{12,4},{1,9},{5,13},{9,1},{13,5},{2,10},{6,14},... | collective-permute-start | bytes 393224 | tf_op jit(solution)/shard_map/ppermute | solution.py:367
  106.1 10.6 %collective-permute-start.21 = (bf16[128,512]{1,0:T(8,128)(2,1)S(1)}, bf16[128,512]{1,0:T(8,128)(2,1)S(1)}, u32[]{:S(2)}, u32[]{:S(2)}) collective-permute-start(bf16[128,512]{1,0:T(8,128)(2,1)S(1)} %add_convert_fusion.1.refs_1_), channel_id=1, source_target_pairs={{0,12},{4,0},{8,4},{12,8},{1,13},{5,1},{9,5},{13,9},{2,14},{6,2},{... | collective-permute-start | bytes 393224 | tf_op jit(solution)/shard_map/ppermute | solution.py:367
  109.2 8.2 %collective-permute-start.27 = (bf16[256,512]{1,0:T(8,128)(2,1)S(1)}, bf16[256,512]{1,0:T(8,128)(2,1)S(1)}, u32[]{:S(2)}, u32[]{:S(2)}) collective-permute-start(bf16[256,512]{1,0:T(8,128)(2,1)S(1)} %weight_grad.2.refs_0_), channel_id=1, source_target_pairs={{0,2},{2,0},{1,3},{3,1},{4,6},{6,4},{5,7},{7,5},{8,10},{10,8},{9,1... | collective-permute-start | bytes 786440 | tf_op jit(solution)/shard_map/ppermute | solution.py:376
  116.7 4.4 %collective-permute-start.30 = (bf16[1024,512]{1,0:T(8,128)(2,1)S(1)}, bf16[1024,512]{1,0:T(8,128)(2,1)S(1)}, u32[]{:S(2)}, u32[]{:S(2)}) collective-permute-start(bf16[1024,512]{1,0:T(8,128)(2,1)S(1)} %collective-permute-done.22.refs_4_), channel_id=1, source_target_pairs={{0,1},{1,0},{2,3},{3,2},{4,5},{5,4},{6,7},{7,6},{8,9},{9,8},{10,11... | collective-permute-start | bytes 3145736 | tf_op jit(solution)/shard_map/ppermute | solution.py:376
  117.4 2.7 %collective-permute-start.28 = (bf16[512,512]{1,0:T(8,128)(2,1)S(1)}, bf16[512,512]{1,0:T(8,128)(2,1)S(1)}, u32[]{:S(2)}, u32[]{:S(2)}) collective-permute-start(bf16[512,512]{1,0:T(8,128)(2,1)S(1)} %pad_maximum_fusion.g_own), channel_id=1, source_target_pairs={{0,1},{1,0},{2,3},{3,2},{4,5},{5,4},{6,7},{7,6},{8,9},{9,8},{10,11... | collective-permute-start | bytes 1572872 | tf_op jit(solution)/shard_map/ppermute | solution.py:376
  120.5 8.4 %collective-permute-start.29 = (bf16[256,512]{1,0:T(8,128)(2,1)S(1)}, bf16[256,512]{1,0:T(8,128)(2,1)S(1)}, u32[]{:S(2)}, u32[]{:S(2)}) collective-permute-start(bf16[256,512]{1,0:T(8,128)(2,1)S(1)} %weight_grad.3.refs_2_), channel_id=1, source_target_pairs={{0,2},{2,0},{1,3},{3,1},{4,6},{6,4},{5,7},{7,5},{8,10},{10,8},{9,1... | collective-permute-start | bytes 786440 | tf_op jit(solution)/shard_map/ppermute | solution.py:376

commit v8 on v7

--- a/solution.py
+++ b/solution.py
@@ -148,6 +148,8 @@
 
 def attend_kernel(place, q_ref, do_ref, *refs, count, block, opening):
     pair_refs, refs = refs[:count], refs[count:]
+    if not opening:
+        value_refs, refs = refs[:count], refs[count:]
     if opening:
         cols = refs[: count - 1]
         ctx_ref, dq_ref, bias = refs[count - 1 : count + 2]
@@ -176,8 +178,12 @@
     even = place[2] == 0
     at_key = pl.multiple_of(pl.program_id(0) * HEAD_DIM, HEAD_DIM)
     at_value = pl.multiple_of(at_key + KV_WIDTH // PARTS, HEAD_DIM)
-    a = jnp.concatenate([r[:block, pl.ds(at_key, HEAD_DIM)] for r in pair_refs], axis=0)
-    b = jnp.concatenate([r[:block, pl.ds(at_value, HEAD_DIM)] for r in pair_refs], axis=0)
+    if opening:
+        a = [r[:block, pl.ds(at_key, HEAD_DIM)] for r in pair_refs]
+        b = [r[:block, pl.ds(at_value, HEAD_DIM)] for r in pair_refs]
+    else:
+        a, b = [r[...] for r in pair_refs], [r[...] for r in value_refs]
+    a, b = jnp.concatenate(a, axis=0), jnp.concatenate(b, axis=0)
     key = jnp.where(even, a, b)
     value = jnp.where(even, b, a)
 
@@ -239,9 +245,14 @@
         aliases = {}
     else:
         context, query_grad, mask = before
+        operands += far(*pairs)
+        in_specs = [wide, wide]
+        in_specs += [pl.BlockSpec((block, HEAD_DIM), lambda g, place: (0, g))] * count
+        in_specs += [pl.BlockSpec((block, HEAD_DIM), lambda g, place: (0, steps + g))] * count
         aliases = {len(operands) + 1: 0, len(operands) + 2: 1}
         operands += [*far(mask), context, query_grad]
-        in_specs += [vspec()] + [pl.BlockSpec(memory_space=pl.ANY)] * 2
+        in_specs += [pl.BlockSpec((block, count * block), lambda g, place: (0, 0))]
+        in_specs += [pl.BlockSpec(memory_space=pl.ANY)] * 2
         out_specs = [wide, wide] + [vspec()] * count
         out_shape = [rows, rows]
     outs = pl.pallas_call(

time: 131 us -> 131 us (level)
  no operation moved by 1% of the time
where the time goes in v8:
time: 131 us; the launch traced here: 130 us
  starting transfers between devices  54.5 us (42%)
  waiting for transfers between devices  51.8 us (40%)
  Pallas kernels  19.1 us (15%)
  other arithmetic  2.35 us (2%)
  local copies, waits for them, and re-layouts  1.56 us (1%)
    ppermute x15, starting transfers between devices, around(): return lax.ppermute(x, 'seq', [(i, (i + k) % n) for i in range(n)])  36 us
    ppermute x15, waiting for transfers between devices, around(): return lax.ppermute(x, 'seq', [(i, (i + k) % n) for i in range(n)])  28.7 us
    ppermute x10, waiting for transfers between devices, pairwise(): lax.ppermute(x, axis, [(j, j ^ 1) for j in range(lax.axis_size(axis))])  15.8 us
    pallas_call x2, Pallas kernels, attend(): pl.pallas_call(functools.partial(attend_kernel, count=count, block=block,...  9.32 us
    ppermute x3, starting transfers between devices, up(): return lax.ppermute(x, 'seq', [(i, i + k) for i in range(n - k)])  8.99 us
    ppermute x3, waiting for transfers between devices, down(): return lax.ppermute(x, 'seq', [(i, i - k) for i in range(k, n)])  7.26 us
    ppermute x10, starting transfers between devices, pairwise(): lax.ppermute(x, axis, [(j, j ^ 1) for j in range(lax.axis_size(axis))])  5.61 us
    ppermute x3, starting transfers between devices, down(): return lax.ppermute(x, 'seq', [(i, i - k) for i in range(k, n)])  3.87 us
  transfers between devices with their start and end apart: 31, of which 13 were waited for; matrix products, arithmetic and copies ran while one was open for 2% of the time, Pallas kernels for 12%

profile of v8, /device:TPU:0, one launch (start us, length us, event | category | flops | bytes accessed | tf_op | source)
XLA Modules:
  0.0 130.3 jit_solution(3205265311381056999)
XLA Ops:
  0.6 0.5 collective-permute-start.4
  1.2 2.6 %collective-permute-start.3 = (bf16[128,2048]{1,0:T(8,128)(2,1)}, bf16[128,2048]{1,0:T(8,128)(2,1)S(1)}, u32[]{:S(2)}, u32[]{:S(2)}) collective-permute-start(bf16[128,2048]{1,0:T(8,128)(2,1)} %bitcast.14), channel_id=1, source_target_pairs={{0,2},{2,0},{1,3},{3,1},{4,6},{6,4},{5,7},{7,5},{8,10},{10,8},{9,1... | collective-permute-start | bytes 1572872 | tf_op jit(solution)/shard_map/ppermute | solution.py:387
  3.7 1.0 broadcast_select_fusion
  4.7 1.6 %collective-permute-start = (bf16[256,512]{1,0:T(8,128)(2,1)S(1)}, bf16[256,512]{1,0:T(8,128)(2,1)S(1)}, u32[]{:S(2)}, u32[]{:S(2)}) collective-permute-start(bf16[256,512]{1,0:T(8,128)(2,1)S(1)} %broadcast_select_fusion), channel_id=1, source_target_pairs={{0,4},{4,8},{8,12},{12,0},{1,5},{5,9},{9,13},{13,1},{2,6},{6,10},{... | collective-permute-start | bytes 786440 | tf_op jit(solution)/shard_map/ppermute | solution.py:378
  6.3 2.6 %collective-permute-start.1 = (bf16[256,512]{1,0:T(8,128)(2,1)S(1)}, bf16[256,512]{1,0:T(8,128)(2,1)S(1)}, u32[]{:S(2)}, u32[]{:S(2)}) collective-permute-start(bf16[256,512]{1,0:T(8,128)(2,1)S(1)} %broadcast_select_fusion), channel_id=1, source_target_pairs={{0,8},{4,12},{8,0},{12,4},{1,9},{5,13},{9,1},{13,5},{2,10},{6,14},... | collective-permute-start | bytes 786440 | tf_op jit(solution)/shard_map/ppermute | solution.py:378
  8.9 1.3 %collective-permute-start.2 = (bf16[256,512]{1,0:T(8,128)(2,1)S(1)}, bf16[256,512]{1,0:T(8,128)(2,1)S(1)}, u32[]{:S(2)}, u32[]{:S(2)}) collective-permute-start(bf16[256,512]{1,0:T(8,128)(2,1)S(1)} %broadcast_select_fusion), channel_id=1, source_target_pairs={{0,12},{4,0},{8,4},{12,8},{1,13},{5,1},{9,5},{13,9},{2,14},{6,2},{... | collective-permute-start | bytes 786440 | tf_op jit(solution)/shard_map/ppermute | solution.py:378
  10.3 0.1 pad_add_fusion.place
  10.4 0.0 collective-permute-done.4.other
  10.4 0.6 cut.1
  11.0 0.6 copy-done.7
  11.6 4.2 %collective-permute-done = bf16[256,512]{1,0:T(8,128)(2,1)S(1)} collective-permute-done((bf16[256,512]{1,0:T(8,128)(2,1)S(1)}, bf16[256,512]{1,0:T(8,128)(2,1)S(1)}, u32[]{:S(2)}, u32[]{:S(2)}) %collective-permute-start) | collective-permute-done | bytes 262176 | tf_op jit(solution)/shard_map/ppermute | solution.py:378
  15.8 10.5 %collective-permute-done.1 = bf16[256,512]{1,0:T(8,128)(2,1)S(1)} collective-permute-done((bf16[256,512]{1,0:T(8,128)(2,1)S(1)}, bf16[256,512]{1,0:T(8,128)(2,1)S(1)}, u32[]{:S(2)}, u32[]{:S(2)}) %collective-permute-start.1) | collective-permute-done | bytes 262176 | tf_op jit(solution)/shard_map/ppermute | solution.py:378
  26.4 0.0 collective-permute-done.2
  26.4 0.0 collective-permute-done.3.x_next
  26.4 0.8 copy-done.5
  27.2 0.0 copy-start.6
  27.3 0.0 copy-start.9
  27.3 0.1 collective-permute-start.5
  27.4 2.6 %collective-permute-done.5.w_other.refs_3_ = bf16[1024,512]{1,0:T(8,128)(2,1)S(1)} collective-permute-done((bf16[1024,512]{1,0:T(8,128)(2,1)S(1)}, bf16[1024,512]{1,0:T(8,128)(2,1)S(1)}, u32[]{:S(2)}, u32[]{:S(2)}) %collective-permute-start.5) | collective-permute-done | bytes 1048608 | tf_op jit(solution)/shard_map/ppermute | solution.py:387
  30.0 1.4 %project.1 = (bf16[144,512]{1,0:T(8,128)(2,1)S(1)}, bf16[128,512]{1,0:T(8,128)(2,1)S(1)}) custom-call(s32[3]{0:T(128)S(1)} %pad_add_fusion.place, s32[1,128]{1,0:T(1,128)S(1)} %copy-done.9, bf16[128,2048]{1,0:T(8,128)(2,1)S(1)} %bitcast.16, bf16[128,2048]{1,0:T(8,128)(2,1)S(1)} %copy-done.6, ...), custom_call_target="tpu_custom_call" | custom-call | tf_op jit(solution)/shard_map/project/pallas_call | solution.py:70
  31.5 0.0 copy-start
  31.5 0.6 collective-permute-start.6
  32.1 5.0 %collective-permute-done.6.mate = bf16[128,512]{1,0:T(8,128)(2,1)S(1)} collective-permute-done((bf16[128,512]{1,0:T(8,128)(2,1)S(1)}, bf16[128,512]{1,0:T(8,128)(2,1)S(1)}, u32[]{:S(2)}, u32[]{:S(2)}) %collective-permute-start.6) | collective-permute-done | bytes 131104 | tf_op jit(solution)/shard_map/ppermute | solution.py:387
  37.1 1.2 pack.1
  38.3 6.1 %collective-permute-start.10 = (bf16[144,512]{1,0:T(8,128)(2,1)S(1)}, bf16[144,512]{1,0:T(8,128)(2,1)S(1)}, u32[]{:S(2)}, u32[]{:S(2)}) collective-permute-start(bf16[144,512]{1,0:T(8,128)(2,1)S(1)} %get-tuple-element.82), channel_id=1, source_target_pairs={{0,4},{4,8},{8,12},{12,0},{1,5},{5,9},{9,13},{13,1},{2,6},{6,10},{... | collective-permute-start | bytes 442376 | tf_op jit(solution)/shard_map/ppermute | solution.py:378
  44.4 1.6 %collective-permute-start.11 = (bf16[144,512]{1,0:T(8,128)(2,1)S(1)}, bf16[144,512]{1,0:T(8,128)(2,1)S(1)}, u32[]{:S(2)}, u32[]{:S(2)}) collective-permute-start(bf16[144,512]{1,0:T(8,128)(2,1)S(1)} %get-tuple-element.83), channel_id=1, source_target_pairs={{0,8},{4,12},{8,0},{12,4},{1,9},{5,13},{9,1},{13,5},{2,10},{6,14},... | collective-permute-start | bytes 442376 | tf_op jit(solution)/shard_map/ppermute | solution.py:378
  46.0 0.8 collective-permute-start.12
  46.8 3.8 %collective-permute-start.7 = (bf16[128,512]{1,0:T(8,128)(2,1)}, bf16[128,512]{1,0:T(8,128)(2,1)}, u32[]{:S(2)}, u32[]{:S(2)}) collective-permute-start(bf16[128,512]{1,0:T(8,128)(2,1)} %get-tuple-element.80.refs_0_.refs_4_), channel_id=1, source_target_pairs={{0,4},{4,8},{8,12},{1,5},{5,9},{9,13},{2,6},{6,10},{10,14},{3,7},{... | collective-permute-start | bytes 393224 | tf_op jit(solution)/shard_map/ppermute | solution.py:381
  50.6 3.3 %collective-permute-start.8 = (bf16[128,512]{1,0:T(8,128)(2,1)}, bf16[128,512]{1,0:T(8,128)(2,1)}, u32[]{:S(2)}, u32[]{:S(2)}) collective-permute-start(bf16[128,512]{1,0:T(8,128)(2,1)} %get-tuple-element.80.refs_0_.refs_4_), channel_id=1, source_target_pairs={{0,8},{4,12},{1,9},{5,13},{2,10},{6,14},{3,11},{7,15},{16,24},{20,... | collective-permute-start | bytes 393224 | tf_op jit(solution)/shard_map/ppermute | solution.py:381
  53.8 0.0 collective-permute-done.10.refs_1_.refs_0_
  53.8 1.9 %collective-permute-start.9 = (bf16[128,512]{1,0:T(8,128)(2,1)}, bf16[128,512]{1,0:T(8,128)(2,1)}, u32[]{:S(2)}, u32[]{:S(2)}) collective-permute-start(bf16[128,512]{1,0:T(8,128)(2,1)} %get-tuple-element.80.refs_0_.refs_4_), channel_id=1, source_target_pairs={{0,12},{1,13},{2,14},{3,15},{16,28},{17,29},{18,30},{19,31}} | collective-permute-start | bytes 393224 | tf_op jit(solution)/shard_map/ppermute | solution.py:381
  55.8 4.3 %attend.2 = (bf16[128,2048]{1,0:T(8,128)(2,1)}, bf16[128,2048]{1,0:T(8,128)(2,1)}, f32[128,512]{1,0:T(8,128)}, bf16[128,512]{1,0:T(8,128)(2,1)}, bf16[128,512]{1...) custom-call(s32[3]{0:T(128)S(1)} %pad_add_fusion.place, bf16[128,2048]{1,0:T(8,128)(2,1)S(1)} %bitcast.9, ...), custom_call_target="tpu_custom_call" | custom-call | tf_op jit(solution)/shard_map/attend/pallas_call | solution.py:258
  60.1 12.3 %collective-permute-start.13 = (bf16[128,512]{1,0:T(8,128)(2,1)}, bf16[128,512]{1,0:T(8,128)(2,1)}, u32[]{:S(2)}, u32[]{:S(2)}) collective-permute-start(bf16[128,512]{1,0:T(8,128)(2,1)} %get-tuple-element.94), channel_id=1, source_target_pairs={{0,12},{4,0},{8,4},{12,8},{1,13},{5,1},{9,5},{13,9},{2,14},{6,2},{... | collective-permute-start | bytes 393224 | tf_op jit(solution)/shard_map/ppermute | solution.py:378
  72.4 0.0 collective-permute-start.14
  72.4 0.6 collective-permute-start.15
  73.1 5.0 %attend.3 = (bf16[128,2048]{1,0:T(8,128)(2,1)}, bf16[128,2048]{1,0:T(8,128)(2,1)}, bf16[128,512]{1,0:T(8,128)(2,1)S(1)}, bf16[128,512]{1,0:T(8,128)(2,1)S(1)}, b...) custom-call(s32[3]{0:T(128)S(1)} %pad_add_fusion.place, ...), custom_call_target="tpu_custom_call", output_to_operand_aliasing={{0}: (12, {}), {1}: (13, {})} | custom-call | tf_op jit(solution)/shard_map/attend/pallas_call | solution.py:258
  78.1 2.3 %collective-permute-done.14.refs_4_ = bf16[128,512]{1,0:T(8,128)(2,1)} collective-permute-done((bf16[128,512]{1,0:T(8,128)(2,1)}, bf16[128,512]{1,0:T(8,128)(2,1)}, u32[]{:S(2)}, u32[]{:S(2)}) %collective-permute-start.14) | collective-permute-done | bytes 131104 | tf_op jit(solution)/shard_map/ppermute | solution.py:378
  80.4 1.3 collective-permute-start.16
  81.7 1.3 collective-permute-start.17
  83.0 1.3 collective-permute-start.18
  84.3 0.6 collective-permute-start.22
  84.9 1.2 add_convert_fusion.refs_0_
  86.0 2.0 %collective-permute-start.23 = (bf16[128,512]{1,0:T(8,128)(2,1)S(1)}, bf16[128,512]{1,0:T(8,128)(2,1)S(1)}, u32[]{:S(2)}, u32[]{:S(2)}) collective-permute-start(bf16[128,512]{1,0:T(8,128)(2,1)S(1)} %add_convert_fusion.refs_0_), channel_id=1, source_target_pairs={{0,4},{4,8},{8,12},{12,0},{1,5},{5,9},{9,13},{13,1},{2,6},{6,10},{... | collective-permute-start | bytes 393224 | tf_op jit(solution)/shard_map/ppermute | solution.py:378
  88.0 3.2 %collective-permute-start.24 = (bf16[128,512]{1,0:T(8,128)(2,1)S(1)}, bf16[128,512]{1,0:T(8,128)(2,1)S(1)}, u32[]{:S(2)}, u32[]{:S(2)}) collective-permute-start(bf16[128,512]{1,0:T(8,128)(2,1)S(1)} %add_convert_fusion.refs_0_), channel_id=1, source_target_pairs={{0,8},{4,12},{8,0},{12,4},{1,9},{5,13},{9,1},{13,5},{2,10},{6,14},... | collective-permute-start | bytes 393224 | tf_op jit(solution)/shard_map/ppermute | solution.py:378
  91.2 7.3 %collective-permute-done.17 = bf16[128,512]{1,0:T(8,128)(2,1)S(1)} collective-permute-done((bf16[128,512]{1,0:T(8,128)(2,1)S(1)}, bf16[128,512]{1,0:T(8,128)(2,1)S(1)}, u32[]{:S(2)}, u32[]{:S(2)}) %collective-permute-start.17) | collective-permute-done | bytes 131104 | tf_op jit(solution)/shard_map/ppermute | solution.py:384
  98.5 0.1 add_convert_fusion.1.refs_1_
  98.6 2.5 %collective-permute-done.24 = bf16[128,512]{1,0:T(8,128)(2,1)S(1)} collective-permute-done((bf16[128,512]{1,0:T(8,128)(2,1)S(1)}, bf16[128,512]{1,0:T(8,128)(2,1)S(1)}, u32[]{:S(2)}, u32[]{:S(2)}) %collective-permute-start.24) | collective-permute-done | bytes 131104 | tf_op jit(solution)/shard_map/ppermute | solution.py:378
  101.0 2.4 %collective-permute-done.25 = bf16[128,512]{1,0:T(8,128)(2,1)S(1)} collective-permute-done((bf16[128,512]{1,0:T(8,128)(2,1)S(1)}, bf16[128,512]{1,0:T(8,128)(2,1)S(1)}, u32[]{:S(2)}, u32[]{:S(2)}) %collective-permute-start.25) | collective-permute-done | bytes 131104 | tf_op jit(solution)/shard_map/ppermute | solution.py:378
  103.5 0.1 collective-permute-start.26
  103.5 0.1 collective-permute-start.19
  103.6 2.4 %collective-permute-start.20 = (bf16[128,512]{1,0:T(8,128)(2,1)S(1)}, bf16[128,512]{1,0:T(8,128)(2,1)S(1)}, u32[]{:S(2)}, u32[]{:S(2)}) collective-permute-start(bf16[128,512]{1,0:T(8,128)(2,1)S(1)} %add_convert_fusion.1.refs_1_), channel_id=1, source_target_pairs={{0,8},{4,12},{8,0},{12,4},{1,9},{5,13},{9,1},{13,5},{2,10},{6,14},... | collective-permute-start | bytes 393224 | tf_op jit(solution)/shard_map/ppermute | solution.py:378
  106.0 1.5 %collective-permute-start.21 = (bf16[128,512]{1,0:T(8,128)(2,1)S(1)}, bf16[128,512]{1,0:T(8,128)(2,1)S(1)}, u32[]{:S(2)}, u32[]{:S(2)}) collective-permute-start(bf16[128,512]{1,0:T(8,128)(2,1)S(1)} %add_convert_fusion.1.refs_1_), channel_id=1, source_target_pairs={{0,12},{4,0},{8,4},{12,8},{1,13},{5,1},{9,5},{13,9},{2,14},{6,2},{... | collective-permute-start | bytes 393224 | tf_op jit(solution)/shard_map/ppermute | solution.py:378
  107.4 1.2 turn.1.x_turned
  108.7 0.4 weight_grad.2.refs_0_
  109.1 0.6 collective-permute-start.27
  109.7 2.1 %collective-permute-done.19 = bf16[128,512]{1,0:T(8,128)(2,1)S(1)} collective-permute-done((bf16[128,512]{1,0:T(8,128)(2,1)S(1)}, bf16[128,512]{1,0:T(8,128)(2,1)S(1)}, u32[]{:S(2)}, u32[]{:S(2)}) %collective-permute-start.19) | collective-permute-done | bytes 131104 | tf_op jit(solution)/shard_map/ppermute | solution.py:378
  111.8 4.7 %collective-permute-done.20 = bf16[128,512]{1,0:T(8,128)(2,1)S(1)} collective-permute-done((bf16[128,512]{1,0:T(8,128)(2,1)S(1)}, bf16[128,512]{1,0:T(8,128)(2,1)S(1)}, u32[]{:S(2)}, u32[]{:S(2)}) %collective-permute-start.20) | collective-permute-done | bytes 131104 | tf_op jit(solution)/shard_map/ppermute | solution.py:378
  116.6 0.7 collective-permute-done.27.refs_1_
  117.3 2.7 %collective-permute-done.28.g_other = bf16[512,512]{1,0:T(8,128)(2,1)S(1)} collective-permute-done((bf16[512,512]{1,0:T(8,128)(2,1)S(1)}, bf16[512,512]{1,0:T(8,128)(2,1)S(1)}, u32[]{:S(2)}, u32[]{:S(2)}) %collective-permute-start.28) | collective-permute-done | bytes 524320 | tf_op jit(solution)/shard_map/ppermute | solution.py:387
  120.0 0.4 weight_grad.3.refs_2_
  120.4 0.6 collective-permute-start.29
  121.0 3.0 %input_grad.1 = bf16[128,2048]{1,0:T(8,128)(2,1)} custom-call(s32[3]{0:T(128)S(1)} %pad_add_fusion.place, bf16[128,512]{1,0:T(8,128)(2,1)S(1)} %add_convert_fusion.refs_0_, bf16[128,512]{1,0:T(8,128)(2,1)S(1)} %add_convert_fusion.1.refs_1_, bf16[1024,512]{1,0:T(8,128)(2,1)S(1)} %constant_dynamic-update-slice_fusion.w_own.refs_2_, ...), custom_call_target="tpu_custom_call" | custom-call | tf_op jit(solution)/shard_map/input_grad/pallas_call | solution.py:288
  124.0 4.8 %collective-permute-done.29.refs_3_ = bf16[256,512]{1,0:T(8,128)(2,1)S(1)} collective-permute-done((bf16[256,512]{1,0:T(8,128)(2,1)S(1)}, bf16[256,512]{1,0:T(8,128)(2,1)S(1)}, u32[]{:S(2)}, u32[]{:S(2)}) %collective-permute-start.29) | collective-permute-done | bytes 262176 | tf_op jit(solution)/shard_map/ppermute | solution.py:387
  128.8 1.4 %finish.1 = (bf16[256,512]{1,0:T(8,128)(2,1)}, bf16[256,512]{1,0:T(8,128)(2,1)}) custom-call(s32[3]{0:T(128)S(1)} %pad_add_fusion.place, bf16[256,512]{1,0:T(8,128)(2,1)S(1)} %weight_grad.2.refs_0_, bf16[256,512]{1,0:T(8,128)(2,1)S(1)} %collective-permute-done.27.refs_1_, bf16[256,512]{1,0:T(8,128)(2,1)S(1)} %weight_grad.3.refs_2_, ...), custom_call_target="tpu_custom_call" | custom-call | tf_op jit(solution)/shard_map/finish/pallas_call | solution.py:356
  (42 shorter events, 0.2 us)
Async XLA Ops:
  0.6 9.7 %copy-start.2 = (bf16[1,128,2048]{2,1,0:T(8,128)(2,1)S(1)}, bf16[1,128,2048]{2,1,0:T(8,128)(2,1)}, u32[]{:S(2)}) copy-start(bf16[1,128,2048]{2,1,0:T(8,128)(2,1)} %param.6) | copy-start | bytes 1572868
  0.6 9.7 %collective-permute-start.4 = (bf16[128,2048]{1,0:T(8,128)(2,1)}, bf16[128,2048]{1,0:T(8,128)(2,1)S(1)}, u32[]{:S(2)}, u32[]{:S(2)}) collective-permute-start(bf16[128,2048]{1,0:T(8,128)(2,1)} %bitcast.13), channel_id=1, source_target_pairs={{0,1},{1,0},{2,3},{3,2},{4,5},{5,4},{6,7},{7,6},{8,9},{9,8},{10,11... | collective-permute-start | bytes 1572872 | tf_op jit(solution)/shard_map/ppermute | solution.py:387
  1.2 25.2 %collective-permute-start.3 = (bf16[128,2048]{1,0:T(8,128)(2,1)}, bf16[128,2048]{1,0:T(8,128)(2,1)S(1)}, u32[]{:S(2)}, u32[]{:S(2)}) collective-permute-start(bf16[128,2048]{1,0:T(8,128)(2,1)} %bitcast.14), channel_id=1, source_target_pairs={{0,2},{2,0},{1,3},{3,1},{4,6},{6,4},{5,7},{7,5},{8,10},{10,8},{9,1... | collective-permute-start | bytes 1572872 | tf_op jit(solution)/shard_map/ppermute | solution.py:387
  4.7 11.1 %collective-permute-start = (bf16[256,512]{1,0:T(8,128)(2,1)S(1)}, bf16[256,512]{1,0:T(8,128)(2,1)S(1)}, u32[]{:S(2)}, u32[]{:S(2)}) collective-permute-start(bf16[256,512]{1,0:T(8,128)(2,1)S(1)} %broadcast_select_fusion), channel_id=1, source_target_pairs={{0,4},{4,8},{8,12},{12,0},{1,5},{5,9},{9,13},{13,1},{2,6},{6,10},{... | collective-permute-start | bytes 786440 | tf_op jit(solution)/shard_map/ppermute | solution.py:378
  6.3 20.0 %collective-permute-start.1 = (bf16[256,512]{1,0:T(8,128)(2,1)S(1)}, bf16[256,512]{1,0:T(8,128)(2,1)S(1)}, u32[]{:S(2)}, u32[]{:S(2)}) collective-permute-start(bf16[256,512]{1,0:T(8,128)(2,1)S(1)} %broadcast_select_fusion), channel_id=1, source_target_pairs={{0,8},{4,12},{8,0},{12,4},{1,9},{5,13},{9,1},{13,5},{2,10},{6,14},... | collective-permute-start | bytes 786440 | tf_op jit(solution)/shard_map/ppermute | solution.py:378
  8.9 17.4 %collective-permute-start.2 = (bf16[256,512]{1,0:T(8,128)(2,1)S(1)}, bf16[256,512]{1,0:T(8,128)(2,1)S(1)}, u32[]{:S(2)}, u32[]{:S(2)}) collective-permute-start(bf16[256,512]{1,0:T(8,128)(2,1)S(1)} %broadcast_select_fusion), channel_id=1, source_target_pairs={{0,12},{4,0},{8,4},{12,8},{1,13},{5,1},{9,5},{13,9},{2,14},{6,2},{... | collective-permute-start | bytes 786440 | tf_op jit(solution)/shard_map/ppermute | solution.py:378
  11.0 0.7 copy-start.7
  26.4 0.8 copy-start.5
  27.2 2.8 %copy-start.6 = (bf16[128,2048]{1,0:T(8,128)(2,1)S(1)}, bf16[128,2048]{1,0:T(8,128)(2,1)}, u32[]{:S(2)}) copy-start(bf16[128,2048]{1,0:T(8,128)(2,1)} %copy-done.5) | copy-start | bytes 1572868
  27.3 2.8 %copy-start.9 = (s32[1,128]{1,0:T(1,128)S(1)}, s32[1,128]{1,0:T(1,128)}, u32[]{:S(2)}) copy-start(s32[1,128]{1,0:T(1,128)} %seg.1) | copy-start | bytes 1540
  27.3 2.7 %collective-permute-start.5 = (bf16[1024,512]{1,0:T(8,128)(2,1)S(1)}, bf16[1024,512]{1,0:T(8,128)(2,1)S(1)}, u32[]{:S(2)}, u32[]{:S(2)}) collective-permute-start(bf16[1024,512]{1,0:T(8,128)(2,1)S(1)} %constant_dynamic-update-slice_fusion.w_own.refs_2_), channel_id=1, source_target_pairs={{0,1},{1,0},{2,3},{3,2},{4,5},{5,4},{6,7},{7,6},{8,9},{9,8},{10,11... | collective-permute-start | bytes 3145736 | tf_op jit(solution)/shard_map/ppermute | solution.py:387
  30.0 25.8 %copy-start.1 = (bf16[1,128,2048]{2,1,0:T(8,128)(2,1)S(1)}, bf16[1,128,2048]{2,1,0:T(8,128)(2,1)}, u32[]{:S(2)}) copy-start(bf16[1,128,2048]{2,1,0:T(8,128)(2,1)} %param.11) | copy-start | bytes 1572868
  31.5 24.3 %copy-start = (bf16[1,128,2048]{2,1,0:T(8,128)(2,1)S(1)}, bf16[1,128,2048]{2,1,0:T(8,128)(2,1)}, u32[]{:S(2)}) copy-start(bf16[1,128,2048]{2,1,0:T(8,128)(2,1)} %param.7) | copy-start | bytes 1572868
  31.5 5.6 %collective-permute-start.6 = (bf16[128,512]{1,0:T(8,128)(2,1)S(1)}, bf16[128,512]{1,0:T(8,128)(2,1)S(1)}, u32[]{:S(2)}, u32[]{:S(2)}) collective-permute-start(bf16[128,512]{1,0:T(8,128)(2,1)S(1)} %get-tuple-element.76), channel_id=1, source_target_pairs={{0,2},{2,0},{1,3},{3,1},{4,6},{6,4},{5,7},{7,5},{8,10},{10,8},{9,1... | collective-permute-start | bytes 393224 | tf_op jit(solution)/shard_map/ppermute | solution.py:387
  38.3 15.5 %collective-permute-start.10 = (bf16[144,512]{1,0:T(8,128)(2,1)S(1)}, bf16[144,512]{1,0:T(8,128)(2,1)S(1)}, u32[]{:S(2)}, u32[]{:S(2)}) collective-permute-start(bf16[144,512]{1,0:T(8,128)(2,1)S(1)} %get-tuple-element.82), channel_id=1, source_target_pairs={{0,4},{4,8},{8,12},{12,0},{1,5},{5,9},{9,13},{13,1},{2,6},{6,10},{... | collective-permute-start | bytes 442376 | tf_op jit(solution)/shard_map/ppermute | solution.py:378
  44.4 11.4 %collective-permute-start.11 = (bf16[144,512]{1,0:T(8,128)(2,1)S(1)}, bf16[144,512]{1,0:T(8,128)(2,1)S(1)}, u32[]{:S(2)}, u32[]{:S(2)}) collective-permute-start(bf16[144,512]{1,0:T(8,128)(2,1)S(1)} %get-tuple-element.83), channel_id=1, source_target_pairs={{0,8},{4,12},{8,0},{12,4},{1,9},{5,13},{9,1},{13,5},{2,10},{6,14},... | collective-permute-start | bytes 442376 | tf_op jit(solution)/shard_map/ppermute | solution.py:378
  46.0 9.8 %collective-permute-start.12 = (bf16[144,512]{1,0:T(8,128)(2,1)S(1)}, bf16[144,512]{1,0:T(8,128)(2,1)S(1)}, u32[]{:S(2)}, u32[]{:S(2)}) collective-permute-start(bf16[144,512]{1,0:T(8,128)(2,1)S(1)} %get-tuple-element.84), channel_id=1, source_target_pairs={{0,12},{4,0},{8,4},{12,8},{1,13},{5,1},{9,5},{13,9},{2,14},{6,2},{... | collective-permute-start | bytes 442376 | tf_op jit(solution)/shard_map/ppermute | solution.py:378
  46.8 25.6 %collective-permute-start.7 = (bf16[128,512]{1,0:T(8,128)(2,1)}, bf16[128,512]{1,0:T(8,128)(2,1)}, u32[]{:S(2)}, u32[]{:S(2)}) collective-permute-start(bf16[128,512]{1,0:T(8,128)(2,1)} %get-tuple-element.80.refs_0_.refs_4_), channel_id=1, source_target_pairs={{0,4},{4,8},{8,12},{1,5},{5,9},{9,13},{2,6},{6,10},{10,14},{3,7},{... | collective-permute-start | bytes 393224 | tf_op jit(solution)/shard_map/ppermute | solution.py:381
  50.6 22.5 %collective-permute-start.8 = (bf16[128,512]{1,0:T(8,128)(2,1)}, bf16[128,512]{1,0:T(8,128)(2,1)}, u32[]{:S(2)}, u32[]{:S(2)}) collective-permute-start(bf16[128,512]{1,0:T(8,128)(2,1)} %get-tuple-element.80.refs_0_.refs_4_), channel_id=1, source_target_pairs={{0,8},{4,12},{1,9},{5,13},{2,10},{6,14},{3,11},{7,15},{16,24},{20,... | collective-permute-start | bytes 393224 | tf_op jit(solution)/shard_map/ppermute | solution.py:381
  53.8 19.2 %collective-permute-start.9 = (bf16[128,512]{1,0:T(8,128)(2,1)}, bf16[128,512]{1,0:T(8,128)(2,1)}, u32[]{:S(2)}, u32[]{:S(2)}) collective-permute-start(bf16[128,512]{1,0:T(8,128)(2,1)} %get-tuple-element.80.refs_0_.refs_4_), channel_id=1, source_target_pairs={{0,12},{1,13},{2,14},{3,15},{16,28},{17,29},{18,30},{19,31}} | collective-permute-start | bytes 393224 | tf_op jit(solution)/shard_map/ppermute | solution.py:381
  55.8 4.3 %copy-start.3 = (bf16[144,512]{1,0:T(8,128)(2,1)}, bf16[144,512]{1,0:T(8,128)(2,1)S(1)}, u32[]{:S(2)}) copy-start(bf16[144,512]{1,0:T(8,128)(2,1)S(1)} %collective-permute-done.12.refs_3_.refs_2_) | copy-start | bytes 442372
  60.1 18.0 %collective-permute-start.13 = (bf16[128,512]{1,0:T(8,128)(2,1)}, bf16[128,512]{1,0:T(8,128)(2,1)}, u32[]{:S(2)}, u32[]{:S(2)}) collective-permute-start(bf16[128,512]{1,0:T(8,128)(2,1)} %get-tuple-element.94), channel_id=1, source_target_pairs={{0,12},{4,0},{8,4},{12,8},{1,13},{5,1},{9,5},{13,9},{2,14},{6,2},{... | collective-permute-start | bytes 393224 | tf_op jit(solution)/shard_map/ppermute | solution.py:378
  72.4 8.0 %collective-permute-start.14 = (bf16[128,512]{1,0:T(8,128)(2,1)}, bf16[128,512]{1,0:T(8,128)(2,1)}, u32[]{:S(2)}, u32[]{:S(2)}) collective-permute-start(bf16[128,512]{1,0:T(8,128)(2,1)} %get-tuple-element.95), channel_id=1, source_target_pairs={{0,8},{4,12},{8,0},{12,4},{1,9},{5,13},{9,1},{13,5},{2,10},{6,14},... | collective-permute-start | bytes 393224 | tf_op jit(solution)/shard_map/ppermute | solution.py:378
  72.4 8.0 %collective-permute-start.15 = (bf16[128,512]{1,0:T(8,128)(2,1)}, bf16[128,512]{1,0:T(8,128)(2,1)}, u32[]{:S(2)}, u32[]{:S(2)}) collective-permute-start(bf16[128,512]{1,0:T(8,128)(2,1)} %get-tuple-element.96), channel_id=1, source_target_pairs={{0,4},{4,8},{8,12},{12,0},{1,5},{5,9},{9,13},{13,1},{2,6},{6,10},{... | collective-permute-start | bytes 393224 | tf_op jit(solution)/shard_map/ppermute | solution.py:378
  73.1 11.8 %copy-start.11 = (f32[128,512]{1,0:T(8,128)S(1)}, f32[128,512]{1,0:T(8,128)}, u32[]{:S(2)}) copy-start(f32[128,512]{1,0:T(8,128)} %get-tuple-element.109) | copy-start | bytes 786436
  80.4 7.7 %collective-permute-start.16 = (bf16[128,512]{1,0:T(8,128)(2,1)S(1)}, bf16[128,512]{1,0:T(8,128)(2,1)S(1)}, u32[]{:S(2)}, u32[]{:S(2)}) collective-permute-start(bf16[128,512]{1,0:T(8,128)(2,1)S(1)} %get-tuple-element.97), channel_id=1, source_target_pairs={{4,0},{8,4},{12,8},{5,1},{9,5},{13,9},{6,2},{10,6},{14,10},{7,3},{... | collective-permute-start | bytes 393224 | tf_op jit(solution)/shard_map/ppermute | solution.py:384
  81.7 16.8 %collective-permute-start.17 = (bf16[128,512]{1,0:T(8,128)(2,1)S(1)}, bf16[128,512]{1,0:T(8,128)(2,1)S(1)}, u32[]{:S(2)}, u32[]{:S(2)}) collective-permute-start(bf16[128,512]{1,0:T(8,128)(2,1)S(1)} %get-tuple-element.98), channel_id=1, source_target_pairs={{8,0},{12,4},{9,1},{13,5},{10,2},{14,6},{11,3},{15,7},{24,16},{28,... | collective-permute-start | bytes 393224 | tf_op jit(solution)/shard_map/ppermute | solution.py:384
  83.0 15.5 %collective-permute-start.18 = (bf16[128,512]{1,0:T(8,128)(2,1)S(1)}, bf16[128,512]{1,0:T(8,128)(2,1)S(1)}, u32[]{:S(2)}, u32[]{:S(2)}) collective-permute-start(bf16[128,512]{1,0:T(8,128)(2,1)S(1)} %get-tuple-element.99), channel_id=1, source_target_pairs={{12,0},{13,1},{14,2},{15,3},{28,16},{29,17},{30,18},{31,19}} | collective-permute-start | bytes 393224 | tf_op jit(solution)/shard_map/ppermute | solution.py:384
  84.3 32.3 %collective-permute-start.22 = (bf16[1024,512]{1,0:T(8,128)(2,1)S(1)}, bf16[1024,512]{1,0:T(8,128)(2,1)S(1)}, u32[]{:S(2)}, u32[]{:S(2)}) collective-permute-start(bf16[1024,512]{1,0:T(8,128)(2,1)S(1)} %constant_dynamic-update-slice_fusion.w_own.refs_2_), channel_id=1, source_target_pairs={{0,2},{2,0},{1,3},{3,1},{4,6},{6,4},{5,7},{7,5},{8,10},{10,8},{9,1... | collective-permute-start | bytes 3145736 | tf_op jit(solution)/shard_map/ppermute | solution.py:387
  84.9 13.6 %copy-start.10 = (f32[128,512]{1,0:T(8,128)S(1)}, f32[128,512]{1,0:T(8,128)}, u32[]{:S(2)}) copy-start(f32[128,512]{1,0:T(8,128)} %get-tuple-element.90) | copy-start | bytes 786436
  86.0 12.5 %collective-permute-start.23 = (bf16[128,512]{1,0:T(8,128)(2,1)S(1)}, bf16[128,512]{1,0:T(8,128)(2,1)S(1)}, u32[]{:S(2)}, u32[]{:S(2)}) collective-permute-start(bf16[128,512]{1,0:T(8,128)(2,1)S(1)} %add_convert_fusion.refs_0_), channel_id=1, source_target_pairs={{0,4},{4,8},{8,12},{12,0},{1,5},{5,9},{9,13},{13,1},{2,6},{6,10},{... | collective-permute-start | bytes 393224 | tf_op jit(solution)/shard_map/ppermute | solution.py:378
  88.0 13.0 %collective-permute-start.24 = (bf16[128,512]{1,0:T(8,128)(2,1)S(1)}, bf16[128,512]{1,0:T(8,128)(2,1)S(1)}, u32[]{:S(2)}, u32[]{:S(2)}) collective-permute-start(bf16[128,512]{1,0:T(8,128)(2,1)S(1)} %add_convert_fusion.refs_0_), channel_id=1, source_target_pairs={{0,8},{4,12},{8,0},{12,4},{1,9},{5,13},{9,1},{13,5},{2,10},{6,14},... | collective-permute-start | bytes 393224 | tf_op jit(solution)/shard_map/ppermute | solution.py:378
  98.5 5.0 %collective-permute-start.25 = (bf16[128,512]{1,0:T(8,128)(2,1)S(1)}, bf16[128,512]{1,0:T(8,128)(2,1)S(1)}, u32[]{:S(2)}, u32[]{:S(2)}) collective-permute-start(bf16[128,512]{1,0:T(8,128)(2,1)S(1)} %add_convert_fusion.refs_0_), channel_id=1, source_target_pairs={{0,12},{4,0},{8,4},{12,8},{1,13},{5,1},{9,5},{13,9},{2,14},{6,2},{... | collective-permute-start | bytes 393224 | tf_op jit(solution)/shard_map/ppermute | solution.py:378
  98.5 8.9 %copy-start.4 = (bf16[144,512]{1,0:T(8,128)(2,1)S(1)}, bf16[144,512]{1,0:T(8,128)(2,1)}, u32[]{:S(2)}) copy-start(bf16[144,512]{1,0:T(8,128)(2,1)} %copy-done.3) | copy-start | bytes 442372
  98.6 8.9 %copy-start.8 = (bf16[128,512]{1,0:T(8,128)(2,1)S(1)}, bf16[128,512]{1,0:T(8,128)(2,1)}, u32[]{:S(2)}) copy-start(bf16[128,512]{1,0:T(8,128)(2,1)} %copy-done.7) | copy-start | bytes 393220
  103.5 5.2 %collective-permute-start.26 = (bf16[512,512]{1,0:T(8,128)(2,1)S(1)}, bf16[512,512]{1,0:T(8,128)(2,1)S(1)}, u32[]{:S(2)}, u32[]{:S(2)}) collective-permute-start(bf16[512,512]{1,0:T(8,128)(2,1)S(1)} %pad_maximum_fusion.1.g_own), channel_id=1, source_target_pairs={{0,1},{1,0},{2,3},{3,2},{4,5},{5,4},{6,7},{7,6},{8,9},{9,8},{10,11... | collective-permute-start | bytes 1572872 | tf_op jit(solution)/shard_map/ppermute | solution.py:387
  103.5 8.3 %collective-permute-start.19 = (bf16[128,512]{1,0:T(8,128)(2,1)S(1)}, bf16[128,512]{1,0:T(8,128)(2,1)S(1)}, u32[]{:S(2)}, u32[]{:S(2)}) collective-permute-start(bf16[128,512]{1,0:T(8,128)(2,1)S(1)} %add_convert_fusion.1.refs_1_), channel_id=1, source_target_pairs={{0,4},{4,8},{8,12},{12,0},{1,5},{5,9},{9,13},{13,1},{2,6},{6,10},{... | collective-permute-start | bytes 393224 | tf_op jit(solution)/shard_map/ppermute | solution.py:378
  103.6 13.0 %collective-permute-start.20 = (bf16[128,512]{1,0:T(8,128)(2,1)S(1)}, bf16[128,512]{1,0:T(8,128)(2,1)S(1)}, u32[]{:S(2)}, u32[]{:S(2)}) collective-permute-start(bf16[128,512]{1,0:T(8,128)(2,1)S(1)} %add_convert_fusion.1.refs_1_), channel_id=1, source_target_pairs={{0,8},{4,12},{8,0},{12,4},{1,9},{5,13},{9,1},{13,5},{2,10},{6,14},... | collective-permute-start | bytes 393224 | tf_op jit(solution)/shard_map/ppermute | solution.py:378
  106.0 10.6 %collective-permute-start.21 = (bf16[128,512]{1,0:T(8,128)(2,1)S(1)}, bf16[128,512]{1,0:T(8,128)(2,1)S(1)}, u32[]{:S(2)}, u32[]{:S(2)}) collective-permute-start(bf16[128,512]{1,0:T(8,128)(2,1)S(1)} %add_convert_fusion.1.refs_1_), channel_id=1, source_target_pairs={{0,12},{4,0},{8,4},{12,8},{1,13},{5,1},{9,5},{13,9},{2,14},{6,2},{... | collective-permute-start | bytes 393224 | tf_op jit(solution)/shard_map/ppermute | solution.py:378
  109.1 8.2 %collective-permute-start.27 = (bf16[256,512]{1,0:T(8,128)(2,1)S(1)}, bf16[256,512]{1,0:T(8,128)(2,1)S(1)}, u32[]{:S(2)}, u32[]{:S(2)}) collective-permute-start(bf16[256,512]{1,0:T(8,128)(2,1)S(1)} %weight_grad.2.refs_0_), channel_id=1, source_target_pairs={{0,2},{2,0},{1,3},{3,1},{4,6},{6,4},{5,7},{7,5},{8,10},{10,8},{9,1... | collective-permute-start | bytes 786440 | tf_op jit(solution)/shard_map/ppermute | solution.py:387
  116.6 4.4 %collective-permute-start.30 = (bf16[1024,512]{1,0:T(8,128)(2,1)S(1)}, bf16[1024,512]{1,0:T(8,128)(2,1)S(1)}, u32[]{:S(2)}, u32[]{:S(2)}) collective-permute-start(bf16[1024,512]{1,0:T(8,128)(2,1)S(1)} %collective-permute-done.22.refs_4_), channel_id=1, source_target_pairs={{0,1},{1,0},{2,3},{3,2},{4,5},{5,4},{6,7},{7,6},{8,9},{9,8},{10,11... | collective-permute-start | bytes 3145736 | tf_op jit(solution)/shard_map/ppermute | solution.py:387
  117.3 2.7 %collective-permute-start.28 = (bf16[512,512]{1,0:T(8,128)(2,1)S(1)}, bf16[512,512]{1,0:T(8,128)(2,1)S(1)}, u32[]{:S(2)}, u32[]{:S(2)}) collective-permute-start(bf16[512,512]{1,0:T(8,128)(2,1)S(1)} %pad_maximum_fusion.g_own), channel_id=1, source_target_pairs={{0,1},{1,0},{2,3},{3,2},{4,5},{5,4},{6,7},{7,6},{8,9},{9,8},{10,11... | collective-permute-start | bytes 1572872 | tf_op jit(solution)/shard_map/ppermute | solution.py:387
  120.4 8.4 %collective-permute-start.29 = (bf16[256,512]{1,0:T(8,128)(2,1)S(1)}, bf16[256,512]{1,0:T(8,128)(2,1)S(1)}, u32[]{:S(2)}, u32[]{:S(2)}) collective-permute-start(bf16[256,512]{1,0:T(8,128)(2,1)S(1)} %weight_grad.3.refs_2_), channel_id=1, source_target_pairs={{0,2},{2,0},{1,3},{3,1},{4,6},{6,4},{5,7},{7,5},{8,10},{10,8},{9,1... | collective-permute-start | bytes 786440 | tf_op jit(solution)/shard_map/ppermute | solution.py:387
